TPU v7x, 128 devices: a whole 4x4x4 slice. The times are simulated.
128 devices in a mesh: seq: 16 (over y_lo, x, core), tp: 8 (over y_hi, z).
Axes of the slice: x: 4, y: 4 (y_hi: 2, y_lo: 2; y = y_hi * 2 + y_lo), z: 4, core: 2. Of those that a mesh axis runs over, the one named last changes fastest.
Arguments:
- queries: bfloat16 [8192, 6144], P('seq', 'tp'), may hold values from -6 to 6
- keys: bfloat16 [8192, 1024], P('seq', 'tp'), may hold values from -6 to 6
- values: bfloat16 [8192, 1024], P('seq', 'tp'), may hold values from -6 to 6
- segment_ids: int32 [8192], replicated, may hold values from 0 to 7, never falling along the last dimension, each value on 1 to 6144 neighbouring positions
- packing: int32 [64, 2], replicated, may hold values from 0 to 15, as said below
- out_weight: bfloat16 [6144, 12288], P('tp', 'seq'), may hold values from -0.625 to 0.625
Outputs:
- attended: bfloat16 [8192, 12288], P('seq', 'tp')
Inputs may be any that keep to these rules, and one draw needn't show every extreme that they name: `packing`: each arriving block gets a distinct packed place, so every packed shard receives exactly 4 blocks at offsets 0 to 3; the blocks of one shard go to 4 different packed shards. `segment_ids`: document ids never fall along the tokens; each document has 1 to 6144 tokens and one has exactly 6144.
All inputs are finite; a program needn't handle non-finite values.
Results may differ from a plain program's by a relative error of at most 0.015.
Values may be sent and summed in bfloat16 or wider, within the bound.
A program may use at most 128 MiB of HBM per device.

v0:
```python
import math

import jax
import jax.numpy as jnp
from jax import lax
from jax.sharding import PartitionSpec as P

HEAD_DIM = 128
WINDOW = 4096
BLOCK = 128


def passed_along(block, axis, distance):
    devices = range(lax.axis_size(axis))
    route = [(i - distance, i) for i in devices if i - distance in devices]
    return lax.ppermute(block, axis, route)


def attend_head(q_rows, k_rows, v_rows, q_pos, k_pos, q_seg, k_seg):
    scores = lax.dot_general(
        q_rows, k_rows, (((1,), (1,)), ((), ())), preferred_element_type=jnp.float32
    )
    scores = scores * (1.0 / math.sqrt(HEAD_DIM))
    allowed = (k_pos[None, :] <= q_pos[:, None]) & (k_pos[None, :] > q_pos[:, None] - WINDOW)
    allowed = allowed & (k_seg[None, :] == q_seg[:, None])
    scores = jnp.where(allowed, scores, -jnp.inf)
    top_score = jnp.max(scores, axis=1, keepdims=True)
    expo = jnp.exp(scores - top_score)
    weights = (expo / jnp.sum(expo, axis=1, keepdims=True)).astype(jnp.bfloat16)
    return jnp.dot(weights, v_rows, preferred_element_type=jnp.float32).astype(jnp.bfloat16)


def shards(queries, keys, values, segment_ids, packing, out_weight):
    tok_rows = queries.shape[0]
    q_cols = queries.shape[1]
    kv_cols = keys.shape[1]
    seq_count = lax.axis_size("seq")
    shard_index = lax.axis_index("seq")
    per_shard = tok_rows // BLOCK
    blocks_all = packing.shape[0]
    joined = jnp.concatenate([queries, keys, values], axis=1)
    row_width = joined.shape[1]
    own_blocks = joined.reshape(per_shard, BLOCK, row_width)
    own_list = lax.dynamic_slice_in_dim(packing, shard_index * per_shard, per_shard, 0)
    slot_ids = jnp.arange(seq_count, dtype=jnp.int32)
    routing = (own_list[:, 0][None, :] == slot_ids[:, None]).astype(jnp.bfloat16)
    outgoing = jnp.einsum(
        "db,brc->drc", routing, own_blocks, preferred_element_type=jnp.float32
    ).astype(jnp.bfloat16)
    incoming = lax.all_to_all(outgoing, "seq", split_axis=0, concat_axis=0, tiled=True)
    arriving = packing[:, 0] == shard_index
    offset_ids = jnp.arange(per_shard, dtype=jnp.int32)
    at_offset = ((packing[:, 1][None, :] == offset_ids[:, None]) & arriving[None, :]).astype(
        jnp.float32
    )
    senders = jnp.arange(blocks_all, dtype=jnp.int32) // per_shard
    from_sender = (senders[:, None] == slot_ids[None, :]).astype(jnp.float32)
    placing = jnp.dot(at_offset, from_sender, precision=lax.Precision.HIGHEST).astype(jnp.bfloat16)
    packed = jnp.einsum(
        "od,drc->orc", placing, incoming, preferred_element_type=jnp.float32
    ).astype(jnp.bfloat16)
    packed = packed.reshape(tok_rows, row_width)
    queries_here = packed[:, :q_cols]
    key_values = packed[:, q_cols:]
    span_shards = WINDOW // tok_rows
    earlier_pieces = []
    for distance in range(span_shards, 0, -1):
        earlier_pieces.append(passed_along(key_values, "seq", distance))
    context = jnp.concatenate(earlier_pieces + [key_values], axis=0)
    ctx_keys = context[:, :kv_cols]
    ctx_values = context[:, kv_cols:]
    ctx_rows = context.shape[0]
    q_pos = shard_index * tok_rows + jnp.arange(tok_rows, dtype=jnp.int32)
    k_pos = (shard_index - span_shards) * tok_rows + jnp.arange(ctx_rows, dtype=jnp.int32)
    padded_seg = jnp.concatenate([jnp.full((WINDOW,), -1, jnp.int32), segment_ids], axis=0)
    q_seg = lax.dynamic_slice_in_dim(segment_ids, shard_index * tok_rows, tok_rows, 0)
    k_seg = lax.dynamic_slice_in_dim(padded_seg, shard_index * tok_rows, ctx_rows, 0)
    heads_here = q_cols // HEAD_DIM

    def one_head(head_index):
        q_head = lax.dynamic_slice_in_dim(queries_here, head_index * HEAD_DIM, HEAD_DIM, 1)
        return attend_head(q_head, ctx_keys, ctx_values, q_pos, k_pos, q_seg, k_seg)

    per_head = lax.map(one_head, jnp.arange(heads_here, dtype=jnp.int32))
    attended = jnp.transpose(per_head, (1, 0, 2)).reshape(tok_rows, q_cols)
    terms = jnp.dot(
        attended,
        lax.all_gather(out_weight, "seq", axis=1, tiled=True),
        preferred_element_type=jnp.float32,
    )
    result = lax.psum_scatter(terms.astype(jnp.bfloat16), "tp", scatter_dimension=1, tiled=True)
    return result


def solution(mesh):
    in_specs = (P("seq", "tp"), P("seq", "tp"), P("seq", "tp"), P(), P(), P("tp", "seq"))
    out_specs = P("seq", "tp")
    return jax.shard_map(shards, mesh=mesh, in_specs=in_specs, out_specs=out_specs, check_vma=False)
```

profile of v0, /device:TPU:1, one launch (start us, length us, event | category | flops | bytes accessed | tf_op | source)
XLA Modules:
  0.0 414.2 jit_solution(16515502241630908779)
XLA Ops:
  6.5 0.7 all-gather.2.cloned.1.call-update
  7.3 0.8 constant_dynamic-slice_fusion
  8.0 1.4 pad_maximum_fusion
  9.4 1.8 convolution_convert_fusion.1
  11.2 4.3 %copy.14 = bf16[16,128,1024]{2,1,0:T(8,128)(2,1)} copy(bf16[16,128,1024]{2,0,1:T(8,128)(2,1)S(1)} %convolution_convert_fusion.1) | data formatting | bytes 8388608 | tf_op jit(solution)/shard_map/convert_element_type | solution.py:49
  15.6 7.0 %all-to-all-start = ((bf16[16,128,1024]{2,1,0:T(8,128)(2,1)}), bf16[16,128,1024]{2,1,0:T(8,128)(2,1)}, u32[]{:S(2)}, u32[]{:S(2)}) async-start(bf16[16,128,1024]{2,1,0:T(8,128)(2,1)} %copy.14), calls=%async_computation | async-start | bytes 8388608 | tf_op jit(solution)/shard_map/all_to_all | solution.py:50
  22.8 94.0 %all-to-all-done = bf16[16,128,1024]{2,1,0:T(8,128)(2,1)} async-done(((bf16[16,128,1024]{2,1,0:T(8,128)(2,1)}), bf16[16,128,1024]{2,1,0:T(8,128)(2,1)}, u32[]{:S(2)}, u32[]{:S(2)}) %all-to-all-start) | async-done | bytes 4194336 | tf_op jit(solution)/shard_map/all_to_all | solution.py:50
  116.8 4.8 %fusion.12 = bf16[4,128,1024]{2,0,1:T(4,128)(2,1)S(1)} fusion(bf16[4,16,1]{1,0,2:T(4,128)(2,1)S(1)} %fusion.15, bf16[16,128,1024]{2,1,0:T(8,128)(2,1)} %all-to-all-done), kind=kOutput, calls=%fused_computation.19 | convolution fusion | flops 17301504 | bytes 5243008 | tf_op jit(solution)/shard_map/od,drc->orc/dot_general | solution.py:59
  122.0 3.3 collective-permute-start
  125.3 1.3 collective-permute-start.1
  126.6 3.5 collective-permute-start.2
  130.2 2.2 collective-permute-start.3
  132.5 1.3 collective-permute-start.4
  133.9 22.7 %collective-permute-done = bf16[512,256]{1,0:T(8,128)(2,1)S(1)} collective-permute-done((bf16[512,256]{1,0:T(8,128)(2,1)S(1)}, bf16[512,256]{1,0:T(8,128)(2,1)S(1)}, u32[]{:S(2)}, u32[]{:S(2)}) %collective-permute-start) | collective-permute-done | bytes 262176 | tf_op jit(solution)/shard_map/ppermute | solution.py:16
  156.6 1.3 collective-permute-start.5
  157.9 14.9 %collective-permute-done.1 = bf16[512,256]{1,0:T(8,128)(2,1)S(1)} collective-permute-done((bf16[512,256]{1,0:T(8,128)(2,1)S(1)}, bf16[512,256]{1,0:T(8,128)(2,1)S(1)}, u32[]{:S(2)}, u32[]{:S(2)}) %collective-permute-start.1) | collective-permute-done | bytes 262176 | tf_op jit(solution)/shard_map/ppermute | solution.py:16
  172.8 1.3 collective-permute-start.6
  174.1 2.1 collective-permute-start.7
  176.4 1.0 collective-permute-done.6
  177.4 2.8 collective-permute-done.7
  180.4 52.3 %while.13 = (s32[]{:T(128)}, bf16[6,512,128]{1,2,0:T(8,128)(2,1)}, s32[4608]{0:T(1024)S(1)}, s32[512]{0:T(512)S(1)}, s32[6]{0:T(128)S(1)}, /*index=5*/bf16[512,7...) while((s32[]{:T(128)}, bf16[6,512,128]{1,2,0:T(8,128)(2,1)}, ...), condition=%wide.region_3.4_spmd.clone, body=%wide.region_0.3_spmd.clone.sunk | while | flops 1238700544 | bytes 31537868 | solution.py:84
  180.4 0.6 dynamic_slice.36
  181.7 3.0 fusion.39
  184.7 1.4 fusion.40
  186.1 2.3 fusion.41
  188.5 0.7 constant_dynamic-update-slice_fusion.11
  190.4 3.0 fusion.39
  193.4 1.4 fusion.40
  194.8 2.3 fusion.41
  197.2 0.7 constant_dynamic-update-slice_fusion.11
  199.1 3.0 fusion.39
  202.1 1.4 fusion.40
  203.5 2.3 fusion.41
  205.9 0.7 constant_dynamic-update-slice_fusion.11
  207.8 3.0 fusion.39
  210.8 1.4 fusion.40
  212.2 2.3 fusion.41
  214.6 0.7 constant_dynamic-update-slice_fusion.11
  216.6 3.0 fusion.39
  219.5 1.4 fusion.40
  220.9 2.3 fusion.41
  223.4 0.7 constant_dynamic-update-slice_fusion.11
  225.3 3.0 fusion.39
  228.3 1.4 fusion.40
  229.7 2.3 fusion.41
  232.1 0.7 constant_dynamic-update-slice_fusion.11
  232.7 16.8 %convolution_convert_fusion = bf16[512,12288]{1,0:T(8,128)(2,1)} fusion(bf16[512,768]{0,1:T(8,128)(2,1)} %bitcast.36, bf16[768,12288]{1,0:T(8,128)(2,1)} %all-gather.2.cloned.1.call-done), kind=kOutput, calls=%fused_computation.15 | convolution fusion | flops 9669967872 | bytes 32243712 | tf_op jit(solution)/shard_map/dot_general | solution.py:86
  249.6 157.8 %reduce-scatter.2.cloned.1.call-done = bf16[512,1536]{1,0:T(8,128)(2,1)} async-done(((bf16[512,12288]{1,0:T(8,128)(2,1)}), bf16[512,1536]{1,0:T(8,128)(2,1)}) %reduce-scatter.2.cloned.1.call-update) | async-done | bytes 1572880 | tf_op jit(solution)/shard_map/reduce_scatter | solution.py:91
  (57 shorter events, 4.9 us)
Async XLA Ops:
  6.5 226.2 %all-gather.2.cloned.1.call-start = ((), (), s32[]{:S(2)}) async-start(), calls=%async_computation.2 | async-start | bytes 20054016 | tf_op jit(solution)/shard_map/all_gather | solution.py:88
  15.6 7.0 %copy-start.1 = (s32[64,2]{0,1:T(2,128)S(1)}, s32[64,2]{0,1:T(2,128)}, u32[]{:S(2)}) copy-start(s32[64,2]{0,1:T(2,128)} %param.12) | copy-start | bytes 1540
  15.6 101.2 %all-to-all-start = ((bf16[16,128,1024]{2,1,0:T(8,128)(2,1)}), bf16[16,128,1024]{2,1,0:T(8,128)(2,1)}, u32[]{:S(2)}, u32[]{:S(2)}) async-start(bf16[16,128,1024]{2,1,0:T(8,128)(2,1)} %copy.14), calls=%async_computation | async-start | bytes 8388608 | tf_op jit(solution)/shard_map/all_to_all | solution.py:50
  22.5 384.9 %reduce-scatter.2.cloned.1.call-start = ((), (), s32[]{:S(2)}) async-start(), calls=%async_computation.3 | async-start | bytes 14155776 | tf_op jit(solution)/shard_map/reduce_scatter | solution.py:91
  121.6 8.4 %copy-start = (s32[8192]{0:T(1024)S(1)}, s32[8192]{0:T(1024)}, u32[]{:S(2)}) copy-start(s32[8192]{0:T(1024)} %param.11) | copy-start | bytes 98308
  122.0 34.6 %collective-permute-start = (bf16[512,256]{1,0:T(8,128)(2,1)S(1)}, bf16[512,256]{1,0:T(8,128)(2,1)S(1)}, u32[]{:S(2)}, u32[]{:S(2)}) collective-permute-start(bf16[512,256]{1,0:T(8,128)(2,1)S(1)} %slice.29), channel_id=1, source_target_pairs={{0,64},{8,72},{16,80},{24,88},{32,96},{40,104},{48,112},{56,120},{... | collective-permute-start | bytes 786440 | tf_op jit(solution)/shard_map/ppermute | solution.py:16
  125.3 47.5 %collective-permute-start.1 = (bf16[512,256]{1,0:T(8,128)(2,1)S(1)}, bf16[512,256]{1,0:T(8,128)(2,1)S(1)}, u32[]{:S(2)}, u32[]{:S(2)}) collective-permute-start(bf16[512,256]{1,0:T(8,128)(2,1)S(1)} %slice.29), channel_id=1, source_target_pairs={{0,56},{8,64},{16,72},{24,80},{32,88},{40,96},{48,104},{56,112},{6... | collective-permute-start | bytes 786440 | tf_op jit(solution)/shard_map/ppermute | solution.py:16
  126.6 47.5 %collective-permute-start.2 = (bf16[512,256]{1,0:T(8,128)(2,1)S(1)}, bf16[512,256]{1,0:T(8,128)(2,1)S(1)}, u32[]{:S(2)}, u32[]{:S(2)}) collective-permute-start(bf16[512,256]{1,0:T(8,128)(2,1)S(1)} %slice.29), channel_id=1, source_target_pairs={{0,48},{8,56},{16,64},{24,72},{32,80},{40,88},{48,96},{56,104},{64... | collective-permute-start | bytes 786440 | tf_op jit(solution)/shard_map/ppermute | solution.py:16
  130.2 46.0 %collective-permute-start.3 = (bf16[512,256]{1,0:T(8,128)(2,1)S(1)}, bf16[512,256]{1,0:T(8,128)(2,1)S(1)}, u32[]{:S(2)}, u32[]{:S(2)}) collective-permute-start(bf16[512,256]{1,0:T(8,128)(2,1)S(1)} %slice.29), channel_id=1, source_target_pairs={{0,40},{8,48},{16,56},{24,64},{32,72},{40,80},{48,88},{56,96},{64,... | collective-permute-start | bytes 786440 | tf_op jit(solution)/shard_map/ppermute | solution.py:16
  132.5 43.8 %collective-permute-start.4 = (bf16[512,256]{1,0:T(8,128)(2,1)S(1)}, bf16[512,256]{1,0:T(8,128)(2,1)S(1)}, u32[]{:S(2)}, u32[]{:S(2)}) collective-permute-start(bf16[512,256]{1,0:T(8,128)(2,1)S(1)} %slice.29), channel_id=1, source_target_pairs={{0,32},{8,40},{16,48},{24,56},{32,64},{40,72},{48,80},{56,88},{64,... | collective-permute-start | bytes 786440 | tf_op jit(solution)/shard_map/ppermute | solution.py:16
  156.6 19.8 %collective-permute-start.5 = (bf16[512,256]{1,0:T(8,128)(2,1)S(1)}, bf16[512,256]{1,0:T(8,128)(2,1)S(1)}, u32[]{:S(2)}, u32[]{:S(2)}) collective-permute-start(bf16[512,256]{1,0:T(8,128)(2,1)S(1)} %slice.29), channel_id=1, source_target_pairs={{0,24},{8,32},{16,40},{24,48},{32,56},{40,64},{48,72},{56,80},{64,... | collective-permute-start | bytes 786440 | tf_op jit(solution)/shard_map/ppermute | solution.py:16
  172.8 4.6 %collective-permute-start.6 = (bf16[512,256]{1,0:T(8,128)(2,1)S(1)}, bf16[512,256]{1,0:T(8,128)(2,1)S(1)}, u32[]{:S(2)}, u32[]{:S(2)}) collective-permute-start(bf16[512,256]{1,0:T(8,128)(2,1)S(1)} %slice.29), channel_id=1, source_target_pairs={{0,16},{8,24},{16,32},{24,40},{32,48},{40,56},{48,64},{56,72},{64,... | collective-permute-start | bytes 786440 | tf_op jit(solution)/shard_map/ppermute | solution.py:16
  174.1 6.1 %collective-permute-start.7 = (bf16[512,256]{1,0:T(8,128)(2,1)S(1)}, bf16[512,256]{1,0:T(8,128)(2,1)S(1)}, u32[]{:S(2)}, u32[]{:S(2)}) collective-permute-start(bf16[512,256]{1,0:T(8,128)(2,1)S(1)} %slice.29), channel_id=1, source_target_pairs={{0,8},{8,16},{16,24},{24,32},{32,40},{40,48},{48,56},{56,64},{64,7... | collective-permute-start | bytes 786440 | tf_op jit(solution)/shard_map/ppermute | solution.py:16
Sparse Core Ops, SparseCore 0:
  9.0 187.6 all-gather.1
  249.7 157.6 reduce-scatter.1
where the time goes:
time: 415 us; the launch traced here: 414 us
  waiting for transfers between devices  294 us (71%)
  matrix products  55.1 us (13%)
  starting transfers between devices  23.2 us (6%)
  local copies, waits for them, and re-layouts  14.3 us (3%)
  between operations  13.7 us (3%)
  other arithmetic  9.95 us (2%)
    reduce_scatter x1, waiting for transfers between devices, shards(): lax.psum_scatter(terms.astype(jnp.bfloat16), 'tp', scatter_dimension=1, t...  158 us
    all_to_all x1, waiting for transfers between devices, shards(): lax.all_to_all(outgoing, 'seq', split_axis=0, concat_axis=0, tiled=True)  94 us
    ppermute x8, waiting for transfers between devices, passed_along(): return lax.ppermute(block, axis, route)  41.4 us
    dot_general x6, matrix products, attend_head(): lax.dot_general(q_rows, k_rows, (((1,), (1,)), ((), ())), preferred_eleme...  17.8 us
    dot_general x1, matrix products, shards(): jnp.dot(attended, lax.all_gather(out_weight, 'seq', axis=1, tiled=True),...  16.8 us
    ppermute x8, starting transfers between devices, passed_along(): return lax.ppermute(block, axis, route)  16.2 us
    dot_general x6, matrix products, attend_head(): jnp.dot(weights, v_rows, preferred_element_type=jnp.float32)  13.7 us
    reduce_sum x6, other arithmetic, attend_head(): weights = (expo / jnp.sum(expo, axis=1, keepdims=True)).astype(jnp.bfloat16)  8.47 us
  transfers between devices with their start and end apart: 11, of which 6 were waited for; matrix products, arithmetic and copies ran while one was open for 15% of the time, Pallas kernels for 0%

commit v1 on v0

v1 whole, which is shorter than its diff:
```python
import functools
import math

import jax
import jax.numpy as jnp
from jax import lax
from jax.sharding import Mesh, PartitionSpec as P

HEAD_DIM = 128
WINDOW = 4096
BLOCK = 128
SEQ = ("ylo", "x", "c")
TP = ("yhi", "z")


def attend_head(q_rows, k_rows, v_rows, q_pos, k_pos, q_seg, k_seg):
    scores = lax.dot_general(
        q_rows, k_rows, (((1,), (1,)), ((), ())), preferred_element_type=jnp.float32
    )
    scores = scores * (1.0 / math.sqrt(HEAD_DIM))
    allowed = (k_pos[None, :] <= q_pos[:, None]) & (k_pos[None, :] > q_pos[:, None] - WINDOW)
    allowed = allowed & (k_seg[None, :] == q_seg[:, None])
    scores = jnp.where(allowed, scores, -jnp.inf)
    top_score = jnp.max(scores, axis=1, keepdims=True)
    expo = jnp.exp(scores - top_score)
    weights = (expo / jnp.sum(expo, axis=1, keepdims=True)).astype(jnp.bfloat16)
    return jnp.dot(weights, v_rows, preferred_element_type=jnp.float32).astype(jnp.bfloat16)


def shards(seq_count, queries, keys, values, segment_ids, packing, out_weight):
    tok_rows = queries.shape[0]
    q_cols = queries.shape[1]
    kv_cols = keys.shape[1]
    shard_index = lax.axis_index(SEQ)
    per_shard = tok_rows // BLOCK
    blocks_all = packing.shape[0]

    kv_local = jnp.concatenate([keys, values], axis=1)
    kv_all = lax.all_gather(kv_local, SEQ, axis=0, tiled=True)
    kv_blocks = kv_all.reshape(blocks_all, BLOCK, 2 * kv_cols)
    target = packing[:, 0] * per_shard + packing[:, 1]
    source = jnp.zeros((blocks_all,), jnp.int32).at[target].set(
        jnp.arange(blocks_all, dtype=jnp.int32)
    )
    span_blocks = WINDOW // BLOCK
    ctx_blocks = span_blocks + per_shard
    blk_ids = shard_index * per_shard - span_blocks + jnp.arange(ctx_blocks, dtype=jnp.int32)
    src = jnp.take(source, jnp.clip(blk_ids, 0, blocks_all - 1))
    context = jnp.take(kv_blocks, src, axis=0).reshape(ctx_blocks * BLOCK, 2 * kv_cols)

    own_blocks = queries.reshape(per_shard, BLOCK, q_cols)
    own_list = lax.dynamic_slice_in_dim(packing, shard_index * per_shard, per_shard, 0)
    slot_ids = jnp.arange(seq_count, dtype=jnp.int32)
    routing = (own_list[:, 0][None, :] == slot_ids[:, None]).astype(jnp.bfloat16)
    outgoing = jnp.einsum(
        "db,brc->drc", routing, own_blocks, preferred_element_type=jnp.float32
    ).astype(jnp.bfloat16)
    incoming = lax.all_to_all(outgoing, SEQ, split_axis=0, concat_axis=0, tiled=True)
    arriving = packing[:, 0] == shard_index
    offset_ids = jnp.arange(per_shard, dtype=jnp.int32)
    at_offset = ((packing[:, 1][None, :] == offset_ids[:, None]) & arriving[None, :]).astype(
        jnp.float32
    )
    senders = jnp.arange(blocks_all, dtype=jnp.int32) // per_shard
    from_sender = (senders[:, None] == slot_ids[None, :]).astype(jnp.float32)
    placing = jnp.dot(at_offset, from_sender, precision=lax.Precision.HIGHEST).astype(jnp.bfloat16)
    packed = jnp.einsum(
        "od,drc->orc", placing, incoming, preferred_element_type=jnp.float32
    ).astype(jnp.bfloat16)
    queries_here = packed.reshape(tok_rows, q_cols)

    w_swapped = lax.ppermute(out_weight, ("ylo", "yhi"), perm=[(0, 0), (1, 2), (2, 1), (3, 3)])
    w_cols = lax.all_gather(w_swapped, "x", axis=1, tiled=True)
    w_here = lax.all_gather(w_cols, "ylo", axis=0, tiled=True)
    context, w_here = lax.optimization_barrier((context, w_here))

    ctx_keys = context[:, :kv_cols]
    ctx_values = context[:, kv_cols:]
    ctx_rows = context.shape[0]
    q_pos = shard_index * tok_rows + jnp.arange(tok_rows, dtype=jnp.int32)
    k_pos = shard_index * tok_rows - WINDOW + jnp.arange(ctx_rows, dtype=jnp.int32)
    padded_seg = jnp.concatenate([jnp.full((WINDOW,), -1, jnp.int32), segment_ids], axis=0)
    q_seg = lax.dynamic_slice_in_dim(segment_ids, shard_index * tok_rows, tok_rows, 0)
    k_seg = lax.dynamic_slice_in_dim(padded_seg, shard_index * tok_rows, ctx_rows, 0)
    heads_here = q_cols // HEAD_DIM

    def one_head(head_index):
        q_head = lax.dynamic_slice_in_dim(queries_here, head_index * HEAD_DIM, HEAD_DIM, 1)
        return attend_head(q_head, ctx_keys, ctx_values, q_pos, k_pos, q_seg, k_seg)

    per_head = lax.map(one_head, jnp.arange(heads_here, dtype=jnp.int32))
    attended = jnp.transpose(per_head, (1, 0, 2)).reshape(tok_rows, q_cols)

    h_groups = lax.all_gather(attended, "yhi", axis=1, tiled=True)
    h_here = lax.all_gather(h_groups, "c", axis=0, tiled=True)
    part = jnp.dot(h_here, w_here, preferred_element_type=jnp.float32).astype(jnp.bfloat16)
    summed = lax.psum_scatter(part, "z", scatter_dimension=1, tiled=True)
    swapped = lax.all_to_all(summed, "c", split_axis=0, concat_axis=0, tiled=True)
    return jnp.concatenate([swapped[:tok_rows], swapped[tok_rows:]], axis=1)


def solution(mesh):
    seq_count, tp_count = mesh.devices.shape
    fine = Mesh(mesh.devices.reshape(2, seq_count // 4, 2, 2, tp_count // 2), SEQ + TP)
    in_specs = (P(SEQ, TP), P(SEQ, TP), P(SEQ, TP), P(), P(), P(TP, SEQ))
    out_specs = P(SEQ, TP)
    return jax.shard_map(
        functools.partial(shards, seq_count),
        mesh=fine,
        in_specs=in_specs,
        out_specs=out_specs,
        check_vma=False,
    )
```

time: 415 us -> 491 us (1.18)
  waiting for transfers between devices: 294 us -> 365 us
  starting transfers between devices: 23.2 us -> 7.67 us
  local copies, waits for them, and re-layouts: 14.3 us -> 21.2 us
  blocking collectives: 0 us -> 6.54 us
  other arithmetic: 9.95 us -> 15.4 us
    all_gather x1 -> x5, waiting for transfers between devices: 0.01 us -> 252 us  [the longest x1 114 us: shards(): w_here = lax.all_gather(w_cols, 'ylo', axis=0, tiled=True)]
    reduce_scatter x1, waiting for transfers between devices: 158 us -> 65.3 us  [shards(): summed = lax.psum_scatter(part, 'z', scatter_dimension=1, tiled=True)]
    all_to_all x1, waiting for transfers between devices: 94 us -> 48.2 us  [shards(): lax.all_to_all(outgoing, SEQ, split_axis=0, concat_axis=0, tiled=True)]
    ppermute x8 -> x1, waiting for transfers between devices: 41.4 us -> 0.01 us  [shards(): lax.ppermute(out_weight, ('ylo', 'yhi'), perm=[(0, 0), (1, 2), (2, 1), (3...]
    ppermute x8 -> x1, starting transfers between devices: 16.2 us -> 2.05 us  [shards(): lax.ppermute(out_weight, ('ylo', 'yhi'), perm=[(0, 0), (1, 2), (2, 1), (3...]
    dot_general x6, matrix products: 17.8 us -> 25.4 us  [attend_head(): lax.dot_general(q_rows, k_rows, (((1,), (1,)), ((), ())), preferred_eleme...]
    all_to_all x0 -> x1, blocking collectives: none -> 6.54 us  [shards(): lax.all_to_all(summed, 'c', split_axis=0, concat_axis=0, tiled=True)]
    gather x0 -> x2, local copies, waits for them, and re-layouts: none -> 5.21 us  [the longest x1 4.43 us: shards(): jnp.take(kv_blocks, src, axis=0).reshape(ctx_blocks * BLOCK, 2 * kv_cols)]
  transfers between devices with their start and end apart: 11 -> 8, of which waited for: 6 -> 7; matrix products, arithmetic and copies ran while one was open for 15% -> 4% of each run, Pallas kernels for 0% -> 0%
where the time goes in v1:
time: 491 us
  waiting for transfers between devices  365 us (74%)
  matrix products  57.6 us (12%)
  local copies, waits for them, and re-layouts  21.2 us (4%)
  other arithmetic  15.4 us (3%)
  between operations  13.6 us (3%)
  starting transfers between devices  7.67 us (2%)
  blocking collectives  6.54 us (1%)
    all_gather x1, waiting for transfers between devices, shards(): w_here = lax.all_gather(w_cols, 'ylo', axis=0, tiled=True)  114 us
    all_gather x1, waiting for transfers between devices, shards(): w_cols = lax.all_gather(w_swapped, 'x', axis=1, tiled=True)  82 us
    reduce_scatter x1, waiting for transfers between devices, shards(): summed = lax.psum_scatter(part, 'z', scatter_dimension=1, tiled=True)  65.3 us
    all_to_all x1, waiting for transfers between devices, shards(): lax.all_to_all(outgoing, SEQ, split_axis=0, concat_axis=0, tiled=True)  48.2 us
    all_gather x1, waiting for transfers between devices, shards(): h_groups = lax.all_gather(attended, 'yhi', axis=1, tiled=True)  32.3 us
    dot_general x6, matrix products, attend_head(): lax.dot_general(q_rows, k_rows, (((1,), (1,)), ((), ())), preferred_eleme...  25.4 us
    all_gather x1, waiting for transfers between devices, shards(): h_here = lax.all_gather(h_groups, 'c', axis=0, tiled=True)  15.9 us
    dot_general x1, matrix products, shards(): jnp.dot(h_here, w_here, preferred_element_type=jnp.float32)  15.3 us
  transfers between devices with their start and end apart: 8, of which 7 were waited for; matrix products, arithmetic and copies ran while one was open for 4% of the time, Pallas kernels for 0%

profile of v1, /device:TPU:1, one launch (start us, length us, event | category | flops | bytes accessed | tf_op | source)
XLA Modules:
  0.0 490.7 jit_solution(2651547205642408613)
XLA Ops:
  6.5 2.0 collective-permute-start
  8.6 1.0 copy-done.2
  9.7 1.7 pad_maximum_fusion.1
  11.5 82.0 %all-gather.8.cloned.1.call-done = bf16[768,3072]{1,0:T(8,128)(2,1)} async-done(((bf16[768,768]{1,0:T(8,128)(2,1)}), bf16[768,3072]{1,0:T(8,128)(2,1)}) %all-gather.8.cloned.1.call-update) | async-done | bytes 4718608 | tf_op jit(solution)/shard_map/all_gather | solution.py:73
  93.6 1.5 convolution_convert_fusion.1
  95.0 2.7 copy.10
  97.7 5.2 %all-to-all-start = ((bf16[16,128,768]{2,1,0:T(8,128)(2,1)}), bf16[16,128,768]{2,1,0:T(8,128)(2,1)S(1)}, u32[]{:S(2)}, u32[]{:S(2)}) async-start(bf16[16,128,768]{2,1,0:T(8,128)(2,1)} %copy.10), calls=%async_computation | async-start | bytes 6291456 | tf_op jit(solution)/shard_map/all_to_all | solution.py:58
  103.0 1.0 scatter_custom_fusion
  104.0 0.8 gather_fusion
  104.9 0.7 pad_dynamic-slice_fusion
  105.9 48.2 %all-to-all-done = bf16[16,128,768]{2,1,0:T(8,128)(2,1)S(1)} async-done(((bf16[16,128,768]{2,1,0:T(8,128)(2,1)}), bf16[16,128,768]{2,1,0:T(8,128)(2,1)S(1)}, u32[]{:S(2)}, u32[]{:S(2)}) %all-to-all-start) | async-done | bytes 3145760 | tf_op jit(solution)/shard_map/all_to_all | solution.py:58
  154.0 1.9 fusion.12
  156.0 1.0 copy.12
  156.9 7.8 %all-gather.6.cloned.1.call-done = bf16[8192,256]{1,0:T(8,128)(2,1)} async-done(((bf16[512,256]{1,0:T(8,128)(2,1)}), bf16[8192,256]{1,0:T(8,128)(2,1)}) %all-gather.6.cloned.1.call-update) | async-done | bytes 4194320 | tf_op jit(solution)/shard_map/all_gather | solution.py:39
  164.7 4.4 gather_fusion.1
  169.1 3.8 bitcast_select_fusion
  173.0 113.7 %all-gather.10.cloned.1.call-done = bf16[1536,3072]{1,0:T(8,128)(2,1)} async-done(((bf16[768,3072]{1,0:T(8,128)(2,1)}), bf16[1536,3072]{1,0:T(8,128)(2,1)}) %all-gather.10.cloned.1.call-update) | async-done | bytes 9437200 | tf_op jit(solution)/shard_map/all_gather | solution.py:74
  286.6 1.2 fusion.31
  287.8 59.0 %while.13 = (s32[]{:T(128)}, bf16[6,512,128]{1,2,0:T(8,128)(2,1)}, s32[4608]{0:T(1024)}, s32[512]{0:T(512)S(1)}, s32[6]{0:T(128)S(1)}, /*index=5*/bf16[512,768]{...) while((s32[]{:T(128)}, bf16[6,512,128]{1,2,0:T(8,128)(2,1)}, ...), condition=%wide.region_4.5_spmd.clone, body=%wide.region_1.0_spmd.clone.sunk | while | flops 1238700544 | bytes 31535820 | solution.py:91
  289.0 4.2 fusion.44
  293.2 1.4 fusion.45
  294.6 2.2 fusion.46
  297.0 0.7 constant_dynamic-update-slice_fusion.2
  298.8 4.2 fusion.44
  303.0 1.4 fusion.45
  304.4 2.2 fusion.46
  306.8 0.7 constant_dynamic-update-slice_fusion.2
  308.6 4.2 fusion.44
  312.9 1.4 fusion.45
  314.3 2.2 fusion.46
  318.5 4.2 fusion.44
  322.7 1.4 fusion.45
  324.1 2.2 fusion.46
  326.4 0.7 constant_dynamic-update-slice_fusion.2
  328.3 4.2 fusion.44
  332.5 1.4 fusion.45
  333.9 2.2 fusion.46
  336.3 0.7 constant_dynamic-update-slice_fusion.2
  338.1 4.2 fusion.44
  342.3 1.4 fusion.45
  343.8 2.2 fusion.46
  346.1 0.7 constant_dynamic-update-slice_fusion.2
  346.8 32.3 %all-gather.12.cloned.1.call-done = bf16[512,1536]{0,1:T(8,128)(2,1)} async-done(((bf16[512,768]{0,1:T(8,128)(2,1)}), bf16[512,1536]{0,1:T(8,128)(2,1)}) %all-gather.12.cloned.1.call-update) | async-done | bytes 1572880 | tf_op jit(solution)/shard_map/all_gather | solution.py:94
  379.5 15.9 %all-gather.14.cloned.1.call-done = bf16[1024,1536]{0,1:T(8,128)(2,1)} async-done(((bf16[512,1536]{0,1:T(8,128)(2,1)}), bf16[1024,1536]{0,1:T(8,128)(2,1)}) %all-gather.14.cloned.1.call-update) | async-done | bytes 3145744 | tf_op jit(solution)/shard_map/all_gather | solution.py:95
  395.4 15.3 %convolution_convert_fusion = bf16[1024,3072]{1,0:T(8,128)(2,1)} fusion(bf16[1024,1536]{0,1:T(8,128)(2,1)} %all-gather.14.cloned.1.call-done, bf16[1536,3072]{1,0:T(8,128)(2,1)} %all-gather.10.cloned.1.call-done), kind=kOutput, calls=%fused_computation.18 | convolution fusion | flops 9666822144 | bytes 18874368 | tf_op jit(solution)/shard_map/dot_general | solution.py:96
  410.7 65.3 %reduce-scatter.2.cloned.1.call-done = bf16[1024,768]{1,0:T(8,128)(2,1)} async-done(((bf16[1024,3072]{1,0:T(8,128)(2,1)}), bf16[1024,768]{1,0:T(8,128)(2,1)}) %reduce-scatter.2.cloned.1.call-update) | async-done | bytes 1572880 | tf_op jit(solution)/shard_map/reduce_scatter | solution.py:97
  476.0 6.5 %all_to_all.14 = bf16[2,512,768]{2,1,0:T(8,128)(2,1)S(1)} all-to-all(bf16[2,512,768]{2,1,0:T(8,128)(2,1)} %bitcast.53), channel_id=1, replica_groups=mesh['ylo'=2,'x'=4,'c'=2,'yhi'=2,'z'=4] {'c'}, dimensions={0} | all-to-all | bytes 3145728 | tf_op jit(solution)/shard_map/all_to_all | solution.py:98
  482.6 1.3 pad_maximum_fusion
  (64 shorter events, 6.0 us)
Async XLA Ops:
  6.5 87.0 %copy-start = (bf16[512,768]{1,0:T(8,128)(2,1)S(1)}, bf16[512,768]{1,0:T(8,128)(2,1)}, u32[]{:S(2)}) copy-start(bf16[512,768]{1,0:T(8,128)(2,1)} %param.8) | copy-start | bytes 2359300
  6.5 86.9 %all-gather.8.cloned.1.call-start = ((), (), s32[]{:S(2)}) async-start(), calls=%async_computation.4 | async-start | bytes 5898240 | tf_op jit(solution)/shard_map/all_gather | solution.py:73
  6.5 2.1 collective-permute-start
  8.6 1.0 copy-start.2
  8.6 84.9 %copy-start.4 = (s32[64,2]{0,1:T(2,128)S(1)}, s32[64,2]{0,1:T(2,128)}, u32[]{:S(2)}) copy-start(s32[64,2]{0,1:T(2,128)} %param.12) | copy-start | bytes 1540
  9.6 155.1 %all-gather.6.cloned.1.call-start = ((), (), s32[]{:S(2)}) async-start(), calls=%async_computation.3 | async-start | bytes 4456448 | tf_op jit(solution)/shard_map/all_gather | solution.py:39
  11.4 275.2 %all-gather.10.cloned.1.call-start = ((), (), s32[]{:S(2)}) async-start(), calls=%async_computation.5 | async-start | bytes 14155776 | tf_op jit(solution)/shard_map/all_gather | solution.py:74
  97.7 7.1 %copy-start.3 = (s32[8192]{0:T(1024)S(1)}, s32[8192]{0:T(1024)}, u32[]{:S(2)}) copy-start(s32[8192]{0:T(1024)} %param.11) | copy-start | bytes 98308
  97.7 56.3 %all-to-all-start = ((bf16[16,128,768]{2,1,0:T(8,128)(2,1)}), bf16[16,128,768]{2,1,0:T(8,128)(2,1)S(1)}, u32[]{:S(2)}, u32[]{:S(2)}) async-start(bf16[16,128,768]{2,1,0:T(8,128)(2,1)} %copy.10), calls=%async_computation | async-start | bytes 6291456 | tf_op jit(solution)/shard_map/all_to_all | solution.py:58
  102.9 276.2 %all-gather.12.cloned.1.call-start = ((), (), s32[]{:S(2)}) async-start(), calls=%async_computation.6 | async-start | bytes 2359296 | tf_op jit(solution)/shard_map/all_gather | solution.py:94
  346.8 48.6 %all-gather.14.cloned.1.call-start = ((), (), s32[]{:S(2)}) async-start(), calls=%async_computation.7 | async-start | bytes 4718592 | tf_op jit(solution)/shard_map/all_gather | solution.py:95
  379.2 96.8 %reduce-scatter.2.cloned.1.call-start = ((), (), s32[]{:S(2)}) async-start(), calls=%async_computation.8 | async-start | bytes 7864320 | tf_op jit(solution)/shard_map/reduce_scatter | solution.py:97
  476.0 7.9 %copy-start.1 = (bf16[512,768]{1,0:T(8,128)(2,1)S(1)}, bf16[512,768]{1,0:T(8,128)(2,1)}, u32[]{:S(2)}) copy-start(bf16[512,768]{1,0:T(8,128)(2,1)} %param.8) | copy-start | bytes 2359300
Sparse Core Ops, SparseCore 0:
  9.8 83.6 all-gather.7
  95.1 69.5 all-gather.5
  166.4 120.2 all-gather.9
  346.9 32.2 all-gather.11
  380.7 14.6 all-gather.13
  410.8 65.1 reduce-scatter.1

commit v2 on v1

--- a/solution.py
+++ b/solution.py
@@ -70,9 +70,11 @@
     queries_here = packed.reshape(tok_rows, q_cols)
 
     w_swapped = lax.ppermute(out_weight, ("ylo", "yhi"), perm=[(0, 0), (1, 2), (2, 1), (3, 3)])
-    w_cols = lax.all_gather(w_swapped, "x", axis=1, tiled=True)
-    w_here = lax.all_gather(w_cols, "ylo", axis=0, tiled=True)
-    context, w_here = lax.optimization_barrier((context, w_here))
+    context, w_swapped = lax.optimization_barrier((context, w_swapped))
+    w_stack = lax.all_gather(w_swapped, ("ylo", "x"), axis=0, tiled=False)
+    w_rows, w_cols = out_weight.shape
+    w_here = w_stack.reshape(2, -1, w_rows, w_cols).transpose(0, 2, 1, 3)
+    w_here = w_here.reshape(2 * w_rows, -1)
 
     ctx_keys = context[:, :kv_cols]
     ctx_values = context[:, kv_cols:]
@@ -91,8 +93,21 @@
     per_head = lax.map(one_head, jnp.arange(heads_here, dtype=jnp.int32))
     attended = jnp.transpose(per_head, (1, 0, 2)).reshape(tok_rows, q_cols)
 
-    h_groups = lax.all_gather(attended, "yhi", axis=1, tiled=True)
-    h_here = lax.all_gather(h_groups, "c", axis=0, tiled=True)
+    pair = [(0, 1), (1, 0)]
+    h_far = lax.ppermute(attended, "yhi", pair)
+    low_hi = lax.axis_index("yhi") == 0
+    h_groups = jnp.where(
+        low_hi,
+        jnp.concatenate([attended, h_far], axis=1),
+        jnp.concatenate([h_far, attended], axis=1),
+    )
+    h_near = lax.ppermute(h_groups, "c", pair)
+    low_core = lax.axis_index("c") == 0
+    h_here = jnp.where(
+        low_core,
+        jnp.concatenate([h_groups, h_near], axis=0),
+        jnp.concatenate([h_near, h_groups], axis=0),
+    )
     part = jnp.dot(h_here, w_here, preferred_element_type=jnp.float32).astype(jnp.bfloat16)
     summed = lax.psum_scatter(part, "z", scatter_dimension=1, tiled=True)
     swapped = lax.all_to_all(summed, "c", split_axis=0, concat_axis=0, tiled=True)

time: 491 us -> 331 us (0.67)
  waiting for transfers between devices: 365 us -> 162 us
  local copies, waits for them, and re-layouts: 21.2 us -> 43.1 us
  starting transfers between devices: 7.67 us -> 21.2 us
    all_gather x4 -> x1, waiting for transfers between devices: 244 us -> 0.01 us  [shards(): w_stack = lax.all_gather(w_swapped, ('ylo', 'x'), axis=0, tiled=False)]
    ppermute x0 -> x2, waiting for transfers between devices: none -> 57.5 us  [the longest x1 57.5 us: shards(): h_far = lax.ppermute(attended, 'yhi', pair)]
    reshape x0 -> x1, local copies, waits for them, and re-layouts: none -> 12.4 us  [shards(): w_here = w_stack.reshape(2, -1, w_rows, w_cols).transpose(0, 2, 1, 3)]
    all_to_all x1, waiting for transfers between devices: 48.2 us -> 39.5 us  [shards(): lax.all_to_all(outgoing, SEQ, split_axis=0, concat_axis=0, tiled=True)]
    unnamed x10 -> x9, local copies, waits for them, and re-layouts: 1.03 us -> 9.58 us
    ppermute x1, starting transfers between devices: 2.05 us -> 10.4 us  [shards(): lax.ppermute(out_weight, ('ylo', 'yhi'), perm=[(0, 0), (1, 2), (2, 1), (3...]
  transfers between devices with their start and end apart: 8 -> 7, of which waited for: 7 -> 4; matrix products, arithmetic and copies ran while one was open for 4% -> 30% of each run, Pallas kernels for 0% -> 0%
where the time goes in v2:
time: 331 us; the launch traced here: 330 us
  waiting for transfers between devices  162 us (49%)
  matrix products  61.5 us (19%)
  local copies, waits for them, and re-layouts  43.1 us (13%)
  starting transfers between devices  21.2 us (6%)
  other arithmetic  17.4 us (5%)
  between operations  13.2 us (4%)
  blocking collectives  6.53 us (2%)
  loops' own time  4.42 us (1%)
    reduce_scatter x1, waiting for transfers between devices, shards(): summed = lax.psum_scatter(part, 'z', scatter_dimension=1, tiled=True)  60.8 us
    ppermute x1, waiting for transfers between devices, shards(): h_far = lax.ppermute(attended, 'yhi', pair)  57.5 us
    all_to_all x1, waiting for transfers between devices, shards(): lax.all_to_all(outgoing, SEQ, split_axis=0, concat_axis=0, tiled=True)  39.5 us
    dot_general x6, matrix products, attend_head(): lax.dot_general(q_rows, k_rows, (((1,), (1,)), ((), ())), preferred_eleme...  25.9 us
    dot_general x1, matrix products, shards(): jnp.dot(h_here, w_here, preferred_element_type=jnp.float32)  16.7 us
    dot_general x6, matrix products, attend_head(): jnp.dot(weights, v_rows, preferred_element_type=jnp.float32)  13.3 us
    reshape x1, local copies, waits for them, and re-layouts, shards(): w_here = w_stack.reshape(2, -1, w_rows, w_cols).transpose(0, 2, 1, 3)  12.4 us
    ppermute x1, starting transfers between devices, shards(): lax.ppermute(out_weight, ('ylo', 'yhi'), perm=[(0, 0), (1, 2), (2, 1), (3...  10.4 us
  transfers between devices with their start and end apart: 7, of which 4 were waited for; matrix products, arithmetic and copies ran while one was open for 30% of the time, Pallas kernels for 0%

profile of v2, /device:TPU:1, one launch (start us, length us, event | category | flops | bytes accessed | tf_op | source)
XLA Modules:
  0.0 329.6 jit_solution(9110586054742099660)
XLA Ops:
  6.5 1.8 pad_maximum_fusion.1
  8.3 0.8 constant_dynamic-slice_fusion
  9.1 1.5 convolution_convert_fusion.1
  10.6 2.7 copy.11
  13.3 7.0 %all-to-all-start = ((bf16[16,128,768]{2,1,0:T(8,128)(2,1)}), bf16[16,128,768]{2,1,0:T(8,128)(2,1)}, u32[]{:S(2)}, u32[]{:S(2)}) async-start(bf16[16,128,768]{2,1,0:T(8,128)(2,1)} %copy.11), calls=%async_computation | async-start | bytes 6291456 | tf_op jit(solution)/shard_map/all_to_all | solution.py:58
  20.4 10.4 %collective-permute-start = (bf16[768,768]{1,0:T(8,128)(2,1)}, bf16[768,768]{1,0:T(8,128)(2,1)}, u32[]{:S(2)}, u32[]{:S(2)}) collective-permute-start(bf16[768,768]{1,0:T(8,128)(2,1)} %param.13), channel_id=1, source_target_pairs={{0,0},{4,64},{64,4},{68,68},{1,1},{5,65},{65,5},{69,69},{2,2},{6,6... | collective-permute-start | bytes 3538952 | tf_op jit(solution)/shard_map/ppermute | solution.py:72
  30.8 0.8 scatter_custom_fusion
  31.6 0.8 gather_fusion
  32.9 39.5 %all-to-all-done = bf16[16,128,768]{2,1,0:T(8,128)(2,1)} async-done(((bf16[16,128,768]{2,1,0:T(8,128)(2,1)}), bf16[16,128,768]{2,1,0:T(8,128)(2,1)}, u32[]{:S(2)}, u32[]{:S(2)}) %all-to-all-start) | async-done | bytes 3145760 | tf_op jit(solution)/shard_map/all_to_all | solution.py:58
  72.4 3.9 %fusion.18 = bf16[4,128,768]{2,0,1:T(4,128)(2,1)S(1)} fusion(bf16[4,16,1]{1,0,2:T(4,128)(2,1)S(1)} %fusion.21, bf16[16,128,768]{2,1,0:T(8,128)(2,1)} %all-to-all-done), kind=kOutput, calls=%fused_computation.32 | convolution fusion | flops 12976128 | bytes 3932288 | tf_op jit(solution)/shard_map/od,drc->orc/dot_general | solution.py:67
  76.3 1.0 copy.13
  77.3 4.4 %all-gather.4.cloned.1.call-done = bf16[8192,256]{1,0:T(8,128)(2,1)} async-done(((bf16[512,256]{1,0:T(8,128)(2,1)}), bf16[8192,256]{1,0:T(8,128)(2,1)}) %all-gather.4.cloned.1.call-update) | async-done | bytes 4194320 | tf_op jit(solution)/shard_map/all_gather | solution.py:39
  81.7 4.5 %gather_fusion.1 = bf16[36,128,256]{2,1,0:T(8,128)(2,1)} fusion(bf16[64,128,256]{2,1,0:T(8,128)(2,1)} %bitcast.61, s32[1024]{0:T(1024)S(1)} %pad_clamp_fusion), kind=kCustom, calls=%fused_computation.1 | custom fusion | bytes 4718736 | tf_op jit(solution)/shard_map/jit(_take)/gather | solution.py:49
  86.2 3.8 %bitcast_select_fusion = bf16[4608,256]{1,0:T(8,128)(2,1)S(1)} fusion(bf16[36,128,256]{2,1,0:T(8,128)(2,1)} %gather_fusion.1, pred[4608]{0:T(1024)(128)(4,1)S(1)} %broadcast_bitcast_fusion), kind=kLoop, calls=%fused_computation.28 | loop fusion | flops 1179648 | bytes 4723200 | tf_op jit(solution)/shard_map/jit(_take)/select_n | solution.py:49
  90.1 1.6 fusion.38
  92.0 60.8 %while.13 = (s32[]{:T(128)}, bf16[6,512,128]{1,2,0:T(8,128)(2,1)}, s32[4608]{0:T(1024)S(1)}, s32[512]{0:T(512)S(1)}, s32[6]{0:T(128)S(1)}, /*index=5*/bf16[512,7...) while((s32[]{:T(128)}, bf16[6,512,128]{1,2,0:T(8,128)(2,1)}, ...), condition=%wide.region_4.5_spmd.clone, body=%wide.region_1.0_spmd.clone.sunk | while | flops 1238700544 | bytes 36252392 | solution.py:93
  93.3 4.3 %fusion.50 = (f32[512]{0:T(512)S(1)}, f32[512,4608]{1,0:T(8,128)S(1)}) fusion(bf16[4608,128]{1,0:T(8,128)(2,1)} %get-tuple-element.293, bf16[512,768]{1,0:T(8,128)(2,1)} %get-tuple-element.292, s32[]{:T(128)S(6)} %select_n.163, s32[512]{0:T(512)S(1)} %get-tuple-element.290, s32[4608]{0:T(1024)S(1)} %get-tuple-element.289, ...), kind=kOutput, calls=%fused_computation.74.clone.1 | convolution fusion | flops 622853632 | bytes 10792964 | tf_op jit(solution)/shard_map/while/body/eval_jaxpr/dot_general | solution.py:17
  97.7 1.4 fusion.51
  99.1 2.2 fusion.52
  101.4 0.7 constant_dynamic-update-slice_fusion.2
  103.5 4.3 %fusion.50 = (f32[512]{0:T(512)S(1)}, f32[512,4608]{1,0:T(8,128)S(1)}) fusion(bf16[4608,128]{1,0:T(8,128)(2,1)} %get-tuple-element.293, bf16[512,768]{1,0:T(8,128)(2,1)} %get-tuple-element.292, s32[]{:T(128)S(6)} %select_n.163, s32[512]{0:T(512)S(1)} %get-tuple-element.290, s32[4608]{0:T(1024)S(1)} %get-tuple-element.289, ...), kind=kOutput, calls=%fused_computation.74.clone.1 | convolution fusion | flops 622853632 | bytes 10792964 | tf_op jit(solution)/shard_map/while/body/eval_jaxpr/dot_general | solution.py:17
  107.8 1.4 fusion.51
  109.2 2.2 fusion.52
  111.6 0.7 constant_dynamic-update-slice_fusion.2
  113.6 4.3 %fusion.50 = (f32[512]{0:T(512)S(1)}, f32[512,4608]{1,0:T(8,128)S(1)}) fusion(bf16[4608,128]{1,0:T(8,128)(2,1)} %get-tuple-element.293, bf16[512,768]{1,0:T(8,128)(2,1)} %get-tuple-element.292, s32[]{:T(128)S(6)} %select_n.163, s32[512]{0:T(512)S(1)} %get-tuple-element.290, s32[4608]{0:T(1024)S(1)} %get-tuple-element.289, ...), kind=kOutput, calls=%fused_computation.74.clone.1 | convolution fusion | flops 622853632 | bytes 10792964 | tf_op jit(solution)/shard_map/while/body/eval_jaxpr/dot_general | solution.py:17
  117.9 1.4 fusion.51
  119.4 2.2 fusion.52
  121.7 0.7 constant_dynamic-update-slice_fusion.2
  123.7 4.3 %fusion.50 = (f32[512]{0:T(512)S(1)}, f32[512,4608]{1,0:T(8,128)S(1)}) fusion(bf16[4608,128]{1,0:T(8,128)(2,1)} %get-tuple-element.293, bf16[512,768]{1,0:T(8,128)(2,1)} %get-tuple-element.292, s32[]{:T(128)S(6)} %select_n.163, s32[512]{0:T(512)S(1)} %get-tuple-element.290, s32[4608]{0:T(1024)S(1)} %get-tuple-element.289, ...), kind=kOutput, calls=%fused_computation.74.clone.1 | convolution fusion | flops 622853632 | bytes 10792964 | tf_op jit(solution)/shard_map/while/body/eval_jaxpr/dot_general | solution.py:17
  128.1 1.4 fusion.51
  129.5 2.2 fusion.52
  133.8 4.3 %fusion.50 = (f32[512]{0:T(512)S(1)}, f32[512,4608]{1,0:T(8,128)S(1)}) fusion(bf16[4608,128]{1,0:T(8,128)(2,1)} %get-tuple-element.293, bf16[512,768]{1,0:T(8,128)(2,1)} %get-tuple-element.292, s32[]{:T(128)S(6)} %select_n.163, s32[512]{0:T(512)S(1)} %get-tuple-element.290, s32[4608]{0:T(1024)S(1)} %get-tuple-element.289, ...), kind=kOutput, calls=%fused_computation.74.clone.1 | convolution fusion | flops 622853632 | bytes 10792964 | tf_op jit(solution)/shard_map/while/body/eval_jaxpr/dot_general | solution.py:17
  138.2 1.4 fusion.51
  139.6 2.2 fusion.52
  144.0 4.3 %fusion.50 = (f32[512]{0:T(512)S(1)}, f32[512,4608]{1,0:T(8,128)S(1)}) fusion(bf16[4608,128]{1,0:T(8,128)(2,1)} %get-tuple-element.293, bf16[512,768]{1,0:T(8,128)(2,1)} %get-tuple-element.292, s32[]{:T(128)S(6)} %select_n.163, s32[512]{0:T(512)S(1)} %get-tuple-element.290, s32[4608]{0:T(1024)S(1)} %get-tuple-element.289, ...), kind=kOutput, calls=%fused_computation.74.clone.1 | convolution fusion | flops 622853632 | bytes 10792964 | tf_op jit(solution)/shard_map/while/body/eval_jaxpr/dot_general | solution.py:17
  148.3 1.4 fusion.51
  149.7 2.2 fusion.52
  152.0 0.7 constant_dynamic-update-slice_fusion.2
  152.7 2.7 collective-permute-start.1
  155.4 57.5 %collective-permute-done.1 = bf16[512,768]{0,1:T(8,128)(2,1)S(1)} collective-permute-done((bf16[512,768]{0,1:T(8,128)(2,1)}, bf16[512,768]{0,1:T(8,128)(2,1)S(1)}, u32[]{:S(2)}, u32[]{:S(2)}) %collective-permute-start.1) | collective-permute-done | bytes 786464 | tf_op jit(solution)/shard_map/ppermute | solution.py:97
  212.9 2.0 maximum_select_fusion.2
  214.9 0.8 collective-permute-start.2
  215.6 12.4 %copy.15 = bf16[2,4,768,768]{3,1,2,0:T(4,128)(2,1)} copy(bf16[2,4,768,768]{3,2,1,0:T(8,128)(2,1)} %bitcast.58) | data formatting | bytes 18874368 | tf_op jit(solution)/shard_map/reshape | solution.py:76
  228.0 9.6 %copy.18 = bf16[192,8,4,768]{3,1,2,0:T(8,128)(2,1)} copy(bf16[192,8,4,768]{3,2,1,0:T(4,128)(2,1)} %bitcast.57) | data formatting | bytes 18874368
  237.6 16.7 %convolution_convert_fusion = bf16[1024,3072]{1,0:T(8,128)(2,1)} fusion(bf16[1536,3072]{1,0:T(8,128)(2,1)} %bitcast.59, bf16[512,1536]{0,1:T(8,128)(2,1)} %collective-permute-done.2, bf16[512,1536]{0,1:T(8,128)(2,1)S(1)} %maximum_select_fusion.2, pred[]{:T(512)S(6)} %eq.84), kind=kOutput, calls=%fused_computation.18 | convolution fusion | flops 9680977920 | bytes 18874368 | tf_op jit(solution)/shard_map/dot_general | solution.py:111
  254.3 60.8 %reduce-scatter.2.cloned.1.call-done = bf16[1024,768]{1,0:T(8,128)(2,1)} async-done(((bf16[1024,3072]{1,0:T(8,128)(2,1)}), bf16[1024,768]{1,0:T(8,128)(2,1)}) %reduce-scatter.2.cloned.1.call-update) | async-done | bytes 1572880 | tf_op jit(solution)/shard_map/reduce_scatter | solution.py:112
  315.2 6.5 %all_to_all.14 = bf16[2,512,768]{2,1,0:T(8,128)(2,1)S(1)} all-to-all(bf16[2,512,768]{2,1,0:T(8,128)(2,1)} %bitcast.60), channel_id=1, replica_groups=mesh['ylo'=2,'x'=4,'c'=2,'yhi'=2,'z'=4] {'c'}, dimensions={0} | all-to-all | bytes 3145728 | tf_op jit(solution)/shard_map/all_to_all | solution.py:113
  321.8 1.3 pad_maximum_fusion
  (72 shorter events, 7.0 us)
Async XLA Ops:
  6.5 2.6 copy-start
  6.5 75.2 %all-gather.4.cloned.1.call-start = ((), (), s32[]{:S(2)}) async-start(), calls=%async_computation.3 | async-start | bytes 4456448 | tf_op jit(solution)/shard_map/all_gather | solution.py:39
  13.3 17.5 %copy-start.4 = (s32[64,2]{0,1:T(2,128)S(1)}, s32[64,2]{0,1:T(2,128)}, u32[]{:S(2)}) copy-start(s32[64,2]{0,1:T(2,128)} %param.12) | copy-start | bytes 1540
  13.3 19.1 %copy-start.3 = (s32[8192]{0:T(1024)S(1)}, s32[8192]{0:T(1024)}, u32[]{:S(2)}) copy-start(s32[8192]{0:T(1024)} %param.11) | copy-start | bytes 98308
  13.3 59.1 %all-to-all-start = ((bf16[16,128,768]{2,1,0:T(8,128)(2,1)}), bf16[16,128,768]{2,1,0:T(8,128)(2,1)}, u32[]{:S(2)}, u32[]{:S(2)}) async-start(bf16[16,128,768]{2,1,0:T(8,128)(2,1)} %copy.11), calls=%async_computation | async-start | bytes 6291456 | tf_op jit(solution)/shard_map/all_to_all | solution.py:58
  20.3 195.3 %all-gather.6.cloned.1.call-start = ((), (), s32[]{:S(2)}) async-start(), calls=%async_computation.5 | async-start | bytes 10616832 | tf_op jit(solution)/shard_map/all_gather | solution.py:74
  20.4 69.7 %collective-permute-start = (bf16[768,768]{1,0:T(8,128)(2,1)}, bf16[768,768]{1,0:T(8,128)(2,1)}, u32[]{:S(2)}, u32[]{:S(2)}) collective-permute-start(bf16[768,768]{1,0:T(8,128)(2,1)} %param.13), channel_id=1, source_target_pairs={{0,0},{4,64},{64,4},{68,68},{1,1},{5,65},{65,5},{69,69},{2,2},{6,6... | collective-permute-start | bytes 3538952 | tf_op jit(solution)/shard_map/ppermute | solution.py:72
  91.7 223.5 %reduce-scatter.2.cloned.1.call-start = ((), (), s32[]{:S(2)}) async-start(), calls=%async_computation.4 | async-start | bytes 7864320 | tf_op jit(solution)/shard_map/reduce_scatter | solution.py:112
  97.7 1.4 copy-start.2
  107.8 1.4 copy-start.2
  117.9 1.4 copy-start.2
  128.0 1.4 copy-start.2
  138.2 1.4 copy-start.2
  148.3 1.4 copy-start.2
  152.7 60.2 %collective-permute-start.1 = (bf16[512,768]{0,1:T(8,128)(2,1)}, bf16[512,768]{0,1:T(8,128)(2,1)S(1)}, u32[]{:S(2)}, u32[]{:S(2)}) collective-permute-start(bf16[512,768]{0,1:T(8,128)(2,1)} %bitcast.62), channel_id=1, source_target_pairs={{0,4},{4,0},{1,5},{5,1},{2,6},{6,2},{3,7},{7,3},{8,12},{12,8},{9,1... | collective-permute-start | bytes 2359304 | tf_op jit(solution)/shard_map/ppermute | solution.py:97
  214.9 22.7 %collective-permute-start.2 = (bf16[512,1536]{0,1:T(8,128)(2,1)S(1)}, bf16[512,1536]{0,1:T(8,128)(2,1)}, u32[]{:S(2)}, u32[]{:S(2)}) collective-permute-start(bf16[512,1536]{0,1:T(8,128)(2,1)S(1)} %maximum_select_fusion.2), channel_id=1, source_target_pairs={{0,8},{8,0},{1,9},{9,1},{2,10},{10,2},{3,11},{11,3},{4,12},{12,4},... | collective-permute-start | bytes 4718600 | tf_op jit(solution)/shard_map/ppermute | solution.py:104
  315.2 7.9 %copy-start.1 = (bf16[512,768]{1,0:T(8,128)(2,1)S(1)}, bf16[512,768]{1,0:T(8,128)(2,1)}, u32[]{:S(2)}) copy-start(bf16[512,768]{1,0:T(8,128)(2,1)} %param.8) | copy-start | bytes 2359300
Sparse Core Ops, SparseCore 0:
  9.1 72.6 all-gather.3
  91.8 103.1 all-gather.5
  254.5 60.6 reduce-scatter.1

commit v3 on v1

--- a/solution.py
+++ b/solution.py
@@ -70,9 +70,8 @@
     queries_here = packed.reshape(tok_rows, q_cols)
 
     w_swapped = lax.ppermute(out_weight, ("ylo", "yhi"), perm=[(0, 0), (1, 2), (2, 1), (3, 3)])
-    w_cols = lax.all_gather(w_swapped, "x", axis=1, tiled=True)
-    w_here = lax.all_gather(w_cols, "ylo", axis=0, tiled=True)
-    context, w_here = lax.optimization_barrier((context, w_here))
+    context, w_swapped = lax.optimization_barrier((context, w_swapped))
+    w_here = lax.all_gather(w_swapped, ("ylo", "x"), axis=1, tiled=True)
 
     ctx_keys = context[:, :kv_cols]
     ctx_values = context[:, kv_cols:]
@@ -88,12 +87,37 @@
         q_head = lax.dynamic_slice_in_dim(queries_here, head_index * HEAD_DIM, HEAD_DIM, 1)
         return attend_head(q_head, ctx_keys, ctx_values, q_pos, k_pos, q_seg, k_seg)
 
-    per_head = lax.map(one_head, jnp.arange(heads_here, dtype=jnp.int32))
-    attended = jnp.transpose(per_head, (1, 0, 2)).reshape(tok_rows, q_cols)
-
-    h_groups = lax.all_gather(attended, "yhi", axis=1, tiled=True)
-    h_here = lax.all_gather(h_groups, "c", axis=0, tiled=True)
-    part = jnp.dot(h_here, w_here, preferred_element_type=jnp.float32).astype(jnp.bfloat16)
+    pair = [(0, 1), (1, 0)]
+    low_hi = lax.axis_index("yhi") == 0
+    low_core = lax.axis_index("c") == 0
+    half = heads_here // 2
+    half_cols = half * HEAD_DIM
+    w_half = w_here.shape[1] // 2
+    part = None
+    for first in (0, half):
+        per_head = lax.map(one_head, jnp.arange(first, first + half, dtype=jnp.int32))
+        attended = jnp.transpose(per_head, (1, 0, 2)).reshape(tok_rows, half_cols)
+        h_far = lax.ppermute(attended, "yhi", pair)
+        h_groups = jnp.where(
+            low_hi,
+            jnp.concatenate([attended, h_far], axis=1),
+            jnp.concatenate([h_far, attended], axis=1),
+        )
+        h_near = lax.ppermute(h_groups, "c", pair)
+        h_here = jnp.where(
+            low_core,
+            jnp.concatenate([h_groups, h_near], axis=0),
+            jnp.concatenate([h_near, h_groups], axis=0),
+        )
+        for group in range(2):
+            rows = w_here[first * HEAD_DIM:first * HEAD_DIM + half_cols, group * w_half:(group + 1) * w_half]
+            term = jnp.dot(
+                h_here[:, group * half_cols:(group + 1) * half_cols],
+                rows,
+                preferred_element_type=jnp.float32,
+            )
+            part = term if part is None else part + term
+    part = part.astype(jnp.bfloat16)
     summed = lax.psum_scatter(part, "z", scatter_dimension=1, tiled=True)
     swapped = lax.all_to_all(summed, "c", split_axis=0, concat_axis=0, tiled=True)
     return jnp.concatenate([swapped[:tok_rows], swapped[tok_rows:]], axis=1)

time: 491 us -> 334 us (0.68)
  waiting for transfers between devices: 365 us -> 165 us
  matrix products: 57.6 us -> 82.6 us
  starting transfers between devices: 7.67 us -> 22.2 us
  other arithmetic: 15.4 us -> 21 us
    all_gather x4 -> x1, waiting for transfers between devices: 244 us -> 0.01 us  [shards(): w_here = lax.all_gather(w_swapped, ('ylo', 'x'), axis=1, tiled=True)]
    ppermute x0 -> x4, waiting for transfers between devices: none -> 60.3 us  [the longest x2 60.1 us: shards(): h_far = lax.ppermute(attended, 'yhi', pair)]
    dot_general x1 -> x4, matrix products: 15.3 us -> 37.9 us  [shards(): jnp.dot(h_here[:, group * half_cols:(group + 1) * half_cols], rows, prefe...]
    all_to_all x1, waiting for transfers between devices: 48.2 us -> 39.6 us  [shards(): lax.all_to_all(outgoing, SEQ, split_axis=0, concat_axis=0, tiled=True)]
    ppermute x1, starting transfers between devices: 2.05 us -> 10.4 us  [shards(): lax.ppermute(out_weight, ('ylo', 'yhi'), perm=[(0, 0), (1, 2), (2, 1), (3...]
    select_n x1 -> x4, other arithmetic: 0.01 us -> 5.52 us  [the longest x2 4.91 us: shards(): jnp.where(low_core, jnp.concatenate([h_groups, h_near], axis=0), jnp.conc...]
  transfers between devices with their start and end apart: 8 -> 9, of which waited for: 7 -> 6; matrix products, arithmetic and copies ran while one was open for 4% -> 23% of each run, Pallas kernels for 0% -> 0%
where the time goes in v3:
time: 334 us; the launch traced here: 332 us
  waiting for transfers between devices  165 us (49%)
  matrix products  82.6 us (25%)
  starting transfers between devices  22.2 us (7%)
  other arithmetic  21 us (6%)
  local copies, waits for them, and re-layouts  17 us (5%)
  between operations  13.3 us (4%)
  blocking collectives  6.55 us (2%)
  loops' own time  4.26 us (1%)
    reduce_scatter x1, waiting for transfers between devices, shards(): summed = lax.psum_scatter(part, 'z', scatter_dimension=1, tiled=True)  61.1 us
    ppermute x2, waiting for transfers between devices, shards(): h_far = lax.ppermute(attended, 'yhi', pair)  60.1 us
    all_to_all x1, waiting for transfers between devices, shards(): lax.all_to_all(outgoing, SEQ, split_axis=0, concat_axis=0, tiled=True)  39.6 us
    dot_general x4, matrix products, shards(): jnp.dot(h_here[:, group * half_cols:(group + 1) * half_cols], rows, prefe...  37.9 us
    dot_general x6, matrix products, attend_head(): lax.dot_general(q_rows, k_rows, (((1,), (1,)), ((), ())), preferred_eleme...  26 us
    dot_general x6, matrix products, attend_head(): jnp.dot(weights, v_rows, preferred_element_type=jnp.float32)  13.3 us
    ppermute x1, starting transfers between devices, shards(): lax.ppermute(out_weight, ('ylo', 'yhi'), perm=[(0, 0), (1, 2), (2, 1), (3...  10.4 us
    reduce_sum x6, other arithmetic, attend_head(): weights = (expo / jnp.sum(expo, axis=1, keepdims=True)).astype(jnp.bfloat16)  8.42 us
  transfers between devices with their start and end apart: 9, of which 6 were waited for; matrix products, arithmetic and copies ran while one was open for 23% of the time, Pallas kernels for 0%

profile of v3, /device:TPU:1, one launch (start us, length us, event | category | flops | bytes accessed | tf_op | source)
XLA Modules:
  0.0 332.3 jit_solution(15742745206562644036)
XLA Ops:
  6.5 1.8 pad_maximum_fusion.1
  8.3 0.8 constant_dynamic-slice_fusion
  9.1 1.5 convolution_convert_fusion
  10.6 2.7 copy.11
  13.4 7.0 %all-to-all-start = ((bf16[16,128,768]{2,1,0:T(8,128)(2,1)}), bf16[16,128,768]{2,1,0:T(8,128)(2,1)}, u32[]{:S(2)}, u32[]{:S(2)}) async-start(bf16[16,128,768]{2,1,0:T(8,128)(2,1)} %copy.11), calls=%async_computation | async-start | bytes 6291456 | tf_op jit(solution)/shard_map/all_to_all | solution.py:58
  20.4 10.4 %collective-permute-start = (bf16[768,768]{1,0:T(8,128)(2,1)}, bf16[768,768]{1,0:T(8,128)(2,1)}, u32[]{:S(2)}, u32[]{:S(2)}) collective-permute-start(bf16[768,768]{1,0:T(8,128)(2,1)} %param.15), channel_id=1, source_target_pairs={{0,0},{4,64},{64,4},{68,68},{1,1},{5,65},{65,5},{69,69},{2,2},{6,6... | collective-permute-start | bytes 3538952 | tf_op jit(solution)/shard_map/ppermute | solution.py:72
  30.8 0.8 scatter_custom_fusion
  31.7 0.8 gather_fusion
  32.9 39.6 %all-to-all-done = bf16[16,128,768]{2,1,0:T(8,128)(2,1)} async-done(((bf16[16,128,768]{2,1,0:T(8,128)(2,1)}), bf16[16,128,768]{2,1,0:T(8,128)(2,1)}, u32[]{:S(2)}, u32[]{:S(2)}) %all-to-all-start) | async-done | bytes 3145760 | tf_op jit(solution)/shard_map/all_to_all | solution.py:58
  72.5 3.9 %fusion.29 = bf16[4,128,768]{2,0,1:T(4,128)(2,1)S(1)} fusion(bf16[4,16,1]{1,0,2:T(4,128)(2,1)S(1)} %fusion.32, bf16[16,128,768]{2,1,0:T(8,128)(2,1)} %all-to-all-done), kind=kOutput, calls=%fused_computation.48 | convolution fusion | flops 12976128 | bytes 3932288 | tf_op jit(solution)/shard_map/od,drc->orc/dot_general | solution.py:67
  76.4 1.0 copy.13
  77.3 4.4 %all-gather.3.cloned.1.call-done = bf16[8192,256]{1,0:T(8,128)(2,1)} async-done(((bf16[512,256]{1,0:T(8,128)(2,1)}), bf16[8192,256]{1,0:T(8,128)(2,1)}) %all-gather.3.cloned.1.call-update) | async-done | bytes 4194320 | tf_op jit(solution)/shard_map/all_gather | solution.py:39
  81.7 4.5 %gather_fusion.1 = bf16[36,128,256]{2,1,0:T(8,128)(2,1)} fusion(bf16[64,128,256]{2,1,0:T(8,128)(2,1)} %bitcast.73, s32[1024]{0:T(1024)S(1)} %pad_clamp_fusion), kind=kCustom, calls=%fused_computation.1 | custom fusion | bytes 4718736 | tf_op jit(solution)/shard_map/jit(_take)/gather | solution.py:49
  86.3 3.8 %bitcast_select_fusion = bf16[4608,256]{1,0:T(8,128)(2,1)S(1)} fusion(bf16[36,128,256]{2,1,0:T(8,128)(2,1)} %gather_fusion.1, pred[4608]{0:T(1024)(128)(4,1)S(1)} %broadcast_bitcast_fusion), kind=kLoop, calls=%fused_computation.43 | loop fusion | flops 1179648 | bytes 4723200 | tf_op jit(solution)/shard_map/jit(_take)/select_n | solution.py:49
  90.1 1.6 fusion.53
  92.0 28.3 %while.26 = (s32[]{:T(128)}, bf16[3,512,128]{1,2,0:T(8,128)(2,1)S(1)}, s32[4608]{0:T(1024)S(1)}, s32[512]{0:T(512)S(1)}, s32[3]{0:T(128)S(1)}, /*index=5*/bf16[5...) while((s32[]{:T(128)}, ...), condition=%wide.region_4.5_spmd.clone, body=%wide.region_1.0_spmd.clone.sunk | while | flops 1238700544 | bytes 36251892 | solution.py:98
  93.3 4.3 %fusion.71 = (f32[512]{0:T(512)S(1)}, f32[512,4608]{1,0:T(8,128)S(1)}) fusion(bf16[4608,128]{1,0:T(8,128)(2,1)} %get-tuple-element.579, bf16[512,768]{1,0:T(8,128)(2,1)} %get-tuple-element.578, s32[]{:T(128)S(6)} %select_n.189, s32[512]{0:T(512)S(1)} %get-tuple-element.576, s32[4608]{0:T(1024)S(1)} %get-tuple-element.575, ...), kind=kOutput, calls=%fused_computation.96.clone.1 | convolution fusion | flops 622853632 | bytes 10792964 | tf_op jit(solution)/shard_map/while/body/eval_jaxpr/dot_general | solution.py:17
  97.6 1.4 fusion.72
  99.0 2.2 fusion.73
  102.7 4.4 %fusion.71 = (f32[512]{0:T(512)S(1)}, f32[512,4608]{1,0:T(8,128)S(1)}) fusion(bf16[4608,128]{1,0:T(8,128)(2,1)} %get-tuple-element.579, bf16[512,768]{1,0:T(8,128)(2,1)} %get-tuple-element.578, s32[]{:T(128)S(6)} %select_n.189, s32[512]{0:T(512)S(1)} %get-tuple-element.576, s32[4608]{0:T(1024)S(1)} %get-tuple-element.575, ...), kind=kOutput, calls=%fused_computation.96.clone.1 | convolution fusion | flops 622853632 | bytes 10792964 | tf_op jit(solution)/shard_map/while/body/eval_jaxpr/dot_general | solution.py:17
  107.1 1.4 fusion.72
  108.5 2.2 fusion.73
  112.2 4.3 %fusion.71 = (f32[512]{0:T(512)S(1)}, f32[512,4608]{1,0:T(8,128)S(1)}) fusion(bf16[4608,128]{1,0:T(8,128)(2,1)} %get-tuple-element.579, bf16[512,768]{1,0:T(8,128)(2,1)} %get-tuple-element.578, s32[]{:T(128)S(6)} %select_n.189, s32[512]{0:T(512)S(1)} %get-tuple-element.576, s32[4608]{0:T(1024)S(1)} %get-tuple-element.575, ...), kind=kOutput, calls=%fused_computation.96.clone.1 | convolution fusion | flops 622853632 | bytes 10792964 | tf_op jit(solution)/shard_map/while/body/eval_jaxpr/dot_general | solution.py:17
  116.5 1.4 fusion.72
  117.9 2.2 fusion.73
  120.3 2.9 collective-permute-start.1
  123.2 28.2 %while.27 = (s32[]{:T(128)}, bf16[3,512,128]{1,2,0:T(8,128)(2,1)S(1)}, s32[4608]{0:T(1024)S(1)}, s32[512]{0:T(512)S(1)}, s32[3]{0:T(128)S(1)}, /*index=5*/bf16[5...) while((s32[]{:T(128)}, ...), condition=%wide.region_8.9_spmd.clone, body=%wide.region_5.8_spmd.clone.sunk | while | flops 1238700544 | bytes 36251892 | solution.py:98
  124.5 4.3 %fusion.76 = (f32[512]{0:T(512)S(1)}, f32[512,4608]{1,0:T(8,128)S(1)}) fusion(bf16[4608,128]{1,0:T(8,128)(2,1)} %get-tuple-element.537, bf16[512,768]{1,0:T(8,128)(2,1)} %get-tuple-element.536, s32[]{:T(128)S(6)} %select_n.190, s32[512]{0:T(512)S(1)} %get-tuple-element.534, s32[4608]{0:T(1024)S(1)} %get-tuple-element.533, ...), kind=kOutput, calls=%fused_computation.97.clone.1 | convolution fusion | flops 622853632 | bytes 10792964 | tf_op jit(solution)/shard_map/while/body/eval_jaxpr/dot_general | solution.py:17
  128.8 1.4 fusion.77
  130.2 2.2 fusion.78
  133.9 4.3 %fusion.76 = (f32[512]{0:T(512)S(1)}, f32[512,4608]{1,0:T(8,128)S(1)}) fusion(bf16[4608,128]{1,0:T(8,128)(2,1)} %get-tuple-element.537, bf16[512,768]{1,0:T(8,128)(2,1)} %get-tuple-element.536, s32[]{:T(128)S(6)} %select_n.190, s32[512]{0:T(512)S(1)} %get-tuple-element.534, s32[4608]{0:T(1024)S(1)} %get-tuple-element.533, ...), kind=kOutput, calls=%fused_computation.97.clone.1 | convolution fusion | flops 622853632 | bytes 10792964 | tf_op jit(solution)/shard_map/while/body/eval_jaxpr/dot_general | solution.py:17
  138.2 1.4 fusion.77
  139.6 2.2 fusion.78
  143.3 4.3 %fusion.76 = (f32[512]{0:T(512)S(1)}, f32[512,4608]{1,0:T(8,128)S(1)}) fusion(bf16[4608,128]{1,0:T(8,128)(2,1)} %get-tuple-element.537, bf16[512,768]{1,0:T(8,128)(2,1)} %get-tuple-element.536, s32[]{:T(128)S(6)} %select_n.190, s32[512]{0:T(512)S(1)} %get-tuple-element.534, s32[4608]{0:T(1024)S(1)} %get-tuple-element.533, ...), kind=kOutput, calls=%fused_computation.97.clone.1 | convolution fusion | flops 622853632 | bytes 10792964 | tf_op jit(solution)/shard_map/while/body/eval_jaxpr/dot_general | solution.py:17
  147.6 1.4 fusion.77
  149.0 2.2 fusion.78
  151.7 52.8 %collective-permute-done.1 = bf16[512,384]{0,1:T(8,128)(2,1)S(1)} collective-permute-done((bf16[512,384]{0,1:T(8,128)(2,1)S(1)}, bf16[512,384]{0,1:T(8,128)(2,1)S(1)}, u32[]{:S(2)}, u32[]{:S(2)}) %collective-permute-start.1) | collective-permute-done | bytes 393248 | tf_op jit(solution)/shard_map/ppermute | solution.py:100
  204.9 0.8 collective-permute-start.2
  205.7 7.3 %collective-permute-done.3 = bf16[512,384]{0,1:T(8,128)(2,1)S(1)} collective-permute-done((bf16[512,384]{0,1:T(8,128)(2,1)S(1)}, bf16[512,384]{0,1:T(8,128)(2,1)S(1)}, u32[]{:S(2)}, u32[]{:S(2)}) %collective-permute-start.3) | collective-permute-done | bytes 393248 | tf_op jit(solution)/shard_map/ppermute | solution.py:100
  213.8 1.9 maximum_select_fusion
  215.9 3.0 maximum_select_fusion.1
  218.9 8.3 %fusion.25 = f32[1024,3072]{1,0:T(8,128)} fusion(bf16[768,6144]{1,0:T(8,128)(2,1)} %all-gather.5.cloned.1.call-done, bf16[1024,768]{0,1:T(8,128)(2,1)S(1)} %maximum_select_fusion), kind=kOutput, calls=%fused_computation.39 | convolution fusion | flops 2415919104 | bytes 15728640 | tf_op jit(solution)/shard_map/dot_general | solution.py:114
  227.2 6.4 %fusion.27 = f32[1024,3072]{1,0:T(8,128)} fusion(bf16[768,6144]{1,0:T(8,128)(2,1)S(1)} %copy-done.2, bf16[1024,768]{0,1:T(8,128)(2,1)S(1)} %maximum_select_fusion), kind=kOutput, calls=%fused_computation.41 | convolution fusion | flops 2415919104 | bytes 15728640 | tf_op jit(solution)/shard_map/dot_general | solution.py:114
  233.6 6.4 %fusion.23 = f32[1024,3072]{1,0:T(8,128)} fusion(bf16[768,6144]{1,0:T(8,128)(2,1)S(1)} %copy-done.2, bf16[1024,768]{0,1:T(8,128)(2,1)S(1)} %copy-done.3), kind=kOutput, calls=%fused_computation.37 | convolution fusion | flops 2415919104 | bytes 15728640 | tf_op jit(solution)/shard_map/dot_general | solution.py:114
  239.9 16.8 %add_convert_fusion = bf16[1024,3072]{1,0:T(8,128)(2,1)} fusion(f32[1024,3072]{1,0:T(8,128)} %fusion.23, f32[1024,3072]{1,0:T(8,128)} %fusion.27, f32[1024,3072]{1,0:T(8,128)} %fusion.25, bf16[768,6144]{1,0:T(8,128)(2,1)} %all-gather.5.cloned.1.call-done, bf16[1024,768]{0,1:T(8,128)(2,1)S(1)} %copy-done.4), kind=kOutput, calls=%fused_computation.33 | convolution fusion | flops 2428502016 | bytes 47185920 | tf_op jit(solution)/shard_map/dot_general | solution.py:114
  256.8 61.1 %reduce-scatter.2.cloned.1.call-done = bf16[1024,768]{1,0:T(8,128)(2,1)} async-done(((bf16[1024,3072]{1,0:T(8,128)(2,1)}), bf16[1024,768]{1,0:T(8,128)(2,1)}) %reduce-scatter.2.cloned.1.call-update) | async-done | bytes 1572880 | tf_op jit(solution)/shard_map/reduce_scatter | solution.py:121
  317.9 6.5 %all_to_all.14 = bf16[2,512,768]{2,1,0:T(8,128)(2,1)S(1)} all-to-all(bf16[2,512,768]{2,1,0:T(8,128)(2,1)} %bitcast.68), channel_id=1, replica_groups=mesh['ylo'=2,'x'=4,'c'=2,'yhi'=2,'z'=4] {'c'}, dimensions={0} | all-to-all | bytes 3145728 | tf_op jit(solution)/shard_map/all_to_all | solution.py:122
  324.5 1.3 pad_maximum_fusion
  (89 shorter events, 7.3 us)
Async XLA Ops:
  6.5 2.6 copy-start
  6.5 75.2 %all-gather.3.cloned.1.call-start = ((), (), s32[]{:S(2)}) async-start(), calls=%async_computation.3 | async-start | bytes 4456448 | tf_op jit(solution)/shard_map/all_gather | solution.py:39
  13.3 17.4 %copy-start.8 = (s32[64,2]{0,1:T(2,128)S(1)}, s32[64,2]{0,1:T(2,128)}, u32[]{:S(2)}) copy-start(s32[64,2]{0,1:T(2,128)} %param.14) | copy-start | bytes 1540
  13.3 18.2 %copy-start.7 = (s32[8192]{0:T(1024)S(1)}, s32[8192]{0:T(1024)}, u32[]{:S(2)}) copy-start(s32[8192]{0:T(1024)} %param.13) | copy-start | bytes 98308
  13.4 59.1 %all-to-all-start = ((bf16[16,128,768]{2,1,0:T(8,128)(2,1)}), bf16[16,128,768]{2,1,0:T(8,128)(2,1)}, u32[]{:S(2)}, u32[]{:S(2)}) async-start(bf16[16,128,768]{2,1,0:T(8,128)(2,1)} %copy.11), calls=%async_computation | async-start | bytes 6291456 | tf_op jit(solution)/shard_map/all_to_all | solution.py:58
  20.3 198.6 %all-gather.5.cloned.1.call-start = ((), (), s32[]{:S(2)}) async-start(), calls=%async_computation.4 | async-start | bytes 10616832 | tf_op jit(solution)/shard_map/all_gather | solution.py:74
  20.4 69.7 %collective-permute-start = (bf16[768,768]{1,0:T(8,128)(2,1)}, bf16[768,768]{1,0:T(8,128)(2,1)}, u32[]{:S(2)}, u32[]{:S(2)}) collective-permute-start(bf16[768,768]{1,0:T(8,128)(2,1)} %param.15), channel_id=1, source_target_pairs={{0,0},{4,64},{64,4},{68,68},{1,1},{5,65},{65,5},{69,69},{2,2},{6,6... | collective-permute-start | bytes 3538952 | tf_op jit(solution)/shard_map/ppermute | solution.py:72
  91.7 226.2 %reduce-scatter.2.cloned.1.call-start = ((), (), s32[]{:S(2)}) async-start(), calls=%async_computation.5 | async-start | bytes 7864320 | tf_op jit(solution)/shard_map/reduce_scatter | solution.py:121
  97.6 1.4 copy-start.5
  107.1 1.4 copy-start.5
  116.5 1.4 copy-start.5
  120.3 84.3 %collective-permute-start.1 = (bf16[512,384]{0,1:T(8,128)(2,1)S(1)}, bf16[512,384]{0,1:T(8,128)(2,1)S(1)}, u32[]{:S(2)}, u32[]{:S(2)}) collective-permute-start(bf16[512,384]{0,1:T(8,128)(2,1)S(1)} %bitcast.71), channel_id=1, source_target_pairs={{0,4},{4,0},{1,5},{5,1},{2,6},{6,2},{3,7},{7,3},{8,12},{12,8},{9,1... | collective-permute-start | bytes 1179656 | tf_op jit(solution)/shard_map/ppermute | solution.py:100
  128.8 1.4 copy-start.6
  138.2 1.4 copy-start.6
  147.6 1.4 copy-start.6
  151.4 61.6 %collective-permute-start.3 = (bf16[512,384]{0,1:T(8,128)(2,1)S(1)}, bf16[512,384]{0,1:T(8,128)(2,1)S(1)}, u32[]{:S(2)}, u32[]{:S(2)}) collective-permute-start(bf16[512,384]{0,1:T(8,128)(2,1)S(1)} %bitcast.69), channel_id=1, source_target_pairs={{0,4},{4,0},{1,5},{5,1},{2,6},{6,2},{3,7},{7,3},{8,12},{12,8},{9,1... | collective-permute-start | bytes 1179656 | tf_op jit(solution)/shard_map/ppermute | solution.py:100
  204.9 9.0 %collective-permute-start.2 = (bf16[512,768]{0,1:T(8,128)(2,1)S(1)}, bf16[512,768]{0,1:T(8,128)(2,1)}, u32[]{:S(2)}, u32[]{:S(2)}) collective-permute-start(bf16[512,768]{0,1:T(8,128)(2,1)S(1)} %maximum_select_fusion.2), channel_id=1, source_target_pairs={{0,8},{8,0},{1,9},{9,1},{2,10},{10,2},{3,11},{11,3},{4,12},{12,4},... | collective-permute-start | bytes 2359304 | tf_op jit(solution)/shard_map/ppermute | solution.py:106
  213.3 2.6 collective-permute-start.4
  218.9 8.3 %copy-start.2 = (bf16[768,6144]{1,0:T(8,128)(2,1)S(1)}, bf16[768,6144]{1,0:T(8,128)(2,1)}, u32[]{:S(2)}) copy-start(bf16[768,6144]{1,0:T(8,128)(2,1)} %all-gather.5.cloned.1.call-done) | copy-start | bytes 28311556
  227.2 6.4 %copy-start.3 = (bf16[1024,768]{0,1:T(8,128)(2,1)S(1)}, bf16[1024,768]{0,1:T(8,128)(2,1)}, u32[]{:S(2)}) copy-start(bf16[1024,768]{0,1:T(8,128)(2,1)} %maximum_select_fusion.1) | copy-start | bytes 4718596
  233.6 6.4 %copy-start.4 = (bf16[1024,768]{0,1:T(8,128)(2,1)S(1)}, bf16[1024,768]{0,1:T(8,128)(2,1)}, u32[]{:S(2)}) copy-start(bf16[1024,768]{0,1:T(8,128)(2,1)} %maximum_select_fusion.1) | copy-start | bytes 4718596
  317.9 7.9 %copy-start.1 = (bf16[512,768]{1,0:T(8,128)(2,1)S(1)}, bf16[512,768]{1,0:T(8,128)(2,1)}, u32[]{:S(2)}) copy-start(bf16[512,768]{1,0:T(8,128)(2,1)} %param.10) | copy-start | bytes 2359300
Sparse Core Ops, SparseCore 0:
  9.1 72.6 all-gather.2
  91.8 103.1 all-gather.4
  256.9 60.8 reduce-scatter.1

commit v4 on v2

--- a/solution.py
+++ b/solution.py
@@ -71,10 +71,8 @@
 
     w_swapped = lax.ppermute(out_weight, ("ylo", "yhi"), perm=[(0, 0), (1, 2), (2, 1), (3, 3)])
     context, w_swapped = lax.optimization_barrier((context, w_swapped))
-    w_stack = lax.all_gather(w_swapped, ("ylo", "x"), axis=0, tiled=False)
-    w_rows, w_cols = out_weight.shape
-    w_here = w_stack.reshape(2, -1, w_rows, w_cols).transpose(0, 2, 1, 3)
-    w_here = w_here.reshape(2 * w_rows, -1)
+    w_here = lax.all_gather(w_swapped, ("x", "ylo"), axis=0, tiled=True)
+    w_here = w_here.reshape(-1, 2 * out_weight.shape[0], out_weight.shape[1])
 
     ctx_keys = context[:, :kv_cols]
     ctx_values = context[:, kv_cols:]
@@ -108,7 +106,10 @@
         jnp.concatenate([h_groups, h_near], axis=0),
         jnp.concatenate([h_near, h_groups], axis=0),
     )
-    part = jnp.dot(h_here, w_here, preferred_element_type=jnp.float32).astype(jnp.bfloat16)
+    part = lax.dot_general(
+        h_here, w_here, (((1,), (1,)), ((), ())), preferred_element_type=jnp.float32
+    )
+    part = part.astype(jnp.bfloat16).reshape(h_here.shape[0], -1)
     summed = lax.psum_scatter(part, "z", scatter_dimension=1, tiled=True)
     swapped = lax.all_to_all(summed, "c", split_axis=0, concat_axis=0, tiled=True)
     return jnp.concatenate([swapped[:tok_rows], swapped[tok_rows:]], axis=1)

time: 331 us -> 397 us (1.20)
  waiting for transfers between devices: 162 us -> 250 us
  local copies, waits for them, and re-layouts: 43.1 us -> 22.7 us
    all_gather x1, waiting for transfers between devices: 0.01 us -> 85.4 us  [shards(): w_here = lax.all_gather(w_swapped, ('x', 'ylo'), axis=0, tiled=True)]
    reshape x1 -> x0, local copies, waits for them, and re-layouts: 12.4 us -> none  [shards(): w_here = w_stack.reshape(2, -1, w_rows, w_cols).transpose(0, 2, 1, 3)]
    unnamed x9 -> x6, local copies, waits for them, and re-layouts: 9.58 us -> 0.01 us
    ppermute x1, waiting for transfers between devices: 57.5 us -> 51 us  [shards(): h_far = lax.ppermute(attended, 'yhi', pair)]
    reduce_scatter x1, waiting for transfers between devices: 60.8 us -> 66 us  [shards(): summed = lax.psum_scatter(part, 'z', scatter_dimension=1, tiled=True)]
  transfers between devices with their start and end apart: 7 -> 7, of which waited for: 4 -> 6; matrix products, arithmetic and copies ran while one was open for 30% -> 20% of each run, Pallas kernels for 0% -> 0%
where the time goes in v4:
time: 397 us; the launch traced here: 395 us
  waiting for transfers between devices  250 us (63%)
  matrix products  61.5 us (15%)
  local copies, waits for them, and re-layouts  22.7 us (6%)
  starting transfers between devices  21.7 us (5%)
  other arithmetic  17.4 us (4%)
  between operations  13.2 us (3%)
  blocking collectives  5.24 us (1%)
  loops' own time  4.06 us (1%)
    all_gather x1, waiting for transfers between devices, shards(): w_here = lax.all_gather(w_swapped, ('x', 'ylo'), axis=0, tiled=True)  85.4 us
    reduce_scatter x1, waiting for transfers between devices, shards(): summed = lax.psum_scatter(part, 'z', scatter_dimension=1, tiled=True)  66 us
    ppermute x1, waiting for transfers between devices, shards(): h_far = lax.ppermute(attended, 'yhi', pair)  51 us
    all_to_all x1, waiting for transfers between devices, shards(): lax.all_to_all(outgoing, SEQ, split_axis=0, concat_axis=0, tiled=True)  39.5 us
    dot_general x6, matrix products, attend_head(): lax.dot_general(q_rows, k_rows, (((1,), (1,)), ((), ())), preferred_eleme...  26 us
    dot_general x1, matrix products, shards(): lax.dot_general(h_here, w_here, (((1,), (1,)), ((), ())), preferred_eleme...  16.7 us
    dot_general x6, matrix products, attend_head(): jnp.dot(weights, v_rows, preferred_element_type=jnp.float32)  13.3 us
    ppermute x1, starting transfers between devices, shards(): lax.ppermute(out_weight, ('ylo', 'yhi'), perm=[(0, 0), (1, 2), (2, 1), (3...  10.4 us
  transfers between devices with their start and end apart: 7, of which 6 were waited for; matrix products, arithmetic and copies ran while one was open for 20% of the time, Pallas kernels for 0%

profile of v4, /device:TPU:1, one launch (start us, length us, event | category | flops | bytes accessed | tf_op | source)
XLA Modules:
  0.0 395.4 jit_solution(15661701651363020495)
XLA Ops:
  6.5 1.8 pad_maximum_fusion.1
  8.3 0.8 constant_dynamic-slice_fusion
  9.1 1.5 convolution_convert_fusion.1
  10.6 2.7 copy.14
  13.3 7.0 %all-to-all-start = ((bf16[16,128,768]{2,1,0:T(8,128)(2,1)}), bf16[16,128,768]{2,1,0:T(8,128)(2,1)}, u32[]{:S(2)}, u32[]{:S(2)}) async-start(bf16[16,128,768]{2,1,0:T(8,128)(2,1)} %copy.14), calls=%async_computation | async-start | bytes 6291456 | tf_op jit(solution)/shard_map/all_to_all | solution.py:58
  20.3 10.4 %collective-permute-start = (bf16[768,768]{1,0:T(8,128)(2,1)}, bf16[768,768]{1,0:T(8,128)(2,1)}, u32[]{:S(2)}, u32[]{:S(2)}) collective-permute-start(bf16[768,768]{1,0:T(8,128)(2,1)} %param.13), channel_id=1, source_target_pairs={{0,0},{4,64},{64,4},{68,68},{1,1},{5,65},{65,5},{69,69},{2,2},{6,6... | collective-permute-start | bytes 3538952 | tf_op jit(solution)/shard_map/ppermute | solution.py:72
  30.8 0.8 scatter_custom_fusion
  31.6 0.8 gather_fusion
  32.8 39.5 %all-to-all-done = bf16[16,128,768]{2,1,0:T(8,128)(2,1)} async-done(((bf16[16,128,768]{2,1,0:T(8,128)(2,1)}), bf16[16,128,768]{2,1,0:T(8,128)(2,1)}, u32[]{:S(2)}, u32[]{:S(2)}) %all-to-all-start) | async-done | bytes 3145760 | tf_op jit(solution)/shard_map/all_to_all | solution.py:58
  72.4 3.9 fusion.20
  76.2 1.0 copy.16
  77.2 4.5 %all-gather.3.cloned.1.call-done = bf16[8192,256]{1,0:T(8,128)(2,1)} async-done(((bf16[512,256]{1,0:T(8,128)(2,1)}), bf16[8192,256]{1,0:T(8,128)(2,1)}) %all-gather.3.cloned.1.call-update) | async-done | bytes 4194320 | tf_op jit(solution)/shard_map/all_gather | solution.py:39
  81.7 4.5 %gather_fusion.1 = bf16[36,128,256]{2,1,0:T(8,128)(2,1)} fusion(bf16[64,128,256]{2,1,0:T(8,128)(2,1)} %bitcast.59, s32[1024]{0:T(1024)S(1)} %pad_clamp_fusion), kind=kCustom, calls=%fused_computation.1 | custom fusion | bytes 4718736 | tf_op jit(solution)/shard_map/jit(_take)/gather | solution.py:49
  86.2 3.8 bitcast_select_fusion
  90.1 1.6 fusion.40
  91.9 60.4 %while.13 = (s32[]{:T(128)}, bf16[6,512,128]{1,2,0:T(8,128)(2,1)}, s32[4608]{0:T(1024)S(1)}, s32[512]{0:T(512)S(1)}, s32[6]{0:T(128)S(1)}, /*index=5*/bf16[512,7...) while((s32[]{:T(128)}, bf16[6,512,128]{1,2,0:T(8,128)(2,1)}, ...), condition=%wide.region_4.5_spmd.clone, body=%wide.region_1.0_spmd.clone.sunk | while | flops 1238700544 | bytes 36252392 | solution.py:91
  93.2 4.3 %fusion.52 = (f32[512]{0:T(512)S(1)}, f32[512,4608]{1,0:T(8,128)S(1)}) fusion(bf16[4608,128]{1,0:T(8,128)(2,1)} %get-tuple-element.293, bf16[512,768]{1,0:T(8,128)(2,1)} %get-tuple-element.292, s32[]{:T(128)S(6)} %select_n.165, s32[512]{0:T(512)S(1)} %get-tuple-element.290, s32[4608]{0:T(1024)S(1)} %get-tuple-element.289, ...), kind=kOutput, calls=%fused_computation.75.clone.1 | convolution fusion | flops 622853632 | bytes 10792964 | tf_op jit(solution)/shard_map/while/body/eval_jaxpr/dot_general | solution.py:17
  97.6 1.4 fusion.53
  99.0 2.2 fusion.54
  101.3 0.7 constant_dynamic-update-slice_fusion.2
  103.3 4.3 %fusion.52 = (f32[512]{0:T(512)S(1)}, f32[512,4608]{1,0:T(8,128)S(1)}) fusion(bf16[4608,128]{1,0:T(8,128)(2,1)} %get-tuple-element.293, bf16[512,768]{1,0:T(8,128)(2,1)} %get-tuple-element.292, s32[]{:T(128)S(6)} %select_n.165, s32[512]{0:T(512)S(1)} %get-tuple-element.290, s32[4608]{0:T(1024)S(1)} %get-tuple-element.289, ...), kind=kOutput, calls=%fused_computation.75.clone.1 | convolution fusion | flops 622853632 | bytes 10792964 | tf_op jit(solution)/shard_map/while/body/eval_jaxpr/dot_general | solution.py:17
  107.6 1.4 fusion.53
  109.0 2.2 fusion.54
  111.4 0.7 constant_dynamic-update-slice_fusion.2
  113.3 4.3 %fusion.52 = (f32[512]{0:T(512)S(1)}, f32[512,4608]{1,0:T(8,128)S(1)}) fusion(bf16[4608,128]{1,0:T(8,128)(2,1)} %get-tuple-element.293, bf16[512,768]{1,0:T(8,128)(2,1)} %get-tuple-element.292, s32[]{:T(128)S(6)} %select_n.165, s32[512]{0:T(512)S(1)} %get-tuple-element.290, s32[4608]{0:T(1024)S(1)} %get-tuple-element.289, ...), kind=kOutput, calls=%fused_computation.75.clone.1 | convolution fusion | flops 622853632 | bytes 10792964 | tf_op jit(solution)/shard_map/while/body/eval_jaxpr/dot_general | solution.py:17
  117.7 1.4 fusion.53
  119.1 2.2 fusion.54
  121.4 0.7 constant_dynamic-update-slice_fusion.2
  123.4 4.4 %fusion.52 = (f32[512]{0:T(512)S(1)}, f32[512,4608]{1,0:T(8,128)S(1)}) fusion(bf16[4608,128]{1,0:T(8,128)(2,1)} %get-tuple-element.293, bf16[512,768]{1,0:T(8,128)(2,1)} %get-tuple-element.292, s32[]{:T(128)S(6)} %select_n.165, s32[512]{0:T(512)S(1)} %get-tuple-element.290, s32[4608]{0:T(1024)S(1)} %get-tuple-element.289, ...), kind=kOutput, calls=%fused_computation.75.clone.1 | convolution fusion | flops 622853632 | bytes 10792964 | tf_op jit(solution)/shard_map/while/body/eval_jaxpr/dot_general | solution.py:17
  127.7 1.4 fusion.53
  129.2 2.2 fusion.54
  133.4 4.4 %fusion.52 = (f32[512]{0:T(512)S(1)}, f32[512,4608]{1,0:T(8,128)S(1)}) fusion(bf16[4608,128]{1,0:T(8,128)(2,1)} %get-tuple-element.293, bf16[512,768]{1,0:T(8,128)(2,1)} %get-tuple-element.292, s32[]{:T(128)S(6)} %select_n.165, s32[512]{0:T(512)S(1)} %get-tuple-element.290, s32[4608]{0:T(1024)S(1)} %get-tuple-element.289, ...), kind=kOutput, calls=%fused_computation.75.clone.1 | convolution fusion | flops 622853632 | bytes 10792964 | tf_op jit(solution)/shard_map/while/body/eval_jaxpr/dot_general | solution.py:17
  137.8 1.4 fusion.53
  139.2 2.2 fusion.54
  143.5 4.3 %fusion.52 = (f32[512]{0:T(512)S(1)}, f32[512,4608]{1,0:T(8,128)S(1)}) fusion(bf16[4608,128]{1,0:T(8,128)(2,1)} %get-tuple-element.293, bf16[512,768]{1,0:T(8,128)(2,1)} %get-tuple-element.292, s32[]{:T(128)S(6)} %select_n.165, s32[512]{0:T(512)S(1)} %get-tuple-element.290, s32[4608]{0:T(1024)S(1)} %get-tuple-element.289, ...), kind=kOutput, calls=%fused_computation.75.clone.1 | convolution fusion | flops 622853632 | bytes 10792964 | tf_op jit(solution)/shard_map/while/body/eval_jaxpr/dot_general | solution.py:17
  147.9 1.4 fusion.53
  149.3 2.2 fusion.54
  152.3 2.7 collective-permute-start.1
  155.0 51.0 %collective-permute-done.1 = bf16[512,768]{0,1:T(8,128)(2,1)S(1)} collective-permute-done((bf16[512,768]{0,1:T(8,128)(2,1)}, bf16[512,768]{0,1:T(8,128)(2,1)S(1)}, u32[]{:S(2)}, u32[]{:S(2)}) %collective-permute-start.1) | collective-permute-done | bytes 786464 | tf_op jit(solution)/shard_map/ppermute | solution.py:95
  205.9 2.0 maximum_select_fusion.1
  207.9 1.4 collective-permute-start.2
  209.3 3.2 collective-permute-done.2
  212.5 85.4 %all-gather.5.cloned.1.call-done = bf16[6144,768]{1,0:T(8,128)(2,1)} async-done(((bf16[768,768]{1,0:T(8,128)(2,1)}), bf16[6144,768]{1,0:T(8,128)(2,1)}) %all-gather.5.cloned.1.call-update) | async-done | bytes 9437200 | tf_op jit(solution)/shard_map/all_gather | solution.py:74
  297.9 16.7 %convolution_convert_fusion = bf16[1024,4,768]{0,2,1:T(8,128)(2,1)} fusion(bf16[4,1536,768]{2,1,0:T(8,128)(2,1)} %bitcast.63, bf16[512,1536]{0,1:T(8,128)(2,1)} %collective-permute-done.2, bf16[512,1536]{0,1:T(8,128)(2,1)S(1)} %maximum_select_fusion.1, pred[]{:T(512)S(6)} %eq.84), kind=kOutput, calls=%fused_computation.18 | convolution fusion | flops 9680977920 | bytes 18874368 | tf_op jit(solution)/shard_map/dot_general | solution.py:109
  314.6 66.0 %reduce-scatter.2.cloned.1.call-done = bf16[1024,768]{0,1:T(8,128)(2,1)} async-done(((bf16[1024,3072]{0,1:T(8,128)(2,1)}), bf16[1024,768]{0,1:T(8,128)(2,1)}) %reduce-scatter.2.cloned.1.call-update) | async-done | bytes 1572880 | tf_op jit(solution)/shard_map/reduce_scatter | solution.py:113
  380.6 1.7 copy.20
  382.3 5.2 %all_to_all.14 = bf16[2,512,768]{2,1,0:T(8,128)(2,1)S(1)} all-to-all(bf16[2,512,768]{2,1,0:T(8,128)(2,1)S(1)} %bitcast.58), channel_id=1, replica_groups=mesh['ylo'=2,'x'=4,'c'=2,'yhi'=2,'z'=4] {'c'}, dimensions={0} | all-to-all | bytes 3145728 | tf_op jit(solution)/shard_map/all_to_all | solution.py:114
  387.7 1.3 pad_maximum_fusion
  (69 shorter events, 7.5 us)
Async XLA Ops:
  6.5 2.6 copy-start
  6.5 75.2 %all-gather.3.cloned.1.call-start = ((), (), s32[]{:S(2)}) async-start(), calls=%async_computation.3 | async-start | bytes 4456448 | tf_op jit(solution)/shard_map/all_gather | solution.py:39
  13.3 17.4 %copy-start.3 = (s32[64,2]{0,1:T(2,128)S(1)}, s32[64,2]{0,1:T(2,128)}, u32[]{:S(2)}) copy-start(s32[64,2]{0,1:T(2,128)} %param.12) | copy-start | bytes 1540
  13.3 19.0 %copy-start.2 = (s32[8192]{0:T(1024)S(1)}, s32[8192]{0:T(1024)}, u32[]{:S(2)}) copy-start(s32[8192]{0:T(1024)} %param.11) | copy-start | bytes 98308
  13.3 59.0 %all-to-all-start = ((bf16[16,128,768]{2,1,0:T(8,128)(2,1)}), bf16[16,128,768]{2,1,0:T(8,128)(2,1)}, u32[]{:S(2)}, u32[]{:S(2)}) async-start(bf16[16,128,768]{2,1,0:T(8,128)(2,1)} %copy.14), calls=%async_computation | async-start | bytes 6291456 | tf_op jit(solution)/shard_map/all_to_all | solution.py:58
  20.3 277.6 %all-gather.5.cloned.1.call-start = ((), (), s32[]{:S(2)}) async-start(), calls=%async_computation.4 | async-start | bytes 10616832 | tf_op jit(solution)/shard_map/all_gather | solution.py:74
  20.3 69.7 %collective-permute-start = (bf16[768,768]{1,0:T(8,128)(2,1)}, bf16[768,768]{1,0:T(8,128)(2,1)}, u32[]{:S(2)}, u32[]{:S(2)}) collective-permute-start(bf16[768,768]{1,0:T(8,128)(2,1)} %param.13), channel_id=1, source_target_pairs={{0,0},{4,64},{64,4},{68,68},{1,1},{5,65},{65,5},{69,69},{2,2},{6,6... | collective-permute-start | bytes 3538952 | tf_op jit(solution)/shard_map/ppermute | solution.py:72
  91.7 288.9 %reduce-scatter.2.cloned.1.call-start = ((), (), s32[]{:S(2)}) async-start(), calls=%async_computation.5 | async-start | bytes 7864320 | tf_op jit(solution)/shard_map/reduce_scatter | solution.py:113
  97.6 1.4 copy-start.1
  107.6 1.4 copy-start.1
  117.6 1.4 copy-start.1
  127.7 1.4 copy-start.1
  137.8 1.4 copy-start.1
  147.8 1.4 copy-start.1
  152.3 53.7 %collective-permute-start.1 = (bf16[512,768]{0,1:T(8,128)(2,1)}, bf16[512,768]{0,1:T(8,128)(2,1)S(1)}, u32[]{:S(2)}, u32[]{:S(2)}) collective-permute-start(bf16[512,768]{0,1:T(8,128)(2,1)} %bitcast.61), channel_id=1, source_target_pairs={{0,4},{4,0},{1,5},{5,1},{2,6},{6,2},{3,7},{7,3},{8,12},{12,8},{9,1... | collective-permute-start | bytes 2359304 | tf_op jit(solution)/shard_map/ppermute | solution.py:95
  207.9 4.6 %collective-permute-start.2 = (bf16[512,1536]{0,1:T(8,128)(2,1)S(1)}, bf16[512,1536]{0,1:T(8,128)(2,1)}, u32[]{:S(2)}, u32[]{:S(2)}) collective-permute-start(bf16[512,1536]{0,1:T(8,128)(2,1)S(1)} %maximum_select_fusion.1), channel_id=1, source_target_pairs={{0,8},{8,0},{1,9},{9,1},{2,10},{10,2},{3,11},{11,3},{4,12},{12,4},... | collective-permute-start | bytes 4718600 | tf_op jit(solution)/shard_map/ppermute | solution.py:102
Sparse Core Ops, SparseCore 0:
  9.1 72.5 all-gather.2
  91.8 206.0 all-gather.4
  314.7 65.8 reduce-scatter.1

commit v5 on v4

--- a/solution.py
+++ b/solution.py
@@ -71,8 +71,8 @@
 
     w_swapped = lax.ppermute(out_weight, ("ylo", "yhi"), perm=[(0, 0), (1, 2), (2, 1), (3, 3)])
     context, w_swapped = lax.optimization_barrier((context, w_swapped))
-    w_here = lax.all_gather(w_swapped, ("x", "ylo"), axis=0, tiled=True)
-    w_here = w_here.reshape(-1, 2 * out_weight.shape[0], out_weight.shape[1])
+    w_here = lax.all_gather(w_swapped, ("ylo", "x"), axis=0, tiled=True)
+    w_here = w_here.reshape(2, -1, out_weight.shape[0], out_weight.shape[1])
 
     ctx_keys = context[:, :kv_cols]
     ctx_values = context[:, kv_cols:]
@@ -106,8 +106,9 @@
         jnp.concatenate([h_groups, h_near], axis=0),
         jnp.concatenate([h_near, h_groups], axis=0),
     )
+    h_split = h_here.reshape(h_here.shape[0], 2, -1)
     part = lax.dot_general(
-        h_here, w_here, (((1,), (1,)), ((), ())), preferred_element_type=jnp.float32
+        h_split, w_here, (((1, 2), (0, 2)), ((), ())), preferred_element_type=jnp.float32
     )
     part = part.astype(jnp.bfloat16).reshape(h_here.shape[0], -1)
     summed = lax.psum_scatter(part, "z", scatter_dimension=1, tiled=True)

time: 397 us -> 315 us (0.79)
  waiting for transfers between devices: 250 us -> 164 us
    all_gather x1, waiting for transfers between devices: 85.4 us -> 0.01 us  [shards(): w_here = lax.all_gather(w_swapped, ('ylo', 'x'), axis=0, tiled=True)]
    ppermute x1, waiting for transfers between devices: 51 us -> 57.4 us  [shards(): h_far = lax.ppermute(attended, 'yhi', pair)]
    reduce_scatter x1, waiting for transfers between devices: 66 us -> 61.1 us  [shards(): summed = lax.psum_scatter(part, 'z', scatter_dimension=1, tiled=True)]
  transfers between devices with their start and end apart: 7 -> 7, of which waited for: 6 -> 5; matrix products, arithmetic and copies ran while one was open for 20% -> 26% of each run, Pallas kernels for 0% -> 0%
where the time goes in v5:
time: 315 us; the launch traced here: 313 us
  waiting for transfers between devices  164 us (52%)
  matrix products  62.3 us (20%)
  local copies, waits for them, and re-layouts  22.9 us (7%)
  starting transfers between devices  20.9 us (7%)
  other arithmetic  19.9 us (6%)
  between operations  13.2 us (4%)
  blocking collectives  5.25 us (2%)
  loops' own time  4.42 us (1%)
    reduce_scatter x1, waiting for transfers between devices, shards(): summed = lax.psum_scatter(part, 'z', scatter_dimension=1, tiled=True)  61.1 us
    ppermute x1, waiting for transfers between devices, shards(): h_far = lax.ppermute(attended, 'yhi', pair)  57.4 us
    all_to_all x1, waiting for transfers between devices, shards(): lax.all_to_all(outgoing, SEQ, split_axis=0, concat_axis=0, tiled=True)  39.5 us
    dot_general x6, matrix products, attend_head(): lax.dot_general(q_rows, k_rows, (((1,), (1,)), ((), ())), preferred_eleme...  26 us
    dot_general x1, matrix products, shards(): lax.dot_general(h_split, w_here, (((1, 2), (0, 2)), ((), ())), preferred_...  17.6 us
    dot_general x6, matrix products, attend_head(): jnp.dot(weights, v_rows, preferred_element_type=jnp.float32)  13.3 us
    ppermute x1, starting transfers between devices, shards(): lax.ppermute(out_weight, ('ylo', 'yhi'), perm=[(0, 0), (1, 2), (2, 1), (3...  10.4 us
    reduce_sum x6, other arithmetic, attend_head(): weights = (expo / jnp.sum(expo, axis=1, keepdims=True)).astype(jnp.bfloat16)  8.42 us
  transfers between devices with their start and end apart: 7, of which 5 were waited for; matrix products, arithmetic and copies ran while one was open for 26% of the time, Pallas kernels for 0%

profile of v5, /device:TPU:1, one launch (start us, length us, event | category | flops | bytes accessed | tf_op | source)
XLA Modules:
  0.0 313.4 jit_solution(5879012871563526036)
XLA Ops:
  6.5 1.8 pad_maximum_fusion.1
  8.3 0.8 constant_dynamic-slice_fusion
  9.1 1.5 convolution_convert_fusion
  10.6 2.7 copy.14
  13.3 7.0 %all-to-all-start = ((bf16[16,128,768]{2,1,0:T(8,128)(2,1)}), bf16[16,128,768]{2,1,0:T(8,128)(2,1)}, u32[]{:S(2)}, u32[]{:S(2)}) async-start(bf16[16,128,768]{2,1,0:T(8,128)(2,1)} %copy.14), calls=%async_computation | async-start | bytes 6291456 | tf_op jit(solution)/shard_map/all_to_all | solution.py:58
  20.4 10.4 %collective-permute-start = (bf16[768,768]{1,0:T(8,128)(2,1)}, bf16[768,768]{1,0:T(8,128)(2,1)}, u32[]{:S(2)}, u32[]{:S(2)}) collective-permute-start(bf16[768,768]{1,0:T(8,128)(2,1)} %param.13), channel_id=1, source_target_pairs={{0,0},{4,64},{64,4},{68,68},{1,1},{5,65},{65,5},{69,69},{2,2},{6,6... | collective-permute-start | bytes 3538952 | tf_op jit(solution)/shard_map/ppermute | solution.py:72
  30.8 0.8 scatter_custom_fusion
  31.6 0.8 gather_fusion
  32.9 39.5 %all-to-all-done = bf16[16,128,768]{2,1,0:T(8,128)(2,1)} async-done(((bf16[16,128,768]{2,1,0:T(8,128)(2,1)}), bf16[16,128,768]{2,1,0:T(8,128)(2,1)}, u32[]{:S(2)}, u32[]{:S(2)}) %all-to-all-start) | async-done | bytes 3145760 | tf_op jit(solution)/shard_map/all_to_all | solution.py:58
  72.4 3.9 %fusion.19 = bf16[4,128,768]{2,0,1:T(4,128)(2,1)S(1)} fusion(bf16[4,16,1]{1,0,2:T(4,128)(2,1)S(1)} %fusion.22, bf16[16,128,768]{2,1,0:T(8,128)(2,1)} %all-to-all-done), kind=kOutput, calls=%fused_computation.34 | convolution fusion | flops 12976128 | bytes 3932288 | tf_op jit(solution)/shard_map/od,drc->orc/dot_general | solution.py:67
  76.3 1.0 copy.16
  77.3 4.4 %all-gather.3.cloned.1.call-done = bf16[8192,256]{1,0:T(8,128)(2,1)} async-done(((bf16[512,256]{1,0:T(8,128)(2,1)}), bf16[8192,256]{1,0:T(8,128)(2,1)}) %all-gather.3.cloned.1.call-update) | async-done | bytes 4194320 | tf_op jit(solution)/shard_map/all_gather | solution.py:39
  81.7 4.5 %gather_fusion.1 = bf16[36,128,256]{2,1,0:T(8,128)(2,1)} fusion(bf16[64,128,256]{2,1,0:T(8,128)(2,1)} %bitcast.74, s32[1024]{0:T(1024)S(1)} %pad_clamp_fusion), kind=kCustom, calls=%fused_computation.1 | custom fusion | bytes 4718736 | tf_op jit(solution)/shard_map/jit(_take)/gather | solution.py:49
  86.2 3.8 %bitcast_select_fusion = bf16[4608,256]{1,0:T(8,128)(2,1)S(1)} fusion(bf16[36,128,256]{2,1,0:T(8,128)(2,1)} %gather_fusion.1, pred[4608]{0:T(1024)(128)(4,1)S(1)} %broadcast_bitcast_fusion), kind=kLoop, calls=%fused_computation.29 | loop fusion | flops 1179648 | bytes 4723200 | tf_op jit(solution)/shard_map/jit(_take)/select_n | solution.py:49
  90.1 1.6 fusion.39
  92.0 60.8 %while.13 = (s32[]{:T(128)}, bf16[6,512,128]{1,2,0:T(8,128)(2,1)}, s32[4608]{0:T(1024)S(1)}, s32[512]{0:T(512)S(1)}, s32[6]{0:T(128)S(1)}, /*index=5*/bf16[512,7...) while((s32[]{:T(128)}, bf16[6,512,128]{1,2,0:T(8,128)(2,1)}, ...), condition=%wide.region_4.5_spmd.clone, body=%wide.region_1.0_spmd.clone.sunk | while | flops 1238700544 | bytes 36252392 | solution.py:91
  93.3 4.3 %fusion.51 = (f32[512]{0:T(512)S(1)}, f32[512,4608]{1,0:T(8,128)S(1)}) fusion(bf16[4608,128]{1,0:T(8,128)(2,1)} %get-tuple-element.293, bf16[512,768]{1,0:T(8,128)(2,1)} %get-tuple-element.292, s32[]{:T(128)S(6)} %select_n.175, s32[512]{0:T(512)S(1)} %get-tuple-element.290, s32[4608]{0:T(1024)S(1)} %get-tuple-element.289, ...), kind=kOutput, calls=%fused_computation.76.clone.1 | convolution fusion | flops 622853632 | bytes 10792964 | tf_op jit(solution)/shard_map/while/body/eval_jaxpr/dot_general | solution.py:17
  97.7 1.4 fusion.52
  99.1 2.2 fusion.53
  101.4 0.7 constant_dynamic-update-slice_fusion.2
  103.5 4.3 %fusion.51 = (f32[512]{0:T(512)S(1)}, f32[512,4608]{1,0:T(8,128)S(1)}) fusion(bf16[4608,128]{1,0:T(8,128)(2,1)} %get-tuple-element.293, bf16[512,768]{1,0:T(8,128)(2,1)} %get-tuple-element.292, s32[]{:T(128)S(6)} %select_n.175, s32[512]{0:T(512)S(1)} %get-tuple-element.290, s32[4608]{0:T(1024)S(1)} %get-tuple-element.289, ...), kind=kOutput, calls=%fused_computation.76.clone.1 | convolution fusion | flops 622853632 | bytes 10792964 | tf_op jit(solution)/shard_map/while/body/eval_jaxpr/dot_general | solution.py:17
  107.8 1.4 fusion.52
  109.2 2.2 fusion.53
  111.6 0.7 constant_dynamic-update-slice_fusion.2
  113.6 4.3 %fusion.51 = (f32[512]{0:T(512)S(1)}, f32[512,4608]{1,0:T(8,128)S(1)}) fusion(bf16[4608,128]{1,0:T(8,128)(2,1)} %get-tuple-element.293, bf16[512,768]{1,0:T(8,128)(2,1)} %get-tuple-element.292, s32[]{:T(128)S(6)} %select_n.175, s32[512]{0:T(512)S(1)} %get-tuple-element.290, s32[4608]{0:T(1024)S(1)} %get-tuple-element.289, ...), kind=kOutput, calls=%fused_computation.76.clone.1 | convolution fusion | flops 622853632 | bytes 10792964 | tf_op jit(solution)/shard_map/while/body/eval_jaxpr/dot_general | solution.py:17
  118.0 1.4 fusion.52
  119.4 2.2 fusion.53
  121.7 0.7 constant_dynamic-update-slice_fusion.2
  123.8 4.3 %fusion.51 = (f32[512]{0:T(512)S(1)}, f32[512,4608]{1,0:T(8,128)S(1)}) fusion(bf16[4608,128]{1,0:T(8,128)(2,1)} %get-tuple-element.293, bf16[512,768]{1,0:T(8,128)(2,1)} %get-tuple-element.292, s32[]{:T(128)S(6)} %select_n.175, s32[512]{0:T(512)S(1)} %get-tuple-element.290, s32[4608]{0:T(1024)S(1)} %get-tuple-element.289, ...), kind=kOutput, calls=%fused_computation.76.clone.1 | convolution fusion | flops 622853632 | bytes 10792964 | tf_op jit(solution)/shard_map/while/body/eval_jaxpr/dot_general | solution.py:17
  128.1 1.4 fusion.52
  129.5 2.2 fusion.53
  133.9 4.3 %fusion.51 = (f32[512]{0:T(512)S(1)}, f32[512,4608]{1,0:T(8,128)S(1)}) fusion(bf16[4608,128]{1,0:T(8,128)(2,1)} %get-tuple-element.293, bf16[512,768]{1,0:T(8,128)(2,1)} %get-tuple-element.292, s32[]{:T(128)S(6)} %select_n.175, s32[512]{0:T(512)S(1)} %get-tuple-element.290, s32[4608]{0:T(1024)S(1)} %get-tuple-element.289, ...), kind=kOutput, calls=%fused_computation.76.clone.1 | convolution fusion | flops 622853632 | bytes 10792964 | tf_op jit(solution)/shard_map/while/body/eval_jaxpr/dot_general | solution.py:17
  138.2 1.4 fusion.52
  139.6 2.2 fusion.53
  144.0 4.3 %fusion.51 = (f32[512]{0:T(512)S(1)}, f32[512,4608]{1,0:T(8,128)S(1)}) fusion(bf16[4608,128]{1,0:T(8,128)(2,1)} %get-tuple-element.293, bf16[512,768]{1,0:T(8,128)(2,1)} %get-tuple-element.292, s32[]{:T(128)S(6)} %select_n.175, s32[512]{0:T(512)S(1)} %get-tuple-element.290, s32[4608]{0:T(1024)S(1)} %get-tuple-element.289, ...), kind=kOutput, calls=%fused_computation.76.clone.1 | convolution fusion | flops 622853632 | bytes 10792964 | tf_op jit(solution)/shard_map/while/body/eval_jaxpr/dot_general | solution.py:17
  148.3 1.4 fusion.52
  149.7 2.2 fusion.53
  152.1 0.7 constant_dynamic-update-slice_fusion.2
  152.8 2.7 collective-permute-start.1
  155.5 57.4 %collective-permute-done.1 = bf16[512,768]{0,1:T(8,128)(2,1)S(1)} collective-permute-done((bf16[512,768]{0,1:T(8,128)(2,1)}, bf16[512,768]{0,1:T(8,128)(2,1)S(1)}, u32[]{:S(2)}, u32[]{:S(2)}) %collective-permute-start.1) | collective-permute-done | bytes 786464 | tf_op jit(solution)/shard_map/ppermute | solution.py:95
  212.9 3.1 maximum_select_fusion.3
  216.5 1.4 maximum_select_fusion.2
  217.9 2.0 collective-permute-done.2
  219.9 17.6 %bitcast_convert_fusion = bf16[1024,4,768]{0,2,1:T(8,128)(2,1)} fusion(bf16[2,4,768,768]{3,2,1,0:T(8,128)(2,1)} %bitcast.76, bf16[512,2,768]{0,2,1:T(8,128)(2,1)} %bitcast.20, bf16[512,2,768]{0,2,1:T(8,128)(2,1)} %maximum_select_fusion.2, pred[]{:T(512)S(6)} %eq.84), kind=kOutput, calls=%fused_computation.18 | convolution fusion | flops 9680977920 | bytes 18874368 | tf_op jit(solution)/shard_map/dot_general | solution.py:110
  237.5 61.1 %reduce-scatter.2.cloned.1.call-done = bf16[1024,768]{0,1:T(8,128)(2,1)} async-done(((bf16[1024,3072]{0,1:T(8,128)(2,1)}), bf16[1024,768]{0,1:T(8,128)(2,1)}) %reduce-scatter.2.cloned.1.call-update) | async-done | bytes 1572880 | tf_op jit(solution)/shard_map/reduce_scatter | solution.py:114
  298.5 1.7 copy.20
  300.2 5.3 %all_to_all.14 = bf16[2,512,768]{2,1,0:T(8,128)(2,1)S(1)} all-to-all(bf16[2,512,768]{2,1,0:T(8,128)(2,1)S(1)} %bitcast.69), channel_id=1, replica_groups=mesh['ylo'=2,'x'=4,'c'=2,'yhi'=2,'z'=4] {'c'}, dimensions={0} | all-to-all | bytes 3145728 | tf_op jit(solution)/shard_map/all_to_all | solution.py:115
  305.6 1.3 pad_maximum_fusion
  (72 shorter events, 7.4 us)
Async XLA Ops:
  6.5 2.6 copy-start
  6.5 75.2 %all-gather.3.cloned.1.call-start = ((), (), s32[]{:S(2)}) async-start(), calls=%async_computation.3 | async-start | bytes 4456448 | tf_op jit(solution)/shard_map/all_gather | solution.py:39
  13.3 17.5 %copy-start.4 = (s32[64,2]{0,1:T(2,128)S(1)}, s32[64,2]{0,1:T(2,128)}, u32[]{:S(2)}) copy-start(s32[64,2]{0,1:T(2,128)} %param.12) | copy-start | bytes 1540
  13.3 19.1 %copy-start.3 = (s32[8192]{0:T(1024)S(1)}, s32[8192]{0:T(1024)}, u32[]{:S(2)}) copy-start(s32[8192]{0:T(1024)} %param.11) | copy-start | bytes 98308
  13.3 59.1 %all-to-all-start = ((bf16[16,128,768]{2,1,0:T(8,128)(2,1)}), bf16[16,128,768]{2,1,0:T(8,128)(2,1)}, u32[]{:S(2)}, u32[]{:S(2)}) async-start(bf16[16,128,768]{2,1,0:T(8,128)(2,1)} %copy.14), calls=%async_computation | async-start | bytes 6291456 | tf_op jit(solution)/shard_map/all_to_all | solution.py:58
  20.3 199.6 %all-gather.5.cloned.1.call-start = ((), (), s32[]{:S(2)}) async-start(), calls=%async_computation.4 | async-start | bytes 10616832 | tf_op jit(solution)/shard_map/all_gather | solution.py:74
  20.4 69.7 %collective-permute-start = (bf16[768,768]{1,0:T(8,128)(2,1)}, bf16[768,768]{1,0:T(8,128)(2,1)}, u32[]{:S(2)}, u32[]{:S(2)}) collective-permute-start(bf16[768,768]{1,0:T(8,128)(2,1)} %param.13), channel_id=1, source_target_pairs={{0,0},{4,64},{64,4},{68,68},{1,1},{5,65},{65,5},{69,69},{2,2},{6,6... | collective-permute-start | bytes 3538952 | tf_op jit(solution)/shard_map/ppermute | solution.py:72
  91.7 206.8 %reduce-scatter.2.cloned.1.call-start = ((), (), s32[]{:S(2)}) async-start(), calls=%async_computation.5 | async-start | bytes 7864320 | tf_op jit(solution)/shard_map/reduce_scatter | solution.py:114
  97.7 1.4 copy-start.2
  107.8 1.4 copy-start.2
  118.0 1.4 copy-start.2
  128.1 1.4 copy-start.2
  138.2 1.4 copy-start.2
  148.3 1.4 copy-start.2
  152.8 63.7 %copy-start.1 = (bf16[6,512,128]{1,2,0:T(8,128)(2,1)S(1)}, bf16[6,512,128]{1,2,0:T(8,128)(2,1)}, u32[]{:S(2)}) copy-start(bf16[6,512,128]{1,2,0:T(8,128)(2,1)} %get-tuple-element.133) | copy-start | bytes 2359300
  152.8 60.2 %collective-permute-start.1 = (bf16[512,768]{0,1:T(8,128)(2,1)}, bf16[512,768]{0,1:T(8,128)(2,1)S(1)}, u32[]{:S(2)}, u32[]{:S(2)}) collective-permute-start(bf16[512,768]{0,1:T(8,128)(2,1)} %bitcast.70), channel_id=1, source_target_pairs={{0,4},{4,0},{1,5},{5,1},{2,6},{6,2},{3,7},{7,3},{8,12},{12,8},{9,1... | collective-permute-start | bytes 2359304 | tf_op jit(solution)/shard_map/ppermute | solution.py:95
  216.0 3.8 %collective-permute-start.2 = (bf16[512,1536]{0,1:T(8,128)(2,1)}, bf16[512,1536]{0,1:T(8,128)(2,1)}, u32[]{:S(2)}, u32[]{:S(2)}) collective-permute-start(bf16[512,1536]{0,1:T(8,128)(2,1)} %maximum_select_fusion.3), channel_id=1, source_target_pairs={{0,8},{8,0},{1,9},{9,1},{2,10},{10,2},{3,11},{11,3},{4,12},{12,4},... | collective-permute-start | bytes 4718600 | tf_op jit(solution)/shard_map/ppermute | solution.py:102
Sparse Core Ops, SparseCore 0:
  9.1 72.6 all-gather.2
  91.8 103.2 all-gather.4
  237.6 60.8 reduce-scatter.1

commit v6 on v5

--- a/solution.py
+++ b/solution.py
@@ -36,8 +36,6 @@
     blocks_all = packing.shape[0]
 
     kv_local = jnp.concatenate([keys, values], axis=1)
-    kv_all = lax.all_gather(kv_local, SEQ, axis=0, tiled=True)
-    kv_blocks = kv_all.reshape(blocks_all, BLOCK, 2 * kv_cols)
     target = packing[:, 0] * per_shard + packing[:, 1]
     source = jnp.zeros((blocks_all,), jnp.int32).at[target].set(
         jnp.arange(blocks_all, dtype=jnp.int32)
@@ -46,7 +44,11 @@
     ctx_blocks = span_blocks + per_shard
     blk_ids = shard_index * per_shard - span_blocks + jnp.arange(ctx_blocks, dtype=jnp.int32)
     src = jnp.take(source, jnp.clip(blk_ids, 0, blocks_all - 1))
-    context = jnp.take(kv_blocks, src, axis=0).reshape(ctx_blocks * BLOCK, 2 * kv_cols)
+
+    w_swapped = lax.ppermute(out_weight, ("ylo", "yhi"), perm=[(0, 0), (1, 2), (2, 1), (3, 3)])
+    kv_local, w_swapped = lax.optimization_barrier((kv_local, w_swapped))
+    w_here = lax.all_gather(w_swapped, ("ylo", "x"), axis=0, tiled=True)
+    w_here = w_here.reshape(2, -1, out_weight.shape[0], out_weight.shape[1])
 
     own_blocks = queries.reshape(per_shard, BLOCK, q_cols)
     own_list = lax.dynamic_slice_in_dim(packing, shard_index * per_shard, per_shard, 0)
@@ -56,6 +58,10 @@
         "db,brc->drc", routing, own_blocks, preferred_element_type=jnp.float32
     ).astype(jnp.bfloat16)
     incoming = lax.all_to_all(outgoing, SEQ, split_axis=0, concat_axis=0, tiled=True)
+    kv_copies = jnp.broadcast_to(kv_local[None], (seq_count,) + kv_local.shape)
+    kv_blocks = lax.all_to_all(kv_copies, SEQ, split_axis=0, concat_axis=0, tiled=True)
+    kv_blocks = kv_blocks.reshape(blocks_all, BLOCK, 2 * kv_cols)
+    context = jnp.take(kv_blocks, src, axis=0).reshape(ctx_blocks * BLOCK, 2 * kv_cols)
     arriving = packing[:, 0] == shard_index
     offset_ids = jnp.arange(per_shard, dtype=jnp.int32)
     at_offset = ((packing[:, 1][None, :] == offset_ids[:, None]) & arriving[None, :]).astype(
@@ -68,11 +74,6 @@
         "od,drc->orc", placing, incoming, preferred_element_type=jnp.float32
     ).astype(jnp.bfloat16)
     queries_here = packed.reshape(tok_rows, q_cols)
-
-    w_swapped = lax.ppermute(out_weight, ("ylo", "yhi"), perm=[(0, 0), (1, 2), (2, 1), (3, 3)])
-    context, w_swapped = lax.optimization_barrier((context, w_swapped))
-    w_here = lax.all_gather(w_swapped, ("ylo", "x"), axis=0, tiled=True)
-    w_here = w_here.reshape(2, -1, out_weight.shape[0], out_weight.shape[1])
 
     ctx_keys = context[:, :kv_cols]
     ctx_values = context[:, kv_cols:]

time: 315 us -> 339 us (1.076)
  waiting for transfers between devices: 164 us -> 208 us
  other arithmetic: 19.9 us -> 14.3 us
  starting transfers between devices: 20.9 us -> 15.6 us
  matrix products: 62.3 us -> 58.4 us
  local copies, waits for them, and re-layouts: 22.9 us -> 19.2 us
    all_to_all x0 -> x1, waiting for transfers between devices: none -> 78.2 us  [shards(): lax.all_to_all(kv_copies, SEQ, split_axis=0, concat_axis=0, tiled=True)]
    ppermute x1, waiting for transfers between devices: 57.4 us -> 17.1 us  [shards(): h_far = lax.ppermute(attended, 'yhi', pair)]
    ppermute x1, starting transfers between devices: 10.4 us -> 0.74 us  [shards(): lax.ppermute(out_weight, ('ylo', 'yhi'), perm=[(0, 0), (1, 2), (2, 1), (3...]
    reduce_scatter x1, waiting for transfers between devices: 61.1 us -> 67.7 us  [shards(): summed = lax.psum_scatter(part, 'z', scatter_dimension=1, tiled=True)]
    all_to_all x0 -> x1, starting transfers between devices: none -> 5 us  [shards(): lax.all_to_all(kv_copies, SEQ, split_axis=0, concat_axis=0, tiled=True)]
    all_gather x1 -> x0, waiting for transfers between devices: 4.43 us -> none  [shards(): kv_all = lax.all_gather(kv_local, SEQ, axis=0, tiled=True)]
    dynamic_update_slice x12, local copies, waits for them, and re-layouts: 4.73 us -> 0.78 us  [shards(): per_head = lax.map(one_head, jnp.arange(heads_here, dtype=jnp.int32))]
  transfers between devices with their start and end apart: 7 -> 7, of which waited for: 5 -> 5; matrix products, arithmetic and copies ran while one was open for 26% -> 19% of each run, Pallas kernels for 0% -> 0%
where the time goes in v6:
time: 339 us; the launch traced here: 338 us
  waiting for transfers between devices  208 us (61%)
  matrix products  58.4 us (17%)
  local copies, waits for them, and re-layouts  19.2 us (6%)
  starting transfers between devices  15.6 us (5%)
  other arithmetic  14.3 us (4%)
  between operations  13.6 us (4%)
  blocking collectives  5.39 us (2%)
  loops' own time  4.25 us (1%)
    all_to_all x1, waiting for transfers between devices, shards(): lax.all_to_all(kv_copies, SEQ, split_axis=0, concat_axis=0, tiled=True)  78.2 us
    reduce_scatter x1, waiting for transfers between devices, shards(): summed = lax.psum_scatter(part, 'z', scatter_dimension=1, tiled=True)  67.7 us
    all_to_all x1, waiting for transfers between devices, shards(): lax.all_to_all(outgoing, SEQ, split_axis=0, concat_axis=0, tiled=True)  41.2 us
    dot_general x6, matrix products, attend_head(): lax.dot_general(q_rows, k_rows, (((1,), (1,)), ((), ())), preferred_eleme...  23.1 us
    ppermute x1, waiting for transfers between devices, shards(): h_far = lax.ppermute(attended, 'yhi', pair)  17.1 us
    dot_general x1, matrix products, shards(): lax.dot_general(h_split, w_here, (((1, 2), (0, 2)), ((), ())), preferred_...  16.4 us
    dot_general x6, matrix products, attend_head(): jnp.dot(weights, v_rows, preferred_element_type=jnp.float32)  13.3 us
    reduce_sum x6, other arithmetic, attend_head(): weights = (expo / jnp.sum(expo, axis=1, keepdims=True)).astype(jnp.bfloat16)  8.47 us
  transfers between devices with their start and end apart: 7, of which 5 were waited for; matrix products, arithmetic and copies ran while one was open for 19% of the time, Pallas kernels for 0%

profile of v6, /device:TPU:1, one launch (start us, length us, event | category | flops | bytes accessed | tf_op | source)
XLA Modules:
  0.0 338.4 jit_solution(9630057214145203665)
XLA Ops:
  6.5 0.8 constant_dynamic-slice_fusion
  7.7 1.5 convolution_convert_fusion
  9.2 2.7 copy.14
  11.9 7.0 %all-to-all-start = ((bf16[16,128,768]{2,1,0:T(8,128)(2,1)}), bf16[16,128,768]{2,1,0:T(8,128)(2,1)}, u32[]{:S(2)}, u32[]{:S(2)}) async-start(bf16[16,128,768]{2,1,0:T(8,128)(2,1)} %copy.14), calls=%async_computation | async-start | bytes 6291456 | tf_op jit(solution)/shard_map/all_to_all | solution.py:60
  18.8 0.7 collective-permute-start
  19.6 41.2 %all-to-all-done = bf16[16,128,768]{2,1,0:T(8,128)(2,1)} async-done(((bf16[16,128,768]{2,1,0:T(8,128)(2,1)}), bf16[16,128,768]{2,1,0:T(8,128)(2,1)}, u32[]{:S(2)}, u32[]{:S(2)}) %all-to-all-start) | async-done | bytes 3145760 | tf_op jit(solution)/shard_map/all_to_all | solution.py:60
  60.8 2.4 broadcast_in_dim.65
  63.2 5.0 %all-to-all-start.1 = ((bf16[16,512,256]{2,1,0:T(8,128)(2,1)}), bf16[16,512,256]{2,1,0:T(8,128)(2,1)}, u32[]{:S(2)}, u32[]{:S(2)}) async-start(bf16[16,512,256]{2,1,0:T(8,128)(2,1)} %broadcast_in_dim.65), calls=%async_computation.1 | async-start | bytes 8388608 | tf_op jit(solution)/shard_map/all_to_all | solution.py:62
  68.3 0.8 scatter_custom_fusion
  69.1 0.8 gather_fusion
  70.6 3.8 %fusion.19 = bf16[4,128,768]{2,0,1:T(4,128)(2,1)S(1)} fusion(bf16[4,16,1]{1,0,2:T(4,128)(2,1)S(1)} %fusion.22, bf16[16,128,768]{2,1,0:T(8,128)(2,1)} %all-to-all-done), kind=kOutput, calls=%fused_computation.34 | convolution fusion | flops 12976128 | bytes 3932288 | tf_op jit(solution)/shard_map/od,drc->orc/dot_general | solution.py:73
  74.4 1.0 copy.16
  75.4 78.2 %all-to-all-done.1 = bf16[16,512,256]{2,1,0:T(8,128)(2,1)} async-done(((bf16[16,512,256]{2,1,0:T(8,128)(2,1)}), bf16[16,512,256]{2,1,0:T(8,128)(2,1)}, u32[]{:S(2)}, u32[]{:S(2)}) %all-to-all-start.1) | async-done | bytes 4194336 | tf_op jit(solution)/shard_map/all_to_all | solution.py:62
  153.7 2.9 gather_fusion.1
  156.7 2.4 bitcast_select_fusion
  159.2 1.0 copy-done.2
  160.2 53.5 %while.13 = (s32[]{:T(128)}, bf16[6,512,128]{1,2,0:T(8,128)(2,1)S(1)}, s32[4608]{0:T(1024)S(1)}, s32[512]{0:T(512)S(1)}, s32[6]{0:T(128)S(1)}, /*index=5*/bf16[5...) while((s32[]{:T(128)}, ...), condition=%wide.region_4.5_spmd.clone, body=%wide.region_1.0_spmd.clone.sunk | while | flops 1238700544 | bytes 31533264 | solution.py:92
  161.4 3.9 %fusion.51 = (f32[512]{0:T(512)S(1)}, f32[512,4608]{1,0:T(8,128)S(1)}) fusion(bf16[4608,128]{1,0:T(8,128)(2,1)S(1)} %get-tuple-element.293, bf16[512,768]{1,0:T(8,128)(2,1)} %get-tuple-element.292, s32[]{:T(128)S(6)} %select_n.175, s32[512]{0:T(512)S(1)} %get-tuple-element.290, s32[4608]{0:T(1024)S(1)} %get-tuple-element.289, ...), kind=kOutput, calls=%fused_computation.76.clone.1 | convolution fusion | flops 622853632 | bytes 10792964 | tf_op jit(solution)/shard_map/while/body/eval_jaxpr/dot_general | solution.py:17
  165.3 1.4 fusion.52
  166.7 2.2 fusion.53
  169.1 0.6 dynamic_slice.36
  170.4 3.9 %fusion.51 = (f32[512]{0:T(512)S(1)}, f32[512,4608]{1,0:T(8,128)S(1)}) fusion(bf16[4608,128]{1,0:T(8,128)(2,1)S(1)} %get-tuple-element.293, bf16[512,768]{1,0:T(8,128)(2,1)} %get-tuple-element.292, s32[]{:T(128)S(6)} %select_n.175, s32[512]{0:T(512)S(1)} %get-tuple-element.290, s32[4608]{0:T(1024)S(1)} %get-tuple-element.289, ...), kind=kOutput, calls=%fused_computation.76.clone.1 | convolution fusion | flops 622853632 | bytes 10792964 | tf_op jit(solution)/shard_map/while/body/eval_jaxpr/dot_general | solution.py:17
  174.2 1.4 fusion.52
  175.6 2.2 fusion.53
  179.3 3.9 %fusion.51 = (f32[512]{0:T(512)S(1)}, f32[512,4608]{1,0:T(8,128)S(1)}) fusion(bf16[4608,128]{1,0:T(8,128)(2,1)S(1)} %get-tuple-element.293, bf16[512,768]{1,0:T(8,128)(2,1)} %get-tuple-element.292, s32[]{:T(128)S(6)} %select_n.175, s32[512]{0:T(512)S(1)} %get-tuple-element.290, s32[4608]{0:T(1024)S(1)} %get-tuple-element.289, ...), kind=kOutput, calls=%fused_computation.76.clone.1 | convolution fusion | flops 622853632 | bytes 10792964 | tf_op jit(solution)/shard_map/while/body/eval_jaxpr/dot_general | solution.py:17
  183.2 1.4 fusion.52
  184.6 2.2 fusion.53
  187.0 0.6 dynamic_slice.36
  188.2 3.9 %fusion.51 = (f32[512]{0:T(512)S(1)}, f32[512,4608]{1,0:T(8,128)S(1)}) fusion(bf16[4608,128]{1,0:T(8,128)(2,1)S(1)} %get-tuple-element.293, bf16[512,768]{1,0:T(8,128)(2,1)} %get-tuple-element.292, s32[]{:T(128)S(6)} %select_n.175, s32[512]{0:T(512)S(1)} %get-tuple-element.290, s32[4608]{0:T(1024)S(1)} %get-tuple-element.289, ...), kind=kOutput, calls=%fused_computation.76.clone.1 | convolution fusion | flops 622853632 | bytes 10792964 | tf_op jit(solution)/shard_map/while/body/eval_jaxpr/dot_general | solution.py:17
  192.1 1.4 fusion.52
  193.5 2.2 fusion.53
  195.9 0.6 dynamic_slice.36
  197.2 3.8 %fusion.51 = (f32[512]{0:T(512)S(1)}, f32[512,4608]{1,0:T(8,128)S(1)}) fusion(bf16[4608,128]{1,0:T(8,128)(2,1)S(1)} %get-tuple-element.293, bf16[512,768]{1,0:T(8,128)(2,1)} %get-tuple-element.292, s32[]{:T(128)S(6)} %select_n.175, s32[512]{0:T(512)S(1)} %get-tuple-element.290, s32[4608]{0:T(1024)S(1)} %get-tuple-element.289, ...), kind=kOutput, calls=%fused_computation.76.clone.1 | convolution fusion | flops 622853632 | bytes 10792964 | tf_op jit(solution)/shard_map/while/body/eval_jaxpr/dot_general | solution.py:17
  201.0 1.4 fusion.52
  202.4 2.2 fusion.53
  204.8 0.6 dynamic_slice.36
  206.1 3.9 %fusion.51 = (f32[512]{0:T(512)S(1)}, f32[512,4608]{1,0:T(8,128)S(1)}) fusion(bf16[4608,128]{1,0:T(8,128)(2,1)S(1)} %get-tuple-element.293, bf16[512,768]{1,0:T(8,128)(2,1)} %get-tuple-element.292, s32[]{:T(128)S(6)} %select_n.175, s32[512]{0:T(512)S(1)} %get-tuple-element.290, s32[4608]{0:T(1024)S(1)} %get-tuple-element.289, ...), kind=kOutput, calls=%fused_computation.76.clone.1 | convolution fusion | flops 622853632 | bytes 10792964 | tf_op jit(solution)/shard_map/while/body/eval_jaxpr/dot_general | solution.py:17
  209.9 1.4 fusion.52
  211.3 2.2 fusion.53
  213.7 2.6 collective-permute-start.1
  216.3 17.1 %collective-permute-done.1 = bf16[512,768]{0,1:T(8,128)(2,1)S(1)} collective-permute-done((bf16[512,768]{0,1:T(8,128)(2,1)S(1)}, bf16[512,768]{0,1:T(8,128)(2,1)S(1)}, u32[]{:S(2)}, u32[]{:S(2)}) %collective-permute-start.1) | collective-permute-done | bytes 786464 | tf_op jit(solution)/shard_map/ppermute | solution.py:96
  233.4 1.8 maximum_select_fusion.3
  235.4 3.5 %collective-permute-done.2 = bf16[512,1536]{0,1:T(8,128)(2,1)} collective-permute-done((bf16[512,1536]{0,1:T(8,128)(2,1)}, bf16[512,1536]{0,1:T(8,128)(2,1)}, u32[]{:S(2)}, u32[]{:S(2)}) %collective-permute-start.2) | collective-permute-done | bytes 1572896 | tf_op jit(solution)/shard_map/ppermute | solution.py:103
  238.9 16.4 %bitcast_convert_fusion = bf16[1024,4,768]{0,2,1:T(8,128)(2,1)} fusion(bf16[2,4,768,768]{3,2,1,0:T(8,128)(2,1)} %bitcast.75, bf16[512,2,768]{0,2,1:T(8,128)(2,1)} %bitcast.20, bf16[512,2,768]{0,2,1:T(8,128)(2,1)S(1)} %maximum_select_fusion.2, pred[]{:T(512)S(6)} %eq.84), kind=kOutput, calls=%fused_computation.18 | convolution fusion | flops 9680977920 | bytes 18874368 | tf_op jit(solution)/shard_map/dot_general | solution.py:111
  255.4 67.7 %reduce-scatter.2.cloned.1.call-done = bf16[1024,768]{0,1:T(8,128)(2,1)} async-done(((bf16[1024,3072]{0,1:T(8,128)(2,1)}), bf16[1024,768]{0,1:T(8,128)(2,1)}) %reduce-scatter.2.cloned.1.call-update) | async-done | bytes 1572880 | tf_op jit(solution)/shard_map/reduce_scatter | solution.py:115
  323.1 1.7 copy.20
  324.8 5.4 %all_to_all.19 = bf16[2,512,768]{2,1,0:T(8,128)(2,1)S(1)} all-to-all(bf16[2,512,768]{2,1,0:T(8,128)(2,1)S(1)} %bitcast.69), channel_id=1, replica_groups=mesh['ylo'=2,'x'=4,'c'=2,'yhi'=2,'z'=4] {'c'}, dimensions={0} | all-to-all | bytes 3145728 | tf_op jit(solution)/shard_map/all_to_all | solution.py:116
  330.3 1.3 pad_maximum_fusion
  (70 shorter events, 3.7 us)
Async XLA Ops:
  6.5 1.1 copy-start
  11.8 7.0 %copy-start.8 = (bf16[768,768]{1,0:T(8,128)(2,1)S(1)}, bf16[768,768]{1,0:T(8,128)(2,1)}, u32[]{:S(2)}) copy-start(bf16[768,768]{1,0:T(8,128)(2,1)} %param.13) | copy-start | bytes 3538948
  11.8 7.7 %copy-start.4 = (bf16[512,128]{1,0:T(8,128)(2,1)S(1)}, bf16[512,128]{1,0:T(8,128)(2,1)}, u32[]{:S(2)}) copy-start(bf16[512,128]{1,0:T(8,128)(2,1)} %param.10) | copy-start | bytes 393220
  11.9 7.7 %copy-start.5 = (bf16[512,128]{1,0:T(8,128)(2,1)S(1)}, bf16[512,128]{1,0:T(8,128)(2,1)}, u32[]{:S(2)}) copy-start(bf16[512,128]{1,0:T(8,128)(2,1)} %param.9) | copy-start | bytes 393220
  11.9 48.9 %all-to-all-start = ((bf16[16,128,768]{2,1,0:T(8,128)(2,1)}), bf16[16,128,768]{2,1,0:T(8,128)(2,1)}, u32[]{:S(2)}, u32[]{:S(2)}) async-start(bf16[16,128,768]{2,1,0:T(8,128)(2,1)} %copy.14), calls=%async_computation | async-start | bytes 6291456 | tf_op jit(solution)/shard_map/all_to_all | solution.py:60
  18.8 0.8 collective-permute-start
  19.6 43.5 %copy-start.3 = (bf16[768,768]{1,0:T(8,128)(2,1)}, bf16[768,768]{1,0:T(8,128)(2,1)S(1)}, u32[]{:S(2)}) copy-start(bf16[768,768]{1,0:T(8,128)(2,1)S(1)} %collective-permute-done) | copy-start | bytes 3538948
  63.2 5.1 %copy-start.7 = (s32[64,2]{0,1:T(2,128)S(1)}, s32[64,2]{0,1:T(2,128)}, u32[]{:S(2)}) copy-start(s32[64,2]{0,1:T(2,128)} %param.12) | copy-start | bytes 1540
  63.2 6.7 %copy-start.6 = (s32[8192]{0:T(1024)S(1)}, s32[8192]{0:T(1024)}, u32[]{:S(2)}) copy-start(s32[8192]{0:T(1024)} %param.11) | copy-start | bytes 98308
  63.2 90.5 %all-to-all-start.1 = ((bf16[16,512,256]{2,1,0:T(8,128)(2,1)}), bf16[16,512,256]{2,1,0:T(8,128)(2,1)}, u32[]{:S(2)}, u32[]{:S(2)}) async-start(bf16[16,512,256]{2,1,0:T(8,128)(2,1)} %broadcast_in_dim.65), calls=%async_computation.1 | async-start | bytes 8388608 | tf_op jit(solution)/shard_map/all_to_all | solution.py:62
  68.2 170.8 %all-gather.2.cloned.1.call-start = ((), (), s32[]{:S(2)}) async-start(), calls=%async_computation.4 | async-start | bytes 10616832 | tf_op jit(solution)/shard_map/all_gather | solution.py:50
  70.4 252.7 %reduce-scatter.2.cloned.1.call-start = ((), (), s32[]{:S(2)}) async-start(), calls=%async_computation.5 | async-start | bytes 7864320 | tf_op jit(solution)/shard_map/reduce_scatter | solution.py:115
  159.0 1.1 copy-start.2
  213.7 19.7 %collective-permute-start.1 = (bf16[512,768]{0,1:T(8,128)(2,1)S(1)}, bf16[512,768]{0,1:T(8,128)(2,1)S(1)}, u32[]{:S(2)}, u32[]{:S(2)}) collective-permute-start(bf16[512,768]{0,1:T(8,128)(2,1)S(1)} %bitcast.70), channel_id=1, source_target_pairs={{0,4},{4,0},{1,5},{5,1},{2,6},{6,2},{3,7},{7,3},{8,12},{12,8},{9,1... | collective-permute-start | bytes 2359304 | tf_op jit(solution)/shard_map/ppermute | solution.py:96
  235.2 3.8 %collective-permute-start.2 = (bf16[512,1536]{0,1:T(8,128)(2,1)}, bf16[512,1536]{0,1:T(8,128)(2,1)}, u32[]{:S(2)}, u32[]{:S(2)}) collective-permute-start(bf16[512,1536]{0,1:T(8,128)(2,1)} %maximum_select_fusion.3), channel_id=1, source_target_pairs={{0,8},{8,0},{1,9},{9,1},{2,10},{10,2},{3,11},{11,3},{4,12},{12,4},... | collective-permute-start | bytes 4718600 | tf_op jit(solution)/shard_map/ppermute | solution.py:103
  324.8 6.8 %copy-start.1 = (bf16[512,768]{1,0:T(8,128)(2,1)S(1)}, bf16[512,768]{1,0:T(8,128)(2,1)}, u32[]{:S(2)}) copy-start(bf16[512,768]{1,0:T(8,128)(2,1)} %param.8) | copy-start | bytes 2359300
Sparse Core Ops, SparseCore 0:
  70.7 139.4 all-gather.1
  255.5 67.5 reduce-scatter.1

commit v7 on v5

--- a/solution.py
+++ b/solution.py
@@ -38,6 +38,11 @@
     kv_local = jnp.concatenate([keys, values], axis=1)
     kv_all = lax.all_gather(kv_local, SEQ, axis=0, tiled=True)
     kv_blocks = kv_all.reshape(blocks_all, BLOCK, 2 * kv_cols)
+    w_swapped = lax.ppermute(out_weight, ("ylo", "yhi"), perm=[(0, 0), (1, 2), (2, 1), (3, 3)])
+    kv_blocks, w_swapped = lax.optimization_barrier((kv_blocks, w_swapped))
+    w_here = lax.all_gather(w_swapped, ("ylo", "x"), axis=0, tiled=True)
+    w_here = w_here.reshape(2, -1, out_weight.shape[0], out_weight.shape[1])
+
     target = packing[:, 0] * per_shard + packing[:, 1]
     source = jnp.zeros((blocks_all,), jnp.int32).at[target].set(
         jnp.arange(blocks_all, dtype=jnp.int32)
@@ -68,11 +73,6 @@
         "od,drc->orc", placing, incoming, preferred_element_type=jnp.float32
     ).astype(jnp.bfloat16)
     queries_here = packed.reshape(tok_rows, q_cols)
-
-    w_swapped = lax.ppermute(out_weight, ("ylo", "yhi"), perm=[(0, 0), (1, 2), (2, 1), (3, 3)])
-    context, w_swapped = lax.optimization_barrier((context, w_swapped))
-    w_here = lax.all_gather(w_swapped, ("ylo", "x"), axis=0, tiled=True)
-    w_here = w_here.reshape(2, -1, out_weight.shape[0], out_weight.shape[1])
 
     ctx_keys = context[:, :kv_cols]
     ctx_values = context[:, kv_cols:]
@@ -107,11 +107,18 @@
         jnp.concatenate([h_near, h_groups], axis=0),
     )
     h_split = h_here.reshape(h_here.shape[0], 2, -1)
-    part = lax.dot_general(
-        h_split, w_here, (((1, 2), (0, 2)), ((), ())), preferred_element_type=jnp.float32
-    )
-    part = part.astype(jnp.bfloat16).reshape(h_here.shape[0], -1)
-    summed = lax.psum_scatter(part, "z", scatter_dimension=1, tiled=True)
+    chunk = w_here.shape[-1] // 2
+    pieces = []
+    for first in (0, chunk):
+        part = lax.dot_general(
+            h_split,
+            w_here[..., first:first + chunk],
+            (((1, 2), (0, 2)), ((), ())),
+            preferred_element_type=jnp.float32,
+        )
+        part = part.astype(jnp.bfloat16).reshape(h_here.shape[0], -1)
+        pieces.append(lax.psum_scatter(part, "z", scatter_dimension=1, tiled=True))
+    summed = jnp.concatenate(pieces, axis=1)
     swapped = lax.all_to_all(summed, "c", split_axis=0, concat_axis=0, tiled=True)
     return jnp.concatenate([swapped[:tok_rows], swapped[tok_rows:]], axis=1)
 

time: 315 us -> 316 us (level)
  waiting for transfers between devices: 164 us -> 178 us
  local copies, waits for them, and re-layouts: 22.9 us -> 15.3 us
    ppermute x1, waiting for transfers between devices: 57.4 us -> 63.7 us  [shards(): h_far = lax.ppermute(attended, 'yhi', pair)]
    reduce_scatter x1 -> x2, waiting for transfers between devices: 61.1 us -> 65.3 us  [shards(): pieces.append(lax.psum_scatter(part, 'z', scatter_dimension=1, tiled=True))]
    dynamic_update_slice x12, local copies, waits for them, and re-layouts: 4.73 us -> 0.78 us  [shards(): per_head = lax.map(one_head, jnp.arange(heads_here, dtype=jnp.int32))]
    dot_general x1 -> x2, matrix products: 17.6 us -> 20.2 us  [shards(): lax.dot_general(h_split, w_here[..., first:first + chunk], (((1, 2), (0,...]
  transfers between devices with their start and end apart: 7 -> 8, of which waited for: 5 -> 6; matrix products, arithmetic and copies ran while one was open for 26% -> 23% of each run, Pallas kernels for 0% -> 0%
where the time goes in v7:
time: 316 us; the launch traced here: 315 us
  waiting for transfers between devices  178 us (56%)
  matrix products  60.2 us (19%)
  starting transfers between devices  21.2 us (7%)
  other arithmetic  17.5 us (6%)
  local copies, waits for them, and re-layouts  15.3 us (5%)
  between operations  13.3 us (4%)
  blocking collectives  5.39 us (2%)
  loops' own time  4.25 us (1%)
    reduce_scatter x2, waiting for transfers between devices, shards(): pieces.append(lax.psum_scatter(part, 'z', scatter_dimension=1, tiled=True))  65.3 us
    ppermute x1, waiting for transfers between devices, shards(): h_far = lax.ppermute(attended, 'yhi', pair)  63.7 us
    all_to_all x1, waiting for transfers between devices, shards(): lax.all_to_all(outgoing, SEQ, split_axis=0, concat_axis=0, tiled=True)  39.4 us
    dot_general x6, matrix products, attend_head(): lax.dot_general(q_rows, k_rows, (((1,), (1,)), ((), ())), preferred_eleme...  23.2 us
    dot_general x2, matrix products, shards(): lax.dot_general(h_split, w_here[..., first:first + chunk], (((1, 2), (0,...  20.2 us
    dot_general x6, matrix products, attend_head(): jnp.dot(weights, v_rows, preferred_element_type=jnp.float32)  13.3 us
    ppermute x1, starting transfers between devices, shards(): lax.ppermute(out_weight, ('ylo', 'yhi'), perm=[(0, 0), (1, 2), (2, 1), (3...  10.4 us
    reduce_sum x6, other arithmetic, attend_head(): weights = (expo / jnp.sum(expo, axis=1, keepdims=True)).astype(jnp.bfloat16)  8.47 us
  transfers between devices with their start and end apart: 8, of which 6 were waited for; matrix products, arithmetic and copies ran while one was open for 23% of the time, Pallas kernels for 0%

profile of v7, /device:TPU:1, one launch (start us, length us, event | category | flops | bytes accessed | tf_op | source)
XLA Modules:
  0.0 315.2 jit_solution(5673146557612957668)
XLA Ops:
  6.5 1.8 pad_maximum_fusion.2
  8.3 0.8 constant_dynamic-slice_fusion
  9.1 1.5 convolution_convert_fusion
  10.6 2.7 copy.16
  13.3 7.0 %all-to-all-start = ((bf16[16,128,768]{2,1,0:T(8,128)(2,1)}), bf16[16,128,768]{2,1,0:T(8,128)(2,1)S(1)}, u32[]{:S(2)}, u32[]{:S(2)}) async-start(bf16[16,128,768]{2,1,0:T(8,128)(2,1)} %copy.16), calls=%async_computation | async-start | bytes 6291456 | tf_op jit(solution)/shard_map/all_to_all | solution.py:63
  20.3 10.4 %collective-permute-start = (bf16[768,768]{1,0:T(8,128)(2,1)}, bf16[768,768]{1,0:T(8,128)(2,1)}, u32[]{:S(2)}, u32[]{:S(2)}) collective-permute-start(bf16[768,768]{1,0:T(8,128)(2,1)} %param.13), channel_id=1, source_target_pairs={{0,0},{4,64},{64,4},{68,68},{1,1},{5,65},{65,5},{69,69},{2,2},{6,6... | collective-permute-start | bytes 3538952 | tf_op jit(solution)/shard_map/ppermute | solution.py:41
  30.8 0.8 scatter_custom_fusion
  31.6 0.8 gather_fusion
  32.9 39.4 %all-to-all-done = bf16[16,128,768]{2,1,0:T(8,128)(2,1)S(1)} async-done(((bf16[16,128,768]{2,1,0:T(8,128)(2,1)}), bf16[16,128,768]{2,1,0:T(8,128)(2,1)S(1)}, u32[]{:S(2)}, u32[]{:S(2)}) %all-to-all-start) | async-done | bytes 3145760 | tf_op jit(solution)/shard_map/all_to_all | solution.py:63
  72.3 1.9 fusion.26
  74.3 1.0 copy.18
  75.2 6.5 %all-gather.3.cloned.1.call-done = bf16[8192,256]{1,0:T(8,128)(2,1)} async-done(((bf16[512,256]{1,0:T(8,128)(2,1)}), bf16[8192,256]{1,0:T(8,128)(2,1)}) %all-gather.3.cloned.1.call-update) | async-done | bytes 4194320 | tf_op jit(solution)/shard_map/all_gather | solution.py:39
  81.7 2.9 gather_fusion.1
  84.6 2.4 bitcast_select_fusion
  87.2 0.9 copy-done.2
  88.1 53.5 %while.13 = (s32[]{:T(128)}, bf16[6,512,128]{1,2,0:T(8,128)(2,1)S(1)}, s32[4608]{0:T(1024)S(1)}, s32[512]{0:T(512)S(1)}, s32[6]{0:T(128)S(1)}, /*index=5*/bf16[5...) while((s32[]{:T(128)}, ...), condition=%wide.region_4.5_spmd.clone, body=%wide.region_1.0_spmd.clone.sunk | while | flops 1238700544 | bytes 31533264 | solution.py:91
  89.4 3.9 %fusion.58 = (f32[512]{0:T(512)S(1)}, f32[512,4608]{1,0:T(8,128)S(1)}) fusion(bf16[4608,128]{1,0:T(8,128)(2,1)S(1)} %get-tuple-element.293, bf16[512,768]{1,0:T(8,128)(2,1)} %get-tuple-element.292, s32[]{:T(128)S(6)} %select_n.181, s32[512]{0:T(512)S(1)} %get-tuple-element.290, s32[4608]{0:T(1024)S(1)} %get-tuple-element.289, ...), kind=kOutput, calls=%fused_computation.78.clone.1 | convolution fusion | flops 622853632 | bytes 10792964 | tf_op jit(solution)/shard_map/while/body/eval_jaxpr/dot_general | solution.py:17
  93.2 1.4 fusion.59
  94.7 2.2 fusion.60
  98.3 3.9 %fusion.58 = (f32[512]{0:T(512)S(1)}, f32[512,4608]{1,0:T(8,128)S(1)}) fusion(bf16[4608,128]{1,0:T(8,128)(2,1)S(1)} %get-tuple-element.293, bf16[512,768]{1,0:T(8,128)(2,1)} %get-tuple-element.292, s32[]{:T(128)S(6)} %select_n.181, s32[512]{0:T(512)S(1)} %get-tuple-element.290, s32[4608]{0:T(1024)S(1)} %get-tuple-element.289, ...), kind=kOutput, calls=%fused_computation.78.clone.1 | convolution fusion | flops 622853632 | bytes 10792964 | tf_op jit(solution)/shard_map/while/body/eval_jaxpr/dot_general | solution.py:17
  102.2 1.4 fusion.59
  103.6 2.2 fusion.60
  106.0 0.6 dynamic_slice.36
  107.2 3.9 %fusion.58 = (f32[512]{0:T(512)S(1)}, f32[512,4608]{1,0:T(8,128)S(1)}) fusion(bf16[4608,128]{1,0:T(8,128)(2,1)S(1)} %get-tuple-element.293, bf16[512,768]{1,0:T(8,128)(2,1)} %get-tuple-element.292, s32[]{:T(128)S(6)} %select_n.181, s32[512]{0:T(512)S(1)} %get-tuple-element.290, s32[4608]{0:T(1024)S(1)} %get-tuple-element.289, ...), kind=kOutput, calls=%fused_computation.78.clone.1 | convolution fusion | flops 622853632 | bytes 10792964 | tf_op jit(solution)/shard_map/while/body/eval_jaxpr/dot_general | solution.py:17
  111.1 1.4 fusion.59
  112.5 2.2 fusion.60
  114.9 0.6 dynamic_slice.36
  116.2 3.9 %fusion.58 = (f32[512]{0:T(512)S(1)}, f32[512,4608]{1,0:T(8,128)S(1)}) fusion(bf16[4608,128]{1,0:T(8,128)(2,1)S(1)} %get-tuple-element.293, bf16[512,768]{1,0:T(8,128)(2,1)} %get-tuple-element.292, s32[]{:T(128)S(6)} %select_n.181, s32[512]{0:T(512)S(1)} %get-tuple-element.290, s32[4608]{0:T(1024)S(1)} %get-tuple-element.289, ...), kind=kOutput, calls=%fused_computation.78.clone.1 | convolution fusion | flops 622853632 | bytes 10792964 | tf_op jit(solution)/shard_map/while/body/eval_jaxpr/dot_general | solution.py:17
  120.0 1.4 fusion.59
  121.4 2.2 fusion.60
  125.1 3.9 %fusion.58 = (f32[512]{0:T(512)S(1)}, f32[512,4608]{1,0:T(8,128)S(1)}) fusion(bf16[4608,128]{1,0:T(8,128)(2,1)S(1)} %get-tuple-element.293, bf16[512,768]{1,0:T(8,128)(2,1)} %get-tuple-element.292, s32[]{:T(128)S(6)} %select_n.181, s32[512]{0:T(512)S(1)} %get-tuple-element.290, s32[4608]{0:T(1024)S(1)} %get-tuple-element.289, ...), kind=kOutput, calls=%fused_computation.78.clone.1 | convolution fusion | flops 622853632 | bytes 10792964 | tf_op jit(solution)/shard_map/while/body/eval_jaxpr/dot_general | solution.py:17
  128.9 1.4 fusion.59
  130.3 2.2 fusion.60
  134.0 3.9 %fusion.58 = (f32[512]{0:T(512)S(1)}, f32[512,4608]{1,0:T(8,128)S(1)}) fusion(bf16[4608,128]{1,0:T(8,128)(2,1)S(1)} %get-tuple-element.293, bf16[512,768]{1,0:T(8,128)(2,1)} %get-tuple-element.292, s32[]{:T(128)S(6)} %select_n.181, s32[512]{0:T(512)S(1)} %get-tuple-element.290, s32[4608]{0:T(1024)S(1)} %get-tuple-element.289, ...), kind=kOutput, calls=%fused_computation.78.clone.1 | convolution fusion | flops 622853632 | bytes 10792964 | tf_op jit(solution)/shard_map/while/body/eval_jaxpr/dot_general | solution.py:17
  137.9 1.4 fusion.59
  139.3 2.2 fusion.60
  141.6 3.0 collective-permute-start.1
  144.7 63.7 %collective-permute-done.1 = bf16[512,768]{0,1:T(8,128)(2,1)S(1)} collective-permute-done((bf16[512,768]{0,1:T(8,128)(2,1)S(1)}, bf16[512,768]{0,1:T(8,128)(2,1)S(1)}, u32[]{:S(2)}, u32[]{:S(2)}) %collective-permute-start.1) | collective-permute-done | bytes 786464 | tf_op jit(solution)/shard_map/ppermute | solution.py:95
  208.3 1.8 maximum_select_fusion.2
  210.8 3.1 collective-permute-done.2
  213.9 10.0 %bitcast_convert_fusion.1 = bf16[1024,4,384]{0,2,1:T(8,128)(2,1)} fusion(bf16[2,4,768,768]{3,2,1,0:T(8,128)(2,1)} %bitcast.90, bf16[512,2,768]{0,2,1:T(8,128)(2,1)} %bitcast.20, bf16[512,2,768]{0,2,1:T(8,128)(2,1)S(1)} %maximum_select_fusion.1, pred[]{:T(512)S(6)} %eq.84), kind=kOutput, calls=%fused_computation.19 | convolution fusion | flops 4847566848 | bytes 11010049 | tf_op jit(solution)/shard_map/dot_general | solution.py:113
  224.3 10.1 %bitcast_convert_fusion = bf16[1024,4,384]{0,2,1:T(8,128)(2,1)} fusion(bf16[2,4,768,768]{3,2,1,0:T(8,128)(2,1)} %bitcast.91, bf16[512,2,768]{0,2,1:T(8,128)(2,1)} %bitcast.20, bf16[512,2,768]{0,2,1:T(8,128)(2,1)S(1)} %maximum_select_fusion.1, pred[]{:T(512)S(6)} %eq.84), kind=kOutput, calls=%fused_computation.18 | convolution fusion | flops 4847566848 | bytes 11010049 | tf_op jit(solution)/shard_map/dot_general | solution.py:113
  234.4 24.9 %reduce-scatter.3.cloned.1.call-done = bf16[1024,384]{0,1:T(8,128)(2,1)} async-done(((bf16[1024,1536]{0,1:T(8,128)(2,1)}), bf16[1024,384]{0,1:T(8,128)(2,1)}) %reduce-scatter.3.cloned.1.call-update) | async-done | bytes 786448 | tf_op jit(solution)/shard_map/reduce_scatter | solution.py:120
  259.3 40.3 %reduce-scatter.5.cloned.1.call-done = bf16[1024,384]{0,1:T(8,128)(2,1)} async-done(((bf16[1024,1536]{0,1:T(8,128)(2,1)}), bf16[1024,384]{0,1:T(8,128)(2,1)}) %reduce-scatter.5.cloned.1.call-update) | async-done | bytes 786448 | tf_op jit(solution)/shard_map/reduce_scatter | solution.py:120
  299.7 1.5 pad_maximum_fusion
  301.2 0.7 copy.24
  301.9 5.4 %all_to_all.14 = bf16[2,512,768]{2,1,0:T(8,128)(2,1)S(1)} all-to-all(bf16[2,512,768]{2,1,0:T(8,128)(2,1)S(1)} %bitcast.81), channel_id=1, replica_groups=mesh['ylo'=2,'x'=4,'c'=2,'yhi'=2,'z'=4] {'c'}, dimensions={0} | all-to-all | bytes 3145728 | tf_op jit(solution)/shard_map/all_to_all | solution.py:122
  307.4 1.3 pad_maximum_fusion.1
  (67 shorter events, 5.1 us)
Async XLA Ops:
  6.5 2.6 copy-start
  6.5 75.2 %all-gather.3.cloned.1.call-start = ((), (), s32[]{:S(2)}) async-start(), calls=%async_computation.4 | async-start | bytes 4456448 | tf_op jit(solution)/shard_map/all_gather | solution.py:39
  13.3 17.5 %copy-start.4 = (s32[64,2]{0,1:T(2,128)S(1)}, s32[64,2]{0,1:T(2,128)}, u32[]{:S(2)}) copy-start(s32[64,2]{0,1:T(2,128)} %param.12) | copy-start | bytes 1540
  13.3 19.1 %copy-start.3 = (s32[8192]{0:T(1024)S(1)}, s32[8192]{0:T(1024)}, u32[]{:S(2)}) copy-start(s32[8192]{0:T(1024)} %param.11) | copy-start | bytes 98308
  13.3 59.0 %all-to-all-start = ((bf16[16,128,768]{2,1,0:T(8,128)(2,1)}), bf16[16,128,768]{2,1,0:T(8,128)(2,1)S(1)}, u32[]{:S(2)}, u32[]{:S(2)}) async-start(bf16[16,128,768]{2,1,0:T(8,128)(2,1)} %copy.16), calls=%async_computation | async-start | bytes 6291456 | tf_op jit(solution)/shard_map/all_to_all | solution.py:63
  20.3 193.6 %all-gather.5.cloned.1.call-start = ((), (), s32[]{:S(2)}) async-start(), calls=%async_computation.5 | async-start | bytes 10616832 | tf_op jit(solution)/shard_map/all_gather | solution.py:43
  20.3 54.9 %collective-permute-start = (bf16[768,768]{1,0:T(8,128)(2,1)}, bf16[768,768]{1,0:T(8,128)(2,1)}, u32[]{:S(2)}, u32[]{:S(2)}) collective-permute-start(bf16[768,768]{1,0:T(8,128)(2,1)} %param.13), channel_id=1, source_target_pairs={{0,0},{4,64},{64,4},{68,68},{1,1},{5,65},{65,5},{69,69},{2,2},{6,6... | collective-permute-start | bytes 3538952 | tf_op jit(solution)/shard_map/ppermute | solution.py:41
  87.0 1.1 copy-start.2
  87.2 172.1 %reduce-scatter.3.cloned.1.call-start = ((), (), s32[]{:S(2)}) async-start(), calls=%async_computation.6 | async-start | bytes 3932160 | tf_op jit(solution)/shard_map/reduce_scatter | solution.py:120
  141.6 66.7 %collective-permute-start.1 = (bf16[512,768]{0,1:T(8,128)(2,1)S(1)}, bf16[512,768]{0,1:T(8,128)(2,1)S(1)}, u32[]{:S(2)}, u32[]{:S(2)}) collective-permute-start(bf16[512,768]{0,1:T(8,128)(2,1)S(1)} %bitcast.84), channel_id=1, source_target_pairs={{0,4},{4,0},{1,5},{5,1},{2,6},{6,2},{3,7},{7,3},{8,12},{12,8},{9,1... | collective-permute-start | bytes 2359304 | tf_op jit(solution)/shard_map/ppermute | solution.py:95
  210.1 3.8 %collective-permute-start.2 = (bf16[512,1536]{0,1:T(8,128)(2,1)}, bf16[512,1536]{0,1:T(8,128)(2,1)}, u32[]{:S(2)}, u32[]{:S(2)}) collective-permute-start(bf16[512,1536]{0,1:T(8,128)(2,1)} %maximum_select_fusion.2), channel_id=1, source_target_pairs={{0,8},{8,0},{1,9},{9,1},{2,10},{10,2},{3,11},{11,3},{4,12},{12,4},... | collective-permute-start | bytes 4718600 | tf_op jit(solution)/shard_map/ppermute | solution.py:102
  224.0 75.7 %reduce-scatter.5.cloned.1.call-start = ((), (), s32[]{:S(2)}) async-start(), calls=%async_computation.7 | async-start | bytes 3932160 | tf_op jit(solution)/shard_map/reduce_scatter | solution.py:120
  301.9 6.8 %copy-start.1 = (bf16[512,768]{1,0:T(8,128)(2,1)S(1)}, bf16[512,768]{1,0:T(8,128)(2,1)}, u32[]{:S(2)}) copy-start(bf16[512,768]{1,0:T(8,128)(2,1)} %param.8) | copy-start | bytes 2359300
Sparse Core Ops, SparseCore 0:
  9.1 72.5 all-gather.2
  87.3 103.0 all-gather.4
  224.1 35.1 reduce-scatter.2
  261.6 38.0 reduce-scatter.4

commit v8 on v6

--- a/solution.py
+++ b/solution.py
@@ -4,6 +4,8 @@
 import jax
 import jax.numpy as jnp
 from jax import lax
+from jax.experimental import pallas as pl
+from jax.experimental.pallas import tpu as pltpu
 from jax.sharding import Mesh, PartitionSpec as P
 
 HEAD_DIM = 128
@@ -11,6 +13,79 @@
 BLOCK = 128
 SEQ = ("ylo", "x", "c")
 TP = ("yhi", "z")
+
+
+def route_kernel(n_x, n_c, q_out_ref, kv_ref, q_in_ref, kv_in_ref,
+                 q_send, q_recv, kv_send, kv_recv, own_sem):
+    n = q_out_ref.shape[0]
+    me = (lax.axis_index("ylo") * n_x + lax.axis_index("x")) * n_c + lax.axis_index("c")
+
+    def where(r):
+        return {"ylo": r // (n_x * n_c), "x": (r // n_c) % n_x, "c": r % n_c}
+
+    barrier = pltpu.get_barrier_semaphore()
+    for k in range(1, n):
+        r = lax.rem(me + k, n)
+        pl.semaphore_signal(barrier, inc=1, device_id=where(r), device_id_type=pl.DeviceIdType.MESH)
+    pl.semaphore_wait(barrier, n - 1)
+
+    own_q = pltpu.make_async_copy(q_out_ref.at[me], q_in_ref.at[me], own_sem.at[0])
+    own_kv = pltpu.make_async_copy(kv_ref, kv_in_ref.at[me], own_sem.at[1])
+    own_q.start()
+    own_kv.start()
+    sends = []
+    for k in range(1, n):
+        r = lax.rem(me + k, n)
+        cq = pltpu.make_async_remote_copy(
+            src_ref=q_out_ref.at[r], dst_ref=q_in_ref.at[me],
+            send_sem=q_send.at[k], recv_sem=q_recv.at[me],
+            device_id=where(r), device_id_type=pl.DeviceIdType.MESH)
+        ckv = pltpu.make_async_remote_copy(
+            src_ref=kv_ref, dst_ref=kv_in_ref.at[me],
+            send_sem=kv_send.at[k], recv_sem=kv_recv.at[me],
+            device_id=where(r), device_id_type=pl.DeviceIdType.MESH)
+        cq.start()
+        ckv.start()
+        sends.append((cq, ckv))
+    for cq, ckv in sends:
+        cq.wait_send()
+        ckv.wait_send()
+    for k in range(1, n):
+        s = lax.rem(me + n - k, n)
+        pltpu.make_async_remote_copy(
+            src_ref=q_out_ref.at[s], dst_ref=q_in_ref.at[s],
+            send_sem=q_send.at[k], recv_sem=q_recv.at[s],
+            device_id=where(s), device_id_type=pl.DeviceIdType.MESH).wait_recv()
+        pltpu.make_async_remote_copy(
+            src_ref=kv_ref, dst_ref=kv_in_ref.at[s],
+            send_sem=kv_send.at[k], recv_sem=kv_recv.at[s],
+            device_id=where(s), device_id_type=pl.DeviceIdType.MESH).wait_recv()
+    own_q.wait()
+    own_kv.wait()
+
+
+def route(outgoing, kv_local, n_x, n_c):
+    n = outgoing.shape[0]
+    any_spec = pl.BlockSpec(memory_space=pl.ANY)
+    sent = n * (outgoing[0].size + kv_local.size) * 2
+    return pl.pallas_call(
+        functools.partial(route_kernel, n_x, n_c),
+        out_shape=(
+            jax.ShapeDtypeStruct(outgoing.shape, outgoing.dtype),
+            jax.ShapeDtypeStruct((n,) + kv_local.shape, kv_local.dtype),
+        ),
+        in_specs=[any_spec, any_spec],
+        out_specs=(any_spec, any_spec),
+        scratch_shapes=[
+            pltpu.SemaphoreType.DMA((n,)),
+            pltpu.SemaphoreType.DMA((n,)),
+            pltpu.SemaphoreType.DMA((n,)),
+            pltpu.SemaphoreType.DMA((n,)),
+            pltpu.SemaphoreType.DMA((2,)),
+        ],
+        compiler_params=pltpu.CompilerParams(collective_id=0, has_side_effects=True),
+        cost_estimate=pl.CostEstimate(flops=0, bytes_accessed=2 * sent, transcendentals=0),
+    )(outgoing, kv_local)
 
 
 def attend_head(q_rows, k_rows, v_rows, q_pos, k_pos, q_seg, k_seg):
@@ -27,7 +102,7 @@
     return jnp.dot(weights, v_rows, preferred_element_type=jnp.float32).astype(jnp.bfloat16)
 
 
-def shards(seq_count, queries, keys, values, segment_ids, packing, out_weight):
+def shards(seq_count, n_x, n_c, queries, keys, values, segment_ids, packing, out_weight):
     tok_rows = queries.shape[0]
     q_cols = queries.shape[1]
     kv_cols = keys.shape[1]
@@ -44,11 +119,6 @@
     ctx_blocks = span_blocks + per_shard
     blk_ids = shard_index * per_shard - span_blocks + jnp.arange(ctx_blocks, dtype=jnp.int32)
     src = jnp.take(source, jnp.clip(blk_ids, 0, blocks_all - 1))
-
-    w_swapped = lax.ppermute(out_weight, ("ylo", "yhi"), perm=[(0, 0), (1, 2), (2, 1), (3, 3)])
-    kv_local, w_swapped = lax.optimization_barrier((kv_local, w_swapped))
-    w_here = lax.all_gather(w_swapped, ("ylo", "x"), axis=0, tiled=True)
-    w_here = w_here.reshape(2, -1, out_weight.shape[0], out_weight.shape[1])
 
     own_blocks = queries.reshape(per_shard, BLOCK, q_cols)
     own_list = lax.dynamic_slice_in_dim(packing, shard_index * per_shard, per_shard, 0)
@@ -57,10 +127,13 @@
     outgoing = jnp.einsum(
         "db,brc->drc", routing, own_blocks, preferred_element_type=jnp.float32
     ).astype(jnp.bfloat16)
-    incoming = lax.all_to_all(outgoing, SEQ, split_axis=0, concat_axis=0, tiled=True)
-    kv_copies = jnp.broadcast_to(kv_local[None], (seq_count,) + kv_local.shape)
-    kv_blocks = lax.all_to_all(kv_copies, SEQ, split_axis=0, concat_axis=0, tiled=True)
-    kv_blocks = kv_blocks.reshape(blocks_all, BLOCK, 2 * kv_cols)
+    w_swapped = lax.ppermute(out_weight, ("ylo", "yhi"), perm=[(0, 0), (1, 2), (2, 1), (3, 3)])
+    outgoing, w_swapped = lax.optimization_barrier((outgoing, w_swapped))
+    w_here = lax.all_gather(w_swapped, ("ylo", "x"), axis=0, tiled=True)
+    w_here = w_here.reshape(2, -1, out_weight.shape[0], out_weight.shape[1])
+
+    incoming, kv_in = route(outgoing, kv_local, n_x, n_c)
+    kv_blocks = kv_in.reshape(blocks_all, BLOCK, 2 * kv_cols)
     context = jnp.take(kv_blocks, src, axis=0).reshape(ctx_blocks * BLOCK, 2 * kv_cols)
     arriving = packing[:, 0] == shard_index
     offset_ids = jnp.arange(per_shard, dtype=jnp.int32)
@@ -123,7 +196,7 @@
     in_specs = (P(SEQ, TP), P(SEQ, TP), P(SEQ, TP), P(), P(), P(TP, SEQ))
     out_specs = P(SEQ, TP)
     return jax.shard_map(
-        functools.partial(shards, seq_count),
+        functools.partial(shards, seq_count, seq_count // 4, 2),
         mesh=fine,
         in_specs=in_specs,
         out_specs=out_specs,

time: 339 us -> 391 us (1.15)
  Pallas kernels: 0 us -> 142 us
  waiting for transfers between devices: 208 us -> 123 us
  starting transfers between devices: 15.6 us -> 4.74 us
    pallas_call x0 -> x1, Pallas kernels: none -> 142 us  [route(): pl.pallas_call(functools.partial(route_kernel, n_x, n_c), out_shape=(jax....]
    all_to_all x2 -> x0, waiting for transfers between devices: 119 us -> none  [the longest x1 78.2 us: shards(): lax.all_to_all(kv_copies, SEQ, split_axis=0, concat_axis=0, tiled=True)]
    ppermute x1, waiting for transfers between devices: 17.1 us -> 59.6 us  [shards(): h_far = lax.ppermute(attended, 'yhi', pair)]
    all_to_all x2 -> x0, starting transfers between devices: 12 us -> none  [the longest x1 6.96 us: shards(): lax.all_to_all(outgoing, SEQ, split_axis=0, concat_axis=0, tiled=True)]
    reduce_scatter x1, waiting for transfers between devices: 67.7 us -> 61.1 us  [shards(): summed = lax.psum_scatter(part, 'z', scatter_dimension=1, tiled=True)]
    dot_general x0 -> x1, local copies, waits for them, and re-layouts: none -> 4.63 us  [shards(): jnp.einsum('db,brc->drc', routing, own_blocks, preferred_element_type=jnp...]
  transfers between devices with their start and end apart: 7 -> 5, of which waited for: 5 -> 3; matrix products, arithmetic and copies ran while one was open for 19% -> 17% of each run, Pallas kernels for 0% -> 0%
where the time goes in v8:
time: 391 us
  Pallas kernels  142 us (36%)
  waiting for transfers between devices  123 us (31%)
  matrix products  61.6 us (16%)
  local copies, waits for them, and re-layouts  19.8 us (5%)
  other arithmetic  16.9 us (4%)
  between operations  13.5 us (3%)
  blocking collectives  5.23 us (1%)
  starting transfers between devices  4.74 us (1%)
  loops' own time  4.1 us (1%)
    pallas_call x1, Pallas kernels, route(): pl.pallas_call(functools.partial(route_kernel, n_x, n_c), out_shape=(jax....  142 us
    reduce_scatter x1, waiting for transfers between devices, shards(): summed = lax.psum_scatter(part, 'z', scatter_dimension=1, tiled=True)  61.1 us
    ppermute x1, waiting for transfers between devices, shards(): h_far = lax.ppermute(attended, 'yhi', pair)  59.6 us
    dot_general x6, matrix products, attend_head(): lax.dot_general(q_rows, k_rows, (((1,), (1,)), ((), ())), preferred_eleme...  25.9 us
    dot_general x1, matrix products, shards(): lax.dot_general(h_split, w_here, (((1, 2), (0, 2)), ((), ())), preferred_...  17.7 us
    dot_general x6, matrix products, attend_head(): jnp.dot(weights, v_rows, preferred_element_type=jnp.float32)  13.2 us
    reduce_sum x6, other arithmetic, attend_head(): weights = (expo / jnp.sum(expo, axis=1, keepdims=True)).astype(jnp.bfloat16)  8.48 us
  transfers between devices with their start and end apart: 5, of which 3 were waited for; matrix products, arithmetic and copies ran while one was open for 17% of the time, Pallas kernels for 0%

profile of v8, /device:TPU:1, one launch (start us, length us, event | category | flops | bytes accessed | tf_op | source)
XLA Modules:
  0.0 390.6 jit_solution(16923331795074206691)
XLA Ops:
  6.5 2.0 collective-permute-start
  8.6 0.8 fusion.33
  9.3 0.7 constant_dynamic-slice_fusion
  10.1 0.8 scatter_custom_fusion
  10.9 0.8 gather_fusion
  11.7 2.7 fusion.23
  14.4 4.6 %copy.33.q_out_ref = bf16[16,128,768]{2,1,0:T(8,128)(2,1)} copy(bf16[16,128,768]{2,0,1:T(8,128)(2,1)} %fusion.23) | data formatting | bytes 6291456 | tf_op jit(solution)/shard_map/db,brc->drc/dot_general | solution.py:127
  19.4 0.7 pad_maximum_fusion.1.kv_ref
  20.3 142.0 %shard_map.64 = (bf16[16,128,768]{2,1,0:T(8,128)(2,1)}, bf16[16,512,256]{2,1,0:T(8,128)(2,1)}) custom-call(bf16[16,128,768]{2,1,0:T(8,128)(2,1)} %copy.33.q_out_ref, bf16[512,256]{1,0:T(8,128)(2,1)} %pad_maximum_fusion.1.kv_ref), custom_call_target="tpu_custom_call" | custom-call | bytes 14680064 | tf_op jit(solution)/shard_map/pallas_call | solution.py:71
  162.3 2.9 gather_fusion.1
  165.2 2.4 bitcast_select_fusion
  167.6 1.2 fusion.40
  168.8 1.1 copy-done.1
  169.9 1.9 fusion.19
  171.9 1.0 copy.14
  173.1 56.4 %while.13 = (s32[]{:T(128)}, bf16[6,512,128]{1,2,0:T(8,128)(2,1)S(1)}, s32[4608]{0:T(1024)S(1)}, s32[512]{0:T(512)S(1)}, s32[6]{0:T(128)S(1)}, /*index=5*/bf16[5...) while((s32[]{:T(128)}, ...), condition=%wide.region_4.5_spmd.clone, body=%wide.region_1.0_spmd.clone.sunk | while | flops 1238700544 | bytes 31533264 | solution.py:165
  173.1 0.6 dynamic_slice.36
  174.4 4.3 %fusion.52 = (f32[512]{0:T(512)S(1)}, f32[512,4608]{1,0:T(8,128)S(1)}) fusion(bf16[4608,128]{1,0:T(8,128)(2,1)} %get-tuple-element.297, bf16[512,768]{1,0:T(8,128)(2,1)} %get-tuple-element.296, s32[]{:T(128)S(6)} %select_n.175, s32[512]{0:T(512)S(1)} %get-tuple-element.294, s32[4608]{0:T(1024)S(1)} %get-tuple-element.293, ...), kind=kOutput, calls=%fused_computation.77.clone.1 | convolution fusion | flops 622853632 | bytes 10792964 | tf_op jit(solution)/shard_map/while/body/eval_jaxpr/dot_general | solution.py:92
  178.8 1.4 fusion.53
  180.2 2.2 fusion.54
  182.5 0.6 dynamic_slice.36
  183.8 4.3 %fusion.52 = (f32[512]{0:T(512)S(1)}, f32[512,4608]{1,0:T(8,128)S(1)}) fusion(bf16[4608,128]{1,0:T(8,128)(2,1)} %get-tuple-element.297, bf16[512,768]{1,0:T(8,128)(2,1)} %get-tuple-element.296, s32[]{:T(128)S(6)} %select_n.175, s32[512]{0:T(512)S(1)} %get-tuple-element.294, s32[4608]{0:T(1024)S(1)} %get-tuple-element.293, ...), kind=kOutput, calls=%fused_computation.77.clone.1 | convolution fusion | flops 622853632 | bytes 10792964 | tf_op jit(solution)/shard_map/while/body/eval_jaxpr/dot_general | solution.py:92
  188.1 1.4 fusion.53
  189.6 2.2 fusion.54
  191.9 0.6 dynamic_slice.36
  193.2 4.3 %fusion.52 = (f32[512]{0:T(512)S(1)}, f32[512,4608]{1,0:T(8,128)S(1)}) fusion(bf16[4608,128]{1,0:T(8,128)(2,1)} %get-tuple-element.297, bf16[512,768]{1,0:T(8,128)(2,1)} %get-tuple-element.296, s32[]{:T(128)S(6)} %select_n.175, s32[512]{0:T(512)S(1)} %get-tuple-element.294, s32[4608]{0:T(1024)S(1)} %get-tuple-element.293, ...), kind=kOutput, calls=%fused_computation.77.clone.1 | convolution fusion | flops 622853632 | bytes 10792964 | tf_op jit(solution)/shard_map/while/body/eval_jaxpr/dot_general | solution.py:92
  197.5 1.4 fusion.53
  199.0 2.2 fusion.54
  201.3 0.6 dynamic_slice.36
  202.6 4.3 %fusion.52 = (f32[512]{0:T(512)S(1)}, f32[512,4608]{1,0:T(8,128)S(1)}) fusion(bf16[4608,128]{1,0:T(8,128)(2,1)} %get-tuple-element.297, bf16[512,768]{1,0:T(8,128)(2,1)} %get-tuple-element.296, s32[]{:T(128)S(6)} %select_n.175, s32[512]{0:T(512)S(1)} %get-tuple-element.294, s32[4608]{0:T(1024)S(1)} %get-tuple-element.293, ...), kind=kOutput, calls=%fused_computation.77.clone.1 | convolution fusion | flops 622853632 | bytes 10792964 | tf_op jit(solution)/shard_map/while/body/eval_jaxpr/dot_general | solution.py:92
  206.9 1.4 fusion.53
  208.4 2.2 fusion.54
  212.0 4.3 %fusion.52 = (f32[512]{0:T(512)S(1)}, f32[512,4608]{1,0:T(8,128)S(1)}) fusion(bf16[4608,128]{1,0:T(8,128)(2,1)} %get-tuple-element.297, bf16[512,768]{1,0:T(8,128)(2,1)} %get-tuple-element.296, s32[]{:T(128)S(6)} %select_n.175, s32[512]{0:T(512)S(1)} %get-tuple-element.294, s32[4608]{0:T(1024)S(1)} %get-tuple-element.293, ...), kind=kOutput, calls=%fused_computation.77.clone.1 | convolution fusion | flops 622853632 | bytes 10792964 | tf_op jit(solution)/shard_map/while/body/eval_jaxpr/dot_general | solution.py:92
  216.3 1.4 fusion.53
  217.8 2.2 fusion.54
  221.4 4.3 %fusion.52 = (f32[512]{0:T(512)S(1)}, f32[512,4608]{1,0:T(8,128)S(1)}) fusion(bf16[4608,128]{1,0:T(8,128)(2,1)} %get-tuple-element.297, bf16[512,768]{1,0:T(8,128)(2,1)} %get-tuple-element.296, s32[]{:T(128)S(6)} %select_n.175, s32[512]{0:T(512)S(1)} %get-tuple-element.294, s32[4608]{0:T(1024)S(1)} %get-tuple-element.293, ...), kind=kOutput, calls=%fused_computation.77.clone.1 | convolution fusion | flops 622853632 | bytes 10792964 | tf_op jit(solution)/shard_map/while/body/eval_jaxpr/dot_general | solution.py:92
  225.7 1.4 fusion.53
  227.2 2.2 fusion.54
  229.5 2.1 collective-permute-start.1
  231.6 59.6 %collective-permute-done.1 = bf16[512,768]{0,1:T(8,128)(2,1)S(1)} collective-permute-done((bf16[512,768]{0,1:T(8,128)(2,1)S(1)}, bf16[512,768]{0,1:T(8,128)(2,1)S(1)}, u32[]{:S(2)}, u32[]{:S(2)}) %collective-permute-start.1) | collective-permute-done | bytes 786464 | tf_op jit(solution)/shard_map/ppermute | solution.py:169
  291.2 1.8 maximum_select_fusion.3
  293.3 1.4 maximum_select_fusion.2
  294.7 2.0 collective-permute-done.2
  296.7 17.7 %bitcast_convert_fusion = bf16[1024,4,768]{0,2,1:T(8,128)(2,1)} fusion(bf16[2,4,768,768]{3,2,1,0:T(8,128)(2,1)} %bitcast.76, bf16[512,2,768]{0,2,1:T(8,128)(2,1)} %bitcast.20, bf16[512,2,768]{0,2,1:T(8,128)(2,1)} %maximum_select_fusion.2, pred[]{:T(512)S(6)} %eq.84), kind=kOutput, calls=%fused_computation.18 | convolution fusion | flops 9680977920 | bytes 18874368 | tf_op jit(solution)/shard_map/dot_general | solution.py:184
  314.4 61.1 %reduce-scatter.2.cloned.1.call-done = bf16[1024,768]{0,1:T(8,128)(2,1)} async-done(((bf16[1024,3072]{0,1:T(8,128)(2,1)}), bf16[1024,768]{0,1:T(8,128)(2,1)}) %reduce-scatter.2.cloned.1.call-update) | async-done | bytes 1572880 | tf_op jit(solution)/shard_map/reduce_scatter | solution.py:188
  375.5 1.7 copy.18
  377.2 5.2 %all_to_all.9 = bf16[2,512,768]{2,1,0:T(8,128)(2,1)S(1)} all-to-all(bf16[2,512,768]{2,1,0:T(8,128)(2,1)S(1)} %bitcast.69), channel_id=1, replica_groups=mesh['ylo'=2,'x'=4,'c'=2,'yhi'=2,'z'=4] {'c'}, dimensions={0} | all-to-all | bytes 3145728 | tf_op jit(solution)/shard_map/all_to_all | solution.py:189
  382.5 1.3 pad_maximum_fusion
  (64 shorter events, 3.4 us)
Async XLA Ops:
  6.5 5.2 %copy-start = (bf16[512,768]{1,0:T(8,128)(2,1)S(1)}, bf16[512,768]{1,0:T(8,128)(2,1)}, u32[]{:S(2)}) copy-start(bf16[512,768]{1,0:T(8,128)(2,1)} %param.8) | copy-start | bytes 2359300
  6.5 290.1 %all-gather.2.cloned.1.call-start = ((), (), s32[]{:S(2)}) async-start(), calls=%async_computation.2 | async-start | bytes 10616832 | tf_op jit(solution)/shard_map/all_gather | solution.py:132
  6.5 13.7 %collective-permute-start = (bf16[768,768]{1,0:T(8,128)(2,1)}, bf16[768,768]{1,0:T(8,128)(2,1)S(1)}, u32[]{:S(2)}, u32[]{:S(2)}) collective-permute-start(bf16[768,768]{1,0:T(8,128)(2,1)} %param.13), channel_id=1, source_target_pairs={{0,0},{4,64},{64,4},{68,68},{1,1},{5,65},{65,5},{69,69},{2,2},{6,6... | collective-permute-start | bytes 3538952 | tf_op jit(solution)/shard_map/ppermute | solution.py:130
  14.4 4.7 %copy-start.6 = (s32[8192]{0:T(1024)S(1)}, s32[8192]{0:T(1024)}, u32[]{:S(2)}) copy-start(s32[8192]{0:T(1024)} %param.11) | copy-start | bytes 98308
  14.4 4.8 %copy-start.7 = (s32[64,2]{0,1:T(2,128)S(1)}, s32[64,2]{0,1:T(2,128)}, u32[]{:S(2)}) copy-start(s32[64,2]{0,1:T(2,128)} %param.12) | copy-start | bytes 1540
  14.4 5.0 %copy-start.4 = (bf16[512,128]{1,0:T(8,128)(2,1)S(1)}, bf16[512,128]{1,0:T(8,128)(2,1)}, u32[]{:S(2)}) copy-start(bf16[512,128]{1,0:T(8,128)(2,1)} %param.10) | copy-start | bytes 393220
  14.4 5.0 %copy-start.5 = (bf16[512,128]{1,0:T(8,128)(2,1)S(1)}, bf16[512,128]{1,0:T(8,128)(2,1)}, u32[]{:S(2)}) copy-start(bf16[512,128]{1,0:T(8,128)(2,1)} %param.9) | copy-start | bytes 393220
  20.3 142.1 %copy-start.3 = (bf16[768,768]{1,0:T(8,128)(2,1)}, bf16[768,768]{1,0:T(8,128)(2,1)S(1)}, u32[]{:S(2)}) copy-start(bf16[768,768]{1,0:T(8,128)(2,1)S(1)} %collective-permute-done) | copy-start | bytes 3538948
  167.6 2.3 copy-start.1
  169.9 3.2 copy-start.2
  172.9 202.6 %reduce-scatter.2.cloned.1.call-start = ((), (), s32[]{:S(2)}) async-start(), calls=%async_computation.3 | async-start | bytes 7864320 | tf_op jit(solution)/shard_map/reduce_scatter | solution.py:188
  229.5 61.6 %collective-permute-start.1 = (bf16[512,768]{0,1:T(8,128)(2,1)S(1)}, bf16[512,768]{0,1:T(8,128)(2,1)S(1)}, u32[]{:S(2)}, u32[]{:S(2)}) collective-permute-start(bf16[512,768]{0,1:T(8,128)(2,1)S(1)} %bitcast.70), channel_id=1, source_target_pairs={{0,4},{4,0},{1,5},{5,1},{2,6},{6,2},{3,7},{7,3},{8,12},{12,8},{9,1... | collective-permute-start | bytes 2359304 | tf_op jit(solution)/shard_map/ppermute | solution.py:169
  292.9 3.8 collective-permute-start.2
Sparse Core Ops, SparseCore 0:
  173.0 100.2 all-gather.1
  314.5 60.9 reduce-scatter.1

commit v9 on v5

--- a/solution.py
+++ b/solution.py
@@ -36,7 +36,13 @@
     blocks_all = packing.shape[0]
 
     kv_local = jnp.concatenate([keys, values], axis=1)
-    kv_all = lax.all_gather(kv_local, SEQ, axis=0, tiled=True)
+    kv_mine = lax.all_gather(kv_local, ("ylo", "x"), axis=0, tiled=False)
+    kv_other = lax.ppermute(kv_mine, "c", [(0, 1), (1, 0)])
+    kv_all = jnp.where(
+        lax.axis_index("c") == 0,
+        jnp.stack([kv_mine, kv_other], axis=1),
+        jnp.stack([kv_other, kv_mine], axis=1),
+    )
     kv_blocks = kv_all.reshape(blocks_all, BLOCK, 2 * kv_cols)
     target = packing[:, 0] * per_shard + packing[:, 1]
     source = jnp.zeros((blocks_all,), jnp.int32).at[target].set(

time: 315 us -> 320 us (1.016)
  waiting for transfers between devices: 164 us -> 174 us
  local copies, waits for them, and re-layouts: 22.9 us -> 18.9 us
    all_gather x1, waiting for transfers between devices: 4.43 us -> 51.4 us  [shards(): kv_mine = lax.all_gather(kv_local, ('ylo', 'x'), axis=0, tiled=False)]
    all_to_all x1, waiting for transfers between devices: 39.5 us -> 0.01 us  [shards(): lax.all_to_all(outgoing, SEQ, split_axis=0, concat_axis=0, tiled=True)]
    select_n x0 -> x1, other arithmetic: none -> 4.55 us  [shards(): jnp.where(lax.axis_index('c') == 0, jnp.stack([kv_mine, kv_other], axis=1...]
    dynamic_update_slice x12, local copies, waits for them, and re-layouts: 4.73 us -> 0.78 us  [shards(): per_head = lax.map(one_head, jnp.arange(heads_here, dtype=jnp.int32))]
    select_n x2, other arithmetic: 4.51 us -> 0.87 us  [shards(): jnp.where(low_hi, jnp.concatenate([attended, h_far], axis=1), jnp.concate...]
  transfers between devices with their start and end apart: 7 -> 8, of which waited for: 5 -> 4; matrix products, arithmetic and copies ran while one was open for 26% -> 24% of each run, Pallas kernels for 0% -> 0%
where the time goes in v9:
time: 320 us; the launch traced here: 319 us
  waiting for transfers between devices  174 us (54%)
  matrix products  59.3 us (19%)
  starting transfers between devices  22.4 us (7%)
  other arithmetic  20.8 us (6%)
  local copies, waits for them, and re-layouts  18.9 us (6%)
  between operations  13.3 us (4%)
  blocking collectives  5.37 us (2%)
  loops' own time  4.6 us (1%)
    reduce_scatter x1, waiting for transfers between devices, shards(): summed = lax.psum_scatter(part, 'z', scatter_dimension=1, tiled=True)  61.1 us
    ppermute x1, waiting for transfers between devices, shards(): h_far = lax.ppermute(attended, 'yhi', pair)  58.7 us
    all_gather x1, waiting for transfers between devices, shards(): kv_mine = lax.all_gather(kv_local, ('ylo', 'x'), axis=0, tiled=False)  51.4 us
    dot_general x6, matrix products, attend_head(): lax.dot_general(q_rows, k_rows, (((1,), (1,)), ((), ())), preferred_eleme...  26 us
    dot_general x1, matrix products, shards(): lax.dot_general(h_split, w_here, (((1, 2), (0, 2)), ((), ())), preferred_...  16.4 us
    dot_general x6, matrix products, attend_head(): jnp.dot(weights, v_rows, preferred_element_type=jnp.float32)  13.3 us
    ppermute x1, starting transfers between devices, shards(): lax.ppermute(out_weight, ('ylo', 'yhi'), perm=[(0, 0), (1, 2), (2, 1), (3...  10.4 us
    reduce_sum x6, other arithmetic, attend_head(): weights = (expo / jnp.sum(expo, axis=1, keepdims=True)).astype(jnp.bfloat16)  8.42 us
  transfers between devices with their start and end apart: 8, of which 4 were waited for; matrix products, arithmetic and copies ran while one was open for 24% of the time, Pallas kernels for 0%

profile of v9, /device:TPU:1, one launch (start us, length us, event | category | flops | bytes accessed | tf_op | source)
XLA Modules:
  0.0 318.8 jit_solution(9570152057925236784)
XLA Ops:
  6.5 1.8 pad_maximum_fusion.1
  8.3 0.8 constant_dynamic-slice_fusion
  9.1 1.5 convolution_convert_fusion
  10.6 2.7 copy.14
  13.3 7.0 %all-to-all-start = ((bf16[16,128,768]{2,1,0:T(8,128)(2,1)}), bf16[16,128,768]{2,1,0:T(8,128)(2,1)S(1)}, u32[]{:S(2)}, u32[]{:S(2)}) async-start(bf16[16,128,768]{2,1,0:T(8,128)(2,1)} %copy.14), calls=%async_computation | async-start | bytes 6291456 | tf_op jit(solution)/shard_map/all_to_all | solution.py:64
  20.3 10.4 %collective-permute-start.1 = (bf16[768,768]{1,0:T(8,128)(2,1)}, bf16[768,768]{1,0:T(8,128)(2,1)}, u32[]{:S(2)}, u32[]{:S(2)}) collective-permute-start(bf16[768,768]{1,0:T(8,128)(2,1)} %param.13), channel_id=1, source_target_pairs={{0,0},{4,64},{64,4},{68,68},{1,1},{5,65},{65,5},{69,69},{2,2},{6,6... | collective-permute-start | bytes 3538952 | tf_op jit(solution)/shard_map/ppermute | solution.py:78
  30.7 51.4 %all-gather.6.cloned.1.call-done = bf16[4096,256]{1,0:T(8,128)(2,1)} async-done(((bf16[512,256]{1,0:T(8,128)(2,1)}), bf16[4096,256]{1,0:T(8,128)(2,1)}) %all-gather.6.cloned.1.call-update) | async-done | bytes 2097168 | tf_op jit(solution)/shard_map/all_gather | solution.py:39
  82.0 0.8 collective-permute-start
  82.8 0.8 scatter_custom_fusion
  83.7 0.8 gather_fusion
  84.9 1.9 fusion.19
  86.9 1.0 copy.16
  87.9 4.5 %maximum_select_fusion = bf16[8,2,512,256]{3,2,1,0:T(8,128)(2,1)} fusion(bf16[8,1,512,256]{3,2,1,0:T(8,128)(2,1)} %bitcast.12, bf16[8,1,512,256]{3,2,1,0:T(8,128)(2,1)S(1)} %bitcast.79, pred[]{:T(512)S(6)} %eq.85), kind=kLoop, calls=%fused_computation.19 | loop fusion | flops 6291456 | bytes 8388609 | tf_op jit(solution)/shard_map/jit(_where)/select_n | solution.py:41
  92.4 4.5 %gather_fusion.1 = bf16[36,128,256]{2,1,0:T(8,128)(2,1)} fusion(bf16[64,128,256]{2,1,0:T(8,128)(2,1)} %bitcast.71, s32[1024]{0:T(1024)S(1)} %pad_clamp_fusion), kind=kCustom, calls=%fused_computation.1 | custom fusion | bytes 4718736 | tf_op jit(solution)/shard_map/jit(_take)/gather | solution.py:55
  96.9 3.8 %bitcast_select_fusion = bf16[4608,256]{1,0:T(8,128)(2,1)S(1)} fusion(bf16[36,128,256]{2,1,0:T(8,128)(2,1)} %gather_fusion.1, pred[4608]{0:T(1024)(128)(4,1)S(1)} %broadcast_bitcast_fusion), kind=kLoop, calls=%fused_computation.30 | loop fusion | flops 1179648 | bytes 4723200 | tf_op jit(solution)/shard_map/jit(_take)/select_n | solution.py:55
  100.8 1.6 fusion.39
  102.6 57.2 %while.13 = (s32[]{:T(128)}, bf16[6,512,128]{1,2,0:T(8,128)(2,1)S(1)}, s32[4608]{0:T(1024)S(1)}, s32[512]{0:T(512)S(1)}, s32[6]{0:T(128)S(1)}, /*index=5*/bf16[5...) while((s32[]{:T(128)}, ...), condition=%wide.region_4.5_spmd.clone, body=%wide.region_1.4_spmd.clone.sunk | while | flops 1238700544 | bytes 36251884 | solution.py:97
  102.6 0.7 dynamic_slice.36
  104.0 4.3 %fusion.51 = (f32[512]{0:T(512)S(1)}, f32[512,4608]{1,0:T(8,128)S(1)}) fusion(bf16[4608,128]{1,0:T(8,128)(2,1)} %get-tuple-element.293, bf16[512,768]{1,0:T(8,128)(2,1)} %get-tuple-element.292, s32[]{:T(128)S(6)} %select_n.192, s32[512]{0:T(512)S(1)} %get-tuple-element.290, s32[4608]{0:T(1024)S(1)} %get-tuple-element.289, ...), kind=kOutput, calls=%fused_computation.77.clone.1 | convolution fusion | flops 622853632 | bytes 10792964 | tf_op jit(solution)/shard_map/while/body/eval_jaxpr/dot_general | solution.py:17
  108.4 1.4 fusion.52
  109.8 2.2 fusion.53
  112.2 0.7 dynamic_slice.36
  113.5 4.3 %fusion.51 = (f32[512]{0:T(512)S(1)}, f32[512,4608]{1,0:T(8,128)S(1)}) fusion(bf16[4608,128]{1,0:T(8,128)(2,1)} %get-tuple-element.293, bf16[512,768]{1,0:T(8,128)(2,1)} %get-tuple-element.292, s32[]{:T(128)S(6)} %select_n.192, s32[512]{0:T(512)S(1)} %get-tuple-element.290, s32[4608]{0:T(1024)S(1)} %get-tuple-element.289, ...), kind=kOutput, calls=%fused_computation.77.clone.1 | convolution fusion | flops 622853632 | bytes 10792964 | tf_op jit(solution)/shard_map/while/body/eval_jaxpr/dot_general | solution.py:17
  117.9 1.4 fusion.52
  119.3 2.2 fusion.53
  121.7 0.7 dynamic_slice.36
  123.1 4.3 %fusion.51 = (f32[512]{0:T(512)S(1)}, f32[512,4608]{1,0:T(8,128)S(1)}) fusion(bf16[4608,128]{1,0:T(8,128)(2,1)} %get-tuple-element.293, bf16[512,768]{1,0:T(8,128)(2,1)} %get-tuple-element.292, s32[]{:T(128)S(6)} %select_n.192, s32[512]{0:T(512)S(1)} %get-tuple-element.290, s32[4608]{0:T(1024)S(1)} %get-tuple-element.289, ...), kind=kOutput, calls=%fused_computation.77.clone.1 | convolution fusion | flops 622853632 | bytes 10792964 | tf_op jit(solution)/shard_map/while/body/eval_jaxpr/dot_general | solution.py:17
  127.4 1.4 fusion.52
  128.9 2.2 fusion.53
  131.2 0.7 dynamic_slice.36
  132.6 4.3 %fusion.51 = (f32[512]{0:T(512)S(1)}, f32[512,4608]{1,0:T(8,128)S(1)}) fusion(bf16[4608,128]{1,0:T(8,128)(2,1)} %get-tuple-element.293, bf16[512,768]{1,0:T(8,128)(2,1)} %get-tuple-element.292, s32[]{:T(128)S(6)} %select_n.192, s32[512]{0:T(512)S(1)} %get-tuple-element.290, s32[4608]{0:T(1024)S(1)} %get-tuple-element.289, ...), kind=kOutput, calls=%fused_computation.77.clone.1 | convolution fusion | flops 622853632 | bytes 10792964 | tf_op jit(solution)/shard_map/while/body/eval_jaxpr/dot_general | solution.py:17
  137.0 1.4 fusion.52
  138.4 2.2 fusion.53
  142.2 4.3 %fusion.51 = (f32[512]{0:T(512)S(1)}, f32[512,4608]{1,0:T(8,128)S(1)}) fusion(bf16[4608,128]{1,0:T(8,128)(2,1)} %get-tuple-element.293, bf16[512,768]{1,0:T(8,128)(2,1)} %get-tuple-element.292, s32[]{:T(128)S(6)} %select_n.192, s32[512]{0:T(512)S(1)} %get-tuple-element.290, s32[4608]{0:T(1024)S(1)} %get-tuple-element.289, ...), kind=kOutput, calls=%fused_computation.77.clone.1 | convolution fusion | flops 622853632 | bytes 10792964 | tf_op jit(solution)/shard_map/while/body/eval_jaxpr/dot_general | solution.py:17
  146.5 1.4 fusion.52
  147.9 2.2 fusion.53
  151.7 4.3 %fusion.51 = (f32[512]{0:T(512)S(1)}, f32[512,4608]{1,0:T(8,128)S(1)}) fusion(bf16[4608,128]{1,0:T(8,128)(2,1)} %get-tuple-element.293, bf16[512,768]{1,0:T(8,128)(2,1)} %get-tuple-element.292, s32[]{:T(128)S(6)} %select_n.192, s32[512]{0:T(512)S(1)} %get-tuple-element.290, s32[4608]{0:T(1024)S(1)} %get-tuple-element.289, ...), kind=kOutput, calls=%fused_computation.77.clone.1 | convolution fusion | flops 622853632 | bytes 10792964 | tf_op jit(solution)/shard_map/while/body/eval_jaxpr/dot_general | solution.py:17
  156.0 1.4 fusion.52
  157.5 2.2 fusion.53
  159.8 3.2 %collective-permute-start.2 = (bf16[512,768]{0,1:T(8,128)(2,1)S(1)}, bf16[512,768]{0,1:T(8,128)(2,1)S(1)}, u32[]{:S(2)}, u32[]{:S(2)}) collective-permute-start(bf16[512,768]{0,1:T(8,128)(2,1)S(1)} %bitcast.74), channel_id=1, source_target_pairs={{0,4},{4,0},{1,5},{5,1},{2,6},{6,2},{3,7},{7,3},{8,12},{12,8},{9,1... | collective-permute-start | bytes 2359304 | tf_op jit(solution)/shard_map/ppermute | solution.py:101
  163.1 58.7 %collective-permute-done.2 = bf16[512,768]{0,1:T(8,128)(2,1)S(1)} collective-permute-done((bf16[512,768]{0,1:T(8,128)(2,1)S(1)}, bf16[512,768]{0,1:T(8,128)(2,1)S(1)}, u32[]{:S(2)}, u32[]{:S(2)}) %collective-permute-start.2) | collective-permute-done | bytes 786464 | tf_op jit(solution)/shard_map/ppermute | solution.py:101
  222.3 0.7 collective-permute-start.3
  223.3 2.9 collective-permute-done.3
  226.2 16.4 %bitcast_convert_fusion = bf16[1024,4,768]{0,2,1:T(8,128)(2,1)} fusion(bf16[2,4,768,768]{3,2,1,0:T(8,128)(2,1)} %bitcast.81, bf16[512,2,768]{0,2,1:T(8,128)(2,1)} %bitcast.23, bf16[512,2,768]{0,2,1:T(8,128)(2,1)S(1)} %maximum_select_fusion.3, pred[]{:T(512)S(6)} %eq.85), kind=kOutput, calls=%fused_computation.18 | convolution fusion | flops 9680977920 | bytes 18874368 | tf_op jit(solution)/shard_map/dot_general | solution.py:116
  242.7 61.1 %reduce-scatter.2.cloned.1.call-done = bf16[1024,768]{0,1:T(8,128)(2,1)} async-done(((bf16[1024,3072]{0,1:T(8,128)(2,1)}), bf16[1024,768]{0,1:T(8,128)(2,1)}) %reduce-scatter.2.cloned.1.call-update) | async-done | bytes 1572880 | tf_op jit(solution)/shard_map/reduce_scatter | solution.py:120
  303.8 1.7 copy.20
  305.5 5.4 %all_to_all.14 = bf16[2,512,768]{2,1,0:T(8,128)(2,1)S(1)} all-to-all(bf16[2,512,768]{2,1,0:T(8,128)(2,1)S(1)} %bitcast.73), channel_id=1, replica_groups=mesh['ylo'=2,'x'=4,'c'=2,'yhi'=2,'z'=4] {'c'}, dimensions={0} | all-to-all | bytes 3145728 | tf_op jit(solution)/shard_map/all_to_all | solution.py:121
  311.0 1.3 pad_maximum_fusion
  (79 shorter events, 4.1 us)
Async XLA Ops:
  6.5 2.6 copy-start
  6.5 75.5 %all-gather.6.cloned.1.call-start = ((), (), s32[]{:S(2)}) async-start(), calls=%async_computation.5 | async-start | bytes 2359296 | tf_op jit(solution)/shard_map/all_gather | solution.py:39
  13.3 69.6 %copy-start.6 = (s32[64,2]{0,1:T(2,128)S(1)}, s32[64,2]{0,1:T(2,128)}, u32[]{:S(2)}) copy-start(s32[64,2]{0,1:T(2,128)} %param.12) | copy-start | bytes 1540
  13.3 71.2 %copy-start.5 = (s32[8192]{0:T(1024)S(1)}, s32[8192]{0:T(1024)}, u32[]{:S(2)}) copy-start(s32[8192]{0:T(1024)} %param.11) | copy-start | bytes 98308
  13.3 71.7 %all-to-all-start = ((bf16[16,128,768]{2,1,0:T(8,128)(2,1)}), bf16[16,128,768]{2,1,0:T(8,128)(2,1)S(1)}, u32[]{:S(2)}, u32[]{:S(2)}) async-start(bf16[16,128,768]{2,1,0:T(8,128)(2,1)} %copy.14), calls=%async_computation | async-start | bytes 6291456 | tf_op jit(solution)/shard_map/all_to_all | solution.py:64
  20.2 206.0 %all-gather.4.cloned.1.call-start = ((), (), s32[]{:S(2)}) async-start(), calls=%async_computation.3 | async-start | bytes 10616832 | tf_op jit(solution)/shard_map/all_gather | solution.py:80
  20.3 80.5 %collective-permute-start.1 = (bf16[768,768]{1,0:T(8,128)(2,1)}, bf16[768,768]{1,0:T(8,128)(2,1)}, u32[]{:S(2)}, u32[]{:S(2)}) collective-permute-start(bf16[768,768]{1,0:T(8,128)(2,1)} %param.13), channel_id=1, source_target_pairs={{0,0},{4,64},{64,4},{68,68},{1,1},{5,65},{65,5},{69,69},{2,2},{6,6... | collective-permute-start | bytes 3538952 | tf_op jit(solution)/shard_map/ppermute | solution.py:78
  82.0 5.8 %collective-permute-start = (bf16[8,512,256]{2,1,0:T(8,128)(2,1)}, bf16[8,512,256]{2,1,0:T(8,128)(2,1)}, u32[]{:S(2)}, u32[]{:S(2)}) collective-permute-start(bf16[8,512,256]{2,1,0:T(8,128)(2,1)} %bitcast.78), channel_id=1, source_target_pairs={{0,8},{8,0},{1,9},{9,1},{2,10},{10,2},{3,11},{11,3},{4,12},{12,4},... | collective-permute-start | bytes 6291464 | tf_op jit(solution)/shard_map/ppermute | solution.py:40
  84.9 2.9 copy-start.3
  100.8 1.9 copy-start.2
  102.4 201.4 %reduce-scatter.2.cloned.1.call-start = ((), (), s32[]{:S(2)}) async-start(), calls=%async_computation.4 | async-start | bytes 7864320 | tf_op jit(solution)/shard_map/reduce_scatter | solution.py:120
  108.3 1.4 copy-start.4
  117.9 1.4 copy-start.4
  127.4 1.4 copy-start.4
  137.0 1.4 copy-start.4
  146.5 1.4 copy-start.4
  156.0 1.4 copy-start.4
  159.8 61.9 %collective-permute-start.2 = (bf16[512,768]{0,1:T(8,128)(2,1)S(1)}, bf16[512,768]{0,1:T(8,128)(2,1)S(1)}, u32[]{:S(2)}, u32[]{:S(2)}) collective-permute-start(bf16[512,768]{0,1:T(8,128)(2,1)S(1)} %bitcast.74), channel_id=1, source_target_pairs={{0,4},{4,0},{1,5},{5,1},{2,6},{6,2},{3,7},{7,3},{8,12},{12,8},{9,1... | collective-permute-start | bytes 2359304 | tf_op jit(solution)/shard_map/ppermute | solution.py:101
  222.3 3.9 %collective-permute-start.3 = (bf16[512,1536]{0,1:T(8,128)(2,1)S(1)}, bf16[512,1536]{0,1:T(8,128)(2,1)}, u32[]{:S(2)}, u32[]{:S(2)}) collective-permute-start(bf16[512,1536]{0,1:T(8,128)(2,1)S(1)} %maximum_select_fusion.4), channel_id=1, source_target_pairs={{0,8},{8,0},{1,9},{9,1},{2,10},{10,2},{3,11},{11,3},{4,12},{12,4},... | collective-permute-start | bytes 4718600 | tf_op jit(solution)/shard_map/ppermute | solution.py:108
  305.5 6.8 %copy-start.1 = (bf16[512,768]{1,0:T(8,128)(2,1)S(1)}, bf16[512,768]{1,0:T(8,128)(2,1)}, u32[]{:S(2)}) copy-start(bf16[512,768]{1,0:T(8,128)(2,1)} %param.8) | copy-start | bytes 2359300
Sparse Core Ops, SparseCore 0:
  9.0 72.9 all-gather.5
  102.5 101.2 all-gather.3
  242.8 60.9 reduce-scatter.1

commit v10 on v9

--- a/solution.py
+++ b/solution.py
@@ -36,7 +36,12 @@
     blocks_all = packing.shape[0]
 
     kv_local = jnp.concatenate([keys, values], axis=1)
-    kv_mine = lax.all_gather(kv_local, ("ylo", "x"), axis=0, tiled=False)
+    w_swapped = lax.ppermute(out_weight, ("ylo", "yhi"), perm=[(0, 0), (1, 2), (2, 1), (3, 3)])
+    kv_size = kv_local.size
+    both = jnp.concatenate([kv_local.reshape(-1), w_swapped.reshape(-1)])
+    gathered = lax.all_gather(both, ("ylo", "x"), axis=0, tiled=False)
+    kv_mine = gathered[:, :kv_size].reshape((-1,) + kv_local.shape)
+    w_here = gathered[:, kv_size:].reshape((2, -1) + out_weight.shape)
     kv_other = lax.ppermute(kv_mine, "c", [(0, 1), (1, 0)])
     kv_all = jnp.where(
         lax.axis_index("c") == 0,
@@ -74,11 +79,6 @@
         "od,drc->orc", placing, incoming, preferred_element_type=jnp.float32
     ).astype(jnp.bfloat16)
     queries_here = packed.reshape(tok_rows, q_cols)
-
-    w_swapped = lax.ppermute(out_weight, ("ylo", "yhi"), perm=[(0, 0), (1, 2), (2, 1), (3, 3)])
-    context, w_swapped = lax.optimization_barrier((context, w_swapped))
-    w_here = lax.all_gather(w_swapped, ("ylo", "x"), axis=0, tiled=True)
-    w_here = w_here.reshape(2, -1, out_weight.shape[0], out_weight.shape[1])
 
     ctx_keys = context[:, :kv_cols]
     ctx_values = context[:, kv_cols:]

time: 320 us -> 432 us (1.35)
  waiting for transfers between devices: 174 us -> 235 us
  local copies, waits for them, and re-layouts: 18.9 us -> 52.8 us
  starting transfers between devices: 22.4 us -> 38.6 us
    all_gather x2 -> x1, waiting for transfers between devices: 51.4 us -> 151 us  [shards(): gathered = lax.all_gather(both, ('ylo', 'x'), axis=0, tiled=False)]
    ppermute x1, waiting for transfers between devices: 58.7 us -> 19.3 us  [shards(): h_far = lax.ppermute(attended, 'yhi', pair)]
    all_to_all x1, starting transfers between devices: 6.96 us -> 33.5 us  [shards(): lax.all_to_all(outgoing, SEQ, split_axis=0, concat_axis=0, tiled=True)]
    all_gather x0 -> x1, local copies, waits for them, and re-layouts: none -> 13.4 us  [shards(): gathered = lax.all_gather(both, ('ylo', 'x'), axis=0, tiled=False)]
    unnamed x12 -> x13, local copies, waits for them, and re-layouts: 0.03 us -> 11.3 us
    slice x0 -> x3, local copies, waits for them, and re-layouts: none -> 10.7 us  [the longest x1 9.12 us: shards(): w_here = gathered[:, kv_size:].reshape((2, -1) + out_weight.shape)]
    ppermute x1, starting transfers between devices: 10.4 us -> 2.05 us  [shards(): lax.ppermute(out_weight, ('ylo', 'yhi'), perm=[(0, 0), (1, 2), (2, 1), (3...]
  transfers between devices with their start and end apart: 8 -> 7, of which waited for: 4 -> 3; matrix products, arithmetic and copies ran while one was open for 24% -> 11% of each run, Pallas kernels for 0% -> 0%
where the time goes in v10:
time: 432 us; the launch traced here: 431 us
  waiting for transfers between devices  235 us (54%)
  matrix products  61.2 us (14%)
  local copies, waits for them, and re-layouts  52.8 us (12%)
  starting transfers between devices  38.6 us (9%)
  other arithmetic  19.8 us (5%)
  between operations  13.6 us (3%)
  blocking collectives  5.4 us (1%)
  loops' own time  4.51 us (1%)
    all_gather x1, waiting for transfers between devices, shards(): gathered = lax.all_gather(both, ('ylo', 'x'), axis=0, tiled=False)  151 us
    reduce_scatter x1, waiting for transfers between devices, shards(): summed = lax.psum_scatter(part, 'z', scatter_dimension=1, tiled=True)  64.6 us
    all_to_all x1, starting transfers between devices, shards(): lax.all_to_all(outgoing, SEQ, split_axis=0, concat_axis=0, tiled=True)  33.5 us
    dot_general x6, matrix products, attend_head(): lax.dot_general(q_rows, k_rows, (((1,), (1,)), ((), ())), preferred_eleme...  25.9 us
    ppermute x1, waiting for transfers between devices, shards(): h_far = lax.ppermute(attended, 'yhi', pair)  19.3 us
    dot_general x1, matrix products, shards(): lax.dot_general(h_split, w_here, (((1, 2), (0, 2)), ((), ())), preferred_...  16.6 us
    all_gather x1, local copies, waits for them, and re-layouts, shards(): gathered = lax.all_gather(both, ('ylo', 'x'), axis=0, tiled=False)  13.4 us
    dot_general x6, matrix products, attend_head(): jnp.dot(weights, v_rows, preferred_element_type=jnp.float32)  13.2 us
  transfers between devices with their start and end apart: 7, of which 3 were waited for; matrix products, arithmetic and copies ran while one was open for 11% of the time, Pallas kernels for 0%

profile of v10, /device:TPU:1, one launch (start us, length us, event | category | flops | bytes accessed | tf_op | source)
XLA Modules:
  0.0 431.3 jit_solution(976213207575801397)
XLA Ops:
  6.5 2.0 collective-permute-start
  8.6 1.0 maximum_bitcast_fusion
  9.8 1.0 reshape.141
  10.9 1.2 pad_maximum_fusion.1
  12.2 1.5 convolution_convert_fusion
  13.7 2.7 copy.20
  16.3 33.5 %all-to-all-start = ((bf16[16,128,768]{2,1,0:T(8,128)(2,1)}), bf16[16,128,768]{2,1,0:T(8,128)(2,1)}, u32[]{:S(2)}, u32[]{:S(2)}) async-start(bf16[16,128,768]{2,1,0:T(8,128)(2,1)} %copy.20), calls=%async_computation | async-start | bytes 6291456 | tf_op jit(solution)/shard_map/all_to_all | solution.py:69
  49.9 151.5 %all-gather.3.cloned.1.call-done = bf16[5767168]{0:T(1024)(128)(2,1)} async-done(((bf16[720896]{0:T(1024)(128)(2,1)}), bf16[5767168]{0:T(1024)(128)(2,1)}) %all-gather.3.cloned.1.call-update) | async-done | bytes 11534352 | tf_op jit(solution)/shard_map/all_gather | solution.py:42
  201.3 13.4 %reshape.170 = bf16[8,720896]{1,0:T(8,128)(2,1)} reshape(bf16[5767168]{0:T(1024)(128)(2,1)} %all-gather.3.cloned.1.call-done) | data formatting | bytes 23068672 | tf_op jit(solution)/shard_map/all_gather | solution.py:42
  214.8 1.6 slice-done
  216.4 1.7 copy.46
  218.6 1.0 scatter_custom_fusion
  219.6 0.8 gather_fusion
  220.8 3.8 fusion.19
  224.7 1.0 copy.22
  225.7 4.5 %maximum_select_fusion = bf16[8,2,512,256]{3,2,1,0:T(8,128)(2,1)} fusion(bf16[8,1,512,256]{3,2,1,0:T(8,128)(2,1)S(1)} %bitcast.93, bf16[8,1,512,256]{3,2,1,0:T(8,128)(2,1)} %bitcast.72, pred[]{:T(512)S(6)} %eq.85), kind=kLoop, calls=%fused_computation.19 | loop fusion | flops 6291456 | bytes 8388609 | tf_op jit(solution)/shard_map/jit(_where)/select_n | solution.py:46
  230.2 2.9 gather_fusion.1
  233.0 2.4 bitcast_select_fusion
  235.4 1.2 fusion.39
  236.7 56.9 %while.13 = (s32[]{:T(128)}, bf16[6,512,128]{1,2,0:T(8,128)(2,1)S(1)}, s32[4608]{0:T(1024)S(1)}, s32[512]{0:T(512)S(1)}, s32[6]{0:T(128)S(1)}, /*index=5*/bf16[5...) while((s32[]{:T(128)}, ...), condition=%wide.region_4.5_spmd.clone, body=%wide.region_1.4_spmd.clone.sunk | while | flops 1238700544 | bytes 31533272 | solution.py:97
  238.1 4.3 %fusion.51 = (f32[512]{0:T(512)S(1)}, f32[512,4608]{1,0:T(8,128)S(1)}) fusion(bf16[4608,128]{1,0:T(8,128)(2,1)} %get-tuple-element.291, bf16[512,768]{1,0:T(8,128)(2,1)} %get-tuple-element.290, s32[]{:T(128)S(6)} %select_n.192, s32[512]{0:T(512)S(1)} %get-tuple-element.288, s32[4608]{0:T(1024)S(1)} %get-tuple-element.287, ...), kind=kOutput, calls=%fused_computation.80.clone.1 | convolution fusion | flops 622853632 | bytes 10792964 | tf_op jit(solution)/shard_map/while/body/eval_jaxpr/dot_general | solution.py:17
  242.4 1.4 fusion.52
  243.8 2.2 fusion.53
  247.6 4.3 fusion.51
  251.9 1.4 fusion.52
  253.3 2.2 fusion.53
  257.1 4.3 fusion.51
  261.4 1.4 fusion.52
  262.8 2.2 fusion.53
  266.6 4.3 fusion.51
  270.9 1.4 fusion.52
  272.3 2.2 fusion.53
  276.1 4.3 fusion.51
  280.4 1.4 fusion.52
  281.8 2.2 fusion.53
  285.6 4.3 fusion.51
  289.9 1.4 fusion.52
  291.3 2.2 fusion.53
  293.7 1.4 collective-permute-start.2
  295.1 19.3 %collective-permute-done.2 = bf16[512,768]{0,1:T(8,128)(2,1)S(1)} collective-permute-done((bf16[512,768]{0,1:T(8,128)(2,1)S(1)}, bf16[512,768]{0,1:T(8,128)(2,1)S(1)}, u32[]{:S(2)}, u32[]{:S(2)}) %collective-permute-start.2) | collective-permute-done | bytes 786464 | tf_op jit(solution)/shard_map/ppermute | solution.py:101
  315.0 1.1 collective-permute-start.3
  316.1 9.1 %slice.53 = bf16[8,589824]{1,0:T(8,128)(2,1)} slice(bf16[8,720896]{1,0:T(8,128)(2,1)} %reshape.170), slice={[0:8], [131072:720896]} | slice | bytes 18874368 | tf_op jit(solution)/shard_map/slice | solution.py:44
  325.2 9.2 %copy.37 = bf16[1,8,768,768]{3,2,1,0:T(8,128)(2,1)} copy(bf16[1,8,768,768]{3,1,2,0:T(8,128)(2,1)} %bitcast.84) | data formatting | bytes 18874368
  334.7 16.6 %bitcast_convert_fusion = bf16[1024,4,768]{0,2,1:T(8,128)(2,1)} fusion(bf16[2,4,768,768]{3,2,1,0:T(8,128)(2,1)} %bitcast.86, bf16[512,2,768]{0,2,1:T(8,128)(2,1)} %bitcast.21, bf16[512,2,768]{0,2,1:T(8,128)(2,1)S(1)} %maximum_select_fusion.3, pred[]{:T(512)S(6)} %eq.85), kind=kOutput, calls=%fused_computation.18 | convolution fusion | flops 9680977920 | bytes 18874368 | tf_op jit(solution)/shard_map/dot_general | solution.py:116
  351.4 64.6 %reduce-scatter.2.cloned.1.call-done = bf16[1024,768]{0,1:T(8,128)(2,1)} async-done(((bf16[1024,3072]{0,1:T(8,128)(2,1)}), bf16[1024,768]{0,1:T(8,128)(2,1)}) %reduce-scatter.2.cloned.1.call-update) | async-done | bytes 1572880 | tf_op jit(solution)/shard_map/reduce_scatter | solution.py:120
  416.0 1.7 copy.26
  417.7 5.4 %all_to_all.14 = bf16[2,512,768]{2,1,0:T(8,128)(2,1)S(1)} all-to-all(bf16[2,512,768]{2,1,0:T(8,128)(2,1)S(1)} %bitcast.88), channel_id=1, replica_groups=mesh['ylo'=2,'x'=4,'c'=2,'yhi'=2,'z'=4] {'c'}, dimensions={0} | all-to-all | bytes 3145728 | tf_op jit(solution)/shard_map/all_to_all | solution.py:121
  423.2 1.3 pad_maximum_fusion
  (71 shorter events, 7.3 us)
Async XLA Ops:
  6.5 5.6 %copy-start = (bf16[512,768]{1,0:T(8,128)(2,1)S(1)}, bf16[512,768]{1,0:T(8,128)(2,1)}, u32[]{:S(2)}) copy-start(bf16[512,768]{1,0:T(8,128)(2,1)} %param.8) | copy-start | bytes 2359300
  6.5 194.8 %all-gather.3.cloned.1.call-start = ((), (), s32[]{:S(2)}) async-start(), calls=%async_computation.4 | async-start | bytes 12976128 | tf_op jit(solution)/shard_map/all_gather | solution.py:42
  6.5 3.3 collective-permute-start
  9.8 2.3 copy-start.4
  16.3 204.5 %all-to-all-start = ((bf16[16,128,768]{2,1,0:T(8,128)(2,1)}), bf16[16,128,768]{2,1,0:T(8,128)(2,1)}, u32[]{:S(2)}, u32[]{:S(2)}) async-start(bf16[16,128,768]{2,1,0:T(8,128)(2,1)} %copy.20), calls=%async_computation | async-start | bytes 6291456 | tf_op jit(solution)/shard_map/all_to_all | solution.py:69
  49.8 366.2 %reduce-scatter.2.cloned.1.call-start = ((), (), s32[]{:S(2)}) async-start(), calls=%async_computation.3 | async-start | bytes 7864320 | tf_op jit(solution)/shard_map/reduce_scatter | solution.py:120
  214.8 1.6 slice-start
  214.8 4.7 %copy-start.3 = (s32[8192]{0:T(1024)S(1)}, s32[8192]{0:T(1024)}, u32[]{:S(2)}) copy-start(s32[8192]{0:T(1024)} %param.11) | copy-start | bytes 98308
  218.1 7.6 %collective-permute-start.1 = (bf16[8,512,256]{2,1,0:T(8,128)(2,1)}, bf16[8,512,256]{2,1,0:T(8,128)(2,1)S(1)}, u32[]{:S(2)}, u32[]{:S(2)}) collective-permute-start(bf16[8,512,256]{2,1,0:T(8,128)(2,1)} %bitcast.51.clone.2), channel_id=1, source_target_pairs={{0,8},{8,0},{1,9},{9,1},{2,10},{10,2},{3,11},{11,3},{4,12},{12,4},... | collective-permute-start | bytes 6291464 | tf_op jit(solution)/shard_map/ppermute | solution.py:45
  235.4 1.3 copy-start.2
  293.7 20.7 %collective-permute-start.2 = (bf16[512,768]{0,1:T(8,128)(2,1)S(1)}, bf16[512,768]{0,1:T(8,128)(2,1)S(1)}, u32[]{:S(2)}, u32[]{:S(2)}) collective-permute-start(bf16[512,768]{0,1:T(8,128)(2,1)S(1)} %bitcast.89), channel_id=1, source_target_pairs={{0,4},{4,0},{1,5},{5,1},{2,6},{6,2},{3,7},{7,3},{8,12},{12,8},{9,1... | collective-permute-start | bytes 2359304 | tf_op jit(solution)/shard_map/ppermute | solution.py:101
  315.0 19.7 %collective-permute-start.3 = (bf16[512,1536]{0,1:T(8,128)(2,1)S(1)}, bf16[512,1536]{0,1:T(8,128)(2,1)}, u32[]{:S(2)}, u32[]{:S(2)}) collective-permute-start(bf16[512,1536]{0,1:T(8,128)(2,1)S(1)} %maximum_select_fusion.4), channel_id=1, source_target_pairs={{0,8},{8,0},{1,9},{9,1},{2,10},{10,2},{3,11},{11,3},{4,12},{12,4},... | collective-permute-start | bytes 4718600 | tf_op jit(solution)/shard_map/ppermute | solution.py:108
  417.7 6.8 %copy-start.1 = (bf16[512,768]{1,0:T(8,128)(2,1)S(1)}, bf16[512,768]{1,0:T(8,128)(2,1)}, u32[]{:S(2)}) copy-start(bf16[512,768]{1,0:T(8,128)(2,1)} %param.8) | copy-start | bytes 2359300
Sparse Core Ops, SparseCore 0:
  12.2 189.1 all-gather.2
  351.5 64.4 reduce-scatter.1

commit v11 on v5

--- a/solution.py
+++ b/solution.py
@@ -36,8 +36,6 @@
     blocks_all = packing.shape[0]
 
     kv_local = jnp.concatenate([keys, values], axis=1)
-    kv_all = lax.all_gather(kv_local, SEQ, axis=0, tiled=True)
-    kv_blocks = kv_all.reshape(blocks_all, BLOCK, 2 * kv_cols)
     target = packing[:, 0] * per_shard + packing[:, 1]
     source = jnp.zeros((blocks_all,), jnp.int32).at[target].set(
         jnp.arange(blocks_all, dtype=jnp.int32)
@@ -46,7 +44,6 @@
     ctx_blocks = span_blocks + per_shard
     blk_ids = shard_index * per_shard - span_blocks + jnp.arange(ctx_blocks, dtype=jnp.int32)
     src = jnp.take(source, jnp.clip(blk_ids, 0, blocks_all - 1))
-    context = jnp.take(kv_blocks, src, axis=0).reshape(ctx_blocks * BLOCK, 2 * kv_cols)
 
     own_blocks = queries.reshape(per_shard, BLOCK, q_cols)
     own_list = lax.dynamic_slice_in_dim(packing, shard_index * per_shard, per_shard, 0)
@@ -55,7 +52,19 @@
     outgoing = jnp.einsum(
         "db,brc->drc", routing, own_blocks, preferred_element_type=jnp.float32
     ).astype(jnp.bfloat16)
-    incoming = lax.all_to_all(outgoing, SEQ, split_axis=0, concat_axis=0, tiled=True)
+    lanes = kv_local.shape[1]
+    q_rows = BLOCK * q_cols // lanes
+    payload = jnp.concatenate(
+        [
+            outgoing.reshape(seq_count, q_rows, lanes),
+            jnp.broadcast_to(kv_local[None], (seq_count,) + kv_local.shape),
+        ],
+        axis=1,
+    )
+    arrived = lax.all_to_all(payload, SEQ, split_axis=0, concat_axis=0, tiled=True)
+    incoming = arrived[:, :q_rows].reshape(seq_count, BLOCK, q_cols)
+    kv_blocks = arrived[:, q_rows:].reshape(blocks_all, BLOCK, 2 * kv_cols)
+    context = jnp.take(kv_blocks, src, axis=0).reshape(ctx_blocks * BLOCK, 2 * kv_cols)
     arriving = packing[:, 0] == shard_index
     offset_ids = jnp.arange(per_shard, dtype=jnp.int32)
     at_offset = ((packing[:, 1][None, :] == offset_ids[:, None]) & arriving[None, :]).astype(
@@ -70,9 +79,9 @@
     queries_here = packed.reshape(tok_rows, q_cols)
 
     w_swapped = lax.ppermute(out_weight, ("ylo", "yhi"), perm=[(0, 0), (1, 2), (2, 1), (3, 3)])
-    context, w_swapped = lax.optimization_barrier((context, w_swapped))
     w_here = lax.all_gather(w_swapped, ("ylo", "x"), axis=0, tiled=True)
     w_here = w_here.reshape(2, -1, out_weight.shape[0], out_weight.shape[1])
+    context, w_here = lax.optimization_barrier((context, w_here))
 
     ctx_keys = context[:, :kv_cols]
     ctx_values = context[:, kv_cols:]

time: 315 us -> 427 us (1.36)
  waiting for transfers between devices: 164 us -> 237 us
  local copies, waits for them, and re-layouts: 22.9 us -> 44.4 us
  starting transfers between devices: 20.9 us -> 39.2 us
    all_to_all x1, waiting for transfers between devices: 39.5 us -> 149 us  [shards(): lax.all_to_all(payload, SEQ, split_axis=0, concat_axis=0, tiled=True)]
    ppermute x1, waiting for transfers between devices: 57.4 us -> 19.9 us  [shards(): h_far = lax.ppermute(attended, 'yhi', pair)]
    all_to_all x1, starting transfers between devices: 6.96 us -> 35 us  [shards(): lax.all_to_all(payload, SEQ, split_axis=0, concat_axis=0, tiled=True)]
    reshape x0 -> x2, local copies, waits for them, and re-layouts: none -> 11.8 us  [the longest x1 5.91 us: shards(): incoming = arrived[:, :q_rows].reshape(seq_count, BLOCK, q_cols)]
    ppermute x1, starting transfers between devices: 10.4 us -> 2.05 us  [shards(): lax.ppermute(out_weight, ('ylo', 'yhi'), perm=[(0, 0), (1, 2), (2, 1), (3...]
    slice x0 -> x2, local copies, waits for them, and re-layouts: none -> 8.33 us  [the longest x1 4.51 us: shards(): kv_blocks = arrived[:, q_rows:].reshape(blocks_all, BLOCK, 2 * kv_cols)]
    concatenate x0 -> x1, other arithmetic: none -> 5.4 us  [shards(): jnp.concatenate([outgoing.reshape(seq_count, q_rows, lanes), jnp.broadcas...]
    all_gather x1 -> x0, waiting for transfers between devices: 4.43 us -> none  [shards(): kv_all = lax.all_gather(kv_local, SEQ, axis=0, tiled=True)]
  transfers between devices with their start and end apart: 7 -> 6, of which waited for: 5 -> 4; matrix products, arithmetic and copies ran while one was open for 26% -> 11% of each run, Pallas kernels for 0% -> 0%
where the time goes in v11:
time: 427 us; the launch traced here: 426 us
  waiting for transfers between devices  237 us (56%)
  matrix products  61.2 us (14%)
  local copies, waits for them, and re-layouts  44.4 us (10%)
  starting transfers between devices  39.2 us (9%)
  other arithmetic  21.2 us (5%)
  between operations  13.6 us (3%)
  blocking collectives  5.36 us (1%)
    all_to_all x1, waiting for transfers between devices, shards(): lax.all_to_all(payload, SEQ, split_axis=0, concat_axis=0, tiled=True)  149 us
    reduce_scatter x1, waiting for transfers between devices, shards(): summed = lax.psum_scatter(part, 'z', scatter_dimension=1, tiled=True)  65.2 us
    all_to_all x1, starting transfers between devices, shards(): lax.all_to_all(payload, SEQ, split_axis=0, concat_axis=0, tiled=True)  35 us
    dot_general x6, matrix products, attend_head(): lax.dot_general(q_rows, k_rows, (((1,), (1,)), ((), ())), preferred_eleme...  25.9 us
    ppermute x1, waiting for transfers between devices, shards(): h_far = lax.ppermute(attended, 'yhi', pair)  19.9 us
    dot_general x1, matrix products, shards(): lax.dot_general(h_split, w_here, (((1, 2), (0, 2)), ((), ())), preferred_...  16.5 us
    dot_general x6, matrix products, attend_head(): jnp.dot(weights, v_rows, preferred_element_type=jnp.float32)  13.3 us
  transfers between devices with their start and end apart: 6, of which 4 were waited for; matrix products, arithmetic and copies ran while one was open for 11% of the time, Pallas kernels for 0%

profile of v11, /device:TPU:1, one launch (start us, length us, event | category | flops | bytes accessed | tf_op | source)
XLA Modules:
  0.0 426.4 jit_solution(17883012521440666535)
XLA Ops:
  6.5 2.0 collective-permute-start
  8.6 1.0 copy-done.3
  9.6 0.8 constant_dynamic-slice_fusion
  10.4 1.5 convolution_convert_fusion
  11.9 2.7 copy.11
  14.6 5.9 %reshape.135 = bf16[16,384,256]{2,1,0:T(8,128)(2,1)} reshape(bf16[16,128,768]{2,1,0:T(8,128)(2,1)} %copy.11) | data formatting | bytes 6291456 | tf_op jit(solution)/shard_map/reshape | solution.py:59
  20.9 5.4 %pad_maximum_fusion = bf16[16,896,256]{2,1,0:T(8,128)(2,1)} fusion(bf16[16,512,256]{2,1,0:T(8,128)(2,1)S(1)} %broadcast_in_dim.61, bf16[16,384,256]{2,1,0:T(8,128)(2,1)} %reshape.135), kind=kLoop, calls=%fused_computation.19 | loop fusion | flops 14680064 | bytes 14680064 | tf_op jit(solution)/shard_map/concatenate | solution.py:57
  26.3 35.0 %all-to-all-start = ((bf16[16,896,256]{2,1,0:T(8,128)(2,1)}), bf16[16,896,256]{2,1,0:T(8,128)(2,1)}, u32[]{:S(2)}, u32[]{:S(2)}) async-start(bf16[16,896,256]{2,1,0:T(8,128)(2,1)} %pad_maximum_fusion), calls=%async_computation | async-start | bytes 14680064 | tf_op jit(solution)/shard_map/all_to_all | solution.py:64
  61.4 1.0 scatter_custom_fusion
  62.4 0.8 gather_fusion
  63.7 149.4 %all-to-all-done = bf16[16,896,256]{2,1,0:T(8,128)(2,1)} async-done(((bf16[16,896,256]{2,1,0:T(8,128)(2,1)}), bf16[16,896,256]{2,1,0:T(8,128)(2,1)}, u32[]{:S(2)}, u32[]{:S(2)}) %all-to-all-start) | async-done | bytes 7340064 | tf_op jit(solution)/shard_map/all_to_all | solution.py:64
  213.0 3.8 slice.50
  216.9 5.9 %reshape.136 = bf16[16,128,768]{2,1,0:T(8,128)(2,1)} reshape(bf16[16,384,256]{2,1,0:T(8,128)(2,1)} %slice.50) | data formatting | bytes 6291456 | tf_op jit(solution)/shard_map/reshape | solution.py:65
  222.8 3.8 fusion.19
  226.6 1.0 copy.13
  227.6 4.5 %slice.51 = bf16[16,512,256]{2,1,0:T(8,128)(2,1)} slice(bf16[16,896,256]{2,1,0:T(8,128)(2,1)} %all-to-all-done), slice={[0:16], [384:896], [0:256]} | slice | bytes 8388608 | tf_op jit(solution)/shard_map/slice | solution.py:66
  232.1 4.5 %gather_fusion.1 = bf16[36,128,256]{2,1,0:T(8,128)(2,1)} fusion(bf16[64,128,256]{2,1,0:T(8,128)(2,1)} %bitcast.68, s32[1024]{0:T(1024)S(1)} %pad_clamp_fusion), kind=kCustom, calls=%fused_computation.1 | custom fusion | bytes 4718736 | tf_op jit(solution)/shard_map/jit(_take)/gather | solution.py:67
  236.5 3.8 bitcast_select_fusion
  240.4 1.6 fusion.39
  242.0 60.4 %while.13 = (s32[]{:T(128)}, bf16[6,512,128]{1,2,0:T(8,128)(2,1)}, s32[4608]{0:T(1024)S(1)}, s32[512]{0:T(512)S(1)}, s32[6]{0:T(128)S(1)}, /*index=5*/bf16[512,7...) while((s32[]{:T(128)}, bf16[6,512,128]{1,2,0:T(8,128)(2,1)}, ...), condition=%wide.region_4.5_spmd.clone, body=%wide.region_1.0_spmd.clone.sunk | while | flops 1238700544 | bytes 36252392 | solution.py:100
  243.3 4.3 %fusion.51 = (f32[512]{0:T(512)S(1)}, f32[512,4608]{1,0:T(8,128)S(1)}) fusion(bf16[4608,128]{1,0:T(8,128)(2,1)} %get-tuple-element.293, bf16[512,768]{1,0:T(8,128)(2,1)} %get-tuple-element.292, s32[]{:T(128)S(6)} %select_n.175, s32[512]{0:T(512)S(1)} %get-tuple-element.290, s32[4608]{0:T(1024)S(1)} %get-tuple-element.289, ...), kind=kOutput, calls=%fused_computation.77.clone.1 | convolution fusion | flops 622853632 | bytes 10792964 | tf_op jit(solution)/shard_map/while/body/eval_jaxpr/dot_general | solution.py:17
  247.6 1.4 fusion.52
  249.0 2.2 fusion.53
  253.4 4.3 %fusion.51 = (f32[512]{0:T(512)S(1)}, f32[512,4608]{1,0:T(8,128)S(1)}) fusion(bf16[4608,128]{1,0:T(8,128)(2,1)} %get-tuple-element.293, bf16[512,768]{1,0:T(8,128)(2,1)} %get-tuple-element.292, s32[]{:T(128)S(6)} %select_n.175, s32[512]{0:T(512)S(1)} %get-tuple-element.290, s32[4608]{0:T(1024)S(1)} %get-tuple-element.289, ...), kind=kOutput, calls=%fused_computation.77.clone.1 | convolution fusion | flops 622853632 | bytes 10792964 | tf_op jit(solution)/shard_map/while/body/eval_jaxpr/dot_general | solution.py:17
  257.7 1.4 fusion.52
  259.1 2.2 fusion.53
  263.4 4.3 %fusion.51 = (f32[512]{0:T(512)S(1)}, f32[512,4608]{1,0:T(8,128)S(1)}) fusion(bf16[4608,128]{1,0:T(8,128)(2,1)} %get-tuple-element.293, bf16[512,768]{1,0:T(8,128)(2,1)} %get-tuple-element.292, s32[]{:T(128)S(6)} %select_n.175, s32[512]{0:T(512)S(1)} %get-tuple-element.290, s32[4608]{0:T(1024)S(1)} %get-tuple-element.289, ...), kind=kOutput, calls=%fused_computation.77.clone.1 | convolution fusion | flops 622853632 | bytes 10792964 | tf_op jit(solution)/shard_map/while/body/eval_jaxpr/dot_general | solution.py:17
  267.7 1.4 fusion.52
  269.2 2.2 fusion.53
  273.5 4.3 %fusion.51 = (f32[512]{0:T(512)S(1)}, f32[512,4608]{1,0:T(8,128)S(1)}) fusion(bf16[4608,128]{1,0:T(8,128)(2,1)} %get-tuple-element.293, bf16[512,768]{1,0:T(8,128)(2,1)} %get-tuple-element.292, s32[]{:T(128)S(6)} %select_n.175, s32[512]{0:T(512)S(1)} %get-tuple-element.290, s32[4608]{0:T(1024)S(1)} %get-tuple-element.289, ...), kind=kOutput, calls=%fused_computation.77.clone.1 | convolution fusion | flops 622853632 | bytes 10792964 | tf_op jit(solution)/shard_map/while/body/eval_jaxpr/dot_general | solution.py:17
  277.8 1.4 fusion.52
  279.2 2.2 fusion.53
  283.5 4.3 %fusion.51 = (f32[512]{0:T(512)S(1)}, f32[512,4608]{1,0:T(8,128)S(1)}) fusion(bf16[4608,128]{1,0:T(8,128)(2,1)} %get-tuple-element.293, bf16[512,768]{1,0:T(8,128)(2,1)} %get-tuple-element.292, s32[]{:T(128)S(6)} %select_n.175, s32[512]{0:T(512)S(1)} %get-tuple-element.290, s32[4608]{0:T(1024)S(1)} %get-tuple-element.289, ...), kind=kOutput, calls=%fused_computation.77.clone.1 | convolution fusion | flops 622853632 | bytes 10792964 | tf_op jit(solution)/shard_map/while/body/eval_jaxpr/dot_general | solution.py:17
  287.9 1.4 fusion.52
  289.3 2.2 fusion.53
  293.6 4.3 %fusion.51 = (f32[512]{0:T(512)S(1)}, f32[512,4608]{1,0:T(8,128)S(1)}) fusion(bf16[4608,128]{1,0:T(8,128)(2,1)} %get-tuple-element.293, bf16[512,768]{1,0:T(8,128)(2,1)} %get-tuple-element.292, s32[]{:T(128)S(6)} %select_n.175, s32[512]{0:T(512)S(1)} %get-tuple-element.290, s32[4608]{0:T(1024)S(1)} %get-tuple-element.289, ...), kind=kOutput, calls=%fused_computation.77.clone.1 | convolution fusion | flops 622853632 | bytes 10792964 | tf_op jit(solution)/shard_map/while/body/eval_jaxpr/dot_general | solution.py:17
  297.9 1.4 fusion.52
  299.3 2.2 fusion.53
  302.4 1.1 collective-permute-start.1
  303.4 19.9 %collective-permute-done.1 = bf16[512,768]{0,1:T(8,128)(2,1)S(1)} collective-permute-done((bf16[512,768]{0,1:T(8,128)(2,1)}, bf16[512,768]{0,1:T(8,128)(2,1)S(1)}, u32[]{:S(2)}, u32[]{:S(2)}) %collective-permute-start.1) | collective-permute-done | bytes 786464 | tf_op jit(solution)/shard_map/ppermute | solution.py:104
  323.3 1.9 maximum_select_fusion.3
  325.2 1.0 collective-permute-start.2
  326.5 2.9 collective-permute-done.2
  329.4 16.5 %bitcast_convert_fusion = bf16[1024,4,768]{0,2,1:T(8,128)(2,1)} fusion(bf16[2,4,768,768]{3,2,1,0:T(8,128)(2,1)} %bitcast.75, bf16[512,2,768]{0,2,1:T(8,128)(2,1)} %bitcast.21, bf16[512,2,768]{0,2,1:T(8,128)(2,1)S(1)} %maximum_select_fusion.2, pred[]{:T(512)S(6)} %eq.84), kind=kOutput, calls=%fused_computation.18 | convolution fusion | flops 9680977920 | bytes 18874368 | tf_op jit(solution)/shard_map/dot_general | solution.py:119
  345.9 65.2 %reduce-scatter.2.cloned.1.call-done = bf16[1024,768]{0,1:T(8,128)(2,1)} async-done(((bf16[1024,3072]{0,1:T(8,128)(2,1)}), bf16[1024,768]{0,1:T(8,128)(2,1)}) %reduce-scatter.2.cloned.1.call-update) | async-done | bytes 1572880 | tf_op jit(solution)/shard_map/reduce_scatter | solution.py:123
  411.1 1.7 copy.17
  412.8 5.4 %all_to_all.14 = bf16[2,512,768]{2,1,0:T(8,128)(2,1)S(1)} all-to-all(bf16[2,512,768]{2,1,0:T(8,128)(2,1)S(1)} %bitcast.70), channel_id=1, replica_groups=mesh['ylo'=2,'x'=4,'c'=2,'yhi'=2,'z'=4] {'c'}, dimensions={0} | all-to-all | bytes 3145728 | tf_op jit(solution)/shard_map/all_to_all | solution.py:124
  418.3 1.3 pad_maximum_fusion.1
  (83 shorter events, 10.1 us)
Async XLA Ops:
  6.5 3.9 copy-start
  6.5 233.8 %all-gather.2.cloned.1.call-start = ((), (), s32[]{:S(2)}) async-start(), calls=%async_computation.3 | async-start | bytes 10616832 | tf_op jit(solution)/shard_map/all_gather | solution.py:82
  6.5 2.1 collective-permute-start
  8.6 1.0 copy-start.3
  14.6 5.9 %copy-start.5 = (bf16[512,128]{1,0:T(8,128)(2,1)S(1)}, bf16[512,128]{1,0:T(8,128)(2,1)}, u32[]{:S(2)}) copy-start(bf16[512,128]{1,0:T(8,128)(2,1)} %param.10) | copy-start | bytes 393220
  14.6 5.9 %copy-start.6 = (bf16[512,128]{1,0:T(8,128)(2,1)S(1)}, bf16[512,128]{1,0:T(8,128)(2,1)}, u32[]{:S(2)}) copy-start(bf16[512,128]{1,0:T(8,128)(2,1)} %param.9) | copy-start | bytes 393220
  26.3 35.1 %copy-start.8 = (s32[64,2]{0,1:T(2,128)S(1)}, s32[64,2]{0,1:T(2,128)}, u32[]{:S(2)}) copy-start(s32[64,2]{0,1:T(2,128)} %param.12) | copy-start | bytes 1540
  26.3 36.9 %copy-start.7 = (s32[8192]{0:T(1024)S(1)}, s32[8192]{0:T(1024)}, u32[]{:S(2)}) copy-start(s32[8192]{0:T(1024)} %param.11) | copy-start | bytes 98308
  26.3 186.7 %all-to-all-start = ((bf16[16,896,256]{2,1,0:T(8,128)(2,1)}), bf16[16,896,256]{2,1,0:T(8,128)(2,1)}, u32[]{:S(2)}, u32[]{:S(2)}) async-start(bf16[16,896,256]{2,1,0:T(8,128)(2,1)} %pad_maximum_fusion), calls=%async_computation | async-start | bytes 14680064 | tf_op jit(solution)/shard_map/all_to_all | solution.py:64
  61.3 349.8 %reduce-scatter.2.cloned.1.call-start = ((), (), s32[]{:S(2)}) async-start(), calls=%async_computation.4 | async-start | bytes 7864320 | tf_op jit(solution)/shard_map/reduce_scatter | solution.py:123
  247.6 1.4 copy-start.4
  257.7 1.4 copy-start.4
  267.7 1.4 copy-start.4
  277.8 1.4 copy-start.4
  287.9 1.4 copy-start.4
  297.9 1.4 copy-start.4
  302.4 23.8 %copy-start.2 = (bf16[6,512,128]{1,2,0:T(8,128)(2,1)S(1)}, bf16[6,512,128]{1,2,0:T(8,128)(2,1)}, u32[]{:S(2)}) copy-start(bf16[6,512,128]{1,2,0:T(8,128)(2,1)} %get-tuple-element.133) | copy-start | bytes 2359300
  302.4 20.9 %collective-permute-start.1 = (bf16[512,768]{0,1:T(8,128)(2,1)}, bf16[512,768]{0,1:T(8,128)(2,1)S(1)}, u32[]{:S(2)}, u32[]{:S(2)}) collective-permute-start(bf16[512,768]{0,1:T(8,128)(2,1)} %bitcast.71), channel_id=1, source_target_pairs={{0,4},{4,0},{1,5},{5,1},{2,6},{6,2},{3,7},{7,3},{8,12},{12,8},{9,1... | collective-permute-start | bytes 2359304 | tf_op jit(solution)/shard_map/ppermute | solution.py:104
  325.2 4.2 collective-permute-start.2
  412.8 6.7 %copy-start.1 = (bf16[512,768]{1,0:T(8,128)(2,1)S(1)}, bf16[512,768]{1,0:T(8,128)(2,1)}, u32[]{:S(2)}) copy-start(bf16[512,768]{1,0:T(8,128)(2,1)} %param.8) | copy-start | bytes 2359300
Sparse Core Ops, SparseCore 0:
  9.8 223.2 all-gather.1
  346.0 65.0 reduce-scatter.1

commit v12 on v5

--- a/solution.py
+++ b/solution.py
@@ -38,6 +38,11 @@
     kv_local = jnp.concatenate([keys, values], axis=1)
     kv_all = lax.all_gather(kv_local, SEQ, axis=0, tiled=True)
     kv_blocks = kv_all.reshape(blocks_all, BLOCK, 2 * kv_cols)
+    w_swapped = lax.ppermute(out_weight, ("ylo", "yhi"), perm=[(0, 0), (1, 2), (2, 1), (3, 3)])
+    kv_blocks, w_swapped = lax.optimization_barrier((kv_blocks, w_swapped))
+    w_here = lax.all_gather(w_swapped, ("ylo", "x"), axis=0, tiled=True)
+    w_here = w_here.reshape(2, -1, out_weight.shape[0], out_weight.shape[1])
+
     target = packing[:, 0] * per_shard + packing[:, 1]
     source = jnp.zeros((blocks_all,), jnp.int32).at[target].set(
         jnp.arange(blocks_all, dtype=jnp.int32)
@@ -68,11 +73,6 @@
         "od,drc->orc", placing, incoming, preferred_element_type=jnp.float32
     ).astype(jnp.bfloat16)
     queries_here = packed.reshape(tok_rows, q_cols)
-
-    w_swapped = lax.ppermute(out_weight, ("ylo", "yhi"), perm=[(0, 0), (1, 2), (2, 1), (3, 3)])
-    context, w_swapped = lax.optimization_barrier((context, w_swapped))
-    w_here = lax.all_gather(w_swapped, ("ylo", "x"), axis=0, tiled=True)
-    w_here = w_here.reshape(2, -1, out_weight.shape[0], out_weight.shape[1])
 
     ctx_keys = context[:, :kv_cols]
     ctx_values = context[:, kv_cols:]

time: 315 us -> 309 us (0.981)
  waiting for transfers between devices: 164 us -> 177 us
  starting transfers between devices: 20.9 us -> 12.6 us
  local copies, waits for them, and re-layouts: 22.9 us -> 16.6 us
    ppermute x1, starting transfers between devices: 10.4 us -> 2.07 us  [shards(): lax.ppermute(out_weight, ('ylo', 'yhi'), perm=[(0, 0), (1, 2), (2, 1), (3...]
    all_to_all x1, waiting for transfers between devices: 39.5 us -> 47.9 us  [shards(): lax.all_to_all(outgoing, SEQ, split_axis=0, concat_axis=0, tiled=True)]
    ppermute x1, waiting for transfers between devices: 57.4 us -> 61.7 us  [shards(): h_far = lax.ppermute(attended, 'yhi', pair)]
    dynamic_update_slice x12, local copies, waits for them, and re-layouts: 4.73 us -> 0.78 us  [shards(): per_head = lax.map(one_head, jnp.arange(heads_here, dtype=jnp.int32))]
  transfers between devices with their start and end apart: 7 -> 7, of which waited for: 5 -> 5; matrix products, arithmetic and copies ran while one was open for 26% -> 22% of each run, Pallas kernels for 0% -> 0%
where the time goes in v12:
time: 309 us
  waiting for transfers between devices  177 us (57%)
  matrix products  62.4 us (20%)
  other arithmetic  17.2 us (6%)
  local copies, waits for them, and re-layouts  16.6 us (5%)
  between operations  13.2 us (4%)
  starting transfers between devices  12.6 us (4%)
  blocking collectives  5.24 us (2%)
  loops' own time  4.18 us (1%)
    ppermute x1, waiting for transfers between devices, shards(): h_far = lax.ppermute(attended, 'yhi', pair)  61.7 us
    reduce_scatter x1, waiting for transfers between devices, shards(): summed = lax.psum_scatter(part, 'z', scatter_dimension=1, tiled=True)  61.1 us
    all_to_all x1, waiting for transfers between devices, shards(): lax.all_to_all(outgoing, SEQ, split_axis=0, concat_axis=0, tiled=True)  47.9 us
    dot_general x6, matrix products, attend_head(): lax.dot_general(q_rows, k_rows, (((1,), (1,)), ((), ())), preferred_eleme...  26 us
    dot_general x1, matrix products, shards(): lax.dot_general(h_split, w_here, (((1, 2), (0, 2)), ((), ())), preferred_...  17.6 us
    dot_general x6, matrix products, attend_head(): jnp.dot(weights, v_rows, preferred_element_type=jnp.float32)  13.2 us
    reduce_sum x6, other arithmetic, attend_head(): weights = (expo / jnp.sum(expo, axis=1, keepdims=True)).astype(jnp.bfloat16)  8.47 us
    all_to_all x1, starting transfers between devices, shards(): lax.all_to_all(outgoing, SEQ, split_axis=0, concat_axis=0, tiled=True)  6.96 us
  transfers between devices with their start and end apart: 7, of which 5 were waited for; matrix products, arithmetic and copies ran while one was open for 22% of the time, Pallas kernels for 0%

profile of v12, /device:TPU:1, one launch (start us, length us, event | category | flops | bytes accessed | tf_op | source)
XLA Modules:
  0.0 308.6 jit_solution(6173947843239520260)
XLA Ops:
  6.5 1.8 pad_maximum_fusion.1
  8.3 0.8 constant_dynamic-slice_fusion
  9.1 1.5 convolution_convert_fusion
  10.6 2.7 copy.14
  13.3 7.0 %all-to-all-start = ((bf16[16,128,768]{2,1,0:T(8,128)(2,1)}), bf16[16,128,768]{2,1,0:T(8,128)(2,1)}, u32[]{:S(2)}, u32[]{:S(2)}) async-start(bf16[16,128,768]{2,1,0:T(8,128)(2,1)} %copy.14), calls=%async_computation | async-start | bytes 6291456 | tf_op jit(solution)/shard_map/all_to_all | solution.py:63
  20.4 2.1 collective-permute-start
  22.4 0.8 scatter_custom_fusion
  23.3 0.8 gather_fusion
  24.5 47.9 %all-to-all-done = bf16[16,128,768]{2,1,0:T(8,128)(2,1)} async-done(((bf16[16,128,768]{2,1,0:T(8,128)(2,1)}), bf16[16,128,768]{2,1,0:T(8,128)(2,1)}, u32[]{:S(2)}, u32[]{:S(2)}) %all-to-all-start) | async-done | bytes 3145760 | tf_op jit(solution)/shard_map/all_to_all | solution.py:63
  72.4 3.9 %fusion.19 = bf16[4,128,768]{2,0,1:T(4,128)(2,1)S(1)} fusion(bf16[4,16,1]{1,0,2:T(4,128)(2,1)S(1)} %fusion.22, bf16[16,128,768]{2,1,0:T(8,128)(2,1)} %all-to-all-done), kind=kOutput, calls=%fused_computation.34 | convolution fusion | flops 12976128 | bytes 3932288 | tf_op jit(solution)/shard_map/od,drc->orc/dot_general | solution.py:72
  76.3 1.0 copy.16
  77.3 4.4 %all-gather.3.cloned.1.call-done = bf16[8192,256]{1,0:T(8,128)(2,1)} async-done(((bf16[512,256]{1,0:T(8,128)(2,1)}), bf16[8192,256]{1,0:T(8,128)(2,1)}) %all-gather.3.cloned.1.call-update) | async-done | bytes 4194320 | tf_op jit(solution)/shard_map/all_gather | solution.py:39
  81.7 2.9 gather_fusion.1
  84.6 2.4 bitcast_select_fusion
  87.0 1.2 fusion.39
  88.3 56.4 %while.13 = (s32[]{:T(128)}, bf16[6,512,128]{1,2,0:T(8,128)(2,1)S(1)}, s32[4608]{0:T(1024)S(1)}, s32[512]{0:T(512)S(1)}, s32[6]{0:T(128)S(1)}, /*index=5*/bf16[5...) while((s32[]{:T(128)}, ...), condition=%wide.region_4.5_spmd.clone, body=%wide.region_1.0_spmd.clone.sunk | while | flops 1238700544 | bytes 31533264 | solution.py:91
  88.3 0.6 dynamic_slice.36
  89.6 4.3 %fusion.51 = (f32[512]{0:T(512)S(1)}, f32[512,4608]{1,0:T(8,128)S(1)}) fusion(bf16[4608,128]{1,0:T(8,128)(2,1)} %get-tuple-element.293, bf16[512,768]{1,0:T(8,128)(2,1)} %get-tuple-element.292, s32[]{:T(128)S(6)} %select_n.175, s32[512]{0:T(512)S(1)} %get-tuple-element.290, s32[4608]{0:T(1024)S(1)} %get-tuple-element.289, ...), kind=kOutput, calls=%fused_computation.76.clone.1 | convolution fusion | flops 622853632 | bytes 10792964 | tf_op jit(solution)/shard_map/while/body/eval_jaxpr/dot_general | solution.py:17
  93.9 1.4 fusion.52
  95.3 2.2 fusion.53
  97.7 0.6 dynamic_slice.36
  99.0 4.4 %fusion.51 = (f32[512]{0:T(512)S(1)}, f32[512,4608]{1,0:T(8,128)S(1)}) fusion(bf16[4608,128]{1,0:T(8,128)(2,1)} %get-tuple-element.293, bf16[512,768]{1,0:T(8,128)(2,1)} %get-tuple-element.292, s32[]{:T(128)S(6)} %select_n.175, s32[512]{0:T(512)S(1)} %get-tuple-element.290, s32[4608]{0:T(1024)S(1)} %get-tuple-element.289, ...), kind=kOutput, calls=%fused_computation.76.clone.1 | convolution fusion | flops 622853632 | bytes 10792964 | tf_op jit(solution)/shard_map/while/body/eval_jaxpr/dot_general | solution.py:17
  103.4 1.4 fusion.52
  104.8 2.2 fusion.53
  107.2 0.6 dynamic_slice.36
  108.5 4.3 %fusion.51 = (f32[512]{0:T(512)S(1)}, f32[512,4608]{1,0:T(8,128)S(1)}) fusion(bf16[4608,128]{1,0:T(8,128)(2,1)} %get-tuple-element.293, bf16[512,768]{1,0:T(8,128)(2,1)} %get-tuple-element.292, s32[]{:T(128)S(6)} %select_n.175, s32[512]{0:T(512)S(1)} %get-tuple-element.290, s32[4608]{0:T(1024)S(1)} %get-tuple-element.289, ...), kind=kOutput, calls=%fused_computation.76.clone.1 | convolution fusion | flops 622853632 | bytes 10792964 | tf_op jit(solution)/shard_map/while/body/eval_jaxpr/dot_general | solution.py:17
  112.8 1.4 fusion.52
  114.2 2.2 fusion.53
  116.6 0.6 dynamic_slice.36
  117.9 4.3 %fusion.51 = (f32[512]{0:T(512)S(1)}, f32[512,4608]{1,0:T(8,128)S(1)}) fusion(bf16[4608,128]{1,0:T(8,128)(2,1)} %get-tuple-element.293, bf16[512,768]{1,0:T(8,128)(2,1)} %get-tuple-element.292, s32[]{:T(128)S(6)} %select_n.175, s32[512]{0:T(512)S(1)} %get-tuple-element.290, s32[4608]{0:T(1024)S(1)} %get-tuple-element.289, ...), kind=kOutput, calls=%fused_computation.76.clone.1 | convolution fusion | flops 622853632 | bytes 10792964 | tf_op jit(solution)/shard_map/while/body/eval_jaxpr/dot_general | solution.py:17
  122.2 1.4 fusion.52
  123.6 2.2 fusion.53
  127.2 4.3 %fusion.51 = (f32[512]{0:T(512)S(1)}, f32[512,4608]{1,0:T(8,128)S(1)}) fusion(bf16[4608,128]{1,0:T(8,128)(2,1)} %get-tuple-element.293, bf16[512,768]{1,0:T(8,128)(2,1)} %get-tuple-element.292, s32[]{:T(128)S(6)} %select_n.175, s32[512]{0:T(512)S(1)} %get-tuple-element.290, s32[4608]{0:T(1024)S(1)} %get-tuple-element.289, ...), kind=kOutput, calls=%fused_computation.76.clone.1 | convolution fusion | flops 622853632 | bytes 10792964 | tf_op jit(solution)/shard_map/while/body/eval_jaxpr/dot_general | solution.py:17
  131.6 1.4 fusion.52
  133.0 2.2 fusion.53
  136.6 4.3 %fusion.51 = (f32[512]{0:T(512)S(1)}, f32[512,4608]{1,0:T(8,128)S(1)}) fusion(bf16[4608,128]{1,0:T(8,128)(2,1)} %get-tuple-element.293, bf16[512,768]{1,0:T(8,128)(2,1)} %get-tuple-element.292, s32[]{:T(128)S(6)} %select_n.175, s32[512]{0:T(512)S(1)} %get-tuple-element.290, s32[4608]{0:T(1024)S(1)} %get-tuple-element.289, ...), kind=kOutput, calls=%fused_computation.76.clone.1 | convolution fusion | flops 622853632 | bytes 10792964 | tf_op jit(solution)/shard_map/while/body/eval_jaxpr/dot_general | solution.py:17
  140.9 1.4 fusion.52
  142.4 2.2 fusion.53
  144.7 3.0 collective-permute-start.1
  147.7 61.7 %collective-permute-done.1 = bf16[512,768]{0,1:T(8,128)(2,1)S(1)} collective-permute-done((bf16[512,768]{0,1:T(8,128)(2,1)S(1)}, bf16[512,768]{0,1:T(8,128)(2,1)S(1)}, u32[]{:S(2)}, u32[]{:S(2)}) %collective-permute-start.1) | collective-permute-done | bytes 786464 | tf_op jit(solution)/shard_map/ppermute | solution.py:95
  209.4 1.8 maximum_select_fusion.3
  211.7 1.4 maximum_select_fusion.2
  213.1 2.0 collective-permute-done.2
  215.0 17.6 %bitcast_convert_fusion = bf16[1024,4,768]{0,2,1:T(8,128)(2,1)} fusion(bf16[2,4,768,768]{3,2,1,0:T(8,128)(2,1)} %bitcast.76, bf16[512,2,768]{0,2,1:T(8,128)(2,1)} %bitcast.20, bf16[512,2,768]{0,2,1:T(8,128)(2,1)} %maximum_select_fusion.2, pred[]{:T(512)S(6)} %eq.84), kind=kOutput, calls=%fused_computation.18 | convolution fusion | flops 9680977920 | bytes 18874368 | tf_op jit(solution)/shard_map/dot_general | solution.py:110
  232.6 61.1 %reduce-scatter.2.cloned.1.call-done = bf16[1024,768]{0,1:T(8,128)(2,1)} async-done(((bf16[1024,3072]{0,1:T(8,128)(2,1)}), bf16[1024,768]{0,1:T(8,128)(2,1)}) %reduce-scatter.2.cloned.1.call-update) | async-done | bytes 1572880 | tf_op jit(solution)/shard_map/reduce_scatter | solution.py:114
  293.8 1.7 copy.20
  295.5 5.2 %all_to_all.14 = bf16[2,512,768]{2,1,0:T(8,128)(2,1)S(1)} all-to-all(bf16[2,512,768]{2,1,0:T(8,128)(2,1)S(1)} %bitcast.69), channel_id=1, replica_groups=mesh['ylo'=2,'x'=4,'c'=2,'yhi'=2,'z'=4] {'c'}, dimensions={0} | all-to-all | bytes 3145728 | tf_op jit(solution)/shard_map/all_to_all | solution.py:115
  300.8 1.3 pad_maximum_fusion
  (62 shorter events, 3.3 us)
Async XLA Ops:
  6.5 2.6 copy-start
  6.5 75.2 %all-gather.3.cloned.1.call-start = ((), (), s32[]{:S(2)}) async-start(), calls=%async_computation.3 | async-start | bytes 4456448 | tf_op jit(solution)/shard_map/all_gather | solution.py:39
  13.3 9.1 %copy-start.4 = (s32[64,2]{0,1:T(2,128)S(1)}, s32[64,2]{0,1:T(2,128)}, u32[]{:S(2)}) copy-start(s32[64,2]{0,1:T(2,128)} %param.12) | copy-start | bytes 1540
  13.3 10.7 %copy-start.3 = (s32[8192]{0:T(1024)S(1)}, s32[8192]{0:T(1024)}, u32[]{:S(2)}) copy-start(s32[8192]{0:T(1024)} %param.11) | copy-start | bytes 98308
  13.3 59.1 %all-to-all-start = ((bf16[16,128,768]{2,1,0:T(8,128)(2,1)}), bf16[16,128,768]{2,1,0:T(8,128)(2,1)}, u32[]{:S(2)}, u32[]{:S(2)}) async-start(bf16[16,128,768]{2,1,0:T(8,128)(2,1)} %copy.14), calls=%async_computation | async-start | bytes 6291456 | tf_op jit(solution)/shard_map/all_to_all | solution.py:63
  20.3 194.7 %all-gather.5.cloned.1.call-start = ((), (), s32[]{:S(2)}) async-start(), calls=%async_computation.4 | async-start | bytes 10616832 | tf_op jit(solution)/shard_map/all_gather | solution.py:43
  20.4 56.9 %collective-permute-start = (bf16[768,768]{1,0:T(8,128)(2,1)}, bf16[768,768]{1,0:T(8,128)(2,1)S(1)}, u32[]{:S(2)}, u32[]{:S(2)}) collective-permute-start(bf16[768,768]{1,0:T(8,128)(2,1)} %param.13), channel_id=1, source_target_pairs={{0,0},{4,64},{64,4},{68,68},{1,1},{5,65},{65,5},{69,69},{2,2},{6,6... | collective-permute-start | bytes 3538952 | tf_op jit(solution)/shard_map/ppermute | solution.py:41
  77.3 4.4 %copy-start.2 = (bf16[768,768]{1,0:T(8,128)(2,1)}, bf16[768,768]{1,0:T(8,128)(2,1)S(1)}, u32[]{:S(2)}) copy-start(bf16[768,768]{1,0:T(8,128)(2,1)S(1)} %collective-permute-done) | copy-start | bytes 3538948
  87.0 1.3 copy-start.1
  88.2 205.5 %reduce-scatter.2.cloned.1.call-start = ((), (), s32[]{:S(2)}) async-start(), calls=%async_computation.5 | async-start | bytes 7864320 | tf_op jit(solution)/shard_map/reduce_scatter | solution.py:114
  144.7 64.7 %collective-permute-start.1 = (bf16[512,768]{0,1:T(8,128)(2,1)S(1)}, bf16[512,768]{0,1:T(8,128)(2,1)S(1)}, u32[]{:S(2)}, u32[]{:S(2)}) collective-permute-start(bf16[512,768]{0,1:T(8,128)(2,1)S(1)} %bitcast.70), channel_id=1, source_target_pairs={{0,4},{4,0},{1,5},{5,1},{2,6},{6,2},{3,7},{7,3},{8,12},{12,8},{9,1... | collective-permute-start | bytes 2359304 | tf_op jit(solution)/shard_map/ppermute | solution.py:95
  211.2 3.8 %collective-permute-start.2 = (bf16[512,1536]{0,1:T(8,128)(2,1)}, bf16[512,1536]{0,1:T(8,128)(2,1)}, u32[]{:S(2)}, u32[]{:S(2)}) collective-permute-start(bf16[512,1536]{0,1:T(8,128)(2,1)} %maximum_select_fusion.3), channel_id=1, source_target_pairs={{0,8},{8,0},{1,9},{9,1},{2,10},{10,2},{3,11},{11,3},{4,12},{12,4},... | collective-permute-start | bytes 4718600 | tf_op jit(solution)/shard_map/ppermute | solution.py:102
Sparse Core Ops, SparseCore 0:
  9.1 72.6 all-gather.2
  88.3 103.1 all-gather.4
  232.7 60.9 reduce-scatter.1

commit v13 on v12

--- a/solution.py
+++ b/solution.py
@@ -88,11 +88,16 @@
         q_head = lax.dynamic_slice_in_dim(queries_here, head_index * HEAD_DIM, HEAD_DIM, 1)
         return attend_head(q_head, ctx_keys, ctx_values, q_pos, k_pos, q_seg, k_seg)
 
-    per_head = lax.map(one_head, jnp.arange(heads_here, dtype=jnp.int32))
-    attended = jnp.transpose(per_head, (1, 0, 2)).reshape(tok_rows, q_cols)
-
+    half = heads_here // 2
     pair = [(0, 1), (1, 0)]
-    h_far = lax.ppermute(attended, "yhi", pair)
+    mine, far = [], []
+    for first in (0, half):
+        per_head = lax.map(one_head, jnp.arange(first, first + half, dtype=jnp.int32))
+        piece = jnp.transpose(per_head, (1, 0, 2)).reshape(tok_rows, half * HEAD_DIM)
+        mine.append(piece)
+        far.append(lax.ppermute(piece, "yhi", pair))
+    attended = jnp.concatenate(mine, axis=1)
+    h_far = jnp.concatenate(far, axis=1)
     low_hi = lax.axis_index("yhi") == 0
     h_groups = jnp.where(
         low_hi,

time: 309 us -> 305 us (0.987)
  starting transfers between devices: 12.6 us -> 21.3 us
  matrix products: 62.4 us -> 54.2 us
  waiting for transfers between devices: 177 us -> 173 us
    all_to_all x1, waiting for transfers between devices: 47.9 us -> 38.7 us  [shards(): lax.all_to_all(outgoing, SEQ, split_axis=0, concat_axis=0, tiled=True)]
    ppermute x1, starting transfers between devices: 2.07 us -> 10.4 us  [shards(): lax.ppermute(out_weight, ('ylo', 'yhi'), perm=[(0, 0), (1, 2), (2, 1), (3...]
    dot_general x1, matrix products: 17.6 us -> 14.2 us  [shards(): lax.dot_general(h_split, w_here, (((1, 2), (0, 2)), ((), ())), preferred_...]
    ppermute x1 -> x2, waiting for transfers between devices: 61.7 us -> 63.6 us  [shards(): far.append(lax.ppermute(piece, 'yhi', pair))]
  transfers between devices with their start and end apart: 7 -> 8, of which waited for: 5 -> 6; matrix products, arithmetic and copies ran while one was open for 22% -> 20% of each run, Pallas kernels for 0% -> 0%
where the time goes in v13:
time: 305 us; the launch traced here: 304 us
  waiting for transfers between devices  173 us (57%)
  matrix products  54.2 us (18%)
  starting transfers between devices  21.3 us (7%)
  local copies, waits for them, and re-layouts  16.6 us (5%)
  other arithmetic  15.5 us (5%)
  between operations  13.3 us (4%)
  blocking collectives  5.38 us (2%)
  loops' own time  4.09 us (1%)
    ppermute x2, waiting for transfers between devices, shards(): far.append(lax.ppermute(piece, 'yhi', pair))  63.6 us
    reduce_scatter x1, waiting for transfers between devices, shards(): summed = lax.psum_scatter(part, 'z', scatter_dimension=1, tiled=True)  61.1 us
    all_to_all x1, waiting for transfers between devices, shards(): lax.all_to_all(outgoing, SEQ, split_axis=0, concat_axis=0, tiled=True)  38.7 us
    dot_general x6, matrix products, attend_head(): lax.dot_general(q_rows, k_rows, (((1,), (1,)), ((), ())), preferred_eleme...  23.1 us
    dot_general x1, matrix products, shards(): lax.dot_general(h_split, w_here, (((1, 2), (0, 2)), ((), ())), preferred_...  14.2 us
    dot_general x6, matrix products, attend_head(): jnp.dot(weights, v_rows, preferred_element_type=jnp.float32)  13.3 us
    ppermute x1, starting transfers between devices, shards(): lax.ppermute(out_weight, ('ylo', 'yhi'), perm=[(0, 0), (1, 2), (2, 1), (3...  10.4 us
    reduce_sum x6, other arithmetic, attend_head(): weights = (expo / jnp.sum(expo, axis=1, keepdims=True)).astype(jnp.bfloat16)  8.47 us
  transfers between devices with their start and end apart: 8, of which 6 were waited for; matrix products, arithmetic and copies ran while one was open for 20% of the time, Pallas kernels for 0%

profile of v13, /device:TPU:1, one launch (start us, length us, event | category | flops | bytes accessed | tf_op | source)
XLA Modules:
  0.0 303.6 jit_solution(299496679709431348)
XLA Ops:
  6.5 1.8 pad_maximum_fusion.1
  8.3 0.8 constant_dynamic-slice_fusion
  9.1 1.5 convolution_convert_fusion
  10.6 2.7 copy.15
  13.3 7.0 %all-to-all-start = ((bf16[16,128,768]{2,1,0:T(8,128)(2,1)}), bf16[16,128,768]{2,1,0:T(8,128)(2,1)S(1)}, u32[]{:S(2)}, u32[]{:S(2)}) async-start(bf16[16,128,768]{2,1,0:T(8,128)(2,1)} %copy.15), calls=%async_computation | async-start | bytes 6291456 | tf_op jit(solution)/shard_map/all_to_all | solution.py:63
  20.3 10.4 %collective-permute-start = (bf16[768,768]{1,0:T(8,128)(2,1)}, bf16[768,768]{1,0:T(8,128)(2,1)}, u32[]{:S(2)}, u32[]{:S(2)}) collective-permute-start(bf16[768,768]{1,0:T(8,128)(2,1)} %param.15), channel_id=1, source_target_pairs={{0,0},{4,64},{64,4},{68,68},{1,1},{5,65},{65,5},{69,69},{2,2},{6,6... | collective-permute-start | bytes 3538952 | tf_op jit(solution)/shard_map/ppermute | solution.py:41
  30.7 0.8 scatter_custom_fusion
  31.5 0.8 gather_fusion
  32.4 0.7 pad_dynamic-slice_fusion
  33.4 38.7 %all-to-all-done = bf16[16,128,768]{2,1,0:T(8,128)(2,1)S(1)} async-done(((bf16[16,128,768]{2,1,0:T(8,128)(2,1)}), bf16[16,128,768]{2,1,0:T(8,128)(2,1)S(1)}, u32[]{:S(2)}, u32[]{:S(2)}) %all-to-all-start) | async-done | bytes 3145760 | tf_op jit(solution)/shard_map/all_to_all | solution.py:63
  72.1 1.9 fusion.29
  74.1 1.0 copy.17
  75.1 6.7 %all-gather.3.cloned.1.call-done = bf16[8192,256]{1,0:T(8,128)(2,1)} async-done(((bf16[512,256]{1,0:T(8,128)(2,1)}), bf16[8192,256]{1,0:T(8,128)(2,1)}) %all-gather.3.cloned.1.call-update) | async-done | bytes 4194320 | tf_op jit(solution)/shard_map/all_gather | solution.py:39
  81.8 2.9 gather_fusion.1
  84.7 2.4 bitcast_select_fusion
  87.8 26.7 %while.26 = (s32[]{:T(128)}, bf16[3,512,128]{1,2,0:T(8,128)(2,1)S(1)}, s32[4608]{0:T(1024)S(1)}, s32[512]{0:T(512)S(1)}, s32[3]{0:T(128)S(1)}, /*index=5*/bf16[5...) while((s32[]{:T(128)}, ...), condition=%wide.region_4.5_spmd.clone, body=%wide.region_1.0_spmd.clone.sunk | while | flops 1238700544 | bytes 31533264 | solution.py:95
  89.1 3.8 %fusion.69 = (f32[512]{0:T(512)S(1)}, f32[512,4608]{1,0:T(8,128)S(1)}) fusion(bf16[4608,128]{1,0:T(8,128)(2,1)S(1)} %get-tuple-element.579, bf16[512,768]{1,0:T(8,128)(2,1)} %get-tuple-element.578, s32[]{:T(128)S(6)} %select_n.187, s32[512]{0:T(512)S(1)} %get-tuple-element.576, s32[4608]{0:T(1024)S(1)} %get-tuple-element.575, ...), kind=kOutput, calls=%fused_computation.91.clone.1 | convolution fusion | flops 622853632 | bytes 10792964 | tf_op jit(solution)/shard_map/while/body/eval_jaxpr/dot_general | solution.py:17
  92.9 1.4 fusion.70
  94.3 2.2 fusion.71
  98.0 3.9 %fusion.69 = (f32[512]{0:T(512)S(1)}, f32[512,4608]{1,0:T(8,128)S(1)}) fusion(bf16[4608,128]{1,0:T(8,128)(2,1)S(1)} %get-tuple-element.579, bf16[512,768]{1,0:T(8,128)(2,1)} %get-tuple-element.578, s32[]{:T(128)S(6)} %select_n.187, s32[512]{0:T(512)S(1)} %get-tuple-element.576, s32[4608]{0:T(1024)S(1)} %get-tuple-element.575, ...), kind=kOutput, calls=%fused_computation.91.clone.1 | convolution fusion | flops 622853632 | bytes 10792964 | tf_op jit(solution)/shard_map/while/body/eval_jaxpr/dot_general | solution.py:17
  101.8 1.4 fusion.70
  103.3 2.2 fusion.71
  106.9 3.8 %fusion.69 = (f32[512]{0:T(512)S(1)}, f32[512,4608]{1,0:T(8,128)S(1)}) fusion(bf16[4608,128]{1,0:T(8,128)(2,1)S(1)} %get-tuple-element.579, bf16[512,768]{1,0:T(8,128)(2,1)} %get-tuple-element.578, s32[]{:T(128)S(6)} %select_n.187, s32[512]{0:T(512)S(1)} %get-tuple-element.576, s32[4608]{0:T(1024)S(1)} %get-tuple-element.575, ...), kind=kOutput, calls=%fused_computation.91.clone.1 | convolution fusion | flops 622853632 | bytes 10792964 | tf_op jit(solution)/shard_map/while/body/eval_jaxpr/dot_general | solution.py:17
  110.8 1.4 fusion.70
  112.2 2.2 fusion.71
  114.5 2.9 collective-permute-start.1
  117.5 26.7 %while.27 = (s32[]{:T(128)}, bf16[3,512,128]{1,2,0:T(8,128)(2,1)S(1)}, s32[4608]{0:T(1024)S(1)}, s32[512]{0:T(512)S(1)}, s32[3]{0:T(128)S(1)}, /*index=5*/bf16[5...) while((s32[]{:T(128)}, ...), condition=%wide.region_8.9_spmd.clone, body=%wide.region_5.8_spmd.clone.sunk | while | flops 1238700544 | bytes 31533264 | solution.py:95
  117.5 0.6 dynamic_slice.58
  118.7 3.8 %fusion.74 = (f32[512]{0:T(512)S(1)}, f32[512,4608]{1,0:T(8,128)S(1)}) fusion(bf16[4608,128]{1,0:T(8,128)(2,1)S(1)} %get-tuple-element.537, bf16[512,768]{1,0:T(8,128)(2,1)} %get-tuple-element.536, s32[]{:T(128)S(6)} %select_n.188, s32[512]{0:T(512)S(1)} %get-tuple-element.534, s32[4608]{0:T(1024)S(1)} %get-tuple-element.533, ...), kind=kOutput, calls=%fused_computation.92.clone.1 | convolution fusion | flops 622853632 | bytes 10792964 | tf_op jit(solution)/shard_map/while/body/eval_jaxpr/dot_general | solution.py:17
  122.6 1.4 fusion.75
  124.0 2.2 fusion.76
  126.4 0.6 dynamic_slice.58
  127.6 3.8 %fusion.74 = (f32[512]{0:T(512)S(1)}, f32[512,4608]{1,0:T(8,128)S(1)}) fusion(bf16[4608,128]{1,0:T(8,128)(2,1)S(1)} %get-tuple-element.537, bf16[512,768]{1,0:T(8,128)(2,1)} %get-tuple-element.536, s32[]{:T(128)S(6)} %select_n.188, s32[512]{0:T(512)S(1)} %get-tuple-element.534, s32[4608]{0:T(1024)S(1)} %get-tuple-element.533, ...), kind=kOutput, calls=%fused_computation.92.clone.1 | convolution fusion | flops 622853632 | bytes 10792964 | tf_op jit(solution)/shard_map/while/body/eval_jaxpr/dot_general | solution.py:17
  131.5 1.4 fusion.75
  132.9 2.2 fusion.76
  135.3 0.6 dynamic_slice.58
  136.5 3.8 %fusion.74 = (f32[512]{0:T(512)S(1)}, f32[512,4608]{1,0:T(8,128)S(1)}) fusion(bf16[4608,128]{1,0:T(8,128)(2,1)S(1)} %get-tuple-element.537, bf16[512,768]{1,0:T(8,128)(2,1)} %get-tuple-element.536, s32[]{:T(128)S(6)} %select_n.188, s32[512]{0:T(512)S(1)} %get-tuple-element.534, s32[4608]{0:T(1024)S(1)} %get-tuple-element.533, ...), kind=kOutput, calls=%fused_computation.92.clone.1 | convolution fusion | flops 622853632 | bytes 10792964 | tf_op jit(solution)/shard_map/while/body/eval_jaxpr/dot_general | solution.py:17
  140.4 1.4 fusion.75
  141.8 2.2 fusion.76
  144.6 55.3 %collective-permute-done.1 = bf16[512,384]{0,1:T(8,128)(2,1)} collective-permute-done((bf16[512,384]{0,1:T(8,128)(2,1)S(1)}, bf16[512,384]{0,1:T(8,128)(2,1)}, u32[]{:S(2)}, u32[]{:S(2)}) %collective-permute-start.1) | collective-permute-done | bytes 393248 | tf_op jit(solution)/shard_map/ppermute | solution.py:98
  199.9 8.3 %collective-permute-done.2 = bf16[512,384]{0,1:T(8,128)(2,1)S(1)} collective-permute-done((bf16[512,384]{0,1:T(8,128)(2,1)S(1)}, bf16[512,384]{0,1:T(8,128)(2,1)S(1)}, u32[]{:S(2)}, u32[]{:S(2)}) %collective-permute-start.2) | collective-permute-done | bytes 393248 | tf_op jit(solution)/shard_map/ppermute | solution.py:98
  208.2 1.5 maximum_select_fusion.2
  210.2 3.0 %collective-permute-done.3 = bf16[512,1536]{0,1:T(8,128)(2,1)S(1)} collective-permute-done((bf16[512,1536]{0,1:T(8,128)(2,1)S(1)}, bf16[512,1536]{0,1:T(8,128)(2,1)S(1)}, u32[]{:S(2)}, u32[]{:S(2)}) %collective-permute-start.3) | collective-permute-done | bytes 1572896 | tf_op jit(solution)/shard_map/ppermute | solution.py:107
  213.3 14.2 %bitcast_convert_fusion = bf16[1024,4,768]{0,2,1:T(8,128)(2,1)} fusion(bf16[2,4,768,768]{3,2,1,0:T(8,128)(2,1)} %bitcast.91, bf16[512,2,768]{0,2,1:T(8,128)(2,1)S(1)} %bitcast.92, bf16[512,2,768]{0,2,1:T(8,128)(2,1)S(1)} %bitcast.84, pred[]{:T(512)S(6)} %eq.106), kind=kOutput, calls=%fused_computation.33 | convolution fusion | flops 9680977920 | bytes 18874368 | tf_op jit(solution)/shard_map/dot_general | solution.py:115
  227.5 61.1 %reduce-scatter.2.cloned.1.call-done = bf16[1024,768]{0,1:T(8,128)(2,1)} async-done(((bf16[1024,3072]{0,1:T(8,128)(2,1)}), bf16[1024,768]{0,1:T(8,128)(2,1)}) %reduce-scatter.2.cloned.1.call-update) | async-done | bytes 1572880 | tf_op jit(solution)/shard_map/reduce_scatter | solution.py:119
  288.6 1.7 copy.22
  290.3 5.4 %all_to_all.14 = bf16[2,512,768]{2,1,0:T(8,128)(2,1)S(1)} all-to-all(bf16[2,512,768]{2,1,0:T(8,128)(2,1)S(1)} %bitcast.83), channel_id=1, replica_groups=mesh['ylo'=2,'x'=4,'c'=2,'yhi'=2,'z'=4] {'c'}, dimensions={0} | all-to-all | bytes 3145728 | tf_op jit(solution)/shard_map/all_to_all | solution.py:120
  295.8 1.3 pad_maximum_fusion
  (66 shorter events, 5.0 us)
Async XLA Ops:
  6.5 2.6 copy-start
  6.5 75.3 %all-gather.3.cloned.1.call-start = ((), (), s32[]{:S(2)}) async-start(), calls=%async_computation.3 | async-start | bytes 4456448 | tf_op jit(solution)/shard_map/all_gather | solution.py:39
  13.3 17.4 %copy-start.4 = (s32[64,2]{0,1:T(2,128)S(1)}, s32[64,2]{0,1:T(2,128)}, u32[]{:S(2)}) copy-start(s32[64,2]{0,1:T(2,128)} %param.14) | copy-start | bytes 1540
  13.3 19.0 %copy-start.2 = (s32[8192]{0:T(1024)S(1)}, s32[8192]{0:T(1024)}, u32[]{:S(2)}) copy-start(s32[8192]{0:T(1024)} %param.13) | copy-start | bytes 98308
  13.3 58.9 %all-to-all-start = ((bf16[16,128,768]{2,1,0:T(8,128)(2,1)}), bf16[16,128,768]{2,1,0:T(8,128)(2,1)S(1)}, u32[]{:S(2)}, u32[]{:S(2)}) async-start(bf16[16,128,768]{2,1,0:T(8,128)(2,1)} %copy.15), calls=%async_computation | async-start | bytes 6291456 | tf_op jit(solution)/shard_map/all_to_all | solution.py:63
  20.3 193.0 %all-gather.5.cloned.1.call-start = ((), (), s32[]{:S(2)}) async-start(), calls=%async_computation.4 | async-start | bytes 10616832 | tf_op jit(solution)/shard_map/all_gather | solution.py:43
  20.3 54.8 %collective-permute-start = (bf16[768,768]{1,0:T(8,128)(2,1)}, bf16[768,768]{1,0:T(8,128)(2,1)}, u32[]{:S(2)}, u32[]{:S(2)}) collective-permute-start(bf16[768,768]{1,0:T(8,128)(2,1)} %param.15), channel_id=1, source_target_pairs={{0,0},{4,64},{64,4},{68,68},{1,1},{5,65},{65,5},{69,69},{2,2},{6,6... | collective-permute-start | bytes 3538952 | tf_op jit(solution)/shard_map/ppermute | solution.py:41
  87.1 0.7 copy-start.3
  87.3 201.3 %reduce-scatter.2.cloned.1.call-start = ((), (), s32[]{:S(2)}) async-start(), calls=%async_computation.5 | async-start | bytes 7864320 | tf_op jit(solution)/shard_map/reduce_scatter | solution.py:119
  114.5 85.3 %collective-permute-start.1 = (bf16[512,384]{0,1:T(8,128)(2,1)S(1)}, bf16[512,384]{0,1:T(8,128)(2,1)}, u32[]{:S(2)}, u32[]{:S(2)}) collective-permute-start(bf16[512,384]{0,1:T(8,128)(2,1)S(1)} %bitcast.87), channel_id=1, source_target_pairs={{0,4},{4,0},{1,5},{5,1},{2,6},{6,2},{3,7},{7,3},{8,12},{12,8},{9,1... | collective-permute-start | bytes 1179656 | tf_op jit(solution)/shard_map/ppermute | solution.py:98
  144.1 64.1 %collective-permute-start.2 = (bf16[512,384]{0,1:T(8,128)(2,1)S(1)}, bf16[512,384]{0,1:T(8,128)(2,1)S(1)}, u32[]{:S(2)}, u32[]{:S(2)}) collective-permute-start(bf16[512,384]{0,1:T(8,128)(2,1)S(1)} %bitcast.85), channel_id=1, source_target_pairs={{0,4},{4,0},{1,5},{5,1},{2,6},{6,2},{3,7},{7,3},{8,12},{12,8},{9,1... | collective-permute-start | bytes 1179656 | tf_op jit(solution)/shard_map/ppermute | solution.py:98
  209.7 3.6 %collective-permute-start.3 = (bf16[512,1536]{0,1:T(8,128)(2,1)S(1)}, bf16[512,1536]{0,1:T(8,128)(2,1)S(1)}, u32[]{:S(2)}, u32[]{:S(2)}) collective-permute-start(bf16[512,1536]{0,1:T(8,128)(2,1)S(1)} %maximum_select_fusion.2), channel_id=1, source_target_pairs={{0,8},{8,0},{1,9},{9,1},{2,10},{10,2},{3,11},{11,3},{4,12},{12,4},... | collective-permute-start | bytes 4718600 | tf_op jit(solution)/shard_map/ppermute | solution.py:107
  290.3 6.8 %copy-start.1 = (bf16[512,768]{1,0:T(8,128)(2,1)S(1)}, bf16[512,768]{1,0:T(8,128)(2,1)}, u32[]{:S(2)}) copy-start(bf16[512,768]{1,0:T(8,128)(2,1)} %param.10) | copy-start | bytes 2359300
Sparse Core Ops, SparseCore 0:
  9.1 72.6 all-gather.2
  87.4 102.8 all-gather.4
  227.6 60.8 reduce-scatter.1

commit v14 on v13

--- a/solution.py
+++ b/solution.py
@@ -97,25 +97,26 @@
         mine.append(piece)
         far.append(lax.ppermute(piece, "yhi", pair))
     attended = jnp.concatenate(mine, axis=1)
+    low_core = lax.axis_index("c") == 0
+
+    def both_cores(here, there):
+        return jnp.where(
+            low_core,
+            jnp.concatenate([here, there], axis=0),
+            jnp.concatenate([there, here], axis=0),
+        )
+
+    h_own = both_cores(attended, lax.ppermute(attended, "c", pair))
+    group = lax.axis_index("yhi")
+    w_own = lax.dynamic_index_in_dim(w_here, group, 0, keepdims=False)
+    w_other = lax.dynamic_index_in_dim(w_here, 1 - group, 0, keepdims=False)
+    dims = (((1,), (1,)), ((), ()))
+    part = lax.dot_general(h_own, w_own, dims, preferred_element_type=jnp.float32)
+    part, far = lax.optimization_barrier((part, far))
     h_far = jnp.concatenate(far, axis=1)
-    low_hi = lax.axis_index("yhi") == 0
-    h_groups = jnp.where(
-        low_hi,
-        jnp.concatenate([attended, h_far], axis=1),
-        jnp.concatenate([h_far, attended], axis=1),
-    )
-    h_near = lax.ppermute(h_groups, "c", pair)
-    low_core = lax.axis_index("c") == 0
-    h_here = jnp.where(
-        low_core,
-        jnp.concatenate([h_groups, h_near], axis=0),
-        jnp.concatenate([h_near, h_groups], axis=0),
-    )
-    h_split = h_here.reshape(h_here.shape[0], 2, -1)
-    part = lax.dot_general(
-        h_split, w_here, (((1, 2), (0, 2)), ((), ())), preferred_element_type=jnp.float32
-    )
-    part = part.astype(jnp.bfloat16).reshape(h_here.shape[0], -1)
+    h_other = both_cores(h_far, lax.ppermute(h_far, "c", pair))
+    part = part + lax.dot_general(h_other, w_other, dims, preferred_element_type=jnp.float32)
+    part = part.astype(jnp.bfloat16).reshape(h_own.shape[0], -1)
     summed = lax.psum_scatter(part, "z", scatter_dimension=1, tiled=True)
     swapped = lax.all_to_all(summed, "c", split_axis=0, concat_axis=0, tiled=True)
     return jnp.concatenate([swapped[:tok_rows], swapped[tok_rows:]], axis=1)

time: 305 us -> 314 us (1.030)
  matrix products: 54.2 us -> 66 us
  starting transfers between devices: 21.3 us -> 11.8 us
  waiting for transfers between devices: 173 us -> 164 us
  local copies, waits for them, and re-layouts: 16.6 us -> 25.1 us
  other arithmetic: 15.5 us -> 22.9 us
    ppermute x2, waiting for transfers between devices: 63.6 us -> 2.35 us  [shards(): far.append(lax.ppermute(piece, 'yhi', pair))]
    all_gather x1, waiting for transfers between devices: 0.01 us -> 45.9 us  [shards(): w_here = lax.all_gather(w_swapped, ('ylo', 'x'), axis=0, tiled=True)]
    all_to_all x1, waiting for transfers between devices: 38.7 us -> 48.6 us  [shards(): lax.all_to_all(outgoing, SEQ, split_axis=0, concat_axis=0, tiled=True)]
    dot_general x1 -> x2, matrix products: 14.2 us -> 24.1 us  [the longest x1 15.5 us: shards(): lax.dot_general(h_own, w_own, dims, preferred_element_type=jnp.float32)]
    ppermute x1, starting transfers between devices: 10.4 us -> 0.74 us  [shards(): lax.ppermute(out_weight, ('ylo', 'yhi'), perm=[(0, 0), (1, 2), (2, 1), (3...]
    convert_element_type x0 -> x1, other arithmetic: none -> 8.83 us  [shards(): part = part.astype(jnp.bfloat16).reshape(h_own.shape[0], -1)]
    convert_element_type x0 -> x1, local copies, waits for them, and re-layouts: none -> 8.65 us  [shards(): part = part.astype(jnp.bfloat16).reshape(h_own.shape[0], -1)]
  transfers between devices with their start and end apart: 8 -> 9, of which waited for: 6 -> 6; matrix products, arithmetic and copies ran while one was open for 20% -> 25% of each run, Pallas kernels for 0% -> 0%
where the time goes in v14:
time: 314 us; the launch traced here: 313 us
  waiting for transfers between devices  164 us (52%)
  matrix products  66 us (21%)
  local copies, waits for them, and re-layouts  25.1 us (8%)
  other arithmetic  22.9 us (7%)
  between operations  13.3 us (4%)
  starting transfers between devices  11.8 us (4%)
  blocking collectives  5.38 us (2%)
  loops' own time  3.95 us (1%)
    reduce_scatter x1, waiting for transfers between devices, shards(): summed = lax.psum_scatter(part, 'z', scatter_dimension=1, tiled=True)  61.1 us
    all_to_all x1, waiting for transfers between devices, shards(): lax.all_to_all(outgoing, SEQ, split_axis=0, concat_axis=0, tiled=True)  48.6 us
    all_gather x1, waiting for transfers between devices, shards(): w_here = lax.all_gather(w_swapped, ('ylo', 'x'), axis=0, tiled=True)  45.9 us
    dot_general x6, matrix products, attend_head(): lax.dot_general(q_rows, k_rows, (((1,), (1,)), ((), ())), preferred_eleme...  23.1 us
    dot_general x1, matrix products, shards(): lax.dot_general(h_own, w_own, dims, preferred_element_type=jnp.float32)  15.5 us
    dot_general x6, matrix products, attend_head(): jnp.dot(weights, v_rows, preferred_element_type=jnp.float32)  13.3 us
    convert_element_type x1, other arithmetic, shards(): part = part.astype(jnp.bfloat16).reshape(h_own.shape[0], -1)  8.83 us
    convert_element_type x1, local copies, waits for them, and re-layouts, shards(): part = part.astype(jnp.bfloat16).reshape(h_own.shape[0], -1)  8.65 us
  transfers between devices with their start and end apart: 9, of which 6 were waited for; matrix products, arithmetic and copies ran while one was open for 25% of the time, Pallas kernels for 0%

profile of v14, /device:TPU:1, one launch (start us, length us, event | category | flops | bytes accessed | tf_op | source)
XLA Modules:
  0.0 312.9 jit_solution(7396043473874803113)
XLA Ops:
  6.5 1.8 pad_maximum_fusion.2
  8.4 0.8 constant_dynamic-slice_fusion
  9.1 1.5 convolution_convert_fusion
  10.6 2.7 copy.19
  13.4 7.0 %all-to-all-start = ((bf16[16,128,768]{2,1,0:T(8,128)(2,1)}), bf16[16,128,768]{2,1,0:T(8,128)(2,1)}, u32[]{:S(2)}, u32[]{:S(2)}) async-start(bf16[16,128,768]{2,1,0:T(8,128)(2,1)} %copy.19), calls=%async_computation | async-start | bytes 6291456 | tf_op jit(solution)/shard_map/all_to_all | solution.py:63
  20.4 0.7 collective-permute-start
  21.2 0.8 scatter_custom_fusion
  22.0 0.8 gather_fusion
  22.9 0.7 pad_dynamic-slice_fusion
  23.8 48.6 %all-to-all-done = bf16[16,128,768]{2,1,0:T(8,128)(2,1)} async-done(((bf16[16,128,768]{2,1,0:T(8,128)(2,1)}), bf16[16,128,768]{2,1,0:T(8,128)(2,1)}, u32[]{:S(2)}, u32[]{:S(2)}) %all-to-all-start) | async-done | bytes 3145760 | tf_op jit(solution)/shard_map/all_to_all | solution.py:63
  72.5 3.9 %fusion.48 = bf16[4,128,768]{2,0,1:T(4,128)(2,1)S(1)} fusion(bf16[4,16,1]{1,0,2:T(4,128)(2,1)S(1)} %fusion.51, bf16[16,128,768]{2,1,0:T(8,128)(2,1)} %all-to-all-done), kind=kOutput, calls=%fused_computation.65 | convolution fusion | flops 12976128 | bytes 3932288 | tf_op jit(solution)/shard_map/od,drc->orc/dot_general | solution.py:72
  76.4 1.0 copy.21
  77.3 4.4 %all-gather.3.cloned.1.call-done = bf16[8192,256]{1,0:T(8,128)(2,1)} async-done(((bf16[512,256]{1,0:T(8,128)(2,1)}), bf16[8192,256]{1,0:T(8,128)(2,1)}) %all-gather.3.cloned.1.call-update) | async-done | bytes 4194320 | tf_op jit(solution)/shard_map/all_gather | solution.py:39
  81.8 2.9 gather_fusion.1
  84.7 2.4 bitcast_select_fusion
  87.8 26.5 %while.26 = (s32[]{:T(128)}, bf16[3,512,128]{1,2,0:T(8,128)(2,1)S(1)}, s32[4608]{0:T(1024)S(1)}, s32[512]{0:T(512)S(1)}, s32[3]{0:T(128)S(1)}, /*index=5*/bf16[5...) while((s32[]{:T(128)}, ...), condition=%wide.region_4.5_spmd.clone, body=%wide.region_1.0_spmd.clone.sunk | while | flops 1238700544 | bytes 31533272 | solution.py:95
  89.0 3.8 %fusion.90 = (f32[512]{0:T(512)S(1)}, f32[512,4608]{1,0:T(8,128)S(1)}) fusion(bf16[4608,128]{1,0:T(8,128)(2,1)S(1)} %get-tuple-element.585, bf16[512,768]{1,0:T(8,128)(2,1)} %get-tuple-element.584, s32[]{:T(128)S(6)} %select_n.191, s32[512]{0:T(512)S(1)} %get-tuple-element.582, s32[4608]{0:T(1024)S(1)} %get-tuple-element.581, ...), kind=kOutput, calls=%fused_computation.114.clone.1 | convolution fusion | flops 622853632 | bytes 10792964 | tf_op jit(solution)/shard_map/while/body/eval_jaxpr/dot_general | solution.py:17
  92.8 1.4 fusion.91
  94.2 2.2 fusion.92
  97.8 3.9 %fusion.90 = (f32[512]{0:T(512)S(1)}, f32[512,4608]{1,0:T(8,128)S(1)}) fusion(bf16[4608,128]{1,0:T(8,128)(2,1)S(1)} %get-tuple-element.585, bf16[512,768]{1,0:T(8,128)(2,1)} %get-tuple-element.584, s32[]{:T(128)S(6)} %select_n.191, s32[512]{0:T(512)S(1)} %get-tuple-element.582, s32[4608]{0:T(1024)S(1)} %get-tuple-element.581, ...), kind=kOutput, calls=%fused_computation.114.clone.1 | convolution fusion | flops 622853632 | bytes 10792964 | tf_op jit(solution)/shard_map/while/body/eval_jaxpr/dot_general | solution.py:17
  101.7 1.4 fusion.91
  103.1 2.2 fusion.92
  106.6 3.8 %fusion.90 = (f32[512]{0:T(512)S(1)}, f32[512,4608]{1,0:T(8,128)S(1)}) fusion(bf16[4608,128]{1,0:T(8,128)(2,1)S(1)} %get-tuple-element.585, bf16[512,768]{1,0:T(8,128)(2,1)} %get-tuple-element.584, s32[]{:T(128)S(6)} %select_n.191, s32[512]{0:T(512)S(1)} %get-tuple-element.582, s32[4608]{0:T(1024)S(1)} %get-tuple-element.581, ...), kind=kOutput, calls=%fused_computation.114.clone.1 | convolution fusion | flops 622853632 | bytes 10792964 | tf_op jit(solution)/shard_map/while/body/eval_jaxpr/dot_general | solution.py:17
  110.5 1.4 fusion.91
  111.9 2.2 fusion.92
  114.3 26.8 %while.27 = (s32[]{:T(128)}, bf16[3,512,128]{1,2,0:T(8,128)(2,1)S(1)}, s32[4608]{0:T(1024)S(1)}, s32[512]{0:T(512)S(1)}, s32[3]{0:T(128)S(1)}, /*index=5*/bf16[5...) while((s32[]{:T(128)}, ...), condition=%wide.region_8.9_spmd.clone, body=%wide.region_5.8_spmd.clone.sunk | while | flops 1238700544 | bytes 31533272 | solution.py:95
  115.6 3.8 %fusion.95 = (f32[512]{0:T(512)S(1)}, f32[512,4608]{1,0:T(8,128)S(1)}) fusion(bf16[4608,128]{1,0:T(8,128)(2,1)S(1)} %get-tuple-element.543, bf16[512,768]{1,0:T(8,128)(2,1)} %get-tuple-element.542, s32[]{:T(128)S(6)} %select_n.192, s32[512]{0:T(512)S(1)} %get-tuple-element.540, s32[4608]{0:T(1024)S(1)} %get-tuple-element.539, ...), kind=kOutput, calls=%fused_computation.115.clone.1 | convolution fusion | flops 622853632 | bytes 10792964 | tf_op jit(solution)/shard_map/while/body/eval_jaxpr/dot_general | solution.py:17
  119.4 1.4 fusion.96
  120.8 2.2 fusion.97
  123.2 0.6 dynamic_slice.75
  124.5 3.9 %fusion.95 = (f32[512]{0:T(512)S(1)}, f32[512,4608]{1,0:T(8,128)S(1)}) fusion(bf16[4608,128]{1,0:T(8,128)(2,1)S(1)} %get-tuple-element.543, bf16[512,768]{1,0:T(8,128)(2,1)} %get-tuple-element.542, s32[]{:T(128)S(6)} %select_n.192, s32[512]{0:T(512)S(1)} %get-tuple-element.540, s32[4608]{0:T(1024)S(1)} %get-tuple-element.539, ...), kind=kOutput, calls=%fused_computation.115.clone.1 | convolution fusion | flops 622853632 | bytes 10792964 | tf_op jit(solution)/shard_map/while/body/eval_jaxpr/dot_general | solution.py:17
  128.4 1.4 fusion.96
  129.8 2.2 fusion.97
  133.4 3.9 %fusion.95 = (f32[512]{0:T(512)S(1)}, f32[512,4608]{1,0:T(8,128)S(1)}) fusion(bf16[4608,128]{1,0:T(8,128)(2,1)S(1)} %get-tuple-element.543, bf16[512,768]{1,0:T(8,128)(2,1)} %get-tuple-element.542, s32[]{:T(128)S(6)} %select_n.192, s32[512]{0:T(512)S(1)} %get-tuple-element.540, s32[4608]{0:T(1024)S(1)} %get-tuple-element.539, ...), kind=kOutput, calls=%fused_computation.115.clone.1 | convolution fusion | flops 622853632 | bytes 10792964 | tf_op jit(solution)/shard_map/while/body/eval_jaxpr/dot_general | solution.py:17
  137.3 1.4 fusion.96
  138.7 2.2 fusion.97
  141.5 2.7 collective-permute-start.3
  144.5 45.9 %all-gather.5.cloned.1.call-done = bf16[6144,768]{1,0:T(8,128)(2,1)} async-done(((bf16[768,768]{1,0:T(8,128)(2,1)}), bf16[6144,768]{1,0:T(8,128)(2,1)}) %all-gather.5.cloned.1.call-update) | async-done | bytes 9437200 | tf_op jit(solution)/shard_map/all_gather | solution.py:43
  190.3 15.5 %fusion.22 = f32[1024,4,768]{2,0,1:T(8,128)} fusion(bf16[2,4,768,768]{3,2,1,0:T(8,128)(2,1)} %bitcast.92, s32[]{:T(128)S(6)} %select_n.137, bf16[512,768]{0,1:T(8,128)(2,1)S(1)} %collective-permute-done.1, bf16[512,384]{0,1:T(8,128)(2,1)S(1)} %bitcast.87, bf16[512,384]{0,1:T(8,128)(2,1)S(1)} %bitcast.90, pred[]{:T(512)S(6)} %eq.103), kind=kOutput, calls=%fused_computation.36 | convolution fusion | flops 4842061824 | bytes 18874372 | tf_op jit(solution)/shard_map/dot_general | solution.py:114
  205.9 2.4 collective-permute-done.2
  208.8 1.9 collective-permute-done.4
  210.8 8.5 %fusion.20 = f32[1024,4,768]{2,0,1:T(8,128)S(1)} fusion(bf16[2,4,768,768]{3,2,1,0:T(8,128)(2,1)} %bitcast.93, s32[]{:T(128)S(6)} %select_n.139, bf16[512,768]{0,1:T(8,128)(2,1)S(1)} %collective-permute-done.4, bf16[512,768]{0,1:T(8,128)(2,1)S(1)} %constant_dynamic-update-slice_fusion.2, pred[]{:T(512)S(6)} %eq.103), kind=kOutput, calls=%fused_computation.34 | convolution fusion | flops 4838916096 | bytes 18874372 | tf_op jit(solution)/shard_map/dot_general | solution.py:118
  219.3 8.8 %add_convert_fusion = bf16[1024,4,768]{2,0,1:T(8,128)(2,1)} fusion(f32[1024,4,768]{2,0,1:T(8,128)} %fusion.22, f32[1024,4,768]{2,0,1:T(8,128)S(1)} %fusion.20), kind=kLoop, calls=%fused_computation.33 | loop fusion | flops 6291456 | bytes 31457280 | tf_op jit(solution)/shard_map/convert_element_type | solution.py:119
  228.1 8.6 %copy.28 = bf16[1024,4,768]{0,2,1:T(8,128)(2,1)} copy(bf16[1024,4,768]{2,0,1:T(8,128)(2,1)} %add_convert_fusion) | data formatting | bytes 12582912 | tf_op jit(solution)/shard_map/convert_element_type | solution.py:119
  236.8 61.1 %reduce-scatter.2.cloned.1.call-done = bf16[1024,768]{0,1:T(8,128)(2,1)} async-done(((bf16[1024,3072]{0,1:T(8,128)(2,1)}), bf16[1024,768]{0,1:T(8,128)(2,1)}) %reduce-scatter.2.cloned.1.call-update) | async-done | bytes 1572880 | tf_op jit(solution)/shard_map/reduce_scatter | solution.py:120
  297.8 1.7 copy.35
  299.6 5.4 %all_to_all.14 = bf16[2,512,768]{2,1,0:T(8,128)(2,1)S(1)} all-to-all(bf16[2,512,768]{2,1,0:T(8,128)(2,1)S(1)} %bitcast.84), channel_id=1, replica_groups=mesh['ylo'=2,'x'=4,'c'=2,'yhi'=2,'z'=4] {'c'}, dimensions={0} | all-to-all | bytes 3145728 | tf_op jit(solution)/shard_map/all_to_all | solution.py:121
  305.1 1.3 pad_maximum_fusion
  (77 shorter events, 6.5 us)
Async XLA Ops:
  6.5 2.6 copy-start
  6.5 75.2 %all-gather.3.cloned.1.call-start = ((), (), s32[]{:S(2)}) async-start(), calls=%async_computation.3 | async-start | bytes 4456448 | tf_op jit(solution)/shard_map/all_gather | solution.py:39
  13.4 7.0 %copy-start.6 = (bf16[768,768]{1,0:T(8,128)(2,1)S(1)}, bf16[768,768]{1,0:T(8,128)(2,1)}, u32[]{:S(2)}) copy-start(bf16[768,768]{1,0:T(8,128)(2,1)} %param.15) | copy-start | bytes 3538948
  13.4 7.8 %copy-start.5 = (s32[64,2]{0,1:T(2,128)S(1)}, s32[64,2]{0,1:T(2,128)}, u32[]{:S(2)}) copy-start(s32[64,2]{0,1:T(2,128)} %param.14) | copy-start | bytes 1540
  13.4 8.6 %copy-start.3 = (s32[8192]{0:T(1024)S(1)}, s32[8192]{0:T(1024)}, u32[]{:S(2)}) copy-start(s32[8192]{0:T(1024)} %param.13) | copy-start | bytes 98308
  13.4 59.1 %all-to-all-start = ((bf16[16,128,768]{2,1,0:T(8,128)(2,1)}), bf16[16,128,768]{2,1,0:T(8,128)(2,1)}, u32[]{:S(2)}, u32[]{:S(2)}) async-start(bf16[16,128,768]{2,1,0:T(8,128)(2,1)} %copy.19), calls=%async_computation | async-start | bytes 6291456 | tf_op jit(solution)/shard_map/all_to_all | solution.py:63
  20.3 170.0 %all-gather.5.cloned.1.call-start = ((), (), s32[]{:S(2)}) async-start(), calls=%async_computation.4 | async-start | bytes 10616832 | tf_op jit(solution)/shard_map/all_gather | solution.py:43
  20.4 57.0 %collective-permute-start = (bf16[768,768]{1,0:T(8,128)(2,1)S(1)}, bf16[768,768]{1,0:T(8,128)(2,1)S(1)}, u32[]{:S(2)}, u32[]{:S(2)}) collective-permute-start(bf16[768,768]{1,0:T(8,128)(2,1)S(1)} %copy-done.6), channel_id=1, source_target_pairs={{0,0},{4,64},{64,4},{68,68},{1,1},{5,65},{65,5},{69,69},{2,2},{6,6... | collective-permute-start | bytes 3538952 | tf_op jit(solution)/shard_map/ppermute | solution.py:41
  77.3 4.4 %copy-start.2 = (bf16[768,768]{1,0:T(8,128)(2,1)}, bf16[768,768]{1,0:T(8,128)(2,1)S(1)}, u32[]{:S(2)}) copy-start(bf16[768,768]{1,0:T(8,128)(2,1)S(1)} %collective-permute-done) | copy-start | bytes 3538948
  87.1 0.7 copy-start.4
  87.3 210.6 %reduce-scatter.2.cloned.1.call-start = ((), (), s32[]{:S(2)}) async-start(), calls=%async_computation.5 | async-start | bytes 7864320 | tf_op jit(solution)/shard_map/reduce_scatter | solution.py:120
  141.1 3.3 %collective-permute-start.1 = (bf16[512,768]{0,1:T(8,128)(2,1)S(1)}, bf16[512,768]{0,1:T(8,128)(2,1)S(1)}, u32[]{:S(2)}, u32[]{:S(2)}) collective-permute-start(bf16[512,768]{0,1:T(8,128)(2,1)S(1)} %pad_maximum_fusion.1), channel_id=1, source_target_pairs={{0,8},{8,0},{1,9},{9,1},{2,10},{10,2},{3,11},{11,3},{4,12},{12,4},... | collective-permute-start | bytes 2359304 | tf_op jit(solution)/shard_map/ppermute | solution.py:109
  141.5 64.4 %collective-permute-start.3 = (bf16[512,384]{0,1:T(8,128)(2,1)S(1)}, bf16[512,384]{0,1:T(8,128)(2,1)S(1)}, u32[]{:S(2)}, u32[]{:S(2)}) collective-permute-start(bf16[512,384]{0,1:T(8,128)(2,1)S(1)} %bitcast.86), channel_id=1, source_target_pairs={{0,4},{4,0},{1,5},{5,1},{2,6},{6,2},{3,7},{7,3},{8,12},{12,8},{9,1... | collective-permute-start | bytes 1179656 | tf_op jit(solution)/shard_map/ppermute | solution.py:98
  144.2 64.1 %collective-permute-start.2 = (bf16[512,384]{0,1:T(8,128)(2,1)S(1)}, bf16[512,384]{0,1:T(8,128)(2,1)S(1)}, u32[]{:S(2)}, u32[]{:S(2)}) collective-permute-start(bf16[512,384]{0,1:T(8,128)(2,1)S(1)} %bitcast.89), channel_id=1, source_target_pairs={{0,4},{4,0},{1,5},{5,1},{2,6},{6,2},{3,7},{7,3},{8,12},{12,8},{9,1... | collective-permute-start | bytes 1179656 | tf_op jit(solution)/shard_map/ppermute | solution.py:98
  208.3 2.5 collective-permute-start.4
  299.6 6.8 %copy-start.1 = (bf16[512,768]{1,0:T(8,128)(2,1)S(1)}, bf16[512,768]{1,0:T(8,128)(2,1)}, u32[]{:S(2)}) copy-start(bf16[512,768]{1,0:T(8,128)(2,1)} %param.10) | copy-start | bytes 2359300
Sparse Core Ops, SparseCore 0:
  9.1 72.6 all-gather.2
  87.4 102.9 all-gather.4
  236.9 60.8 reduce-scatter.1

commit v15 on v14

--- a/solution.py
+++ b/solution.py
@@ -112,10 +112,12 @@
     w_other = lax.dynamic_index_in_dim(w_here, 1 - group, 0, keepdims=False)
     dims = (((1,), (1,)), ((), ()))
     part = lax.dot_general(h_own, w_own, dims, preferred_element_type=jnp.float32)
+    part = part.astype(jnp.bfloat16)
     part, far = lax.optimization_barrier((part, far))
     h_far = jnp.concatenate(far, axis=1)
     h_other = both_cores(h_far, lax.ppermute(h_far, "c", pair))
-    part = part + lax.dot_general(h_other, w_other, dims, preferred_element_type=jnp.float32)
+    other = lax.dot_general(h_other, w_other, dims, preferred_element_type=jnp.float32)
+    part = part.astype(jnp.float32) + other.astype(jnp.bfloat16).astype(jnp.float32)
     part = part.astype(jnp.bfloat16).reshape(h_own.shape[0], -1)
     summed = lax.psum_scatter(part, "z", scatter_dimension=1, tiled=True)
     swapped = lax.all_to_all(summed, "c", split_axis=0, concat_axis=0, tiled=True)

time: 314 us -> 315 us (level)
  transfers between devices with their start and end apart: 9 -> 9, of which waited for: 6 -> 6; matrix products, arithmetic and copies ran while one was open for 25% -> 24% of each run, Pallas kernels for 0% -> 0%
where the time goes in v15:
time: 315 us; the launch traced here: 314 us
  waiting for transfers between devices  165 us (52%)
  matrix products  66 us (21%)
  local copies, waits for them, and re-layouts  25.4 us (8%)
  other arithmetic  22.8 us (7%)
  between operations  13.3 us (4%)
  starting transfers between devices  11.8 us (4%)
  blocking collectives  5.39 us (2%)
  loops' own time  4.39 us (1%)
    reduce_scatter x1, waiting for transfers between devices, shards(): summed = lax.psum_scatter(part, 'z', scatter_dimension=1, tiled=True)  61.1 us
    all_to_all x1, waiting for transfers between devices, shards(): lax.all_to_all(outgoing, SEQ, split_axis=0, concat_axis=0, tiled=True)  48.6 us
    all_gather x1, waiting for transfers between devices, shards(): w_here = lax.all_gather(w_swapped, ('ylo', 'x'), axis=0, tiled=True)  45.1 us
    dot_general x6, matrix products, attend_head(): lax.dot_general(q_rows, k_rows, (((1,), (1,)), ((), ())), preferred_eleme...  23.1 us
    dot_general x1, matrix products, shards(): lax.dot_general(h_own, w_own, dims, preferred_element_type=jnp.float32)  14.5 us
    dot_general x6, matrix products, attend_head(): jnp.dot(weights, v_rows, preferred_element_type=jnp.float32)  13.3 us
    dot_general x1, matrix products, shards(): lax.dot_general(h_other, w_other, dims, preferred_element_type=jnp.float32)  9.6 us
    convert_element_type x1, other arithmetic, shards(): part = part.astype(jnp.bfloat16).reshape(h_own.shape[0], -1)  8.68 us
  transfers between devices with their start and end apart: 9, of which 6 were waited for; matrix products, arithmetic and copies ran while one was open for 24% of the time, Pallas kernels for 0%

profile of v15, /device:TPU:1, one launch (start us, length us, event | category | flops | bytes accessed | tf_op | source)
XLA Modules:
  0.0 313.8 jit_solution(9831532798369733780)
XLA Ops:
  6.5 1.8 pad_maximum_fusion.2
  8.4 0.8 constant_dynamic-slice_fusion
  9.1 1.5 convolution_convert_fusion
  10.6 2.7 copy.19
  13.4 7.0 %all-to-all-start = ((bf16[16,128,768]{2,1,0:T(8,128)(2,1)}), bf16[16,128,768]{2,1,0:T(8,128)(2,1)}, u32[]{:S(2)}, u32[]{:S(2)}) async-start(bf16[16,128,768]{2,1,0:T(8,128)(2,1)} %copy.19), calls=%async_computation | async-start | bytes 6291456 | tf_op jit(solution)/shard_map/all_to_all | solution.py:63
  20.4 0.7 collective-permute-start
  21.2 0.8 scatter_custom_fusion
  22.0 0.8 gather_fusion
  22.9 0.7 pad_dynamic-slice_fusion
  23.8 48.6 %all-to-all-done = bf16[16,128,768]{2,1,0:T(8,128)(2,1)} async-done(((bf16[16,128,768]{2,1,0:T(8,128)(2,1)}), bf16[16,128,768]{2,1,0:T(8,128)(2,1)}, u32[]{:S(2)}, u32[]{:S(2)}) %all-to-all-start) | async-done | bytes 3145760 | tf_op jit(solution)/shard_map/all_to_all | solution.py:63
  72.5 3.9 %fusion.51 = bf16[4,128,768]{2,0,1:T(4,128)(2,1)S(1)} fusion(bf16[4,16,1]{1,0,2:T(4,128)(2,1)S(1)} %fusion.54, bf16[16,128,768]{2,1,0:T(8,128)(2,1)} %all-to-all-done), kind=kOutput, calls=%fused_computation.66 | convolution fusion | flops 12976128 | bytes 3932288 | tf_op jit(solution)/shard_map/od,drc->orc/dot_general | solution.py:72
  76.4 1.0 copy.21
  77.3 4.4 %all-gather.3.cloned.1.call-done = bf16[8192,256]{1,0:T(8,128)(2,1)} async-done(((bf16[512,256]{1,0:T(8,128)(2,1)}), bf16[8192,256]{1,0:T(8,128)(2,1)}) %all-gather.3.cloned.1.call-update) | async-done | bytes 4194320 | tf_op jit(solution)/shard_map/all_gather | solution.py:39
  81.8 2.9 gather_fusion.1
  84.7 2.4 bitcast_select_fusion
  87.8 27.0 %while.26 = (s32[]{:T(128)}, bf16[3,512,128]{1,2,0:T(8,128)(2,1)S(1)}, s32[4608]{0:T(1024)S(1)}, s32[512]{0:T(512)S(1)}, s32[3]{0:T(128)S(1)}, /*index=5*/bf16[5...) while((s32[]{:T(128)}, ...), condition=%wide.region_4.5_spmd.clone, body=%wide.region_1.0_spmd.clone.sunk | while | flops 1238700544 | bytes 31533272 | solution.py:95
  89.1 3.8 %fusion.93 = (f32[512]{0:T(512)S(1)}, f32[512,4608]{1,0:T(8,128)S(1)}) fusion(bf16[4608,128]{1,0:T(8,128)(2,1)S(1)} %get-tuple-element.585, bf16[512,768]{1,0:T(8,128)(2,1)} %get-tuple-element.584, s32[]{:T(128)S(6)} %select_n.191, s32[512]{0:T(512)S(1)} %get-tuple-element.582, s32[4608]{0:T(1024)S(1)} %get-tuple-element.581, ...), kind=kOutput, calls=%fused_computation.115.clone.1 | convolution fusion | flops 622853632 | bytes 10792964 | tf_op jit(solution)/shard_map/while/body/eval_jaxpr/dot_general | solution.py:17
  93.0 1.4 fusion.94
  94.4 2.2 fusion.95
  98.1 3.9 %fusion.93 = (f32[512]{0:T(512)S(1)}, f32[512,4608]{1,0:T(8,128)S(1)}) fusion(bf16[4608,128]{1,0:T(8,128)(2,1)S(1)} %get-tuple-element.585, bf16[512,768]{1,0:T(8,128)(2,1)} %get-tuple-element.584, s32[]{:T(128)S(6)} %select_n.191, s32[512]{0:T(512)S(1)} %get-tuple-element.582, s32[4608]{0:T(1024)S(1)} %get-tuple-element.581, ...), kind=kOutput, calls=%fused_computation.115.clone.1 | convolution fusion | flops 622853632 | bytes 10792964 | tf_op jit(solution)/shard_map/while/body/eval_jaxpr/dot_general | solution.py:17
  102.0 1.4 fusion.94
  103.4 2.2 fusion.95
  107.1 3.8 %fusion.93 = (f32[512]{0:T(512)S(1)}, f32[512,4608]{1,0:T(8,128)S(1)}) fusion(bf16[4608,128]{1,0:T(8,128)(2,1)S(1)} %get-tuple-element.585, bf16[512,768]{1,0:T(8,128)(2,1)} %get-tuple-element.584, s32[]{:T(128)S(6)} %select_n.191, s32[512]{0:T(512)S(1)} %get-tuple-element.582, s32[4608]{0:T(1024)S(1)} %get-tuple-element.581, ...), kind=kOutput, calls=%fused_computation.115.clone.1 | convolution fusion | flops 622853632 | bytes 10792964 | tf_op jit(solution)/shard_map/while/body/eval_jaxpr/dot_general | solution.py:17
  111.0 1.4 fusion.94
  112.4 2.2 fusion.95
  114.8 27.0 %while.27 = (s32[]{:T(128)}, bf16[3,512,128]{1,2,0:T(8,128)(2,1)S(1)}, s32[4608]{0:T(1024)S(1)}, s32[512]{0:T(512)S(1)}, s32[3]{0:T(128)S(1)}, /*index=5*/bf16[5...) while((s32[]{:T(128)}, ...), condition=%wide.region_8.9_spmd.clone, body=%wide.region_5.8_spmd.clone.sunk | while | flops 1238700544 | bytes 31533272 | solution.py:95
  114.8 0.7 dynamic_slice.77
  116.2 3.8 %fusion.98 = (f32[512]{0:T(512)S(1)}, f32[512,4608]{1,0:T(8,128)S(1)}) fusion(bf16[4608,128]{1,0:T(8,128)(2,1)S(1)} %get-tuple-element.543, bf16[512,768]{1,0:T(8,128)(2,1)} %get-tuple-element.542, s32[]{:T(128)S(6)} %select_n.192, s32[512]{0:T(512)S(1)} %get-tuple-element.540, s32[4608]{0:T(1024)S(1)} %get-tuple-element.539, ...), kind=kOutput, calls=%fused_computation.116.clone.1 | convolution fusion | flops 622853632 | bytes 10792964 | tf_op jit(solution)/shard_map/while/body/eval_jaxpr/dot_general | solution.py:17
  120.0 1.4 fusion.99
  121.4 2.2 fusion.100
  125.2 3.9 %fusion.98 = (f32[512]{0:T(512)S(1)}, f32[512,4608]{1,0:T(8,128)S(1)}) fusion(bf16[4608,128]{1,0:T(8,128)(2,1)S(1)} %get-tuple-element.543, bf16[512,768]{1,0:T(8,128)(2,1)} %get-tuple-element.542, s32[]{:T(128)S(6)} %select_n.192, s32[512]{0:T(512)S(1)} %get-tuple-element.540, s32[4608]{0:T(1024)S(1)} %get-tuple-element.539, ...), kind=kOutput, calls=%fused_computation.116.clone.1 | convolution fusion | flops 622853632 | bytes 10792964 | tf_op jit(solution)/shard_map/while/body/eval_jaxpr/dot_general | solution.py:17
  129.0 1.4 fusion.99
  130.4 2.2 fusion.100
  134.2 3.9 %fusion.98 = (f32[512]{0:T(512)S(1)}, f32[512,4608]{1,0:T(8,128)S(1)}) fusion(bf16[4608,128]{1,0:T(8,128)(2,1)S(1)} %get-tuple-element.543, bf16[512,768]{1,0:T(8,128)(2,1)} %get-tuple-element.542, s32[]{:T(128)S(6)} %select_n.192, s32[512]{0:T(512)S(1)} %get-tuple-element.540, s32[4608]{0:T(1024)S(1)} %get-tuple-element.539, ...), kind=kOutput, calls=%fused_computation.116.clone.1 | convolution fusion | flops 622853632 | bytes 10792964 | tf_op jit(solution)/shard_map/while/body/eval_jaxpr/dot_general | solution.py:17
  138.0 1.4 fusion.99
  139.4 2.2 fusion.100
  142.2 2.7 collective-permute-start.3
  145.2 45.1 %all-gather.5.cloned.1.call-done = bf16[6144,768]{1,0:T(8,128)(2,1)} async-done(((bf16[768,768]{1,0:T(8,128)(2,1)}), bf16[6144,768]{1,0:T(8,128)(2,1)}) %all-gather.5.cloned.1.call-update) | async-done | bytes 9437200 | tf_op jit(solution)/shard_map/all_gather | solution.py:43
  190.3 14.5 %fusion.26 = bf16[1024,4,768]{2,0,1:T(8,128)(2,1)} fusion(bf16[2,4,768,768]{3,2,1,0:T(8,128)(2,1)} %bitcast.94, s32[]{:T(128)S(6)} %select_n.137, bf16[512,768]{0,1:T(8,128)(2,1)S(1)} %collective-permute-done.1, bf16[512,384]{0,1:T(8,128)(2,1)S(1)} %bitcast.89, bf16[512,384]{0,1:T(8,128)(2,1)S(1)} %bitcast.92, pred[]{:T(512)S(6)} %eq.103), kind=kOutput, calls=%fused_computation.40 | convolution fusion | flops 4845207552 | bytes 12582917 | tf_op jit(solution)/shard_map/dot_general | solution.py:114
  204.8 3.4 %collective-permute-done.2 = bf16[512,384]{0,1:T(8,128)(2,1)S(1)} collective-permute-done((bf16[512,384]{0,1:T(8,128)(2,1)S(1)}, bf16[512,384]{0,1:T(8,128)(2,1)S(1)}, u32[]{:S(2)}, u32[]{:S(2)}) %collective-permute-start.2) | collective-permute-done | bytes 393248 | tf_op jit(solution)/shard_map/ppermute | solution.py:98
  208.8 1.9 collective-permute-done.4
  210.8 9.6 %fusion.20 = bf16[1024,4,768]{2,0,1:T(8,128)(2,1)} fusion(bf16[2,4,768,768]{3,2,1,0:T(8,128)(2,1)} %bitcast.95, s32[]{:T(128)S(6)} %select_n.139, bf16[512,768]{0,1:T(8,128)(2,1)S(1)} %collective-permute-done.4, bf16[512,768]{0,1:T(8,128)(2,1)S(1)} %constant_dynamic-update-slice_fusion.2, pred[]{:T(512)S(6)} %eq.103), kind=kOutput, calls=%fused_computation.34 | convolution fusion | flops 4838916096 | bytes 12582917 | tf_op jit(solution)/shard_map/dot_general | solution.py:119
  220.4 8.7 %add_convert_fusion = bf16[1024,4,768]{2,0,1:T(8,128)(2,1)} fusion(bf16[1024,4,768]{2,0,1:T(8,128)(2,1)} %fusion.26, bf16[1024,4,768]{2,0,1:T(8,128)(2,1)} %fusion.20), kind=kLoop, calls=%fused_computation.33 | loop fusion | flops 12582912 | bytes 18874368 | tf_op jit(solution)/shard_map/convert_element_type | solution.py:121
  229.0 8.6 %copy.28 = bf16[1024,4,768]{0,2,1:T(8,128)(2,1)} copy(bf16[1024,4,768]{2,0,1:T(8,128)(2,1)} %add_convert_fusion) | data formatting | bytes 12582912 | tf_op jit(solution)/shard_map/convert_element_type | solution.py:121
  237.7 61.1 %reduce-scatter.2.cloned.1.call-done = bf16[1024,768]{0,1:T(8,128)(2,1)} async-done(((bf16[1024,3072]{0,1:T(8,128)(2,1)}), bf16[1024,768]{0,1:T(8,128)(2,1)}) %reduce-scatter.2.cloned.1.call-update) | async-done | bytes 1572880 | tf_op jit(solution)/shard_map/reduce_scatter | solution.py:122
  298.8 1.7 copy.35
  300.5 5.4 %all_to_all.14 = bf16[2,512,768]{2,1,0:T(8,128)(2,1)S(1)} all-to-all(bf16[2,512,768]{2,1,0:T(8,128)(2,1)S(1)} %bitcast.86), channel_id=1, replica_groups=mesh['ylo'=2,'x'=4,'c'=2,'yhi'=2,'z'=4] {'c'}, dimensions={0} | all-to-all | bytes 3145728 | tf_op jit(solution)/shard_map/all_to_all | solution.py:123
  306.0 1.3 pad_maximum_fusion
  (77 shorter events, 6.8 us)
Async XLA Ops:
  6.5 2.6 copy-start
  6.5 75.2 %all-gather.3.cloned.1.call-start = ((), (), s32[]{:S(2)}) async-start(), calls=%async_computation.3 | async-start | bytes 4456448 | tf_op jit(solution)/shard_map/all_gather | solution.py:39
  13.4 7.0 %copy-start.6 = (bf16[768,768]{1,0:T(8,128)(2,1)S(1)}, bf16[768,768]{1,0:T(8,128)(2,1)}, u32[]{:S(2)}) copy-start(bf16[768,768]{1,0:T(8,128)(2,1)} %param.15) | copy-start | bytes 3538948
  13.4 7.8 %copy-start.5 = (s32[64,2]{0,1:T(2,128)S(1)}, s32[64,2]{0,1:T(2,128)}, u32[]{:S(2)}) copy-start(s32[64,2]{0,1:T(2,128)} %param.14) | copy-start | bytes 1540
  13.4 8.6 %copy-start.3 = (s32[8192]{0:T(1024)S(1)}, s32[8192]{0:T(1024)}, u32[]{:S(2)}) copy-start(s32[8192]{0:T(1024)} %param.13) | copy-start | bytes 98308
  13.4 59.1 %all-to-all-start = ((bf16[16,128,768]{2,1,0:T(8,128)(2,1)}), bf16[16,128,768]{2,1,0:T(8,128)(2,1)}, u32[]{:S(2)}, u32[]{:S(2)}) async-start(bf16[16,128,768]{2,1,0:T(8,128)(2,1)} %copy.19), calls=%async_computation | async-start | bytes 6291456 | tf_op jit(solution)/shard_map/all_to_all | solution.py:63
  20.3 170.0 %all-gather.5.cloned.1.call-start = ((), (), s32[]{:S(2)}) async-start(), calls=%async_computation.4 | async-start | bytes 10616832 | tf_op jit(solution)/shard_map/all_gather | solution.py:43
  20.4 57.0 %collective-permute-start = (bf16[768,768]{1,0:T(8,128)(2,1)S(1)}, bf16[768,768]{1,0:T(8,128)(2,1)S(1)}, u32[]{:S(2)}, u32[]{:S(2)}) collective-permute-start(bf16[768,768]{1,0:T(8,128)(2,1)S(1)} %copy-done.6), channel_id=1, source_target_pairs={{0,0},{4,64},{64,4},{68,68},{1,1},{5,65},{65,5},{69,69},{2,2},{6,6... | collective-permute-start | bytes 3538952 | tf_op jit(solution)/shard_map/ppermute | solution.py:41
  77.3 4.4 %copy-start.2 = (bf16[768,768]{1,0:T(8,128)(2,1)}, bf16[768,768]{1,0:T(8,128)(2,1)S(1)}, u32[]{:S(2)}) copy-start(bf16[768,768]{1,0:T(8,128)(2,1)S(1)} %collective-permute-done) | copy-start | bytes 3538948
  87.1 0.7 copy-start.4
  87.3 211.5 %reduce-scatter.2.cloned.1.call-start = ((), (), s32[]{:S(2)}) async-start(), calls=%async_computation.5 | async-start | bytes 7864320 | tf_op jit(solution)/shard_map/reduce_scatter | solution.py:122
  141.9 3.3 %collective-permute-start.1 = (bf16[512,768]{0,1:T(8,128)(2,1)S(1)}, bf16[512,768]{0,1:T(8,128)(2,1)S(1)}, u32[]{:S(2)}, u32[]{:S(2)}) collective-permute-start(bf16[512,768]{0,1:T(8,128)(2,1)S(1)} %pad_maximum_fusion.1), channel_id=1, source_target_pairs={{0,8},{8,0},{1,9},{9,1},{2,10},{10,2},{3,11},{11,3},{4,12},{12,4},... | collective-permute-start | bytes 2359304 | tf_op jit(solution)/shard_map/ppermute | solution.py:109
  142.2 62.6 %collective-permute-start.3 = (bf16[512,384]{0,1:T(8,128)(2,1)S(1)}, bf16[512,384]{0,1:T(8,128)(2,1)S(1)}, u32[]{:S(2)}, u32[]{:S(2)}) collective-permute-start(bf16[512,384]{0,1:T(8,128)(2,1)S(1)} %bitcast.88), channel_id=1, source_target_pairs={{0,4},{4,0},{1,5},{5,1},{2,6},{6,2},{3,7},{7,3},{8,12},{12,8},{9,1... | collective-permute-start | bytes 1179656 | tf_op jit(solution)/shard_map/ppermute | solution.py:98
  144.9 63.3 %collective-permute-start.2 = (bf16[512,384]{0,1:T(8,128)(2,1)S(1)}, bf16[512,384]{0,1:T(8,128)(2,1)S(1)}, u32[]{:S(2)}, u32[]{:S(2)}) collective-permute-start(bf16[512,384]{0,1:T(8,128)(2,1)S(1)} %bitcast.91), channel_id=1, source_target_pairs={{0,4},{4,0},{1,5},{5,1},{2,6},{6,2},{3,7},{7,3},{8,12},{12,8},{9,1... | collective-permute-start | bytes 1179656 | tf_op jit(solution)/shard_map/ppermute | solution.py:98
  208.3 2.5 collective-permute-start.4
  300.5 6.8 %copy-start.1 = (bf16[512,768]{1,0:T(8,128)(2,1)S(1)}, bf16[512,768]{1,0:T(8,128)(2,1)}, u32[]{:S(2)}) copy-start(bf16[512,768]{1,0:T(8,128)(2,1)} %param.10) | copy-start | bytes 2359300
Sparse Core Ops, SparseCore 0:
  9.1 72.6 all-gather.2
  87.4 102.8 all-gather.4
  237.8 60.8 reduce-scatter.1

commit v16 on v13

--- a/solution.py
+++ b/solution.py
@@ -88,10 +88,10 @@
         q_head = lax.dynamic_slice_in_dim(queries_here, head_index * HEAD_DIM, HEAD_DIM, 1)
         return attend_head(q_head, ctx_keys, ctx_values, q_pos, k_pos, q_seg, k_seg)
 
-    half = heads_here // 2
+    half = heads_here // 3
     pair = [(0, 1), (1, 0)]
     mine, far = [], []
-    for first in (0, half):
+    for first in range(0, heads_here, half):
         per_head = lax.map(one_head, jnp.arange(first, first + half, dtype=jnp.int32))
         piece = jnp.transpose(per_head, (1, 0, 2)).reshape(tok_rows, half * HEAD_DIM)
         mine.append(piece)

time: 305 us -> 306 us (level)
  waiting for transfers between devices: 173 us -> 168 us
  local copies, waits for them, and re-layouts: 16.6 us -> 20.7 us
    ppermute x2 -> x3, waiting for transfers between devices: 63.6 us -> 58.3 us  [shards(): far.append(lax.ppermute(piece, 'yhi', pair))]
  transfers between devices with their start and end apart: 8 -> 9, of which waited for: 6 -> 6; matrix products, arithmetic and copies ran while one was open for 20% -> 21% of each run, Pallas kernels for 0% -> 0%
where the time goes in v16:
time: 306 us; the launch traced here: 304 us
  waiting for transfers between devices  168 us (55%)
  matrix products  54.3 us (18%)
  starting transfers between devices  24.1 us (8%)
  local copies, waits for them, and re-layouts  20.7 us (7%)
  other arithmetic  14.7 us (5%)
  between operations  13.3 us (4%)
  blocking collectives  5.38 us (2%)
  loops' own time  4.05 us (1%)
    reduce_scatter x1, waiting for transfers between devices, shards(): summed = lax.psum_scatter(part, 'z', scatter_dimension=1, tiled=True)  61.1 us
    ppermute x3, waiting for transfers between devices, shards(): far.append(lax.ppermute(piece, 'yhi', pair))  58.3 us
    all_to_all x1, waiting for transfers between devices, shards(): lax.all_to_all(outgoing, SEQ, split_axis=0, concat_axis=0, tiled=True)  38.8 us
    dot_general x6, matrix products, attend_head(): lax.dot_general(q_rows, k_rows, (((1,), (1,)), ((), ())), preferred_eleme...  23.1 us
    dot_general x1, matrix products, shards(): lax.dot_general(h_split, w_here, (((1, 2), (0, 2)), ((), ())), preferred_...  14.2 us
    dot_general x6, matrix products, attend_head(): jnp.dot(weights, v_rows, preferred_element_type=jnp.float32)  13.3 us
    ppermute x1, starting transfers between devices, shards(): lax.ppermute(out_weight, ('ylo', 'yhi'), perm=[(0, 0), (1, 2), (2, 1), (3...  10.4 us
    reduce_sum x6, other arithmetic, attend_head(): weights = (expo / jnp.sum(expo, axis=1, keepdims=True)).astype(jnp.bfloat16)  8.47 us
  transfers between devices with their start and end apart: 9, of which 6 were waited for; matrix products, arithmetic and copies ran while one was open for 21% of the time, Pallas kernels for 0%

profile of v16, /device:TPU:1, one launch (start us, length us, event | category | flops | bytes accessed | tf_op | source)
XLA Modules:
  0.0 304.4 jit_solution(14740064739235814990)
XLA Ops:
  6.5 1.8 pad_maximum_fusion.1
  8.3 0.8 constant_dynamic-slice_fusion
  9.1 1.5 convolution_convert_fusion
  10.6 2.7 copy.16
  13.3 7.0 %all-to-all-start = ((bf16[16,128,768]{2,1,0:T(8,128)(2,1)}), bf16[16,128,768]{2,1,0:T(8,128)(2,1)S(1)}, u32[]{:S(2)}, u32[]{:S(2)}) async-start(bf16[16,128,768]{2,1,0:T(8,128)(2,1)} %copy.16), calls=%async_computation | async-start | bytes 6291456 | tf_op jit(solution)/shard_map/all_to_all | solution.py:63
  20.3 10.4 %collective-permute-start = (bf16[768,768]{1,0:T(8,128)(2,1)}, bf16[768,768]{1,0:T(8,128)(2,1)}, u32[]{:S(2)}, u32[]{:S(2)}) collective-permute-start(bf16[768,768]{1,0:T(8,128)(2,1)} %param.17), channel_id=1, source_target_pairs={{0,0},{4,64},{64,4},{68,68},{1,1},{5,65},{65,5},{69,69},{2,2},{6,6... | collective-permute-start | bytes 3538952 | tf_op jit(solution)/shard_map/ppermute | solution.py:41
  30.7 0.8 scatter_custom_fusion
  31.5 0.8 gather_fusion
  33.4 38.8 %all-to-all-done = bf16[16,128,768]{2,1,0:T(8,128)(2,1)S(1)} async-done(((bf16[16,128,768]{2,1,0:T(8,128)(2,1)}), bf16[16,128,768]{2,1,0:T(8,128)(2,1)S(1)}, u32[]{:S(2)}, u32[]{:S(2)}) %all-to-all-start) | async-done | bytes 3145760 | tf_op jit(solution)/shard_map/all_to_all | solution.py:63
  72.1 1.9 fusion.39
  74.1 1.0 copy.18
  75.1 6.6 %all-gather.3.cloned.1.call-done = bf16[8192,256]{1,0:T(8,128)(2,1)} async-done(((bf16[512,256]{1,0:T(8,128)(2,1)}), bf16[8192,256]{1,0:T(8,128)(2,1)}) %all-gather.3.cloned.1.call-update) | async-done | bytes 4194320 | tf_op jit(solution)/shard_map/all_gather | solution.py:39
  81.7 2.9 gather_fusion.1
  84.5 2.4 bitcast_select_fusion
  87.9 19.1 %while.40 = (s32[]{:T(128)}, bf16[2,512,128]{1,2,0:T(8,128)(2,1)}, s32[4608]{0:T(1024)S(1)}, s32[512]{0:T(512)S(1)}, s32[2]{0:T(128)S(1)}, /*index=5*/bf16[512,7...) while((s32[]{:T(128)}, bf16[2,512,128]{1,2,0:T(8,128)(2,1)}, ...), condition=%wide.region_8.9_spmd.clone, body=%wide.region_5.8_spmd.clone.sunk | while | flops 1238700544 | bytes 31533772 | solution.py:95
  89.2 3.9 %fusion.92 = (f32[512]{0:T(512)S(1)}, f32[512,4608]{1,0:T(8,128)S(1)}) fusion(bf16[4608,128]{1,0:T(8,128)(2,1)S(1)} %get-tuple-element.829, bf16[512,768]{1,0:T(8,128)(2,1)} %get-tuple-element.828, s32[]{:T(128)S(6)} %select_n.204, s32[512]{0:T(512)S(1)} %get-tuple-element.826, s32[4608]{0:T(1024)S(1)} %get-tuple-element.825, ...), kind=kOutput, calls=%fused_computation.120.clone.1 | convolution fusion | flops 622853632 | bytes 10792964 | tf_op jit(solution)/shard_map/while/body/eval_jaxpr/dot_general | solution.py:17
  93.0 1.4 fusion.93
  94.5 2.2 fusion.94
  98.8 3.9 %fusion.92 = (f32[512]{0:T(512)S(1)}, f32[512,4608]{1,0:T(8,128)S(1)}) fusion(bf16[4608,128]{1,0:T(8,128)(2,1)S(1)} %get-tuple-element.829, bf16[512,768]{1,0:T(8,128)(2,1)} %get-tuple-element.828, s32[]{:T(128)S(6)} %select_n.204, s32[512]{0:T(512)S(1)} %get-tuple-element.826, s32[4608]{0:T(1024)S(1)} %get-tuple-element.825, ...), kind=kOutput, calls=%fused_computation.120.clone.1 | convolution fusion | flops 622853632 | bytes 10792964 | tf_op jit(solution)/shard_map/while/body/eval_jaxpr/dot_general | solution.py:17
  102.6 1.4 fusion.93
  104.0 2.2 fusion.94
  107.0 2.8 collective-permute-start.2
  109.8 17.8 %while.39 = (s32[]{:T(128)}, bf16[2,512,128]{1,2,0:T(8,128)(2,1)S(1)}, s32[4608]{0:T(1024)S(1)}, s32[512]{0:T(512)S(1)}, s32[2]{0:T(128)S(1)}, /*index=5*/bf16[5...) while((s32[]{:T(128)}, ...), condition=%wide.region_4.5_spmd.clone, body=%wide.region_1.0_spmd.clone.sunk | while | flops 1238700544 | bytes 31533264 | solution.py:95
  111.1 3.9 %fusion.87 = (f32[512]{0:T(512)S(1)}, f32[512,4608]{1,0:T(8,128)S(1)}) fusion(bf16[4608,128]{1,0:T(8,128)(2,1)S(1)} %get-tuple-element.787, bf16[512,768]{1,0:T(8,128)(2,1)} %get-tuple-element.786, s32[]{:T(128)S(6)} %select_n.203, s32[512]{0:T(512)S(1)} %get-tuple-element.784, s32[4608]{0:T(1024)S(1)} %get-tuple-element.783, ...), kind=kOutput, calls=%fused_computation.119.clone.1 | convolution fusion | flops 622853632 | bytes 10792964 | tf_op jit(solution)/shard_map/while/body/eval_jaxpr/dot_general | solution.py:17
  115.0 1.4 fusion.88
  116.4 2.2 fusion.89
  120.0 3.8 %fusion.87 = (f32[512]{0:T(512)S(1)}, f32[512,4608]{1,0:T(8,128)S(1)}) fusion(bf16[4608,128]{1,0:T(8,128)(2,1)S(1)} %get-tuple-element.787, bf16[512,768]{1,0:T(8,128)(2,1)} %get-tuple-element.786, s32[]{:T(128)S(6)} %select_n.203, s32[512]{0:T(512)S(1)} %get-tuple-element.784, s32[4608]{0:T(1024)S(1)} %get-tuple-element.783, ...), kind=kOutput, calls=%fused_computation.119.clone.1 | convolution fusion | flops 622853632 | bytes 10792964 | tf_op jit(solution)/shard_map/while/body/eval_jaxpr/dot_general | solution.py:17
  123.9 1.4 fusion.88
  125.3 2.2 fusion.89
  128.0 17.8 %while.41 = (s32[]{:T(128)}, bf16[2,512,128]{1,2,0:T(8,128)(2,1)S(1)}, s32[4608]{0:T(1024)S(1)}, s32[512]{0:T(512)S(1)}, s32[2]{0:T(128)S(1)}, /*index=5*/bf16[5...) while((s32[]{:T(128)}, ...), condition=%wide.region_12.13_spmd.clone, body=%wide.region_9.12_spmd.clone.sunk | while | flops 1238700544 | bytes 31533264 | solution.py:95
  129.3 3.9 %fusion.97 = (f32[512]{0:T(512)S(1)}, f32[512,4608]{1,0:T(8,128)S(1)}) fusion(bf16[4608,128]{1,0:T(8,128)(2,1)S(1)} %get-tuple-element.871, bf16[512,768]{1,0:T(8,128)(2,1)} %get-tuple-element.870, s32[]{:T(128)S(6)} %select_n.205, s32[512]{0:T(512)S(1)} %get-tuple-element.868, s32[4608]{0:T(1024)S(1)} %get-tuple-element.867, ...), kind=kOutput, calls=%fused_computation.121.clone.1 | convolution fusion | flops 622853632 | bytes 10792964 | tf_op jit(solution)/shard_map/while/body/eval_jaxpr/dot_general | solution.py:17
  133.1 1.4 fusion.98
  134.5 2.2 fusion.99
  138.2 3.9 %fusion.97 = (f32[512]{0:T(512)S(1)}, f32[512,4608]{1,0:T(8,128)S(1)}) fusion(bf16[4608,128]{1,0:T(8,128)(2,1)S(1)} %get-tuple-element.871, bf16[512,768]{1,0:T(8,128)(2,1)} %get-tuple-element.870, s32[]{:T(128)S(6)} %select_n.205, s32[512]{0:T(512)S(1)} %get-tuple-element.868, s32[4608]{0:T(1024)S(1)} %get-tuple-element.867, ...), kind=kOutput, calls=%fused_computation.121.clone.1 | convolution fusion | flops 622853632 | bytes 10792964 | tf_op jit(solution)/shard_map/while/body/eval_jaxpr/dot_general | solution.py:17
  142.0 1.4 fusion.98
  143.4 2.2 fusion.99
  145.8 3.1 %collective-permute-start.3 = (bf16[512,256]{0,1:T(8,128)(2,1)S(1)}, bf16[512,256]{0,1:T(8,128)(2,1)S(1)}, u32[]{:S(2)}, u32[]{:S(2)}) collective-permute-start(bf16[512,256]{0,1:T(8,128)(2,1)S(1)} %bitcast.102), channel_id=1, source_target_pairs={{0,4},{4,0},{1,5},{5,1},{2,6},{6,2},{3,7},{7,3},{8,12},{12,8},{9,1... | collective-permute-start | bytes 786440 | tf_op jit(solution)/shard_map/ppermute | solution.py:98
  148.9 53.7 %collective-permute-done.1 = bf16[512,256]{0,1:T(8,128)(2,1)S(1)} collective-permute-done((bf16[512,256]{0,1:T(8,128)(2,1)S(1)}, bf16[512,256]{0,1:T(8,128)(2,1)S(1)}, u32[]{:S(2)}, u32[]{:S(2)}) %collective-permute-start.1) | collective-permute-done | bytes 262176 | tf_op jit(solution)/shard_map/ppermute | solution.py:98
  202.6 1.0 constant_dynamic-update-slice_fusion.13
  203.6 4.6 %collective-permute-done.3 = bf16[512,256]{0,1:T(8,128)(2,1)S(1)} collective-permute-done((bf16[512,256]{0,1:T(8,128)(2,1)S(1)}, bf16[512,256]{0,1:T(8,128)(2,1)S(1)}, u32[]{:S(2)}, u32[]{:S(2)}) %collective-permute-start.3) | collective-permute-done | bytes 262176 | tf_op jit(solution)/shard_map/ppermute | solution.py:98
  208.3 1.0 constant_dynamic-update-slice_fusion.10
  209.3 1.0 constant_dynamic-update-slice_fusion.4
  211.1 3.0 collective-permute-done.4
  214.1 14.2 %bitcast_convert_fusion = bf16[1024,4,768]{0,2,1:T(8,128)(2,1)} fusion(bf16[2,4,768,768]{3,2,1,0:T(8,128)(2,1)} %bitcast.106, bf16[512,2,768]{0,2,1:T(8,128)(2,1)S(1)} %bitcast.107, bf16[512,2,768]{0,2,1:T(8,128)(2,1)S(1)} %bitcast.100, pred[]{:T(512)S(6)} %eq.128), kind=kOutput, calls=%fused_computation.48 | convolution fusion | flops 9680977920 | bytes 18874368 | tf_op jit(solution)/shard_map/dot_general | solution.py:115
  228.4 61.1 %reduce-scatter.2.cloned.1.call-done = bf16[1024,768]{0,1:T(8,128)(2,1)} async-done(((bf16[1024,3072]{0,1:T(8,128)(2,1)}), bf16[1024,768]{0,1:T(8,128)(2,1)}) %reduce-scatter.2.cloned.1.call-update) | async-done | bytes 1572880 | tf_op jit(solution)/shard_map/reduce_scatter | solution.py:119
  289.4 1.7 copy.24
  291.1 5.4 %all_to_all.14 = bf16[2,512,768]{2,1,0:T(8,128)(2,1)S(1)} all-to-all(bf16[2,512,768]{2,1,0:T(8,128)(2,1)S(1)} %bitcast.99), channel_id=1, replica_groups=mesh['ylo'=2,'x'=4,'c'=2,'yhi'=2,'z'=4] {'c'}, dimensions={0} | all-to-all | bytes 3145728 | tf_op jit(solution)/shard_map/all_to_all | solution.py:120
  296.6 1.3 pad_maximum_fusion
  (80 shorter events, 9.2 us)
Async XLA Ops:
  6.5 2.6 copy-start
  6.5 75.1 %all-gather.3.cloned.1.call-start = ((), (), s32[]{:S(2)}) async-start(), calls=%async_computation.3 | async-start | bytes 4456448 | tf_op jit(solution)/shard_map/all_gather | solution.py:39
  13.3 17.4 %copy-start.3 = (s32[64,2]{0,1:T(2,128)S(1)}, s32[64,2]{0,1:T(2,128)}, u32[]{:S(2)}) copy-start(s32[64,2]{0,1:T(2,128)} %param.16) | copy-start | bytes 1540
  13.3 19.0 %copy-start.2 = (s32[8192]{0:T(1024)S(1)}, s32[8192]{0:T(1024)}, u32[]{:S(2)}) copy-start(s32[8192]{0:T(1024)} %param.15) | copy-start | bytes 98308
  13.3 58.9 %all-to-all-start = ((bf16[16,128,768]{2,1,0:T(8,128)(2,1)}), bf16[16,128,768]{2,1,0:T(8,128)(2,1)S(1)}, u32[]{:S(2)}, u32[]{:S(2)}) async-start(bf16[16,128,768]{2,1,0:T(8,128)(2,1)} %copy.16), calls=%async_computation | async-start | bytes 6291456 | tf_op jit(solution)/shard_map/all_to_all | solution.py:63
  20.3 193.8 %all-gather.5.cloned.1.call-start = ((), (), s32[]{:S(2)}) async-start(), calls=%async_computation.4 | async-start | bytes 10616832 | tf_op jit(solution)/shard_map/all_gather | solution.py:43
  20.3 54.8 %collective-permute-start = (bf16[768,768]{1,0:T(8,128)(2,1)}, bf16[768,768]{1,0:T(8,128)(2,1)}, u32[]{:S(2)}, u32[]{:S(2)}) collective-permute-start(bf16[768,768]{1,0:T(8,128)(2,1)} %param.17), channel_id=1, source_target_pairs={{0,0},{4,64},{64,4},{68,68},{1,1},{5,65},{65,5},{69,69},{2,2},{6,6... | collective-permute-start | bytes 3538952 | tf_op jit(solution)/shard_map/ppermute | solution.py:41
  87.1 202.3 %reduce-scatter.2.cloned.1.call-start = ((), (), s32[]{:S(2)}) async-start(), calls=%async_computation.5 | async-start | bytes 7864320 | tf_op jit(solution)/shard_map/reduce_scatter | solution.py:119
  107.0 95.6 %collective-permute-start.2 = (bf16[512,256]{0,1:T(8,128)(2,1)}, bf16[512,256]{0,1:T(8,128)(2,1)}, u32[]{:S(2)}, u32[]{:S(2)}) collective-permute-start(bf16[512,256]{0,1:T(8,128)(2,1)} %bitcast.17), channel_id=1, source_target_pairs={{0,4},{4,0},{1,5},{5,1},{2,6},{6,2},{3,7},{7,3},{8,12},{12,8},{9,1... | collective-permute-start | bytes 786440 | tf_op jit(solution)/shard_map/ppermute | solution.py:98
  109.8 18.2 %copy-start.4 = (s32[2]{0:T(128)S(1)}, s32[2]{0:T(128)}, u32[]{:S(2)}) copy-start(s32[2]{0:T(128)} %iota_add_fusion.6) | copy-start | bytes 28
  127.7 74.9 %collective-permute-start.1 = (bf16[512,256]{0,1:T(8,128)(2,1)S(1)}, bf16[512,256]{0,1:T(8,128)(2,1)S(1)}, u32[]{:S(2)}, u32[]{:S(2)}) collective-permute-start(bf16[512,256]{0,1:T(8,128)(2,1)S(1)} %bitcast.104), channel_id=1, source_target_pairs={{0,4},{4,0},{1,5},{5,1},{2,6},{6,2},{3,7},{7,3},{8,12},{12,8},{9,1... | collective-permute-start | bytes 786440 | tf_op jit(solution)/shard_map/ppermute | solution.py:98
  145.8 62.4 %collective-permute-start.3 = (bf16[512,256]{0,1:T(8,128)(2,1)S(1)}, bf16[512,256]{0,1:T(8,128)(2,1)S(1)}, u32[]{:S(2)}, u32[]{:S(2)}) collective-permute-start(bf16[512,256]{0,1:T(8,128)(2,1)S(1)} %bitcast.102), channel_id=1, source_target_pairs={{0,4},{4,0},{1,5},{5,1},{2,6},{6,2},{3,7},{7,3},{8,12},{12,8},{9,1... | collective-permute-start | bytes 786440 | tf_op jit(solution)/shard_map/ppermute | solution.py:98
  210.5 3.6 %collective-permute-start.4 = (bf16[512,1536]{0,1:T(8,128)(2,1)S(1)}, bf16[512,1536]{0,1:T(8,128)(2,1)S(1)}, u32[]{:S(2)}, u32[]{:S(2)}) collective-permute-start(bf16[512,1536]{0,1:T(8,128)(2,1)S(1)} %broadcast_select_fusion), channel_id=1, source_target_pairs={{0,8},{8,0},{1,9},{9,1},{2,10},{10,2},{3,11},{11,3},{4,12},{12,4},... | collective-permute-start | bytes 4718600 | tf_op jit(solution)/shard_map/ppermute | solution.py:107
  291.1 6.8 %copy-start.1 = (bf16[512,768]{1,0:T(8,128)(2,1)S(1)}, bf16[512,768]{1,0:T(8,128)(2,1)}, u32[]{:S(2)}) copy-start(bf16[512,768]{1,0:T(8,128)(2,1)} %param.12) | copy-start | bytes 2359300
Sparse Core Ops, SparseCore 0:
  9.1 72.5 all-gather.2
  87.2 103.0 all-gather.4
  228.5 60.8 reduce-scatter.1

commit v17 on v13

--- a/solution.py
+++ b/solution.py
@@ -117,8 +117,14 @@
     )
     part = part.astype(jnp.bfloat16).reshape(h_here.shape[0], -1)
     summed = lax.psum_scatter(part, "z", scatter_dimension=1, tiled=True)
-    swapped = lax.all_to_all(summed, "c", split_axis=0, concat_axis=0, tiled=True)
-    return jnp.concatenate([swapped[:tok_rows], swapped[tok_rows:]], axis=1)
+    kept = jnp.where(low_core, summed[:tok_rows], summed[tok_rows:])
+    sent = jnp.where(low_core, summed[tok_rows:], summed[:tok_rows])
+    got = lax.ppermute(sent, "c", pair)
+    return jnp.where(
+        low_core,
+        jnp.concatenate([kept, got], axis=1),
+        jnp.concatenate([got, kept], axis=1),
+    )
 
 
 def solution(mesh):

time: 305 us -> 311 us (1.020)
  local copies, waits for them, and re-layouts: 16.6 us -> 23.7 us
  blocking collectives: 5.38 us -> 0 us
    reshape x0 -> x1, local copies, waits for them, and re-layouts: none -> 8.64 us  [shards(): part = part.astype(jnp.bfloat16).reshape(h_here.shape[0], -1)]
    all_to_all x1 -> x0, blocking collectives: 5.38 us -> none  [shards(): lax.all_to_all(summed, 'c', split_axis=0, concat_axis=0, tiled=True)]
  transfers between devices with their start and end apart: 8 -> 9, of which waited for: 6 -> 7; matrix products, arithmetic and copies ran while one was open for 20% -> 20% of each run, Pallas kernels for 0% -> 0%
where the time goes in v17:
time: 311 us; the launch traced here: 310 us
  waiting for transfers between devices  174 us (56%)
  matrix products  54.2 us (17%)
  local copies, waits for them, and re-layouts  23.7 us (8%)
  starting transfers between devices  22.2 us (7%)
  other arithmetic  17.2 us (6%)
  between operations  13.3 us (4%)
  loops' own time  4.47 us (1%)
    ppermute x2, waiting for transfers between devices, shards(): far.append(lax.ppermute(piece, 'yhi', pair))  63.1 us
    reduce_scatter x1, waiting for transfers between devices, shards(): summed = lax.psum_scatter(part, 'z', scatter_dimension=1, tiled=True)  61 us
    all_to_all x1, waiting for transfers between devices, shards(): lax.all_to_all(outgoing, SEQ, split_axis=0, concat_axis=0, tiled=True)  38.7 us
    dot_general x6, matrix products, attend_head(): lax.dot_general(q_rows, k_rows, (((1,), (1,)), ((), ())), preferred_eleme...  23.1 us
    dot_general x1, matrix products, shards(): lax.dot_general(h_split, w_here, (((1, 2), (0, 2)), ((), ())), preferred_...  14.2 us
    dot_general x6, matrix products, attend_head(): jnp.dot(weights, v_rows, preferred_element_type=jnp.float32)  13.3 us
    ppermute x1, starting transfers between devices, shards(): lax.ppermute(out_weight, ('ylo', 'yhi'), perm=[(0, 0), (1, 2), (2, 1), (3...  10.4 us
    reshape x1, local copies, waits for them, and re-layouts, shards(): part = part.astype(jnp.bfloat16).reshape(h_here.shape[0], -1)  8.64 us
  transfers between devices with their start and end apart: 9, of which 7 were waited for; matrix products, arithmetic and copies ran while one was open for 20% of the time, Pallas kernels for 0%

profile of v17, /device:TPU:1, one launch (start us, length us, event | category | flops | bytes accessed | tf_op | source)
XLA Modules:
  0.0 309.6 jit_solution(12080948575846209327)
XLA Ops:
  6.5 1.8 pad_maximum_fusion
  8.3 0.8 constant_dynamic-slice_fusion
  9.1 1.5 convolution_convert_fusion
  10.6 2.7 copy.15
  13.3 7.0 %all-to-all-start = ((bf16[16,128,768]{2,1,0:T(8,128)(2,1)}), bf16[16,128,768]{2,1,0:T(8,128)(2,1)S(1)}, u32[]{:S(2)}, u32[]{:S(2)}) async-start(bf16[16,128,768]{2,1,0:T(8,128)(2,1)} %copy.15), calls=%async_computation | async-start | bytes 6291456 | tf_op jit(solution)/shard_map/all_to_all | solution.py:63
  20.3 10.4 %collective-permute-start = (bf16[768,768]{1,0:T(8,128)(2,1)}, bf16[768,768]{1,0:T(8,128)(2,1)}, u32[]{:S(2)}, u32[]{:S(2)}) collective-permute-start(bf16[768,768]{1,0:T(8,128)(2,1)} %param.15), channel_id=1, source_target_pairs={{0,0},{4,64},{64,4},{68,68},{1,1},{5,65},{65,5},{69,69},{2,2},{6,6... | collective-permute-start | bytes 3538952 | tf_op jit(solution)/shard_map/ppermute | solution.py:41
  30.7 0.8 scatter_custom_fusion
  31.5 0.8 gather_fusion
  32.4 0.7 pad_dynamic-slice_fusion
  33.4 38.7 %all-to-all-done = bf16[16,128,768]{2,1,0:T(8,128)(2,1)S(1)} async-done(((bf16[16,128,768]{2,1,0:T(8,128)(2,1)}), bf16[16,128,768]{2,1,0:T(8,128)(2,1)S(1)}, u32[]{:S(2)}, u32[]{:S(2)}) %all-to-all-start) | async-done | bytes 3145760 | tf_op jit(solution)/shard_map/all_to_all | solution.py:63
  72.1 1.9 fusion.29
  74.1 1.0 copy.17
  75.1 6.6 %all-gather.3.cloned.1.call-done = bf16[8192,256]{1,0:T(8,128)(2,1)} async-done(((bf16[512,256]{1,0:T(8,128)(2,1)}), bf16[8192,256]{1,0:T(8,128)(2,1)}) %all-gather.3.cloned.1.call-update) | async-done | bytes 4194320 | tf_op jit(solution)/shard_map/all_gather | solution.py:39
  81.7 2.9 gather_fusion.1
  84.5 2.4 bitcast_select_fusion
  87.7 27.1 %while.26 = (s32[]{:T(128)}, bf16[3,512,128]{1,2,0:T(8,128)(2,1)S(1)}, s32[4608]{0:T(1024)S(1)}, s32[512]{0:T(512)S(1)}, s32[3]{0:T(128)S(1)}, /*index=5*/bf16[5...) while((s32[]{:T(128)}, ...), condition=%wide.region_4.5_spmd.clone, body=%wide.region_1.0_spmd.clone.sunk | while | flops 1238700544 | bytes 31533264 | solution.py:95
  89.0 3.8 %fusion.69 = (f32[512]{0:T(512)S(1)}, f32[512,4608]{1,0:T(8,128)S(1)}) fusion(bf16[4608,128]{1,0:T(8,128)(2,1)S(1)} %get-tuple-element.579, bf16[512,768]{1,0:T(8,128)(2,1)} %get-tuple-element.578, s32[]{:T(128)S(6)} %select_n.216, s32[512]{0:T(512)S(1)} %get-tuple-element.576, s32[4608]{0:T(1024)S(1)} %get-tuple-element.575, ...), kind=kOutput, calls=%fused_computation.91.clone.1 | convolution fusion | flops 622853632 | bytes 10792964 | tf_op jit(solution)/shard_map/while/body/eval_jaxpr/dot_general | solution.py:17
  92.9 1.4 fusion.70
  94.3 2.2 fusion.71
  98.1 3.9 %fusion.69 = (f32[512]{0:T(512)S(1)}, f32[512,4608]{1,0:T(8,128)S(1)}) fusion(bf16[4608,128]{1,0:T(8,128)(2,1)S(1)} %get-tuple-element.579, bf16[512,768]{1,0:T(8,128)(2,1)} %get-tuple-element.578, s32[]{:T(128)S(6)} %select_n.216, s32[512]{0:T(512)S(1)} %get-tuple-element.576, s32[4608]{0:T(1024)S(1)} %get-tuple-element.575, ...), kind=kOutput, calls=%fused_computation.91.clone.1 | convolution fusion | flops 622853632 | bytes 10792964 | tf_op jit(solution)/shard_map/while/body/eval_jaxpr/dot_general | solution.py:17
  101.9 1.4 fusion.70
  103.4 2.2 fusion.71
  107.1 3.8 %fusion.69 = (f32[512]{0:T(512)S(1)}, f32[512,4608]{1,0:T(8,128)S(1)}) fusion(bf16[4608,128]{1,0:T(8,128)(2,1)S(1)} %get-tuple-element.579, bf16[512,768]{1,0:T(8,128)(2,1)} %get-tuple-element.578, s32[]{:T(128)S(6)} %select_n.216, s32[512]{0:T(512)S(1)} %get-tuple-element.576, s32[4608]{0:T(1024)S(1)} %get-tuple-element.575, ...), kind=kOutput, calls=%fused_computation.91.clone.1 | convolution fusion | flops 622853632 | bytes 10792964 | tf_op jit(solution)/shard_map/while/body/eval_jaxpr/dot_general | solution.py:17
  111.0 1.4 fusion.70
  112.4 2.2 fusion.71
  114.8 3.0 collective-permute-start.1
  117.8 27.0 %while.27 = (s32[]{:T(128)}, bf16[3,512,128]{1,2,0:T(8,128)(2,1)S(1)}, s32[4608]{0:T(1024)S(1)}, s32[512]{0:T(512)S(1)}, s32[3]{0:T(128)S(1)}, /*index=5*/bf16[5...) while((s32[]{:T(128)}, ...), condition=%wide.region_8.9_spmd.clone, body=%wide.region_5.8_spmd.clone.sunk | while | flops 1238700544 | bytes 31533264 | solution.py:95
  119.2 3.8 %fusion.74 = (f32[512]{0:T(512)S(1)}, f32[512,4608]{1,0:T(8,128)S(1)}) fusion(bf16[4608,128]{1,0:T(8,128)(2,1)S(1)} %get-tuple-element.537, bf16[512,768]{1,0:T(8,128)(2,1)} %get-tuple-element.536, s32[]{:T(128)S(6)} %select_n.217, s32[512]{0:T(512)S(1)} %get-tuple-element.534, s32[4608]{0:T(1024)S(1)} %get-tuple-element.533, ...), kind=kOutput, calls=%fused_computation.92.clone.1 | convolution fusion | flops 622853632 | bytes 10792964 | tf_op jit(solution)/shard_map/while/body/eval_jaxpr/dot_general | solution.py:17
  123.0 1.4 fusion.75
  124.4 2.2 fusion.76
  128.2 3.9 %fusion.74 = (f32[512]{0:T(512)S(1)}, f32[512,4608]{1,0:T(8,128)S(1)}) fusion(bf16[4608,128]{1,0:T(8,128)(2,1)S(1)} %get-tuple-element.537, bf16[512,768]{1,0:T(8,128)(2,1)} %get-tuple-element.536, s32[]{:T(128)S(6)} %select_n.217, s32[512]{0:T(512)S(1)} %get-tuple-element.534, s32[4608]{0:T(1024)S(1)} %get-tuple-element.533, ...), kind=kOutput, calls=%fused_computation.92.clone.1 | convolution fusion | flops 622853632 | bytes 10792964 | tf_op jit(solution)/shard_map/while/body/eval_jaxpr/dot_general | solution.py:17
  132.0 1.4 fusion.75
  133.4 2.2 fusion.76
  137.2 3.8 %fusion.74 = (f32[512]{0:T(512)S(1)}, f32[512,4608]{1,0:T(8,128)S(1)}) fusion(bf16[4608,128]{1,0:T(8,128)(2,1)S(1)} %get-tuple-element.537, bf16[512,768]{1,0:T(8,128)(2,1)} %get-tuple-element.536, s32[]{:T(128)S(6)} %select_n.217, s32[512]{0:T(512)S(1)} %get-tuple-element.534, s32[4608]{0:T(1024)S(1)} %get-tuple-element.533, ...), kind=kOutput, calls=%fused_computation.92.clone.1 | convolution fusion | flops 622853632 | bytes 10792964 | tf_op jit(solution)/shard_map/while/body/eval_jaxpr/dot_general | solution.py:17
  141.0 1.4 fusion.75
  142.5 2.2 fusion.76
  145.1 54.8 %collective-permute-done.1 = bf16[512,384]{0,1:T(8,128)(2,1)} collective-permute-done((bf16[512,384]{0,1:T(8,128)(2,1)S(1)}, bf16[512,384]{0,1:T(8,128)(2,1)}, u32[]{:S(2)}, u32[]{:S(2)}) %collective-permute-start.1) | collective-permute-done | bytes 393248 | tf_op jit(solution)/shard_map/ppermute | solution.py:98
  199.9 8.3 %collective-permute-done.2 = bf16[512,384]{0,1:T(8,128)(2,1)S(1)} collective-permute-done((bf16[512,384]{0,1:T(8,128)(2,1)S(1)}, bf16[512,384]{0,1:T(8,128)(2,1)S(1)}, u32[]{:S(2)}, u32[]{:S(2)}) %collective-permute-start.2) | collective-permute-done | bytes 393248 | tf_op jit(solution)/shard_map/ppermute | solution.py:98
  208.2 1.5 maximum_select_fusion.2
  209.7 0.8 collective-permute-start.3
  210.5 3.0 collective-permute-done.3
  213.5 14.2 %bitcast_convert_fusion = bf16[1024,4,768]{0,2,1:T(8,128)(2,1)} fusion(bf16[2,4,768,768]{3,2,1,0:T(8,128)(2,1)} %bitcast.85, bf16[512,2,768]{0,2,1:T(8,128)(2,1)S(1)} %bitcast.86, bf16[512,2,768]{0,2,1:T(8,128)(2,1)S(1)} %bitcast.78, pred[]{:T(512)S(6)} %eq.106), kind=kOutput, calls=%fused_computation.33 | convolution fusion | flops 9680977920 | bytes 18874368 | tf_op jit(solution)/shard_map/dot_general | solution.py:115
  227.7 8.6 %copy.22 = bf16[1024,3072]{1,0:T(8,128)(2,1)} copy(bf16[1024,3072]{0,1:T(8,128)(2,1)} %bitcast.77) | data formatting | bytes 12582912 | tf_op jit(solution)/shard_map/reshape | solution.py:118
  236.4 61.0 %reduce-scatter.2.cloned.1.call-done = bf16[1024,768]{1,0:T(8,128)(2,1)} async-done(((bf16[1024,3072]{1,0:T(8,128)(2,1)}), bf16[1024,768]{1,0:T(8,128)(2,1)}) %reduce-scatter.2.cloned.1.call-update) | async-done | bytes 1572880 | tf_op jit(solution)/shard_map/reduce_scatter | solution.py:119
  297.5 1.5 broadcast_select_fusion.1
  298.9 0.7 collective-permute-start.4
  299.6 1.9 collective-permute-done.4
  301.6 1.5 maximum_select_fusion.3
  (67 shorter events, 6.3 us)
Async XLA Ops:
  6.5 2.6 copy-start
  6.5 75.1 %all-gather.3.cloned.1.call-start = ((), (), s32[]{:S(2)}) async-start(), calls=%async_computation.2 | async-start | bytes 4456448 | tf_op jit(solution)/shard_map/all_gather | solution.py:39
  13.3 17.4 %copy-start.4 = (s32[64,2]{0,1:T(2,128)S(1)}, s32[64,2]{0,1:T(2,128)}, u32[]{:S(2)}) copy-start(s32[64,2]{0,1:T(2,128)} %param.14) | copy-start | bytes 1540
  13.3 19.0 %copy-start.2 = (s32[8192]{0:T(1024)S(1)}, s32[8192]{0:T(1024)}, u32[]{:S(2)}) copy-start(s32[8192]{0:T(1024)} %param.13) | copy-start | bytes 98308
  13.3 58.9 %all-to-all-start = ((bf16[16,128,768]{2,1,0:T(8,128)(2,1)}), bf16[16,128,768]{2,1,0:T(8,128)(2,1)S(1)}, u32[]{:S(2)}, u32[]{:S(2)}) async-start(bf16[16,128,768]{2,1,0:T(8,128)(2,1)} %copy.15), calls=%async_computation | async-start | bytes 6291456 | tf_op jit(solution)/shard_map/all_to_all | solution.py:63
  20.3 193.2 %all-gather.5.cloned.1.call-start = ((), (), s32[]{:S(2)}) async-start(), calls=%async_computation.3 | async-start | bytes 10616832 | tf_op jit(solution)/shard_map/all_gather | solution.py:43
  20.3 54.8 %collective-permute-start = (bf16[768,768]{1,0:T(8,128)(2,1)}, bf16[768,768]{1,0:T(8,128)(2,1)}, u32[]{:S(2)}, u32[]{:S(2)}) collective-permute-start(bf16[768,768]{1,0:T(8,128)(2,1)} %param.15), channel_id=1, source_target_pairs={{0,0},{4,64},{64,4},{68,68},{1,1},{5,65},{65,5},{69,69},{2,2},{6,6... | collective-permute-start | bytes 3538952 | tf_op jit(solution)/shard_map/ppermute | solution.py:41
  86.9 0.7 copy-start.3
  87.1 210.3 %reduce-scatter.2.cloned.1.call-start = ((), (), s32[]{:S(2)}) async-start(), calls=%async_computation.4 | async-start | bytes 7864320 | tf_op jit(solution)/shard_map/reduce_scatter | solution.py:119
  114.8 85.1 %collective-permute-start.1 = (bf16[512,384]{0,1:T(8,128)(2,1)S(1)}, bf16[512,384]{0,1:T(8,128)(2,1)}, u32[]{:S(2)}, u32[]{:S(2)}) collective-permute-start(bf16[512,384]{0,1:T(8,128)(2,1)S(1)} %bitcast.81), channel_id=1, source_target_pairs={{0,4},{4,0},{1,5},{5,1},{2,6},{6,2},{3,7},{7,3},{8,12},{12,8},{9,1... | collective-permute-start | bytes 1179656 | tf_op jit(solution)/shard_map/ppermute | solution.py:98
  144.8 63.4 %collective-permute-start.2 = (bf16[512,384]{0,1:T(8,128)(2,1)S(1)}, bf16[512,384]{0,1:T(8,128)(2,1)S(1)}, u32[]{:S(2)}, u32[]{:S(2)}) collective-permute-start(bf16[512,384]{0,1:T(8,128)(2,1)S(1)} %bitcast.79), channel_id=1, source_target_pairs={{0,4},{4,0},{1,5},{5,1},{2,6},{6,2},{3,7},{7,3},{8,12},{12,8},{9,1... | collective-permute-start | bytes 1179656 | tf_op jit(solution)/shard_map/ppermute | solution.py:98
  209.7 3.8 %collective-permute-start.3 = (bf16[512,1536]{0,1:T(8,128)(2,1)S(1)}, bf16[512,1536]{0,1:T(8,128)(2,1)S(1)}, u32[]{:S(2)}, u32[]{:S(2)}) collective-permute-start(bf16[512,1536]{0,1:T(8,128)(2,1)S(1)} %maximum_select_fusion.2), channel_id=1, source_target_pairs={{0,8},{8,0},{1,9},{9,1},{2,10},{10,2},{3,11},{11,3},{4,12},{12,4},... | collective-permute-start | bytes 4718600 | tf_op jit(solution)/shard_map/ppermute | solution.py:107
  236.4 66.7 %copy-start.1 = (bf16[512,768]{1,0:T(8,128)(2,1)S(1)}, bf16[512,768]{1,0:T(8,128)(2,1)}, u32[]{:S(2)}) copy-start(bf16[512,768]{1,0:T(8,128)(2,1)} %param.10) | copy-start | bytes 2359300
  298.9 2.6 collective-permute-start.4
Sparse Core Ops, SparseCore 0:
  9.1 72.5 all-gather.2
  87.2 102.9 all-gather.4
  236.5 60.8 reduce-scatter.1

commit v18 on v13

--- a/solution.py
+++ b/solution.py
@@ -39,9 +39,14 @@
     kv_all = lax.all_gather(kv_local, SEQ, axis=0, tiled=True)
     kv_blocks = kv_all.reshape(blocks_all, BLOCK, 2 * kv_cols)
     w_swapped = lax.ppermute(out_weight, ("ylo", "yhi"), perm=[(0, 0), (1, 2), (2, 1), (3, 3)])
-    kv_blocks, w_swapped = lax.optimization_barrier((kv_blocks, w_swapped))
-    w_here = lax.all_gather(w_swapped, ("ylo", "x"), axis=0, tiled=True)
-    w_here = w_here.reshape(2, -1, out_weight.shape[0], out_weight.shape[1])
+    w_partner = lax.ppermute(w_swapped, "ylo", [(0, 1), (1, 0)])
+    w_pair = jnp.where(
+        lax.axis_index("ylo") == 0,
+        jnp.stack([w_swapped, w_partner]),
+        jnp.stack([w_partner, w_swapped]),
+    )
+    kv_blocks, w_pair = lax.optimization_barrier((kv_blocks, w_pair))
+    w_here = lax.all_gather(w_pair, "x", axis=1, tiled=False)
 
     target = packing[:, 0] * per_shard + packing[:, 1]
     source = jnp.zeros((blocks_all,), jnp.int32).at[target].set(

time: 305 us -> 303 us (level)
  waiting for transfers between devices: 173 us -> 147 us
  starting transfers between devices: 21.3 us -> 41.6 us
  other arithmetic: 15.5 us -> 18.9 us
    ppermute x2, waiting for transfers between devices: 63.6 us -> 11 us  [shards(): far.append(lax.ppermute(piece, 'yhi', pair))]
    ppermute x0 -> x1, waiting for transfers between devices: none -> 49.2 us  [shards(): w_partner = lax.ppermute(w_swapped, 'ylo', [(0, 1), (1, 0)])]
    all_to_all x1, waiting for transfers between devices: 38.7 us -> 0.01 us  [shards(): lax.all_to_all(outgoing, SEQ, split_axis=0, concat_axis=0, tiled=True)]
    ppermute x0 -> x1, starting transfers between devices: none -> 18.7 us  [shards(): w_partner = lax.ppermute(w_swapped, 'ylo', [(0, 1), (1, 0)])]
    all_gather x1, waiting for transfers between devices: 0.01 us -> 18.7 us  [shards(): w_here = lax.all_gather(w_pair, 'x', axis=1, tiled=False)]
    all_gather x1, waiting for transfers between devices: 6.73 us -> 0.01 us  [shards(): kv_all = lax.all_gather(kv_local, SEQ, axis=0, tiled=True)]
    reduce_scatter x1, waiting for transfers between devices: 61.1 us -> 65.4 us  [shards(): summed = lax.psum_scatter(part, 'z', scatter_dimension=1, tiled=True)]
    select_n x0 -> x1, other arithmetic: none -> 3.43 us  [shards(): jnp.where(lax.axis_index('ylo') == 0, jnp.stack([w_swapped, w_partner]),...]
  transfers between devices with their start and end apart: 8 -> 9, of which waited for: 6 -> 5; matrix products, arithmetic and copies ran while one was open for 20% -> 22% of each run, Pallas kernels for 0% -> 0%
where the time goes in v18:
time: 303 us; the launch traced here: 301 us
  waiting for transfers between devices  147 us (49%)
  matrix products  54.2 us (18%)
  starting transfers between devices  41.6 us (14%)
  other arithmetic  18.9 us (6%)
  local copies, waits for them, and re-layouts  16.4 us (5%)
  between operations  13.3 us (4%)
  blocking collectives  5.35 us (2%)
  loops' own time  4.08 us (1%)
    reduce_scatter x1, waiting for transfers between devices, shards(): summed = lax.psum_scatter(part, 'z', scatter_dimension=1, tiled=True)  65.4 us
    ppermute x1, waiting for transfers between devices, shards(): w_partner = lax.ppermute(w_swapped, 'ylo', [(0, 1), (1, 0)])  49.2 us
    dot_general x6, matrix products, attend_head(): lax.dot_general(q_rows, k_rows, (((1,), (1,)), ((), ())), preferred_eleme...  23.1 us
    ppermute x1, starting transfers between devices, shards(): w_partner = lax.ppermute(w_swapped, 'ylo', [(0, 1), (1, 0)])  18.7 us
    all_gather x1, waiting for transfers between devices, shards(): w_here = lax.all_gather(w_pair, 'x', axis=1, tiled=False)  18.7 us
    dot_general x1, matrix products, shards(): lax.dot_general(h_split, w_here, (((1, 2), (0, 2)), ((), ())), preferred_...  14.2 us
    dot_general x6, matrix products, attend_head(): jnp.dot(weights, v_rows, preferred_element_type=jnp.float32)  13.3 us
    ppermute x2, waiting for transfers between devices, shards(): far.append(lax.ppermute(piece, 'yhi', pair))  11 us
  transfers between devices with their start and end apart: 9, of which 5 were waited for; matrix products, arithmetic and copies ran while one was open for 22% of the time, Pallas kernels for 0%

profile of v18, /device:TPU:1, one launch (start us, length us, event | category | flops | bytes accessed | tf_op | source)
XLA Modules:
  0.0 301.3 jit_solution(14976628069255442830)
XLA Ops:
  6.5 1.8 pad_maximum_fusion.1
  8.4 0.8 constant_dynamic-slice_fusion
  9.1 1.5 convolution_convert_fusion
  10.6 2.7 copy.15
  13.3 7.0 %all-to-all-start = ((bf16[16,128,768]{2,1,0:T(8,128)(2,1)}), bf16[16,128,768]{2,1,0:T(8,128)(2,1)S(1)}, u32[]{:S(2)}, u32[]{:S(2)}) async-start(bf16[16,128,768]{2,1,0:T(8,128)(2,1)} %copy.15), calls=%async_computation | async-start | bytes 6291456 | tf_op jit(solution)/shard_map/all_to_all | solution.py:68
  20.3 10.4 %collective-permute-start = (bf16[768,768]{1,0:T(8,128)(2,1)}, bf16[768,768]{1,0:T(8,128)(2,1)}, u32[]{:S(2)}, u32[]{:S(2)}) collective-permute-start(bf16[768,768]{1,0:T(8,128)(2,1)} %param.15), channel_id=1, source_target_pairs={{0,0},{4,64},{64,4},{68,68},{1,1},{5,65},{65,5},{69,69},{2,2},{6,6... | collective-permute-start | bytes 3538952 | tf_op jit(solution)/shard_map/ppermute | solution.py:41
  30.7 0.8 scatter_custom_fusion
  31.5 0.8 gather_fusion
  32.4 18.7 %collective-permute-start.1 = (bf16[768,768]{1,0:T(8,128)(2,1)}, bf16[768,768]{1,0:T(8,128)(2,1)S(1)}, u32[]{:S(2)}, u32[]{:S(2)}) collective-permute-start(bf16[768,768]{1,0:T(8,128)(2,1)} %collective-permute-done), channel_id=1, source_target_pairs={{0,64},{64,0},{1,65},{65,1},{2,66},{66,2},{3,67},{67,3},{4,68},{68... | collective-permute-start | bytes 3538952 | tf_op jit(solution)/shard_map/ppermute | solution.py:42
  51.1 0.7 pad_dynamic-slice_fusion
  52.1 49.2 %collective-permute-done.1 = bf16[768,768]{1,0:T(8,128)(2,1)S(1)} collective-permute-done((bf16[768,768]{1,0:T(8,128)(2,1)}, bf16[768,768]{1,0:T(8,128)(2,1)S(1)}, u32[]{:S(2)}, u32[]{:S(2)}) %collective-permute-start.1) | collective-permute-done | bytes 1179680 | tf_op jit(solution)/shard_map/ppermute | solution.py:42
  101.3 3.4 %maximum_select_fusion.2 = bf16[2,768,768]{2,1,0:T(8,128)(2,1)} fusion(bf16[1,768,768]{2,1,0:T(8,128)(2,1)S(1)} %bitcast.92, bf16[1,768,768]{2,1,0:T(8,128)(2,1)} %bitcast.11, pred[]{:T(512)S(6)} %eq.125), kind=kLoop, calls=%fused_computation.44 | loop fusion | flops 3538944 | bytes 4718593 | tf_op jit(solution)/shard_map/jit(_where)/select_n | solution.py:43
  104.7 1.9 fusion.29
  106.7 1.0 copy.17
  107.6 2.9 gather_fusion.1
  110.5 2.4 bitcast_select_fusion
  113.6 27.1 %while.26 = (s32[]{:T(128)}, bf16[3,512,128]{1,2,0:T(8,128)(2,1)S(1)}, s32[4608]{0:T(1024)S(1)}, s32[512]{0:T(512)S(1)}, s32[3]{0:T(128)S(1)}, /*index=5*/bf16[5...) while((s32[]{:T(128)}, ...), condition=%wide.region_4.5_spmd.clone, body=%wide.region_1.4_spmd.clone.sunk | while | flops 1238700544 | bytes 31533264 | solution.py:100
  115.0 3.8 %fusion.69 = (f32[512]{0:T(512)S(1)}, f32[512,4608]{1,0:T(8,128)S(1)}) fusion(bf16[4608,128]{1,0:T(8,128)(2,1)S(1)} %get-tuple-element.579, bf16[512,768]{1,0:T(8,128)(2,1)} %get-tuple-element.578, s32[]{:T(128)S(6)} %select_n.199, s32[512]{0:T(512)S(1)} %get-tuple-element.576, s32[4608]{0:T(1024)S(1)} %get-tuple-element.575, ...), kind=kOutput, calls=%fused_computation.92.clone.1 | convolution fusion | flops 622853632 | bytes 10792964 | tf_op jit(solution)/shard_map/while/body/eval_jaxpr/dot_general | solution.py:17
  118.9 1.4 fusion.70
  120.3 2.2 fusion.71
  122.7 0.7 dynamic_slice.56
  124.1 3.9 %fusion.69 = (f32[512]{0:T(512)S(1)}, f32[512,4608]{1,0:T(8,128)S(1)}) fusion(bf16[4608,128]{1,0:T(8,128)(2,1)S(1)} %get-tuple-element.579, bf16[512,768]{1,0:T(8,128)(2,1)} %get-tuple-element.578, s32[]{:T(128)S(6)} %select_n.199, s32[512]{0:T(512)S(1)} %get-tuple-element.576, s32[4608]{0:T(1024)S(1)} %get-tuple-element.575, ...), kind=kOutput, calls=%fused_computation.92.clone.1 | convolution fusion | flops 622853632 | bytes 10792964 | tf_op jit(solution)/shard_map/while/body/eval_jaxpr/dot_general | solution.py:17
  127.9 1.4 fusion.70
  129.3 2.2 fusion.71
  133.1 3.8 %fusion.69 = (f32[512]{0:T(512)S(1)}, f32[512,4608]{1,0:T(8,128)S(1)}) fusion(bf16[4608,128]{1,0:T(8,128)(2,1)S(1)} %get-tuple-element.579, bf16[512,768]{1,0:T(8,128)(2,1)} %get-tuple-element.578, s32[]{:T(128)S(6)} %select_n.199, s32[512]{0:T(512)S(1)} %get-tuple-element.576, s32[4608]{0:T(1024)S(1)} %get-tuple-element.575, ...), kind=kOutput, calls=%fused_computation.92.clone.1 | convolution fusion | flops 622853632 | bytes 10792964 | tf_op jit(solution)/shard_map/while/body/eval_jaxpr/dot_general | solution.py:17
  137.0 1.4 fusion.70
  138.4 2.2 fusion.71
  140.7 2.9 collective-permute-start.2
  143.7 26.3 %while.27 = (s32[]{:T(128)}, bf16[3,512,128]{1,2,0:T(8,128)(2,1)S(1)}, s32[4608]{0:T(1024)S(1)}, s32[512]{0:T(512)S(1)}, s32[3]{0:T(128)S(1)}, /*index=5*/bf16[5...) while((s32[]{:T(128)}, ...), condition=%wide.region_8.9_spmd.clone, body=%wide.region_5.8_spmd.clone.sunk | while | flops 1238700544 | bytes 31533264 | solution.py:100
  144.8 3.8 %fusion.74 = (f32[512]{0:T(512)S(1)}, f32[512,4608]{1,0:T(8,128)S(1)}) fusion(bf16[4608,128]{1,0:T(8,128)(2,1)S(1)} %get-tuple-element.537, bf16[512,768]{1,0:T(8,128)(2,1)} %get-tuple-element.536, s32[]{:T(128)S(6)} %select_n.200, s32[512]{0:T(512)S(1)} %get-tuple-element.534, s32[4608]{0:T(1024)S(1)} %get-tuple-element.533, ...), kind=kOutput, calls=%fused_computation.93.clone.1 | convolution fusion | flops 622853632 | bytes 10792964 | tf_op jit(solution)/shard_map/while/body/eval_jaxpr/dot_general | solution.py:17
  148.7 1.4 fusion.75
  150.1 2.2 fusion.76
  153.6 3.8 %fusion.74 = (f32[512]{0:T(512)S(1)}, f32[512,4608]{1,0:T(8,128)S(1)}) fusion(bf16[4608,128]{1,0:T(8,128)(2,1)S(1)} %get-tuple-element.537, bf16[512,768]{1,0:T(8,128)(2,1)} %get-tuple-element.536, s32[]{:T(128)S(6)} %select_n.200, s32[512]{0:T(512)S(1)} %get-tuple-element.534, s32[4608]{0:T(1024)S(1)} %get-tuple-element.533, ...), kind=kOutput, calls=%fused_computation.93.clone.1 | convolution fusion | flops 622853632 | bytes 10792964 | tf_op jit(solution)/shard_map/while/body/eval_jaxpr/dot_general | solution.py:17
  157.5 1.4 fusion.75
  158.9 2.2 fusion.76
  162.4 3.8 %fusion.74 = (f32[512]{0:T(512)S(1)}, f32[512,4608]{1,0:T(8,128)S(1)}) fusion(bf16[4608,128]{1,0:T(8,128)(2,1)S(1)} %get-tuple-element.537, bf16[512,768]{1,0:T(8,128)(2,1)} %get-tuple-element.536, s32[]{:T(128)S(6)} %select_n.200, s32[512]{0:T(512)S(1)} %get-tuple-element.534, s32[4608]{0:T(1024)S(1)} %get-tuple-element.533, ...), kind=kOutput, calls=%fused_computation.93.clone.1 | convolution fusion | flops 622853632 | bytes 10792964 | tf_op jit(solution)/shard_map/while/body/eval_jaxpr/dot_general | solution.py:17
  166.2 1.4 fusion.75
  167.6 2.2 fusion.76
  170.2 11.0 %collective-permute-done.3 = bf16[512,384]{0,1:T(8,128)(2,1)S(1)} collective-permute-done((bf16[512,384]{0,1:T(8,128)(2,1)S(1)}, bf16[512,384]{0,1:T(8,128)(2,1)S(1)}, u32[]{:S(2)}, u32[]{:S(2)}) %collective-permute-start.3) | collective-permute-done | bytes 393248 | tf_op jit(solution)/shard_map/ppermute | solution.py:103
  181.3 1.5 maximum_select_fusion.3
  182.8 2.2 collective-permute-start.4
  184.9 3.0 %collective-permute-done.4 = bf16[512,1536]{0,1:T(8,128)(2,1)S(1)} collective-permute-done((bf16[512,1536]{0,1:T(8,128)(2,1)S(1)}, bf16[512,1536]{0,1:T(8,128)(2,1)S(1)}, u32[]{:S(2)}, u32[]{:S(2)}) %collective-permute-start.4) | collective-permute-done | bytes 1572896 | tf_op jit(solution)/shard_map/ppermute | solution.py:112
  188.0 18.7 %all-gather.6.cloned.1.call-done = bf16[2,3072,768]{2,1,0:T(8,128)(2,1)} async-done(((bf16[2,768,768]{2,1,0:T(8,128)(2,1)}), bf16[2,3072,768]{2,1,0:T(8,128)(2,1)}) %all-gather.6.cloned.1.call-update) | async-done | bytes 9437200 | tf_op jit(solution)/shard_map/all_gather | solution.py:49
  206.6 14.2 %bitcast_convert_fusion = bf16[1024,4,768]{0,2,1:T(8,128)(2,1)} fusion(bf16[2,4,768,768]{3,2,1,0:T(8,128)(2,1)} %bitcast.94, bf16[512,2,768]{0,2,1:T(8,128)(2,1)S(1)} %bitcast.95, bf16[512,2,768]{0,2,1:T(8,128)(2,1)S(1)} %bitcast.86, pred[]{:T(512)S(6)} %eq.109), kind=kOutput, calls=%fused_computation.33 | convolution fusion | flops 9680977920 | bytes 18874368 | tf_op jit(solution)/shard_map/dot_general | solution.py:120
  220.9 65.4 %reduce-scatter.2.cloned.1.call-done = bf16[1024,768]{0,1:T(8,128)(2,1)} async-done(((bf16[1024,3072]{0,1:T(8,128)(2,1)}), bf16[1024,768]{0,1:T(8,128)(2,1)}) %reduce-scatter.2.cloned.1.call-update) | async-done | bytes 1572880 | tf_op jit(solution)/shard_map/reduce_scatter | solution.py:124
  286.3 1.7 copy.22
  288.0 5.4 %all_to_all.14 = bf16[2,512,768]{2,1,0:T(8,128)(2,1)S(1)} all-to-all(bf16[2,512,768]{2,1,0:T(8,128)(2,1)S(1)} %bitcast.85), channel_id=1, replica_groups=mesh['ylo'=2,'x'=4,'c'=2,'yhi'=2,'z'=4] {'c'}, dimensions={0} | all-to-all | bytes 3145728 | tf_op jit(solution)/shard_map/all_to_all | solution.py:125
  293.5 1.3 pad_maximum_fusion
  (69 shorter events, 5.4 us)
Async XLA Ops:
  6.5 2.6 copy-start
  6.5 101.1 %all-gather.4.cloned.1.call-start = ((), (), s32[]{:S(2)}) async-start(), calls=%async_computation.3 | async-start | bytes 4456448 | tf_op jit(solution)/shard_map/all_gather | solution.py:39
  13.3 17.4 %copy-start.4 = (s32[64,2]{0,1:T(2,128)S(1)}, s32[64,2]{0,1:T(2,128)}, u32[]{:S(2)}) copy-start(s32[64,2]{0,1:T(2,128)} %param.14) | copy-start | bytes 1540
  13.3 19.0 %copy-start.2 = (s32[8192]{0:T(1024)S(1)}, s32[8192]{0:T(1024)}, u32[]{:S(2)}) copy-start(s32[8192]{0:T(1024)} %param.13) | copy-start | bytes 98308
  13.3 91.4 %all-to-all-start = ((bf16[16,128,768]{2,1,0:T(8,128)(2,1)}), bf16[16,128,768]{2,1,0:T(8,128)(2,1)S(1)}, u32[]{:S(2)}, u32[]{:S(2)}) async-start(bf16[16,128,768]{2,1,0:T(8,128)(2,1)} %copy.15), calls=%async_computation | async-start | bytes 6291456 | tf_op jit(solution)/shard_map/all_to_all | solution.py:68
  20.3 186.4 %all-gather.6.cloned.1.call-start = ((), (), s32[]{:S(2)}) async-start(), calls=%async_computation.5 | async-start | bytes 11796480 | tf_op jit(solution)/shard_map/all_gather | solution.py:49
  20.3 12.1 %collective-permute-start = (bf16[768,768]{1,0:T(8,128)(2,1)}, bf16[768,768]{1,0:T(8,128)(2,1)}, u32[]{:S(2)}, u32[]{:S(2)}) collective-permute-start(bf16[768,768]{1,0:T(8,128)(2,1)} %param.15), channel_id=1, source_target_pairs={{0,0},{4,64},{64,4},{68,68},{1,1},{5,65},{65,5},{69,69},{2,2},{6,6... | collective-permute-start | bytes 3538952 | tf_op jit(solution)/shard_map/ppermute | solution.py:41
  32.4 68.9 %collective-permute-start.1 = (bf16[768,768]{1,0:T(8,128)(2,1)}, bf16[768,768]{1,0:T(8,128)(2,1)S(1)}, u32[]{:S(2)}, u32[]{:S(2)}) collective-permute-start(bf16[768,768]{1,0:T(8,128)(2,1)} %collective-permute-done), channel_id=1, source_target_pairs={{0,64},{64,0},{1,65},{65,1},{2,66},{66,2},{3,67},{67,3},{4,68},{68... | collective-permute-start | bytes 3538952 | tf_op jit(solution)/shard_map/ppermute | solution.py:42
  112.9 0.7 copy-start.3
  113.1 173.2 %reduce-scatter.2.cloned.1.call-start = ((), (), s32[]{:S(2)}) async-start(), calls=%async_computation.4 | async-start | bytes 7864320 | tf_op jit(solution)/shard_map/reduce_scatter | solution.py:124
  140.7 29.5 %collective-permute-start.2 = (bf16[512,384]{0,1:T(8,128)(2,1)S(1)}, bf16[512,384]{0,1:T(8,128)(2,1)}, u32[]{:S(2)}, u32[]{:S(2)}) collective-permute-start(bf16[512,384]{0,1:T(8,128)(2,1)S(1)} %bitcast.89), channel_id=1, source_target_pairs={{0,4},{4,0},{1,5},{5,1},{2,6},{6,2},{3,7},{7,3},{8,12},{12,8},{9,1... | collective-permute-start | bytes 1179656 | tf_op jit(solution)/shard_map/ppermute | solution.py:103
  170.0 11.3 %collective-permute-start.3 = (bf16[512,384]{0,1:T(8,128)(2,1)S(1)}, bf16[512,384]{0,1:T(8,128)(2,1)S(1)}, u32[]{:S(2)}, u32[]{:S(2)}) collective-permute-start(bf16[512,384]{0,1:T(8,128)(2,1)S(1)} %bitcast.87), channel_id=1, source_target_pairs={{0,4},{4,0},{1,5},{5,1},{2,6},{6,2},{3,7},{7,3},{8,12},{12,8},{9,1... | collective-permute-start | bytes 1179656 | tf_op jit(solution)/shard_map/ppermute | solution.py:103
  182.8 5.2 %collective-permute-start.4 = (bf16[512,1536]{0,1:T(8,128)(2,1)S(1)}, bf16[512,1536]{0,1:T(8,128)(2,1)S(1)}, u32[]{:S(2)}, u32[]{:S(2)}) collective-permute-start(bf16[512,1536]{0,1:T(8,128)(2,1)S(1)} %maximum_select_fusion.3), channel_id=1, source_target_pairs={{0,8},{8,0},{1,9},{9,1},{2,10},{10,2},{3,11},{11,3},{4,12},{12,4},... | collective-permute-start | bytes 4718600 | tf_op jit(solution)/shard_map/ppermute | solution.py:112
  288.0 6.7 %copy-start.1 = (bf16[512,768]{1,0:T(8,128)(2,1)S(1)}, bf16[512,768]{1,0:T(8,128)(2,1)}, u32[]{:S(2)}) copy-start(bf16[512,768]{1,0:T(8,128)(2,1)} %param.10) | copy-start | bytes 2359300
Sparse Core Ops, SparseCore 0:
  9.1 80.8 all-gather.3
  113.2 93.3 all-gather.5
  221.0 65.2 reduce-scatter.1

commit v19 on v18

--- a/solution.py
+++ b/solution.py
@@ -45,8 +45,6 @@
         jnp.stack([w_swapped, w_partner]),
         jnp.stack([w_partner, w_swapped]),
     )
-    kv_blocks, w_pair = lax.optimization_barrier((kv_blocks, w_pair))
-    w_here = lax.all_gather(w_pair, "x", axis=1, tiled=False)
 
     target = packing[:, 0] * per_shard + packing[:, 1]
     source = jnp.zeros((blocks_all,), jnp.int32).at[target].set(
@@ -65,6 +63,8 @@
     outgoing = jnp.einsum(
         "db,brc->drc", routing, own_blocks, preferred_element_type=jnp.float32
     ).astype(jnp.bfloat16)
+    outgoing, w_pair = lax.optimization_barrier((outgoing, w_pair))
+    w_here = lax.all_gather(w_pair, "x", axis=1, tiled=False)
     incoming = lax.all_to_all(outgoing, SEQ, split_axis=0, concat_axis=0, tiled=True)
     arriving = packing[:, 0] == shard_index
     offset_ids = jnp.arange(per_shard, dtype=jnp.int32)

time: 303 us -> 318 us (1.050)
  waiting for transfers between devices: 147 us -> 160 us
    all_to_all x1, waiting for transfers between devices: 0.01 us -> 57.3 us  [shards(): lax.all_to_all(outgoing, SEQ, split_axis=0, concat_axis=0, tiled=True)]
    ppermute x1, waiting for transfers between devices: 49.2 us -> 27.6 us  [shards(): w_partner = lax.ppermute(w_swapped, 'ylo', [(0, 1), (1, 0)])]
    all_gather x1, waiting for transfers between devices: 18.7 us -> 0.01 us  [shards(): w_here = lax.all_gather(w_pair, 'x', axis=1, tiled=False)]
  transfers between devices with their start and end apart: 9 -> 9, of which waited for: 5 -> 5; matrix products, arithmetic and copies ran while one was open for 22% -> 23% of each run, Pallas kernels for 0% -> 0%
where the time goes in v19:
time: 318 us; the launch traced here: 317 us
  waiting for transfers between devices  160 us (50%)
  matrix products  55.4 us (17%)
  starting transfers between devices  42.3 us (13%)
  other arithmetic  19.7 us (6%)
  local copies, waits for them, and re-layouts  16.5 us (5%)
  between operations  13.3 us (4%)
  blocking collectives  5.38 us (2%)
  loops' own time  3.72 us (1%)
    reduce_scatter x1, waiting for transfers between devices, shards(): summed = lax.psum_scatter(part, 'z', scatter_dimension=1, tiled=True)  63.4 us
    all_to_all x1, waiting for transfers between devices, shards(): lax.all_to_all(outgoing, SEQ, split_axis=0, concat_axis=0, tiled=True)  57.3 us
    ppermute x1, waiting for transfers between devices, shards(): w_partner = lax.ppermute(w_swapped, 'ylo', [(0, 1), (1, 0)])  27.6 us
    dot_general x6, matrix products, attend_head(): lax.dot_general(q_rows, k_rows, (((1,), (1,)), ((), ())), preferred_eleme...  23.1 us
    ppermute x1, starting transfers between devices, shards(): w_partner = lax.ppermute(w_swapped, 'ylo', [(0, 1), (1, 0)])  20.7 us
    dot_general x1, matrix products, shards(): lax.dot_general(h_split, w_here, (((1, 2), (0, 2)), ((), ())), preferred_...  14.2 us
    dot_general x6, matrix products, attend_head(): jnp.dot(weights, v_rows, preferred_element_type=jnp.float32)  13.3 us
    ppermute x1, starting transfers between devices, shards(): lax.ppermute(out_weight, ('ylo', 'yhi'), perm=[(0, 0), (1, 2), (2, 1), (3...  10.4 us
  transfers between devices with their start and end apart: 9, of which 5 were waited for; matrix products, arithmetic and copies ran while one was open for 23% of the time, Pallas kernels for 0%

profile of v19, /device:TPU:1, one launch (start us, length us, event | category | flops | bytes accessed | tf_op | source)
XLA Modules:
  0.0 316.8 jit_solution(17794599313215504810)
XLA Ops:
  6.5 1.8 pad_maximum_fusion.1
  8.4 10.4 %collective-permute-start = (bf16[768,768]{1,0:T(8,128)(2,1)}, bf16[768,768]{1,0:T(8,128)(2,1)}, u32[]{:S(2)}, u32[]{:S(2)}) collective-permute-start(bf16[768,768]{1,0:T(8,128)(2,1)} %param.15), channel_id=1, source_target_pairs={{0,0},{4,64},{64,4},{68,68},{1,1},{5,65},{65,5},{69,69},{2,2},{6,6... | collective-permute-start | bytes 3538952 | tf_op jit(solution)/shard_map/ppermute | solution.py:41
  18.8 20.7 %collective-permute-start.1 = (bf16[768,768]{1,0:T(8,128)(2,1)}, bf16[768,768]{1,0:T(8,128)(2,1)}, u32[]{:S(2)}, u32[]{:S(2)}) collective-permute-start(bf16[768,768]{1,0:T(8,128)(2,1)} %collective-permute-done), channel_id=1, source_target_pairs={{0,64},{64,0},{1,65},{65,1},{2,66},{66,2},{3,67},{67,3},{4,68},{68... | collective-permute-start | bytes 3538952 | tf_op jit(solution)/shard_map/ppermute | solution.py:42
  39.5 0.8 constant_dynamic-slice_fusion
  40.3 2.7 convolution_convert_fusion
  43.0 27.6 %collective-permute-done.1 = bf16[768,768]{1,0:T(8,128)(2,1)} collective-permute-done((bf16[768,768]{1,0:T(8,128)(2,1)}, bf16[768,768]{1,0:T(8,128)(2,1)}, u32[]{:S(2)}, u32[]{:S(2)}) %collective-permute-start.1) | collective-permute-done | bytes 1179680 | tf_op jit(solution)/shard_map/ppermute | solution.py:42
  70.6 4.2 %maximum_select_fusion.2 = bf16[2,768,768]{2,1,0:T(8,128)(2,1)} fusion(bf16[1,768,768]{2,1,0:T(8,128)(2,1)} %bitcast.7, bf16[1,768,768]{2,1,0:T(8,128)(2,1)} %bitcast.6, pred[]{:T(512)S(6)} %eq.125), kind=kLoop, calls=%fused_computation.44 | loop fusion | flops 3538944 | bytes 4718593 | tf_op jit(solution)/shard_map/jit(_where)/select_n | solution.py:43
  74.8 2.6 copy.17
  77.4 4.9 %all-to-all-start = ((bf16[16,128,768]{2,1,0:T(8,128)(2,1)}), bf16[16,128,768]{2,1,0:T(8,128)(2,1)S(1)}, u32[]{:S(2)}, u32[]{:S(2)}) async-start(bf16[16,128,768]{2,1,0:T(8,128)(2,1)} %copy.17), calls=%async_computation | async-start | bytes 6291456 | tf_op jit(solution)/shard_map/all_to_all | solution.py:68
  82.4 0.8 scatter_custom_fusion
  83.2 0.8 gather_fusion
  84.1 0.7 pad_dynamic-slice_fusion
  85.3 57.3 %all-to-all-done = bf16[16,128,768]{2,1,0:T(8,128)(2,1)S(1)} async-done(((bf16[16,128,768]{2,1,0:T(8,128)(2,1)}), bf16[16,128,768]{2,1,0:T(8,128)(2,1)S(1)}, u32[]{:S(2)}, u32[]{:S(2)}) %all-to-all-start) | async-done | bytes 3145760 | tf_op jit(solution)/shard_map/all_to_all | solution.py:68
  142.6 1.9 fusion.29
  144.6 1.0 copy.19
  145.6 2.9 gather_fusion.1
  148.5 2.4 bitcast_select_fusion
  151.6 26.5 %while.26 = (s32[]{:T(128)}, bf16[3,512,128]{1,2,0:T(8,128)(2,1)S(1)}, s32[4608]{0:T(1024)S(1)}, s32[512]{0:T(512)S(1)}, s32[3]{0:T(128)S(1)}, /*index=5*/bf16[5...) while((s32[]{:T(128)}, ...), condition=%wide.region_4.5_spmd.clone, body=%wide.region_1.4_spmd.clone.sunk | while | flops 1238700544 | bytes 31533264 | solution.py:100
  152.8 3.9 %fusion.69 = (f32[512]{0:T(512)S(1)}, f32[512,4608]{1,0:T(8,128)S(1)}) fusion(bf16[4608,128]{1,0:T(8,128)(2,1)S(1)} %get-tuple-element.579, bf16[512,768]{1,0:T(8,128)(2,1)} %get-tuple-element.578, s32[]{:T(128)S(6)} %select_n.199, s32[512]{0:T(512)S(1)} %get-tuple-element.576, s32[4608]{0:T(1024)S(1)} %get-tuple-element.575, ...), kind=kOutput, calls=%fused_computation.92.clone.1 | convolution fusion | flops 622853632 | bytes 10792964 | tf_op jit(solution)/shard_map/while/body/eval_jaxpr/dot_general | solution.py:17
  156.7 1.4 fusion.70
  158.1 2.2 fusion.71
  161.6 3.8 %fusion.69 = (f32[512]{0:T(512)S(1)}, f32[512,4608]{1,0:T(8,128)S(1)}) fusion(bf16[4608,128]{1,0:T(8,128)(2,1)S(1)} %get-tuple-element.579, bf16[512,768]{1,0:T(8,128)(2,1)} %get-tuple-element.578, s32[]{:T(128)S(6)} %select_n.199, s32[512]{0:T(512)S(1)} %get-tuple-element.576, s32[4608]{0:T(1024)S(1)} %get-tuple-element.575, ...), kind=kOutput, calls=%fused_computation.92.clone.1 | convolution fusion | flops 622853632 | bytes 10792964 | tf_op jit(solution)/shard_map/while/body/eval_jaxpr/dot_general | solution.py:17
  165.5 1.4 fusion.70
  166.9 2.2 fusion.71
  170.5 3.8 %fusion.69 = (f32[512]{0:T(512)S(1)}, f32[512,4608]{1,0:T(8,128)S(1)}) fusion(bf16[4608,128]{1,0:T(8,128)(2,1)S(1)} %get-tuple-element.579, bf16[512,768]{1,0:T(8,128)(2,1)} %get-tuple-element.578, s32[]{:T(128)S(6)} %select_n.199, s32[512]{0:T(512)S(1)} %get-tuple-element.576, s32[4608]{0:T(1024)S(1)} %get-tuple-element.575, ...), kind=kOutput, calls=%fused_computation.92.clone.1 | convolution fusion | flops 622853632 | bytes 10792964 | tf_op jit(solution)/shard_map/while/body/eval_jaxpr/dot_general | solution.py:17
  174.3 1.4 fusion.70
  175.7 2.2 fusion.71
  178.1 1.8 collective-permute-start.2
  179.9 26.5 %while.27 = (s32[]{:T(128)}, bf16[3,512,128]{1,2,0:T(8,128)(2,1)S(1)}, s32[4608]{0:T(1024)S(1)}, s32[512]{0:T(512)S(1)}, s32[3]{0:T(128)S(1)}, /*index=5*/bf16[5...) while((s32[]{:T(128)}, ...), condition=%wide.region_8.9_spmd.clone, body=%wide.region_5.8_spmd.clone.sunk | while | flops 1238700544 | bytes 31533264 | solution.py:100
  181.1 3.8 %fusion.74 = (f32[512]{0:T(512)S(1)}, f32[512,4608]{1,0:T(8,128)S(1)}) fusion(bf16[4608,128]{1,0:T(8,128)(2,1)S(1)} %get-tuple-element.537, bf16[512,768]{1,0:T(8,128)(2,1)} %get-tuple-element.536, s32[]{:T(128)S(6)} %select_n.200, s32[512]{0:T(512)S(1)} %get-tuple-element.534, s32[4608]{0:T(1024)S(1)} %get-tuple-element.533, ...), kind=kOutput, calls=%fused_computation.93.clone.1 | convolution fusion | flops 622853632 | bytes 10792964 | tf_op jit(solution)/shard_map/while/body/eval_jaxpr/dot_general | solution.py:17
  184.9 1.4 fusion.75
  186.4 2.2 fusion.76
  189.9 3.8 %fusion.74 = (f32[512]{0:T(512)S(1)}, f32[512,4608]{1,0:T(8,128)S(1)}) fusion(bf16[4608,128]{1,0:T(8,128)(2,1)S(1)} %get-tuple-element.537, bf16[512,768]{1,0:T(8,128)(2,1)} %get-tuple-element.536, s32[]{:T(128)S(6)} %select_n.200, s32[512]{0:T(512)S(1)} %get-tuple-element.534, s32[4608]{0:T(1024)S(1)} %get-tuple-element.533, ...), kind=kOutput, calls=%fused_computation.93.clone.1 | convolution fusion | flops 622853632 | bytes 10792964 | tf_op jit(solution)/shard_map/while/body/eval_jaxpr/dot_general | solution.py:17
  193.7 1.4 fusion.75
  195.2 2.2 fusion.76
  198.7 3.8 %fusion.74 = (f32[512]{0:T(512)S(1)}, f32[512,4608]{1,0:T(8,128)S(1)}) fusion(bf16[4608,128]{1,0:T(8,128)(2,1)S(1)} %get-tuple-element.537, bf16[512,768]{1,0:T(8,128)(2,1)} %get-tuple-element.536, s32[]{:T(128)S(6)} %select_n.200, s32[512]{0:T(512)S(1)} %get-tuple-element.534, s32[4608]{0:T(1024)S(1)} %get-tuple-element.533, ...), kind=kOutput, calls=%fused_computation.93.clone.1 | convolution fusion | flops 622853632 | bytes 10792964 | tf_op jit(solution)/shard_map/while/body/eval_jaxpr/dot_general | solution.py:17
  202.6 1.4 fusion.75
  204.0 2.2 fusion.76
  206.4 1.6 collective-permute-start.3
  207.9 9.0 %collective-permute-done.3 = bf16[512,384]{0,1:T(8,128)(2,1)S(1)} collective-permute-done((bf16[512,384]{0,1:T(8,128)(2,1)S(1)}, bf16[512,384]{0,1:T(8,128)(2,1)S(1)}, u32[]{:S(2)}, u32[]{:S(2)}) %collective-permute-start.3) | collective-permute-done | bytes 393248 | tf_op jit(solution)/shard_map/ppermute | solution.py:103
  216.9 1.5 maximum_select_fusion.3
  218.4 2.6 collective-permute-start.4
  221.0 3.0 collective-permute-done.4
  224.1 14.2 %bitcast_convert_fusion = bf16[1024,4,768]{0,2,1:T(8,128)(2,1)} fusion(bf16[2,4,768,768]{3,2,1,0:T(8,128)(2,1)} %bitcast.93, bf16[512,2,768]{0,2,1:T(8,128)(2,1)S(1)} %bitcast.94, bf16[512,2,768]{0,2,1:T(8,128)(2,1)S(1)} %bitcast.86, pred[]{:T(512)S(6)} %eq.109), kind=kOutput, calls=%fused_computation.33 | convolution fusion | flops 9680977920 | bytes 18874368 | tf_op jit(solution)/shard_map/dot_general | solution.py:120
  238.3 63.4 %reduce-scatter.2.cloned.1.call-done = bf16[1024,768]{0,1:T(8,128)(2,1)} async-done(((bf16[1024,3072]{0,1:T(8,128)(2,1)}), bf16[1024,768]{0,1:T(8,128)(2,1)}) %reduce-scatter.2.cloned.1.call-update) | async-done | bytes 1572880 | tf_op jit(solution)/shard_map/reduce_scatter | solution.py:124
  301.8 1.7 copy.24
  303.5 5.4 %all_to_all.14 = bf16[2,512,768]{2,1,0:T(8,128)(2,1)S(1)} all-to-all(bf16[2,512,768]{2,1,0:T(8,128)(2,1)S(1)} %bitcast.85), channel_id=1, replica_groups=mesh['ylo'=2,'x'=4,'c'=2,'yhi'=2,'z'=4] {'c'}, dimensions={0} | all-to-all | bytes 3145728 | tf_op jit(solution)/shard_map/all_to_all | solution.py:125
  309.0 1.3 pad_maximum_fusion
  (71 shorter events, 6.0 us)
Async XLA Ops:
  6.5 33.8 %copy-start = (bf16[512,768]{1,0:T(8,128)(2,1)S(1)}, bf16[512,768]{1,0:T(8,128)(2,1)}, u32[]{:S(2)}) copy-start(bf16[512,768]{1,0:T(8,128)(2,1)} %param.10) | copy-start | bytes 2359300
  6.5 139.0 %all-gather.4.cloned.1.call-start = ((), (), s32[]{:S(2)}) async-start(), calls=%async_computation.3 | async-start | bytes 4456448 | tf_op jit(solution)/shard_map/all_gather | solution.py:39
  8.4 10.4 %collective-permute-start = (bf16[768,768]{1,0:T(8,128)(2,1)}, bf16[768,768]{1,0:T(8,128)(2,1)}, u32[]{:S(2)}, u32[]{:S(2)}) collective-permute-start(bf16[768,768]{1,0:T(8,128)(2,1)} %param.15), channel_id=1, source_target_pairs={{0,0},{4,64},{64,4},{68,68},{1,1},{5,65},{65,5},{69,69},{2,2},{6,6... | collective-permute-start | bytes 3538952 | tf_op jit(solution)/shard_map/ppermute | solution.py:41
  18.8 51.8 %collective-permute-start.1 = (bf16[768,768]{1,0:T(8,128)(2,1)}, bf16[768,768]{1,0:T(8,128)(2,1)}, u32[]{:S(2)}, u32[]{:S(2)}) collective-permute-start(bf16[768,768]{1,0:T(8,128)(2,1)} %collective-permute-done), channel_id=1, source_target_pairs={{0,64},{64,0},{1,65},{65,1},{2,66},{66,2},{3,67},{67,3},{4,68},{68... | collective-permute-start | bytes 3538952 | tf_op jit(solution)/shard_map/ppermute | solution.py:42
  43.0 31.8 %copy-start.2 = (bf16[16,128,768]{2,0,1:T(8,128)(2,1)S(1)}, bf16[16,128,768]{2,0,1:T(8,128)(2,1)}, u32[]{:S(2)}) copy-start(bf16[16,128,768]{2,0,1:T(8,128)(2,1)} %convolution_convert_fusion) | copy-start | bytes 9437188
  77.4 4.9 %copy-start.5 = (s32[64,2]{0,1:T(2,128)S(1)}, s32[64,2]{0,1:T(2,128)}, u32[]{:S(2)}) copy-start(s32[64,2]{0,1:T(2,128)} %param.14) | copy-start | bytes 1540
  77.4 6.6 %copy-start.3 = (s32[8192]{0:T(1024)S(1)}, s32[8192]{0:T(1024)}, u32[]{:S(2)}) copy-start(s32[8192]{0:T(1024)} %param.13) | copy-start | bytes 98308
  77.4 65.3 %all-to-all-start = ((bf16[16,128,768]{2,1,0:T(8,128)(2,1)}), bf16[16,128,768]{2,1,0:T(8,128)(2,1)S(1)}, u32[]{:S(2)}, u32[]{:S(2)}) async-start(bf16[16,128,768]{2,1,0:T(8,128)(2,1)} %copy.17), calls=%async_computation | async-start | bytes 6291456 | tf_op jit(solution)/shard_map/all_to_all | solution.py:68
  82.3 141.8 %all-gather.6.cloned.1.call-start = ((), (), s32[]{:S(2)}) async-start(), calls=%async_computation.5 | async-start | bytes 11796480 | tf_op jit(solution)/shard_map/all_gather | solution.py:67
  85.1 216.7 %reduce-scatter.2.cloned.1.call-start = ((), (), s32[]{:S(2)}) async-start(), calls=%async_computation.4 | async-start | bytes 7864320 | tf_op jit(solution)/shard_map/reduce_scatter | solution.py:124
  150.9 0.7 copy-start.4
  178.1 29.8 %collective-permute-start.2 = (bf16[512,384]{0,1:T(8,128)(2,1)S(1)}, bf16[512,384]{0,1:T(8,128)(2,1)}, u32[]{:S(2)}, u32[]{:S(2)}) collective-permute-start(bf16[512,384]{0,1:T(8,128)(2,1)S(1)} %bitcast.89), channel_id=1, source_target_pairs={{0,4},{4,0},{1,5},{5,1},{2,6},{6,2},{3,7},{7,3},{8,12},{12,8},{9,1... | collective-permute-start | bytes 1179656 | tf_op jit(solution)/shard_map/ppermute | solution.py:103
  206.4 10.6 %collective-permute-start.3 = (bf16[512,384]{0,1:T(8,128)(2,1)S(1)}, bf16[512,384]{0,1:T(8,128)(2,1)S(1)}, u32[]{:S(2)}, u32[]{:S(2)}) collective-permute-start(bf16[512,384]{0,1:T(8,128)(2,1)S(1)} %bitcast.87), channel_id=1, source_target_pairs={{0,4},{4,0},{1,5},{5,1},{2,6},{6,2},{3,7},{7,3},{8,12},{12,8},{9,1... | collective-permute-start | bytes 1179656 | tf_op jit(solution)/shard_map/ppermute | solution.py:103
  218.4 5.7 %collective-permute-start.4 = (bf16[512,1536]{0,1:T(8,128)(2,1)S(1)}, bf16[512,1536]{0,1:T(8,128)(2,1)S(1)}, u32[]{:S(2)}, u32[]{:S(2)}) collective-permute-start(bf16[512,1536]{0,1:T(8,128)(2,1)S(1)} %maximum_select_fusion.3), channel_id=1, source_target_pairs={{0,8},{8,0},{1,9},{9,1},{2,10},{10,2},{3,11},{11,3},{4,12},{12,4},... | collective-permute-start | bytes 4718600 | tf_op jit(solution)/shard_map/ppermute | solution.py:112
  303.5 6.8 %copy-start.1 = (bf16[512,768]{1,0:T(8,128)(2,1)S(1)}, bf16[512,768]{1,0:T(8,128)(2,1)}, u32[]{:S(2)}) copy-start(bf16[512,768]{1,0:T(8,128)(2,1)} %param.10) | copy-start | bytes 2359300
Sparse Core Ops, SparseCore 0:
  9.1 44.4 all-gather.3
  85.2 111.5 all-gather.5
  238.4 63.2 reduce-scatter.1
